TPU v7x, 32 devices: a whole 2x2x4 slice. The times are simulated.
32 devices in a mesh: seq: 4 (over z), fsdp: 8 (over y, x, core).
Axes of the slice: x: 2, y: 2, z: 4, core: 2. Of those that a mesh axis runs over, the one named last changes fastest.
Arguments:
- tokens: bfloat16 [16, 2048, 768], P('fsdp', 'seq'), may hold values from -6 to 6
- segment_ids: int32 [16, 2048], P('fsdp', 'seq'), may hold values from 0 to 3, never falling along the last dimension, each value on 1 to 1024 neighbouring positions
- mix_weight: bfloat16 [768, 2304], P('fsdp'), may hold values from -0.21875 to 0.21875
- query_bias: bfloat16 [768], P('fsdp'), may hold values from -3 to 3
- value_bias: bfloat16 [768], P('fsdp'), may hold values from -3 to 3
- merge_weight: bfloat16 [768, 768], P('fsdp'), may hold values from -0.875 to 0.875
- merge_bias: bfloat16 [768], P('fsdp'), may hold values from -2 to 2
- first_gain: bfloat16 [768], P('fsdp'), may hold values from 0.5 to 1.5
- first_shift: bfloat16 [768], P('fsdp'), may hold values from -2 to 2
- up_weight: bfloat16 [768, 3072], P('fsdp'), may hold values from -0.21875 to 0.21875
- up_bias: bfloat16 [3072], P('fsdp'), may hold values from -3 to 3
- down_weight: bfloat16 [3072, 768], P('fsdp'), may hold values from -0.109375 to 0.109375
- down_bias: bfloat16 [768], P('fsdp'), may hold values from -2 to 2
- second_gain: bfloat16 [768], P('fsdp'), may hold values from 0.5 to 1.5
- second_shift: bfloat16 [768], P('fsdp'), may hold values from -2 to 2
- output_grad: bfloat16 [16, 2048, 768], P('fsdp', 'seq'), may hold values from -6 to 6
Outputs:
- output: bfloat16 [16, 2048, 768], P('fsdp', 'seq')
- input_grad: float32 [16, 2048, 768], P('fsdp', 'seq')
- mix_weight_grad: float32 [768, 2304], P('fsdp')
- query_bias_grad: float32 [768], P('fsdp')
- value_bias_grad: float32 [768], P('fsdp')
- merge_weight_grad: float32 [768, 768], P('fsdp')
- merge_bias_grad: float32 [768], P('fsdp')
- first_gain_grad: float32 [768], P('fsdp')
- first_shift_grad: float32 [768], P('fsdp')
- up_weight_grad: float32 [768, 3072], P('fsdp')
- up_bias_grad: float32 [3072], P('fsdp')
- down_weight_grad: float32 [3072, 768], P('fsdp')
- down_bias_grad: float32 [768], P('fsdp')
- second_gain_grad: float32 [768], P('fsdp')
- second_shift_grad: float32 [768], P('fsdp')
Inputs may be any that keep to these rules, and one draw needn't show every extreme that they name: `segment_ids`: within a sequence the ids never fall; a document spans 1 to 1024 positions, and one in each draw spans exactly 1024.
All inputs are finite; a program needn't handle non-finite values.
Results may differ from a plain program's by a relative error of at most 0.014.
Values may be sent and summed in bfloat16 or wider, within the bound.
No kernel may reach another device: no remote copies, remote signals or barrier semaphores. Data moves between devices by JAX's collectives and lax.ppermute only.
A program may use at most 192 MiB of HBM per device.

v0:
```python
import math

import jax
import jax.numpy as jnp
from jax import lax
from jax.sharding import PartitionSpec as P

H = 12
HD = 64


eps_norm = 1e-06


def norm_forward(total, gain, shift):
    middle = jnp.mean(total, axis=-1, keepdims=True)
    centred = total - middle
    factor = lax.rsqrt(jnp.mean(centred * centred, axis=-1, keepdims=True) + eps_norm)
    normed = centred * factor
    return (normed * gain + shift, normed, factor)


def norm_backward(grad_out, normed, factor, gain):
    scaled = grad_out * gain
    inner = (
        scaled
        - jnp.mean(scaled, axis=-1, keepdims=True)
        - normed * jnp.mean(scaled * normed, axis=-1, keepdims=True)
    )
    return (factor * inner, jnp.sum(grad_out * normed, axis=0), jnp.sum(grad_out, axis=0))


def gelu_parts(hidden):
    normal_cdf = 0.5 * (1.0 + jax.scipy.special.erf(hidden * (1.0 / math.sqrt(2.0))))
    density = jnp.exp(-0.5 * hidden * hidden) * (1.0 / math.sqrt(2.0 * math.pi))
    return (hidden * normal_cdf, normal_cdf + hidden * density)


def masked_scores(queries, keys_all, row_ids, key_ids, factor):
    scores = (
        jnp.einsum("qhe,khe->hqk", queries, keys_all, preferred_element_type=jnp.float32) * factor
    )
    same = row_ids[:, None] == key_ids[None, :]
    return jnp.where(same[None, :, :], scores, -1000000000.0)


def attend_sequence(packed):
    head_rows, doc_ids = packed
    length, parts, _, size = head_rows.shape
    block = min(512, length)
    count = length // block
    factor = 1.0 / math.sqrt(size)
    keys_all = head_rows[:, :, 1]
    values_all = head_rows[:, :, 2]
    query_blocks = head_rows[:, :, 0].reshape(count, block, parts, size)
    id_blocks = doc_ids.reshape(count, block)

    def one_block(pair):
        queries, row_ids = pair
        scores = masked_scores(queries, keys_all, row_ids, doc_ids, factor)
        largest = jnp.max(scores, axis=-1, keepdims=True)
        weights = jnp.exp(scores - largest)
        totals = jnp.sum(weights, axis=-1, keepdims=True)
        probs_low = (weights / totals).astype(jnp.bfloat16)
        context = jnp.einsum(
            "hqk,khe->qhe", probs_low, values_all, preferred_element_type=jnp.float32
        )
        return (context.astype(jnp.bfloat16), (largest + jnp.log(totals))[:, :, 0])

    context, log_totals = lax.map(one_block, (query_blocks, id_blocks))
    return (context.reshape(length, parts * size), log_totals)


def attend_backward(packed):
    head_rows, doc_ids, log_totals, grad_context = packed
    length, parts, _, size = head_rows.shape
    block = min(512, length)
    count = length // block
    factor = 1.0 / math.sqrt(size)
    keys_all = head_rows[:, :, 1]
    values_all = head_rows[:, :, 2]
    query_blocks = head_rows[:, :, 0].reshape(count, block, parts, size)
    id_blocks = doc_ids.reshape(count, block)
    grad_blocks = grad_context.reshape(count, block, parts, size)

    def one_block(carry, pack):
        grad_keys, grad_values = carry
        queries, row_ids, block_totals, grad_rows = pack
        scores = masked_scores(queries, keys_all, row_ids, doc_ids, factor)
        probs = jnp.exp(scores - block_totals[:, :, None])
        grad_probs = jnp.einsum(
            "qhe,khe->hqk", grad_rows, values_all, preferred_element_type=jnp.float32
        )
        inner = jnp.sum(probs * grad_probs, axis=-1, keepdims=True)
        grad_scores = (probs * (grad_probs - inner)).astype(jnp.bfloat16)
        grad_queries = (
            jnp.einsum("hqk,khe->qhe", grad_scores, keys_all, preferred_element_type=jnp.float32)
            * factor
        )
        grad_keys = (
            grad_keys
            + jnp.einsum("hqk,qhe->khe", grad_scores, queries, preferred_element_type=jnp.float32)
            * factor
        )
        grad_values = grad_values + jnp.einsum(
            "hqk,qhe->khe",
            probs.astype(jnp.bfloat16),
            grad_rows,
            preferred_element_type=jnp.float32,
        )
        return ((grad_keys, grad_values), grad_queries)

    empty = jnp.zeros((length, parts, size), jnp.float32)
    (grad_keys, grad_values), grad_queries = lax.scan(
        one_block, (empty, empty), (query_blocks, id_blocks, log_totals, grad_blocks)
    )
    joined = jnp.stack([grad_queries.reshape(length, parts, size), grad_keys, grad_values], axis=2)
    return joined.astype(jnp.bfloat16).reshape(length, parts * 3 * size)


def column_sums(values):
    return jnp.sum(values.astype(jnp.float32), axis=0)


def per_device(
    tokens,
    segment_ids,
    mix_weight,
    query_bias,
    value_bias,
    merge_weight,
    merge_bias,
    first_gain,
    first_shift,
    up_weight,
    up_bias,
    down_weight,
    down_bias,
    second_gain,
    second_shift,
    output_grad,
):
    (
        mix_full,
        query_full,
        value_full,
        merge_full,
        merge_bias_full,
        gain_one,
        shift_one,
        up_full,
        up_bias_full,
        down_full,
        down_bias_full,
        gain_two,
        shift_two,
    ) = (
        lax.all_gather(mix_weight, "fsdp", axis=0, tiled=True),
        lax.all_gather(query_bias, "fsdp", axis=0, tiled=True),
        lax.all_gather(value_bias, "fsdp", axis=0, tiled=True),
        lax.all_gather(merge_weight, "fsdp", axis=0, tiled=True),
        lax.all_gather(merge_bias, "fsdp", axis=0, tiled=True),
        lax.all_gather(first_gain, "fsdp", axis=0, tiled=True),
        lax.all_gather(first_shift, "fsdp", axis=0, tiled=True),
        lax.all_gather(up_weight, "fsdp", axis=0, tiled=True),
        lax.all_gather(up_bias, "fsdp", axis=0, tiled=True),
        lax.all_gather(down_weight, "fsdp", axis=0, tiled=True),
        lax.all_gather(down_bias, "fsdp", axis=0, tiled=True),
        lax.all_gather(second_gain, "fsdp", axis=0, tiled=True),
        lax.all_gather(second_shift, "fsdp", axis=0, tiled=True),
    )
    groups, piece, width = tokens.shape
    rows = groups * piece
    parts = H // lax.axis_size("seq")
    flat = tokens.reshape(rows, width)
    empty_bias = jnp.zeros((H, HD), jnp.float32)
    mix_bias = jnp.stack(
        [
            query_full.astype(jnp.float32).reshape(H, HD),
            empty_bias,
            value_full.astype(jnp.float32).reshape(H, HD),
        ],
        axis=1,
    ).reshape(3 * width)
    mixed = (jnp.dot(flat, mix_full, preferred_element_type=jnp.float32) + mix_bias).astype(
        jnp.bfloat16
    )
    head_rows = lax.all_to_all(
        mixed.reshape(groups, piece, 3 * width), "seq", split_axis=2, concat_axis=1, tiled=True
    )
    length = head_rows.shape[1]
    head_rows = head_rows.reshape(groups, length, parts, 3, HD)
    full_ids = lax.all_gather(segment_ids, "seq", axis=1, tiled=True)
    context, log_totals = lax.map(attend_sequence, (head_rows, full_ids))
    context_rows = lax.all_to_all(context, "seq", split_axis=1, concat_axis=2, tiled=True).reshape(
        rows, width
    )
    attended = jnp.dot(
        context_rows, merge_full, preferred_element_type=jnp.float32
    ) + merge_bias_full.astype(jnp.float32)
    first_out, normed_one, factor_one = norm_forward(
        flat.astype(jnp.float32) + attended,
        gain_one.astype(jnp.float32),
        shift_one.astype(jnp.float32),
    )
    first_low = first_out.astype(jnp.bfloat16)
    hidden = jnp.dot(first_low, up_full, preferred_element_type=jnp.float32) + up_bias_full.astype(
        jnp.float32
    )
    active, slope = gelu_parts(hidden)
    active_low = active.astype(jnp.bfloat16)
    branch = jnp.dot(
        active_low, down_full, preferred_element_type=jnp.float32
    ) + down_bias_full.astype(jnp.float32)
    result, normed_two, factor_two = norm_forward(
        first_out + branch, gain_two.astype(jnp.float32), shift_two.astype(jnp.float32)
    )
    mix_back, merge_back, gain_one_back, up_back, down_back, gain_two_back = (
        lax.all_gather(mix_weight, "fsdp", axis=0, tiled=True),
        lax.all_gather(merge_weight, "fsdp", axis=0, tiled=True),
        lax.all_gather(first_gain, "fsdp", axis=0, tiled=True),
        lax.all_gather(up_weight, "fsdp", axis=0, tiled=True),
        lax.all_gather(down_weight, "fsdp", axis=0, tiled=True),
        lax.all_gather(second_gain, "fsdp", axis=0, tiled=True),
    )
    cotangent = output_grad.reshape(rows, width).astype(jnp.float32)
    grad_second, second_gain_grad, second_shift_grad = norm_backward(
        cotangent, normed_two, factor_two, gain_two_back.astype(jnp.float32)
    )
    grad_branch = grad_second.astype(jnp.bfloat16)
    down_grad = jnp.dot(active_low.T, grad_branch, preferred_element_type=jnp.float32)
    down_bias_grad = column_sums(grad_branch)
    grad_active = jnp.dot(grad_branch, down_back.T, preferred_element_type=jnp.float32)
    grad_hidden = (grad_active * slope).astype(jnp.bfloat16)
    up_grad = jnp.dot(first_low.T, grad_hidden, preferred_element_type=jnp.float32)
    up_bias_grad = column_sums(grad_hidden)
    grad_first = grad_second + jnp.dot(grad_hidden, up_back.T, preferred_element_type=jnp.float32)
    grad_sum, first_gain_grad, first_shift_grad = norm_backward(
        grad_first, normed_one, factor_one, gain_one_back.astype(jnp.float32)
    )
    grad_attended = grad_sum.astype(jnp.bfloat16)
    merge_grad = jnp.dot(context_rows.T, grad_attended, preferred_element_type=jnp.float32)
    merge_bias_grad = column_sums(grad_attended)
    grad_context = jnp.dot(grad_attended, merge_back.T, preferred_element_type=jnp.float32).astype(
        jnp.bfloat16
    )
    grad_heads = lax.all_to_all(
        grad_context.reshape(groups, piece, width), "seq", split_axis=2, concat_axis=1, tiled=True
    )
    grad_mixed_heads = lax.map(attend_backward, (head_rows, full_ids, log_totals, grad_heads))
    grad_mixed = lax.all_to_all(
        grad_mixed_heads, "seq", split_axis=1, concat_axis=2, tiled=True
    ).reshape(rows, 3 * width)
    mix_grad = jnp.dot(flat.T, grad_mixed, preferred_element_type=jnp.float32)
    bias_sums = column_sums(grad_mixed).reshape(H, 3, HD)
    query_grad = bias_sums[:, 0].reshape(width)
    value_grad = bias_sums[:, 2].reshape(width)
    input_grad = grad_sum + jnp.dot(grad_mixed, mix_back.T, preferred_element_type=jnp.float32)
    (
        owned_mix,
        owned_query,
        owned_value,
        owned_merge,
        owned_merge_bias,
        owned_gain_one,
        owned_shift_one,
        owned_up,
        owned_up_bias,
        owned_down,
        owned_down_bias,
        owned_gain_two,
        owned_shift_two,
    ) = (
        lax.psum_scatter(mix_grad, "fsdp", scatter_dimension=0, tiled=True),
        lax.psum_scatter(query_grad, "fsdp", scatter_dimension=0, tiled=True),
        lax.psum_scatter(value_grad, "fsdp", scatter_dimension=0, tiled=True),
        lax.psum_scatter(merge_grad, "fsdp", scatter_dimension=0, tiled=True),
        lax.psum_scatter(merge_bias_grad, "fsdp", scatter_dimension=0, tiled=True),
        lax.psum_scatter(first_gain_grad, "fsdp", scatter_dimension=0, tiled=True),
        lax.psum_scatter(first_shift_grad, "fsdp", scatter_dimension=0, tiled=True),
        lax.psum_scatter(up_grad, "fsdp", scatter_dimension=0, tiled=True),
        lax.psum_scatter(up_bias_grad, "fsdp", scatter_dimension=0, tiled=True),
        lax.psum_scatter(down_grad, "fsdp", scatter_dimension=0, tiled=True),
        lax.psum_scatter(down_bias_grad, "fsdp", scatter_dimension=0, tiled=True),
        lax.psum_scatter(second_gain_grad, "fsdp", scatter_dimension=0, tiled=True),
        lax.psum_scatter(second_shift_grad, "fsdp", scatter_dimension=0, tiled=True),
    )
    (
        final_mix,
        final_query,
        final_value,
        final_merge,
        final_merge_bias,
        final_gain_one,
        final_shift_one,
        final_up,
        final_up_bias,
        final_down,
        final_down_bias,
        final_gain_two,
        final_shift_two,
    ) = lax.psum(
        (
            owned_mix,
            owned_query,
            owned_value,
            owned_merge,
            owned_merge_bias,
            owned_gain_one,
            owned_shift_one,
            owned_up,
            owned_up_bias,
            owned_down,
            owned_down_bias,
            owned_gain_two,
            owned_shift_two,
        ),
        "seq",
    )
    return (
        result.astype(jnp.bfloat16).reshape(groups, piece, width),
        input_grad.reshape(groups, piece, width),
        final_mix,
        final_query,
        final_value,
        final_merge,
        final_merge_bias,
        final_gain_one,
        final_shift_one,
        final_up,
        final_up_bias,
        final_down,
        final_down_bias,
        final_gain_two,
        final_shift_two,
    )


def solution(mesh):
    return jax.shard_map(
        per_device,
        mesh=mesh,
        in_specs=(
            P("fsdp", "seq", None),
            P("fsdp", "seq"),
            P("fsdp", None),
            P("fsdp"),
            P("fsdp"),
            P("fsdp", None),
            P("fsdp"),
            P("fsdp"),
            P("fsdp"),
            P("fsdp", None),
            P("fsdp"),
            P("fsdp", None),
            P("fsdp"),
            P("fsdp"),
            P("fsdp"),
            P("fsdp", "seq", None),
        ),
        out_specs=(
            P("fsdp", "seq", None),
            P("fsdp", "seq", None),
            P("fsdp", None),
            P("fsdp"),
            P("fsdp"),
            P("fsdp", None),
            P("fsdp"),
            P("fsdp"),
            P("fsdp"),
            P("fsdp", None),
            P("fsdp"),
            P("fsdp", None),
            P("fsdp"),
            P("fsdp"),
            P("fsdp"),
        ),
        check_vma=False,
    )
```

profile of v0, /device:TPU:0, one launch (start us, length us, event | category | flops | bytes accessed | tf_op | source)
XLA Modules:
  0.0 1438.6 jit_solution(8007077807632148036)
XLA Ops:
  18.1 27.4 %all-reduce.20 = (bf16[768]{0:T(1024)(128)(2,1)S(1)}, bf16[768]{0:T(1024)(128)(2,1)S(1)}, bf16[768]{0:T(1024)(128)(2,1)}, bf16[768]{0:T(1024)(128)(2,1)}, bf16[7...) all-reduce(bf16[768]{0:T(1024)(128)(2,1)S(1)} %dynamic-update-slice, ...), channel_id=1, replica_groups=mesh['seq'=4,'fsdp'=8] {'fsdp'}, use_global_device_ids=true, to_apply=%add | all-reduce | flops 6144 | bytes 24576
  46.6 8.5 add_convert_fusion
  55.1 12.4 copy.70
  73.2 109.9 %all_gather.51 = s32[2,2048]{1,0:T(2,128)S(1)} all-gather(s32[2,512]{1,0:T(2,128)S(1)} %copy-done.43), channel_id=1, replica_groups=mesh['seq'=4,'fsdp'=8] {'seq'}, dimensions={1}, use_global_device_ids=true | all-gather | bytes 20480 | tf_op jit(solution)/shard_map/all_gather | solution.py:193
  192.0 9.1 reshape.242
  206.3 181.4 %while.50 = (s32[]{:T(128)}, bf16[2,2048,192]{1,2,0:T(8,128)(2,1)}, f32[2,4,3,512]{3,2,1,0:T(4,128)S(1)}, bf16[2,2048,3,3,64]{1,4,2,3,0:T(8,128)(2,1)}, s32[2,20...) while((s32[]{:T(128)}, bf16[2,2048,192]{1,2,0:T(8,128)(2,1)}, f32[2,4,3,512]{3,2,1,0:T(4,128)S(1)}, ...), condition=%wide.region_5.6_spmd, body=%wide.region_0.5_spmd.sunk | while | flops 844200448 | bytes 73970040 | solution.py:194
  210.4 82.9 %while.53 = (s32[]{:T(128)}, bf16[4,512,3,64]{1,3,2,0:T(8,128)(2,1)}, f32[4,3,512]{2,1,0:T(4,128)S(1)}, s32[4,512]{1,0:T(4,128)S(1)}, s32[2048]{0:T(1024)S(1)}, ...) while((s32[]{:T(128)}, ...), condition=%wide.region_4.4_spmd, body=%wide.region_1.3_spmd.sunk | while | flops 844200448 | bytes 43978868 | solution.py:70
  217.0 6.8 fusion.135
  223.8 7.3 fusion.136
  237.7 6.8 fusion.135
  244.5 7.3 fusion.136
  258.5 6.8 fusion.135
  265.2 7.3 fusion.136
  279.2 6.8 fusion.135
  286.0 7.3 fusion.136
  301.1 82.9 %while.53 = (s32[]{:T(128)}, bf16[4,512,3,64]{1,3,2,0:T(8,128)(2,1)}, f32[4,3,512]{2,1,0:T(4,128)S(1)}, s32[4,512]{1,0:T(4,128)S(1)}, s32[2048]{0:T(1024)S(1)}, ...) while((s32[]{:T(128)}, ...), condition=%wide.region_4.4_spmd, body=%wide.region_1.3_spmd.sunk | while | flops 844200448 | bytes 43978868 | solution.py:70
  307.7 6.8 fusion.135
  314.5 7.3 fusion.136
  328.5 6.8 fusion.135
  335.2 7.3 fusion.136
  349.2 6.8 fusion.135
  356.0 7.3 fusion.136
  369.9 6.8 fusion.135
  376.7 7.3 fusion.136
  387.8 6.2 copy.74
  399.9 8.9 all-gather
  408.8 35.7 %all-to-all-done.1 = bf16[2,2048,192]{2,0,1:T(2,128)(2,1)} async-done(((bf16[2,2048,192]{2,0,1:T(2,128)(2,1)}), bf16[2,2048,192]{2,0,1:T(2,128)(2,1)}, u32[]{:S(2)}, u32[]{:S(2)}) %all-to-all-start.1) | async-done | bytes 1572896 | tf_op jit(solution)/shard_map/all_to_all | solution.py:195
  444.5 20.5 %copy.75 = bf16[2,4,512,192]{2,0,3,1:T(2,128)(2,1)S(1)} copy(bf16[2,4,512,192]{3,0,2,1:T(2,128)(2,1)} %bitcast.23) | data formatting | bytes 3145728 | tf_op jit(solution)/shard_map/all_to_all | solution.py:195
  471.0 12.6 multiply_convert_fusion.1
  483.6 8.8 fusion.71
  498.6 13.7 convert_reduce_fusion
  512.3 6.5 multiply_reduce_fusion.1
  528.9 36.4 %all-to-all-done.2 = bf16[2,512,768]{1,0,2:T(2,128)(2,1)S(1)} async-done(((bf16[2,512,768]{1,0,2:T(2,128)(2,1)}), bf16[2,512,768]{1,0,2:T(2,128)(2,1)S(1)}, u32[]{:S(2)}, u32[]{:S(2)}) %all-to-all-start.2) | async-done | bytes 1572896 | tf_op jit(solution)/shard_map/all_to_all | solution.py:247
  565.7 266.5 %while.52 = (s32[]{:T(128)}, bf16[2,2048,576]{1,2,0:T(8,128)(2,1)}, bf16[2,2048,3,3,64]{1,4,2,3,0:T(8,128)(2,1)}, s32[2,2048]{1,0:T(2,128)S(1)}, f32[2,4,3,512]{...) while((s32[]{:T(128)}, bf16[2,2048,576]{1,2,0:T(8,128)(2,1)}, ...), condition=%wide.region_18.19_spmd, body=%wide.region_14.18_spmd.sunk | while | flops 2066708992 | bytes 248531904 | solution.py:250
  572.0 119.1 %while.54 = (s32[]{:T(128)}, f32[2048,3,64]{0,2,1:T(8,128)}, f32[2048,3,64]{0,2,1:T(8,128)}, bf16[4,512,3,64]{1,3,2,0:T(8,128)(2,1)}, bf16[4,512,3,64]{1,3,2,0:T...) while((s32[]{:T(128)}, f32[2048,3,64]{0,2,1:T(8,128)}, ...), condition=%wide.region_17.17_spmd.clone, body=%wide.region_15.16_spmd.clone.sunk | while | flops 2063563264 | bytes 156690832 | solution.py:114
  585.2 6.1 multiply_convert_fusion.3
  602.2 6.2 fusion.130
  614.2 6.1 multiply_convert_fusion.3
  632.7 6.2 fusion.130
  644.7 6.1 multiply_convert_fusion.3
  663.2 6.2 fusion.130
  675.2 6.1 multiply_convert_fusion.3
  705.0 119.1 %while.54 = (s32[]{:T(128)}, f32[2048,3,64]{0,2,1:T(8,128)}, f32[2048,3,64]{0,2,1:T(8,128)}, bf16[4,512,3,64]{1,3,2,0:T(8,128)(2,1)}, bf16[4,512,3,64]{1,3,2,0:T...) while((s32[]{:T(128)}, f32[2048,3,64]{0,2,1:T(8,128)}, ...), condition=%wide.region_17.17_spmd.clone, body=%wide.region_15.16_spmd.clone.sunk | while | flops 2063563264 | bytes 156690832 | solution.py:114
  718.2 6.1 multiply_convert_fusion.3
  735.2 6.2 fusion.130
  747.2 6.1 multiply_convert_fusion.3
  765.7 6.2 fusion.130
  777.6 6.1 multiply_convert_fusion.3
  796.2 6.2 fusion.130
  832.3 13.8 copy.80
  846.1 121.2 %all_to_all.63 = bf16[2,2048,576]{2,0,1:T(2,128)(2,1)} all-to-all(bf16[2,2048,576]{2,0,1:T(2,128)(2,1)} %copy.80), channel_id=1, replica_groups=mesh['seq'=4,'fsdp'=8] {'seq'}, dimensions={1} | all-to-all | bytes 9437184 | tf_op jit(solution)/shard_map/all_to_all | solution.py:251
  967.3 20.9 %copy.81 = bf16[2,4,512,576]{2,0,3,1:T(2,128)(2,1)} copy(bf16[2,4,512,576]{3,0,2,1:T(2,128)(2,1)} %bitcast.223) | data formatting | bytes 9437184 | tf_op jit(solution)/shard_map/all_to_all | solution.py:251
  1000.2 8.0 copy.83
  1013.8 11.8 fusion.62
  1027.4 10.2 fusion.59
  1037.9 34.1 %reduce-scatter.13.cloned.1.call-done = f32[96,2304]{1,0:T(8,128)} async-done(((f32[768,2304]{1,0:T(8,128)}), f32[96,2304]{1,0:T(8,128)}) %reduce-scatter.13.cloned.1.call-update) | async-done | bytes 884752
  1074.5 43.0 %reduce-scatter.7.cloned.1.call-done = f32[96,768]{1,0:T(8,128)} async-done(((f32[768,768]{1,0:T(8,128)}), f32[96,768]{1,0:T(8,128)}) %reduce-scatter.7.cloned.1.call-update) | async-done | bytes 294928 | tf_op jit(solution)/shard_map/reduce_scatter | solution.py:277
  1117.6 80.3 %reduce-scatter.9.cloned.1.call-done = f32[96,3072]{1,0:T(8,128)} async-done(((f32[768,3072]{1,0:T(8,128)}), f32[96,3072]{1,0:T(8,128)}) %reduce-scatter.9.cloned.1.call-update) | async-done | bytes 1179664 | tf_op jit(solution)/shard_map/reduce_scatter | solution.py:281
  1197.9 80.3 %reduce-scatter.11.cloned.1.call-done = f32[384,768]{1,0:T(8,128)} async-done(((f32[3072,768]{1,0:T(8,128)}), f32[384,768]{1,0:T(8,128)}) %reduce-scatter.11.cloned.1.call-update) | async-done | bytes 1179664 | tf_op jit(solution)/shard_map/reduce_scatter | solution.py:283
  1280.0 10.1 convert_reduce_fusion.1
  1290.4 25.0 %all-reduce.17 = (f32[768]{0:T(1024)S(1)}, f32[768]{0:T(1024)S(1)}, f32[768]{0:T(1024)S(1)}, f32[768]{0:T(1024)S(1)}, f32[768]{0:T(1024)S(1)}, /*index=5*/f32[30...) all-reduce(f32[768]{0:T(1024)S(1)} %reshape_squeeze.6, ...), channel_id=3, replica_groups=mesh['seq'=4,'fsdp'=8] {'fsdp'}, use_global_device_ids=true, to_apply=%region_22.23.clone | all-reduce | flops 9216 | bytes 73728
  1316.0 13.5 all-reduce.18
  1329.6 9.0 convolution_add_fusion.1
  1338.6 86.8 %all-reduce.23.cloned.1.call-done = (f32[96,2304]{0,1:T(8,128)}, f32[96,768]{1,0:T(8,128)}, f32[96,3072]{1,0:T(8,128)}, f32[384,768]{1,0:T(8,128)}) async-done(((f32[96,2304]{0,1:T(8,128)}, f32[96,768]{1,0:T(8,128)}, f32[96,3072]{1,0:T(8,128)}, f32[384,768]{1,0:T(8,128)}), (f32[96,2304]{0,1:T(8,128)}, f32[96,768]{1,0:T(8,128)}, f32[96,3072]{1,0:T(8,128)}, ...) | async-done | bytes 3538960 | tf_op jit(solution)/shard_map/psum | solution.py:302
  (519 shorter events, 341.9 us)
Async XLA Ops:
  7.2 39.5 %all-gather.6.cloned.1.call-start = ((), (), s32[]{:S(2)}) async-start(), calls=%async_computation.8 | async-start | bytes 3981312 | tf_op jit(solution)/shard_map/all_gather | solution.py:158
  7.9 458.7 %all-gather.8.cloned.1.call-start = ((), (), s32[]{:S(2)}) async-start(), calls=%async_computation.9 | async-start | bytes 1327104 | tf_op jit(solution)/shard_map/all_gather | solution.py:161
  8.7 462.4 %all-gather.10.cloned.1.call-start = ((), (), s32[]{:S(2)}) async-start(), calls=%async_computation.10 | async-start | bytes 5308416 | tf_op jit(solution)/shard_map/all_gather | solution.py:165
  67.5 5.7 copy-start.43
  67.5 115.6 %all-to-all-start = ((bf16[2,512,2304]{1,0,2:T(2,128)(2,1)}), bf16[2,512,2304]{1,0,2:T(2,128)(2,1)}, u32[]{:S(2)}, u32[]{:S(2)}) async-start(bf16[2,512,2304]{1,0,2:T(2,128)(2,1)} %copy.70), calls=%async_computation | async-start | bytes 9437184 | tf_op jit(solution)/shard_map/all_to_all | solution.py:188
  72.6 411.0 %all-gather.12.cloned.1.call-start = ((), (), s32[]{:S(2)}) async-start(), calls=%async_computation.11 | async-start | bytes 5308416 | tf_op jit(solution)/shard_map/all_gather | solution.py:167
  387.7 10.7 copy-start.52
  387.7 10.7 copy-start.51
  387.7 10.8 copy-start.50
  387.7 10.8 copy-start.49
  387.8 10.8 copy-start.48
  387.8 10.8 copy-start.47
  387.8 10.8 copy-start.46
  387.8 10.8 copy-start.13
  394.0 50.5 %all-to-all-start.1 = ((bf16[2,2048,192]{2,0,1:T(2,128)(2,1)}), bf16[2,2048,192]{2,0,1:T(2,128)(2,1)}, u32[]{:S(2)}, u32[]{:S(2)}) async-start(bf16[2,2048,192]{2,0,1:T(2,128)(2,1)} %copy.74), calls=%async_computation.1 | async-start | bytes 4194304 | tf_op jit(solution)/shard_map/all_to_all | solution.py:195
  398.5 120.3 %copy-start.34 = (f32[768]{0:T(1024)}, f32[768]{0:T(1024)S(1)}, u32[]{:S(2)}) copy-start(f32[768]{0:T(1024)S(1)} %convert_element_type.104) | copy-start | bytes 9220
  398.5 85.1 %copy-start.36 = (f32[768]{0:T(1024)}, f32[768]{0:T(1024)S(1)}, u32[]{:S(2)}) copy-start(f32[768]{0:T(1024)S(1)} %convert_element_type.105) | copy-start | bytes 9220
  470.5 48.4 %copy-start.9 = (f32[1024,768]{1,0:T(8,128)}, f32[1024,768]{1,0:T(8,128)S(1)}, u32[]{:S(2)}) copy-start(f32[1024,768]{1,0:T(8,128)S(1)} %get-tuple-element.490) | copy-start | bytes 9437188
  470.5 48.3 %copy-start.30 = (f32[1024]{0:T(1024)}, f32[1024]{0:T(1024)S(1)}, u32[]{:S(2)}) copy-start(f32[1024]{0:T(1024)S(1)} %broadcast_multiply_fusion.4) | copy-start | bytes 12292
  471.0 47.9 %copy-start.32 = (f32[1024]{0:T(1024)}, f32[1024]{0:T(1024)S(1)}, u32[]{:S(2)}) copy-start(f32[1024]{0:T(1024)S(1)} %add_rsqrt_fusion.1) | copy-start | bytes 12292
  495.7 16.6 %slice-start.2 = ((s8[4718592]{0:T(1024)(128)(4,1)}), s8[4194304]{0:T(1024)(128)(4,1)S(1)}, s32[]{:S(2)}) async-start(s8[4718592]{0:T(1024)(128)(4,1)} %bitcast.244), calls=%async_computation.19 | async-start | bytes 8388608
  498.6 13.7 copy-start.18
  498.6 13.7 slice-start.3
  512.3 6.5 copy-start.15
  525.2 40.0 %all-to-all-start.2 = ((bf16[2,512,768]{1,0,2:T(2,128)(2,1)}), bf16[2,512,768]{1,0,2:T(2,128)(2,1)S(1)}, u32[]{:S(2)}, u32[]{:S(2)}) async-start(bf16[2,512,768]{1,0,2:T(2,128)(2,1)} %copy.76), calls=%async_computation.2 | async-start | bytes 3145728 | tf_op jit(solution)/shard_map/all_to_all | solution.py:247
  528.8 543.2 %reduce-scatter.13.cloned.1.call-start = ((), (), s32[]{:S(2)}) async-start(), calls=%async_computation.15 | async-start | bytes 7962624
  566.2 4.0 copy-start.26
  566.2 4.0 copy-start.28
  591.3 5.8 copy-start
  591.3 5.8 copy-start.6
  620.3 5.8 copy-start
  620.3 5.8 copy-start.6
  650.8 5.8 copy-start
  650.8 5.8 copy-start.6
  681.3 5.8 copy-start
  681.3 5.8 copy-start.6
  724.3 5.8 copy-start
  724.3 5.8 copy-start.6
  753.3 5.8 copy-start
  753.3 5.8 copy-start.6
  783.8 5.8 copy-start
  783.8 5.8 copy-start.6
  814.3 5.8 copy-start
  814.3 5.8 copy-start.6
  988.2 6.2 copy-start.54
  1008.2 5.5 copy-start.10
  1008.2 5.5 copy-start.31
  1008.2 5.5 copy-start.33
  1008.3 5.5 copy-start.35
  1008.3 5.5 copy-start.37
  1008.3 109.3 %reduce-scatter.7.cloned.1.call-start = ((), (), s32[]{:S(2)}) async-start(), calls=%async_computation.12 | async-start | bytes 2654208 | tf_op jit(solution)/shard_map/reduce_scatter | solution.py:277
  1013.7 184.2 %reduce-scatter.9.cloned.1.call-start = ((), (), s32[]{:S(2)}) async-start(), calls=%async_computation.13 | async-start | bytes 10616832 | tf_op jit(solution)/shard_map/reduce_scatter | solution.py:281
  1025.6 252.7 %reduce-scatter.11.cloned.1.call-start = ((), (), s32[]{:S(2)}) async-start(), calls=%async_computation.14 | async-start | bytes 10616832 | tf_op jit(solution)/shard_map/reduce_scatter | solution.py:283
  1037.6 387.8 %all-reduce.23.cloned.1.call-start = ((), (), s32[]{:S(2)}) async-start(), calls=%async_computation.16 | async-start | bytes 7667712 | tf_op jit(solution)/shard_map/psum | solution.py:302
  1278.3 12.1 copy-start.38
  1278.3 12.0 copy-start.39
  1278.3 12.0 copy-start.40
  1278.3 12.0 copy-start.41
  1278.3 12.0 copy-start.42
  1278.3 12.0 copy-start.44
  1278.3 12.0 copy-start.45
  1278.3 51.2 %copy-start.21 = (f32[1024,768]{1,0:T(8,128)S(1)}, f32[1024,768]{1,0:T(8,128)}, u32[]{:S(2)}) copy-start(f32[1024,768]{1,0:T(8,128)} %copy-done.20) | copy-start | bytes 9437188
  1425.4 4.4 copy-start.25
  1425.4 5.4 copy-start.24
  (76 other events, 200.9 us)
Sparse Core Ops, SparseCore 0:
  9.9 36.7 all-gather.5
  48.5 23.9 all-gather.7
  74.4 38.7 all-gather.9
  114.9 38.7 all-gather.11
  1008.3 63.5 reduce-scatter.12
  1075.2 42.3 reduce-scatter.6
  1121.1 76.7 reduce-scatter.8
  1201.4 76.8 reduce-scatter.10
  1281.5 143.8 all-reduce.22
where the time goes:
time: 1440 us
  waiting for transfers between devices  400 us (28%)
  matrix products  386 us (27%)
  blocking collectives  306 us (21%)
  local copies, waits for them, and re-layouts  177 us (12%)
  other arithmetic  137 us (10%)
  between operations  17.1 us (1%)
    all_to_all x1, blocking collectives, per_device(): lax.all_to_all(grad_mixed_heads, 'seq', split_axis=1, concat_axis=2, tile...  121 us
    all_gather x1, blocking collectives, per_device(): full_ids = lax.all_gather(segment_ids, 'seq', axis=1, tiled=True)  110 us
    psum x1, waiting for transfers between devices, per_device(): lax.psum((owned_mix, owned_query, owned_value, owned_merge, owned_merge_b...  86.8 us
    reduce_scatter x1, waiting for transfers between devices, per_device(): lax.psum_scatter(down_grad, 'fsdp', scatter_dimension=0, tiled=True)  80.3 us
    reduce_scatter x1, waiting for transfers between devices, per_device(): lax.psum_scatter(up_grad, 'fsdp', scatter_dimension=0, tiled=True)  80.3 us
    dot_general x16, matrix products, masked_scores(): jnp.einsum('qhe,khe->hqk', queries, keys_all, preferred_element_type=jnp....  62.3 us
    dot_general x8, matrix products, one_block(): jnp.einsum('hqk,khe->qhe', probs_low, values_all, preferred_element_type=...  58.5 us
    reduce_sum x8, other arithmetic, one_block(): totals = jnp.sum(weights, axis=-1, keepdims=True)  54.1 us
  transfers between devices with their start and end apart: 12, of which 8 were waited for; matrix products, arithmetic and copies ran while one was open for 23% of the time, Pallas kernels for 0%

commit v1 on v0

v1 whole, which is shorter than its diff:
```python
import functools, math
import jax, jax.numpy as jnp
from jax import lax
from jax.experimental import pallas as pl
from jax.experimental.pallas import tpu as pltpu
from jax.sharding import PartitionSpec as P

LANES = 128
FAR = -1000000000.0
IDS = 4
LN2 = math.log(2.0)


def nt(a, b):
    return lax.dot_general(a, b, (((1,), (1,)), ((), ())), preferred_element_type=jnp.float32)


def nn(a, b):
    return lax.dot_general(a, b, (((1,), (0,)), ((), ())), preferred_element_type=jnp.float32)


def lane_of(rows):
    return lax.broadcasted_iota(jnp.int32, (rows, LANES), 1)


def split3(x):
    high = x.astype(jnp.bfloat16).astype(jnp.float32)
    middle = (x - high).astype(jnp.bfloat16).astype(jnp.float32)
    return high, middle, x - high - middle


def gather_blocks(info, block, count, own_ref, mate_ref, put):
    for b in range(count):
        start = pl.multiple_of(((b // 2) ^ info[1]) * block, block)

        @pl.when(info[0] == b % 2)
        def _():
            put(b, own_ref[pl.ds(start, block), :])

        @pl.when(info[0] != b % 2)
        def _():
            put(b, mate_ref[pl.ds(start, block), :])


def forward_kernel(info, q_ref, k_own, k_mate, v_own, v_mate, qx_ref, kx_ref, out_ref, ext_ref, k_all, vt_all, *, size):
    slot = pl.program_id(1)
    block = q_ref.shape[0]
    count = kx_ref.shape[0] // block
    heads = LANES // size
    lane_head = lane_of(block) // size

    @pl.when(slot == 0)
    def _():
        def put_k(b, rows):
            ext = kx_ref[b * block : (b + 1) * block, :]
            for h in range(heads):
                k_all[h, b * block : (b + 1) * block, :] = jnp.where(lane_head == h, rows, ext)

        def put_v(b, rows):
            turned = rows.T
            for h in range(heads):
                vt_all[h, :size, b * block : (b + 1) * block] = turned[h * size : (h + 1) * size]

        gather_blocks(info, block, count, k_own, k_mate, put_k)
        gather_blocks(info, block, count, v_own, v_mate, put_v)
        for h in range(heads):
            vt_all[h, size:, :] = jnp.ones((vt_all.shape[1] - size, vt_all.shape[2]), vt_all.dtype)

    rows = q_ref[...]
    qx = qx_ref[...]
    queries = [jnp.where(lane_head == h, rows, qx) for h in range(heads)]

    def step(kb, carry):
        start = pl.multiple_of(kb * block, block)
        fresh = []
        for h in range(heads):
            m, acc = carry[h]
            st = nt(k_all[h, pl.ds(start, block), :], queries[h])
            m_new = jnp.maximum(m, jnp.max(st, axis=0, keepdims=True))
            p = jnp.exp2(st - m_new).astype(jnp.bfloat16)
            acc = acc * jnp.exp2(m - m_new) + nn(vt_all[h, :, pl.ds(start, block)], p)
            fresh.append((m_new, acc))
        return tuple(fresh)

    start = tuple(
        (jnp.full((1, block), -jnp.inf, jnp.float32), jnp.zeros((vt_all.shape[1], block), jnp.float32))
        for _ in range(heads)
    )
    done = lax.fori_loop(info[2 + 2 * slot], info[3 + 2 * slot], step, start)
    sums = [acc[size : size + 1] for _, acc in done]
    out_t = jnp.concatenate([acc[:size] * (1.0 / l) for (_, acc), l in zip(done, sums)], axis=0)
    out_ref[...] = out_t.T.astype(out_ref.dtype)
    row = lax.broadcasted_iota(jnp.int32, (size, block), 0)
    parts = []
    for (m, _), l in zip(done, sums):
        pieces = split3(-(m + jnp.log2(l)))
        part = jnp.zeros((size, block), jnp.float32)
        for j, piece in enumerate(pieces):
            part = jnp.where(row == IDS + j, piece, part)
        parts.append(part)
    ext_ref[...] = (jnp.concatenate(parts[::-1], axis=0).T + qx.astype(jnp.float32)).astype(ext_ref.dtype)


def attention_forward(info, q, kv_own, kv_mate, qx, kx, size):
    rows, width = q.shape
    length = kx.shape[0]
    slots = (info.shape[0] - 2) // 2
    block = rows // slots
    pairs = width // LANES
    heads = LANES // size
    return pl.pallas_call(
        functools.partial(forward_kernel, size=size),
        grid_spec=pltpu.PrefetchScalarGridSpec(
            num_scalar_prefetch=1,
            grid=(pairs, slots),
            in_specs=[
                pl.BlockSpec((block, LANES), lambda p, s, i: (s, p)),
                pl.BlockSpec((rows, LANES), lambda p, s, i: (0, p)),
                pl.BlockSpec((rows, LANES), lambda p, s, i: (0, p)),
                pl.BlockSpec((rows, LANES), lambda p, s, i: (0, pairs + p)),
                pl.BlockSpec((rows, LANES), lambda p, s, i: (0, pairs + p)),
                pl.BlockSpec((block, LANES), lambda p, s, i: (s, 0)),
                pl.BlockSpec((length, LANES), lambda p, s, i: (0, 0)),
            ],
            out_specs=[pl.BlockSpec((block, LANES), lambda p, s, i: (s, p))] * 2,
            scratch_shapes=[
                pltpu.VMEM((heads, length, LANES), jnp.bfloat16),
                pltpu.VMEM((heads, size + 16, length), jnp.bfloat16),
            ],
        ),
        out_shape=[jax.ShapeDtypeStruct((rows, width), jnp.bfloat16)] * 2,
        compiler_params=pltpu.CompilerParams(dimension_semantics=("arbitrary", "arbitrary")),
        cost_estimate=pl.CostEstimate(
            flops=2 * rows * length * width, bytes_accessed=8 * rows * width * 2, transcendentals=rows * length * pairs
        ),
        name="attention_forward",
    )(info, q, kv_own, kv_mate, kv_own, kv_mate, qx, kx)


def backward_kernel(
    info, q_ref, ext_ref, do_ref, ctx_ref, k_own, k_mate, v_own, v_mate, kx_ref,
    dq_ref, own_ref, mate_ref, k_all, kt_all, v_all, dk_all, dv_all, *, size
):
    slot = pl.program_id(1)
    block = q_ref.shape[0]
    count = kx_ref.shape[0] // block
    heads = LANES // size
    lane = lane_of(block)
    lane_head = lane // size
    place = lane % size
    three = (place >= IDS) & (place < IDS + 3)

    @pl.when(slot == 0)
    def _():
        def put_k(b, rows):
            ext = kx_ref[b * block : (b + 1) * block, :]
            for h in range(heads):
                k_all[h, b * block : (b + 1) * block, :] = jnp.where(lane_head == h, rows, ext)
            kt_all[:, b * block : (b + 1) * block] = rows.T

        def put_v(b, rows):
            one = three.astype(rows.dtype)
            for h in range(heads):
                v_all[h, b * block : (b + 1) * block, :] = jnp.where(lane_head == h, rows, one)

        gather_blocks(info, block, count, k_own, k_mate, put_k)
        gather_blocks(info, block, count, v_own, v_mate, put_v)
        dk_all[...] = jnp.zeros_like(dk_all)
        dv_all[...] = jnp.zeros_like(dv_all)

    rows = q_ref[...]
    ext = ext_ref[...]
    grads = do_ref[...]
    zero = jnp.zeros_like(rows)
    queries = [jnp.where(lane_head == h, rows, ext) for h in range(heads)]
    plain_q = jnp.concatenate([jnp.where(lane_head == h, rows, zero) for h in range(heads)], axis=0)
    plain_do = jnp.concatenate([jnp.where(lane_head == h, grads, zero) for h in range(heads)], axis=0)
    product = grads.astype(jnp.float32) * ctx_ref[...].astype(jnp.float32)
    outs = []
    for h in range(heads):
        delta = jnp.sum(jnp.where(lane_head == h, product, 0.0), axis=1, keepdims=True)
        wide = jnp.zeros((block, LANES), jnp.float32)
        for j, piece in enumerate(split3(-delta)):
            wide = jnp.where(place == IDS + j, piece, wide)
        outs.append(jnp.where(lane_head == h, grads, wide.astype(grads.dtype)))

    def step(kb, carry):
        start = pl.multiple_of(kb * block, block)
        probs, scores, fresh = [], [], []
        for h in range(heads):
            p = jnp.exp2(nt(k_all[h, pl.ds(start, block), :], queries[h]))
            ds = (p * nt(v_all[h, pl.ds(start, block), :], outs[h])).astype(jnp.bfloat16)
            probs.append(p.astype(jnp.bfloat16))
            scores.append(ds)
            fresh.append(carry[h] + nn(kt_all[h * size : (h + 1) * size, pl.ds(start, block)], ds))
        dv_all[pl.ds(start, block), :] += nn(jnp.concatenate(probs, axis=1), plain_do)
        dk_all[pl.ds(start, block), :] += nn(jnp.concatenate(scores, axis=1), plain_q)
        return tuple(fresh)

    dq = lax.fori_loop(
        info[2 + 2 * slot], info[3 + 2 * slot], step,
        tuple(jnp.zeros((size, block), jnp.float32) for _ in range(heads)),
    )
    dq_ref[...] = (jnp.concatenate(dq, axis=0) * (1.0 / math.sqrt(size))).T.astype(dq_ref.dtype)

    @pl.when(slot == pl.num_programs(1) - 1)
    def _():
        for b in range(count):
            spot = pl.multiple_of(((b // 2) ^ info[1]) * block, block)
            for j, (total, factor) in enumerate(((dk_all, LN2), (dv_all, 1.0))):

                @pl.when(info[0] == b % 2)
                def _():
                    own_ref[j, pl.ds(spot, block), :] = (total[pl.ds(b * block, block), :] * factor).astype(own_ref.dtype)

                @pl.when(info[0] != b % 2)
                def _():
                    mate_ref[j, pl.ds(spot, block), :] = (total[pl.ds(b * block, block), :] * factor).astype(mate_ref.dtype)


def attention_backward(info, q, ext, grads, ctx, kv_own, kv_mate, kx, size):
    rows, width = q.shape
    length = kx.shape[0]
    slots = (info.shape[0] - 2) // 2
    block = rows // slots
    pairs = width // LANES
    heads = LANES // size
    tile = pl.BlockSpec((block, LANES), lambda p, s, i: (s, p))
    return pl.pallas_call(
        functools.partial(backward_kernel, size=size),
        grid_spec=pltpu.PrefetchScalarGridSpec(
            num_scalar_prefetch=1,
            grid=(pairs, slots),
            in_specs=[
                tile, tile, tile, tile,
                pl.BlockSpec((rows, LANES), lambda p, s, i: (0, p)),
                pl.BlockSpec((rows, LANES), lambda p, s, i: (0, p)),
                pl.BlockSpec((rows, LANES), lambda p, s, i: (0, pairs + p)),
                pl.BlockSpec((rows, LANES), lambda p, s, i: (0, pairs + p)),
                pl.BlockSpec((length, LANES), lambda p, s, i: (0, 0)),
            ],
            out_specs=[
                tile,
                pl.BlockSpec((2, rows, LANES), lambda p, s, i: (0, 0, p)),
                pl.BlockSpec((2, rows, LANES), lambda p, s, i: (0, 0, p)),
            ],
            scratch_shapes=[
                pltpu.VMEM((heads, length, LANES), jnp.bfloat16),
                pltpu.VMEM((LANES, length), jnp.bfloat16),
                pltpu.VMEM((heads, length, LANES), jnp.bfloat16),
                pltpu.VMEM((length, LANES), jnp.float32),
                pltpu.VMEM((length, LANES), jnp.float32),
            ],
        ),
        out_shape=[
            jax.ShapeDtypeStruct((rows, width), jnp.bfloat16),
            jax.ShapeDtypeStruct((2, rows, width), jnp.float32),
            jax.ShapeDtypeStruct((2, rows, width), jnp.bfloat16),
        ],
        compiler_params=pltpu.CompilerParams(dimension_semantics=("arbitrary", "arbitrary")),
        cost_estimate=pl.CostEstimate(
            flops=5 * rows * length * width, bytes_accessed=12 * rows * width * 2, transcendentals=rows * length * pairs
        ),
        name="attention_backward",
    )(info, q, ext, grads, ctx, kv_own, kv_mate, kv_own, kv_mate, kx)


def key_extension(ids):
    place = jnp.arange(LANES) % (LANES // 2)
    hot = ids[:, None] == place[None, :]
    return (hot | ((place >= IDS) & (place < IDS + 3))[None, :]).astype(jnp.bfloat16)


def query_extension(ids):
    place = jnp.arange(LANES) % (LANES // 2)
    other = (place < IDS)[None, :] & (ids[:, None] != place[None, :])
    return jnp.where(other, FAR, 0.0).astype(jnp.bfloat16)


H = 12
HD = 64
LOG2E = 1.0 / LN2
eps_norm = 1e-06
bf16 = jnp.bfloat16
f32 = jnp.float32


def norm_forward(total, gain, shift):
    middle = jnp.mean(total, axis=-1, keepdims=True)
    centred = total - middle
    factor = lax.rsqrt(jnp.mean(centred * centred, axis=-1, keepdims=True) + eps_norm)
    normed = centred * factor
    return (normed * gain + shift, normed, factor)


def norm_backward(grad_out, normed, factor, gain):
    scaled = grad_out * gain
    inner = (
        scaled
        - jnp.mean(scaled, axis=-1, keepdims=True)
        - normed * jnp.mean(scaled * normed, axis=-1, keepdims=True)
    )
    return (factor * inner, jnp.sum(grad_out * normed, axis=0), jnp.sum(grad_out, axis=0))


def gelu_parts(hidden):
    normal_cdf = 0.5 * (1.0 + jax.scipy.special.erf(hidden * (1.0 / math.sqrt(2.0))))
    density = jnp.exp(-0.5 * hidden * hidden) * (1.0 / math.sqrt(2.0 * math.pi))
    return (hidden * normal_cdf, normal_cdf + hidden * density)


def dot(a, b):
    return jnp.dot(a, b, preferred_element_type=f32)


def column_sums(values):
    return jnp.sum(values.astype(f32), axis=0)


def xor_pairs(size, bits):
    return [(i, i ^ bits) for i in range(size)]


def pick(values, index, axis=0):
    return lax.dynamic_index_in_dim(values, index, axis, keepdims=False)


class Places:
    def __init__(self):
        self.columns = lax.axis_size("seq")
        self.shards = lax.axis_size("fsdp")
        self.column = lax.axis_index("seq")
        shard = lax.axis_index("fsdp")
        self.core = shard & 1
        self.plane = shard >> 1

    def mate(self, values):
        return lax.ppermute(values, "fsdp", xor_pairs(self.shards, 1))

    def across(self, values, bits):
        return lax.ppermute(values, "seq", xor_pairs(self.columns, bits))

    def aside(self, values, bits):
        return lax.ppermute(values, "fsdp", xor_pairs(self.shards, 2 * bits))


def to_sequence(here, values):
    groups, piece, width = values.shape
    halves = values.reshape(groups, 2, piece // 2, width)
    kept = pick(halves, here.core, 1)
    other = here.mate(pick(halves, 1 - here.core, 1))
    both = jnp.concatenate([kept, other], axis=0)
    slots = []
    for k in range(here.columns):
        want = here.column ^ k
        part = pick(both, ((want // groups) ^ here.core) * groups + want % groups)
        slots.append(here.across(part, k) if k else part)
    return jnp.stack(slots)


def from_sequence(here, slots, groups):
    rows = jnp.stack([here.across(slots[k], k) if k else slots[k] for k in range(here.columns)])

    def of(core):
        return jnp.stack([pick(rows, here.column ^ (core * groups + j)) for j in range(groups)])

    kept = of(here.core)
    other = here.mate(of(1 - here.core))
    first = here.core == 0
    return jnp.concatenate([jnp.where(first, kept, other), jnp.where(first, other, kept)], axis=1)


def reduce_share(here, partial):
    shards, rows, width = partial.shape
    pairs = partial.reshape(shards // 2, 2, rows, width)
    total = pick(pairs, here.core, 1).astype(f32) + here.mate(pick(pairs, 1 - here.core, 1).astype(bf16)).astype(f32)
    low = total.astype(bf16)
    share = pick(total, here.plane)
    for k in range(1, shards // 2):
        share = share + here.aside(pick(low, here.plane ^ k), k).astype(f32)
    low = share.astype(bf16).reshape(2, rows // 2, width)
    side = here.column & 1
    half = pick(low, side).astype(f32) + here.across(pick(low, 1 - side), 1).astype(f32)
    step = 2
    while step < here.columns:
        low = half.astype(bf16)
        half = low.astype(f32) + here.across(low, step).astype(f32)
        step *= 2
    half = half.astype(bf16)
    other = here.across(half, 1)
    first = side == 0
    return jnp.concatenate([jnp.where(first, half, other), jnp.where(first, other, half)], axis=0).astype(f32)


def per_device(
    tokens,
    segment_ids,
    mix_weight,
    query_bias,
    value_bias,
    merge_weight,
    merge_bias,
    first_gain,
    first_shift,
    up_weight,
    up_bias,
    down_weight,
    down_bias,
    second_gain,
    second_shift,
    output_grad,
):
    here = Places()
    groups, piece, width = tokens.shape
    shards = here.shards
    own = width // shards
    hidden_size = up_weight.shape[1]
    half = piece // 2
    rows = here.columns * half
    length = here.columns * piece

    mix_local = mix_weight.reshape(own, H, 3, HD).transpose(0, 2, 1, 3).reshape(own, 3 * width)
    mix_full = lax.all_gather(mix_local, "fsdp", axis=0, tiled=True)
    small = (query_bias, value_bias, merge_bias, first_gain, first_shift, down_bias, second_gain, second_shift, up_bias)
    packed = lax.all_gather(jnp.concatenate(small).reshape(1, -1), "fsdp", axis=0, tiled=True).astype(f32)

    def vector(j):
        return packed[:, j * own : (j + 1) * own].reshape(-1)

    query_full, value_full, merge_bias_full, gain_one, shift_one, down_bias_full, gain_two, shift_two = map(vector, range(8))
    up_bias_full = packed[:, 8 * own :].reshape(-1)
    merge_full = lax.all_gather(merge_weight, "fsdp", axis=0, tiled=True)
    up_full = lax.all_gather(up_weight, "fsdp", axis=0, tiled=True)
    down_full = lax.all_gather(down_weight, "fsdp", axis=0, tiled=True)

    ids_own = to_sequence(here, segment_ids.reshape(groups, piece, 1)).reshape(here.columns, half)
    ids_mate = here.mate(ids_own)
    by_core = jnp.stack([jnp.where(here.core == 0, ids_own, ids_mate), jnp.where(here.core == 0, ids_mate, ids_own)], axis=1)
    ids = jnp.stack([pick(by_core, k ^ here.column) for k in range(here.columns)]).reshape(2 * here.columns, half)
    blocks = 2 * (jnp.arange(here.columns) ^ here.column) + here.core
    first_id, last_id = ids[:, 0], ids[:, -1]
    low = jnp.sum(last_id[None, :] < ids_own[:, :1], axis=1)
    high = jnp.sum(first_id[None, :] <= ids_own[:, -1:], axis=1)
    info = jnp.concatenate([jnp.stack([here.core, here.column]), jnp.stack([low, high], axis=1).reshape(-1)]).astype(jnp.int32)
    key_ext = key_extension(ids.reshape(length))
    query_ext = query_extension(ids_own.reshape(rows))

    flat = to_sequence(here, tokens).reshape(rows, width)
    cotangent = to_sequence(here, output_grad).reshape(rows, width).astype(f32)

    kv_bias = jnp.concatenate([jnp.zeros_like(value_full), value_full])
    key_value = (dot(flat, mix_full[:, width:]) + kv_bias).astype(bf16)
    query = ((dot(flat, mix_full[:, :width]) + query_full) * (LOG2E / math.sqrt(HD))).astype(bf16)
    key_value_mate = here.mate(key_value)
    context, ext = attention_forward(info, query, key_value, key_value_mate, query_ext, key_ext, HD)

    attended = dot(context, merge_full) + merge_bias_full
    first_out, normed_one, factor_one = norm_forward(flat.astype(f32) + attended, gain_one, shift_one)
    first_low = first_out.astype(bf16)
    hidden = dot(first_low, up_full) + up_bias_full
    active, slope = gelu_parts(hidden)
    active_low = active.astype(bf16)
    branch = dot(active_low, down_full) + down_bias_full
    result, normed_two, factor_two = norm_forward(first_out + branch, gain_two, shift_two)
    output = from_sequence(here, result.astype(bf16).reshape(here.columns, half, width), groups)

    grad_second, second_gain_grad, second_shift_grad = norm_backward(cotangent, normed_two, factor_two, gain_two)
    grad_branch = grad_second.astype(bf16)
    down_grad = dot(active_low.T, grad_branch)
    down_bias_grad = column_sums(grad_branch)
    grad_active = dot(grad_branch, down_full.T)
    grad_hidden = (grad_active * slope).astype(bf16)
    up_grad = dot(first_low.T, grad_hidden)
    up_bias_grad = column_sums(grad_hidden)
    grad_first = grad_second + dot(grad_hidden, up_full.T)
    grad_sum, first_gain_grad, first_shift_grad = norm_backward(grad_first, normed_one, factor_one, gain_one)
    grad_attended = grad_sum.astype(bf16)
    merge_grad = dot(context.T, grad_attended)
    merge_bias_grad = column_sums(grad_attended)
    grad_context = dot(grad_attended, merge_full.T).astype(bf16)

    final_down = reduce_share(here, down_grad.reshape(shards, -1, width))
    final_up = reduce_share(here, up_grad.reshape(shards, own, hidden_size))
    final_merge = reduce_share(here, merge_grad.reshape(shards, own, width))

    grad_query, grad_own, grad_mate = attention_backward(
        info, query, ext, grad_context, context, key_value, key_value_mate, key_ext, HD
    )
    grad_kv = (grad_own + here.mate(grad_mate).astype(f32)).astype(bf16)
    grad_mixed = jnp.concatenate([grad_query, grad_kv[0], grad_kv[1]], axis=1)
    mix_grad = dot(flat.T, grad_mixed)
    bias_sums = column_sums(grad_mixed)
    query_grad, value_grad = bias_sums[:width], bias_sums[2 * width :]
    input_grad = (grad_sum + dot(grad_mixed, mix_full.T)).astype(bf16)
    final_input = from_sequence(here, input_grad.reshape(here.columns, half, width), groups).astype(f32)

    final_mix = reduce_share(here, mix_grad.reshape(shards, own, 3 * width))
    final_mix = final_mix.reshape(own, 3, H, HD).transpose(0, 2, 1, 3).reshape(own, 3 * width)
    vectors = (
        query_grad,
        value_grad,
        merge_bias_grad,
        first_gain_grad,
        first_shift_grad,
        down_bias_grad,
        second_gain_grad,
        second_shift_grad,
        up_bias_grad,
    )
    packed_grad = jnp.concatenate([v.reshape(shards, -1) for v in vectors], axis=1)
    final_packed = reduce_share(here, packed_grad.reshape(shards, 2, -1)).reshape(-1)
    finals = [final_packed[j * own : (j + 1) * own] for j in range(8)] + [final_packed[8 * own :]]
    (
        final_query,
        final_value,
        final_merge_bias,
        final_gain_one,
        final_shift_one,
        final_down_bias,
        final_gain_two,
        final_shift_two,
        final_up_bias,
    ) = finals
    return (
        output,
        final_input,
        final_mix,
        final_query,
        final_value,
        final_merge,
        final_merge_bias,
        final_gain_one,
        final_shift_one,
        final_up,
        final_up_bias,
        final_down,
        final_down_bias,
        final_gain_two,
        final_shift_two,
    )


def solution(mesh):
    wide, row, thin = P("fsdp", "seq", None), P("fsdp", None), P("fsdp")
    return jax.shard_map(
        per_device,
        mesh=mesh,
        in_specs=(wide, P("fsdp", "seq"), row, thin, thin, row, thin, thin, thin, row, thin, row, thin, thin, thin, wide),
        out_specs=(wide, wide, row, thin, thin, row, thin, thin, thin, row, thin, row, thin, thin, thin),
        check_vma=False,
    )
```

time: 1440 us -> 694 us (0.48)
  matrix products: 386 us -> 90.2 us
  blocking collectives: 306 us -> 10.3 us
  waiting for transfers between devices: 400 us -> 195 us
  Pallas kernels: 0 us -> 168 us
  local copies, waits for them, and re-layouts: 177 us -> 39.7 us
  starting transfers between devices: 13.7 us -> 126 us
  other arithmetic: 137 us -> 46.1 us
    dot_general x68 -> x13, matrix products: 386 us -> 90.2 us  [dot(): return jnp.dot(a, b, preferred_element_type=f32)]
    reduce_scatter x3 -> x0, waiting for transfers between devices: 204 us -> none  [the longest x1 80.3 us: per_device(): lax.psum_scatter(down_grad, 'fsdp', scatter_dimension=0, tiled=True)]
    ppermute x0 -> x58, waiting for transfers between devices: none -> 194 us  [the longest x30 142 us: across(): return lax.ppermute(values, 'seq', xor_pairs(self.columns, bits))]
    pallas_call x0 -> x2, Pallas kernels: none -> 168 us  [the longest x1 88.7 us: attention_backward(): pl.pallas_call(functools.partial(backward_kernel, size=size), grid_spec=p...]
    ppermute x0 -> x58, starting transfers between devices: none -> 126 us  [the longest x15 70.1 us: aside(): return lax.ppermute(values, 'fsdp', xor_pairs(self.shards, 2 * bits))]
    all_to_all x1 -> x0, blocking collectives: 121 us -> none  [per_device(): lax.all_to_all(grad_mixed_heads, 'seq', split_axis=1, concat_axis=2, tile...]
    all_gather x2 -> x1, blocking collectives: 119 us -> 10.3 us  [per_device(): lax.all_gather(jnp.concatenate(small).reshape(1, -1), 'fsdp', axis=0, til...]
    psum x1 -> x0, waiting for transfers between devices: 86.8 us -> none  [per_device(): lax.psum((owned_mix, owned_query, owned_value, owned_merge, owned_merge_b...]
  transfers between devices with their start and end apart: 12 -> 62, of which waited for: 8 -> 24; matrix products, arithmetic and copies ran while one was open for 23% -> 22% of each run, Pallas kernels for 0% -> 24%
where the time goes in v1:
time: 694 us; the launch traced here: 691 us
  waiting for transfers between devices  195 us (28%)
  Pallas kernels  168 us (24%)
  starting transfers between devices  126 us (18%)
  matrix products  90.2 us (13%)
  other arithmetic  46.1 us (7%)
  local copies, waits for them, and re-layouts  39.7 us (6%)
  between operations  15.3 us (2%)
  blocking collectives  10.3 us (1%)
    ppermute x30, waiting for transfers between devices, across(): return lax.ppermute(values, 'seq', xor_pairs(self.columns, bits))  142 us
    dot_general x13, matrix products, dot(): return jnp.dot(a, b, preferred_element_type=f32)  90.2 us
    pallas_call x1, Pallas kernels, attention_backward(): pl.pallas_call(functools.partial(backward_kernel, size=size), grid_spec=p...  88.7 us
    pallas_call x1, Pallas kernels, attention_forward(): pl.pallas_call(functools.partial(forward_kernel, size=size), grid_spec=pl...  78.9 us
    ppermute x15, starting transfers between devices, aside(): return lax.ppermute(values, 'fsdp', xor_pairs(self.shards, 2 * bits))  70.1 us
    ppermute x15, waiting for transfers between devices, aside(): return lax.ppermute(values, 'fsdp', xor_pairs(self.shards, 2 * bits))  51.4 us
    ppermute x30, starting transfers between devices, across(): return lax.ppermute(values, 'seq', xor_pairs(self.columns, bits))  46 us
  transfers between devices with their start and end apart: 62, of which 24 were waited for; matrix products, arithmetic and copies ran while one was open for 22% of the time, Pallas kernels for 24%

profile of v1, /device:TPU:0, one launch (start us, length us, event | category | flops | bytes accessed | tf_op | source)
XLA Modules:
  0.0 690.5 jit_solution(562817108520234437)
XLA Ops:
  13.6 2.4 dynamic-slice_bitcast_fusion
  16.6 10.3 %all-gather.1 = bf16[8,1,1152]{2,1,0:T(2,128)(2,1)S(1)} all-gather(bf16[1,1,1152]{2,1,0:T(2,128)(2,1)S(1)} %reshape.285), channel_id=2, replica_groups=mesh['seq'=4,'fsdp'=8] {'fsdp'}, dimensions={0}, use_global_device_ids=true | all-gather | bytes 20736 | tf_op jit(solution)/shard_map/all_gather | solution.py:425
  29.0 3.6 collective-permute-start.3
  38.9 4.3 collective-permute-done.3
  43.2 23.7 %collective-permute-done.2 = bf16[256,768]{1,0:T(8,128)(2,1)S(1)} collective-permute-done((bf16[256,768]{1,0:T(8,128)(2,1)}, bf16[256,768]{1,0:T(8,128)(2,1)S(1)}, u32[]{:S(2)}, u32[]{:S(2)}) %collective-permute-start.2) | collective-permute-done | bytes 393248 | tf_op jit(solution)/shard_map/ppermute | solution.py:341
  69.3 6.2 add_convert_fusion.1.k_own.v_own
  76.1 1.9 collective-permute-start.7
  78.7 2.5 collective-permute-start.5
  88.3 2.0 collective-permute-start.17
  94.5 7.7 %collective-permute-done.17 = bf16[256,768]{1,0:T(8,128)(2,1)S(1)} collective-permute-done((bf16[256,768]{1,0:T(8,128)(2,1)S(1)}, bf16[256,768]{1,0:T(8,128)(2,1)S(1)}, u32[]{:S(2)}, u32[]{:S(2)}) %collective-permute-start.17) | collective-permute-done | bytes 393248 | tf_op jit(solution)/shard_map/ppermute | solution.py:341
  102.3 23.8 %collective-permute-done.16 = bf16[256,768]{1,0:T(8,128)(2,1)S(1)} collective-permute-done((bf16[256,768]{1,0:T(8,128)(2,1)S(1)}, bf16[256,768]{1,0:T(8,128)(2,1)S(1)}, u32[]{:S(2)}, u32[]{:S(2)}) %collective-permute-start.16) | collective-permute-done | bytes 393248 | tf_op jit(solution)/shard_map/ppermute | solution.py:341
  129.7 3.8 multiply_convert_fusion.1.q_ref
  133.6 78.9 %attention_forward.1 = (bf16[1024,768]{1,0:T(8,128)(2,1)}, bf16[1024,768]{1,0:T(8,128)(2,1)}) custom-call(s32[10]{0:T(128)} %pad_add_fusion.3.info, bf16[1024,768]{1,0:T(8,128)(2,1)} %multiply_convert_fusion.1.q_ref, bf16[1024,1536]{1,0:T(8,128)(2,1)} %add_convert_fusion.1.k_own.v_own, bf16[1024,1536]{1,0:T(8,128)(2,1)} %collective-permute-done.9.k_mate.v_mate, ...), custom_call_target="tpu_custom_call" | custom-call | flops 3221225472 | bytes 12582912 | tf_op jit(solution)/shard_map/attention_forward/pallas_call | solution.py:111
  212.5 3.8 fusion.100
  216.8 12.1 %multiply_convert_fusion = (bf16[1024,3072]{1,0:T(8,128)(2,1)}, f32[1024,3072]{1,0:T(8,128)}) fusion(f32[3072]{0:T(1024)} %add.446, bf16[768,3072]{1,0:T(8,128)(2,1)} %all-gather.11.cloned.1.call-done, f32[1024,768]{1,0:T(8,128)S(1)} %get-tuple-element.202, f32[768]{0:T(1024)} %add.443, f32[768]{0:T(1024)S(1)} %mul.182, f32[1024]{0:T(1024)S(1)} %add_rsqrt_fusion.1, ...), kind=kOutput, calls=%fused_computation.8 | convolution fusion | flops 4854644736 | bytes 26765312 | tf_op jit(solution)/shard_map/dot_general | solution.py:313
  228.9 9.0 %fusion.101 = (f32[1024]{0:T(1024)S(1)}, f32[1024,768]{1,0:T(8,128)S(1)}) fusion(f32[768]{0:T(1024)} %add.451, bf16[1024,3072]{1,0:T(8,128)(2,1)} %get-tuple-element.203, bf16[3072,768]{1,0:T(8,128)(2,1)} %all-gather.13.cloned.1.call-done, f32[768]{0:T(1024)} %add.443, f32[768]{0:T(1024)S(1)} %mul.182, f32[1024]{0:T(1024)S(1)} %add_rsqrt_fusion.1, ...), kind=kOutput, calls=%fused_computation.279 | convolution fusion | flops 4837342208 | bytes 17323008 | tf_op jit(solution)/shard_map/dot_general | solution.py:313
  239.2 3.2 fusion.14
  242.4 1.9 convert_reduce_fusion.3
  245.3 6.1 collective-permute-start.12
  251.4 10.5 %collective-permute-start.11 = (bf16[256,768]{1,0:T(8,128)(2,1)}, bf16[256,768]{1,0:T(8,128)(2,1)S(1)}, u32[]{:S(2)}, u32[]{:S(2)}) collective-permute-start(bf16[256,768]{1,0:T(8,128)(2,1)} %get-tuple-element.147), channel_id=1, source_target_pairs={{0,16},{8,24},{16,0},{24,8},{1,17},{9,25},{17,1},{25,9},{2,18},{10... | collective-permute-start | bytes 1179656 | tf_op jit(solution)/shard_map/ppermute | solution.py:341
  262.5 7.8 %fusion.83 = f32[3072,768]{1,0:T(8,128)} fusion(bf16[1024,3072]{1,0:T(8,128)(2,1)S(1)} %bitcast.314, f32[1024,768]{1,0:T(8,128)S(1)} %get-tuple-element.106), kind=kOutput, calls=%fused_computation.264 | convolution fusion | flops 4832624640 | bytes 18874368 | tf_op jit(solution)/shard_map/dot_general | solution.py:313
  270.3 12.7 %convert_reduce_fusion = (f32[3072]{0:T(1024)}, bf16[1024,3072]{1,0:T(8,128)(2,1)S(1)}) fusion(f32[1024,3072]{1,0:T(8,128)} %get-tuple-element.204, f32[3072]{0:T(1024)S(1)} %copy-done.34, bf16[3072,768]{1,0:T(8,128)(2,1)S(1)} %bitcast.312, f32[1024,768]{1,0:T(8,128)S(1)} %get-tuple-element.106), kind=kOutput, calls=%fused_computation.7 | convolution fusion | flops 4873516032 | bytes 26763264 | tf_op jit(solution)/shard_map/dot_general | solution.py:313
  283.0 5.6 fusion.86
  288.7 13.9 %multiply_reduce_fusion = (f32[768]{0:T(1024)}, f32[1024]{0:T(1024)S(1)}, f32[1024]{0:T(1024)S(1)}, f32[768]{0:T(1024)}, f32[1024,768]{1,0:T(8,128)}) fusion(f32[1024,768]{1,0:T(8,128)S(1)} %get-tuple-element.202, f32[1024]{0:T(1024)S(1)} %add_rsqrt_fusion.1, f32[1024]{0:T(1024)S(1)} %broadcast_multiply_fusion.4, f32[768]{0:T(1024)S(1)} %mul.182, ...), kind=kOutput, calls=%fused_computation.34 | convolution fusion | flops 4839698432 | bytes 20472832 | tf_op jit(solution)/shard_map/dot_general | solution.py:313
  302.6 2.8 convert_reduce_fusion.4
  307.0 8.1 %collective-permute-start.37 = (bf16[4,96,768]{2,1,0:T(8,128)(2,1)S(1)}, bf16[4,96,768]{2,1,0:T(8,128)(2,1)S(1)}, u32[]{:S(2)}, u32[]{:S(2)}) collective-permute-start(bf16[4,96,768]{2,1,0:T(8,128)(2,1)S(1)} %fusion.30), channel_id=1, source_target_pairs={{0,1},{1,0},{2,3},{3,2},{4,5},{5,4},{6,7},{7,6},{8,9},{9,8},{10,11... | collective-permute-start | bytes 1769480 | tf_op jit(solution)/shard_map/ppermute | solution.py:338
  316.8 4.1 fusion.17
  320.9 2.6 convolution_convert_fusion.do_ref
  324.1 8.8 %collective-permute-start.40 = (bf16[96,768]{1,0:T(8,128)(2,1)S(1)}, bf16[96,768]{1,0:T(8,128)(2,1)S(1)}, u32[]{:S(2)}, u32[]{:S(2)}) collective-permute-start(bf16[96,768]{1,0:T(8,128)(2,1)S(1)} %get-tuple-element.160), channel_id=1, source_target_pairs={{0,6},{1,7},{2,4},{3,5},{4,2},{5,3},{6,0},{7,1},{8,14},{9,15},{10,... | collective-permute-start | bytes 442376 | tf_op jit(solution)/shard_map/ppermute | solution.py:344
  332.9 3.4 collective-permute-start.39
  337.3 4.1 collective-permute-done.39
  342.7 4.2 collective-permute-done.41
  347.8 4.8 collective-permute-done.42
  352.7 88.7 %attention_backward.1 = (bf16[1024,768]{1,0:T(8,128)(2,1)}, f32[2,1024,768]{2,1,0:T(8,128)}, bf16[2,1024,768]{2,1,0:T(8,128)(2,1)}) custom-call(s32[10]{0:T(128)} %pad_add_fusion.3.info, bf16[1024,768]{1,0:T(8,128)(2,1)} %multiply_convert_fusion.1.q_ref, bf16[1024,768]{1,0:T(8,128)(2,1)} %get-tuple-element.21.ext_ref, ...), custom_call_target="tpu_custom_call" | custom-call | flops 8053063680 | bytes 18874368 | tf_op jit(solution)/shard_map/attention_backward/pallas_call | solution.py:229
  446.4 4.5 fusion.91
  451.9 2.7 collective-permute-start.47
  454.5 31.8 %collective-permute-start.46 = (bf16[96,3072]{1,0:T(8,128)(2,1)S(1)}, bf16[96,3072]{1,0:T(8,128)(2,1)}, u32[]{:S(2)}, u32[]{:S(2)}) collective-permute-start(bf16[96,3072]{1,0:T(8,128)(2,1)S(1)} %get-tuple-element.119), channel_id=1, source_target_pairs={{0,4},{1,5},{2,6},{3,7},{4,0},{5,1},{6,2},{7,3},{8,12},{9,13},{10,... | collective-permute-start | bytes 1769480 | tf_op jit(solution)/shard_map/ppermute | solution.py:344
  486.4 2.5 fusion.90
  490.4 10.5 %collective-permute-start.53 = (bf16[384,768]{1,0:T(8,128)(2,1)S(1)}, bf16[384,768]{1,0:T(8,128)(2,1)S(1)}, u32[]{:S(2)}, u32[]{:S(2)}) collective-permute-start(bf16[384,768]{1,0:T(8,128)(2,1)S(1)} %get-tuple-element.116), channel_id=1, source_target_pairs={{0,4},{1,5},{2,6},{3,7},{4,0},{5,1},{6,2},{7,3},{8,12},{9,13},{10,... | collective-permute-start | bytes 1769480 | tf_op jit(solution)/shard_map/ppermute | solution.py:344
  500.9 9.9 %collective-permute-done.46 = bf16[96,3072]{1,0:T(8,128)(2,1)} collective-permute-done((bf16[96,3072]{1,0:T(8,128)(2,1)S(1)}, bf16[96,3072]{1,0:T(8,128)(2,1)}, u32[]{:S(2)}, u32[]{:S(2)}) %collective-permute-start.46) | collective-permute-done | bytes 589856 | tf_op jit(solution)/shard_map/ppermute | solution.py:344
  510.7 3.1 collective-permute-start.52
  516.4 19.6 %collective-permute-done.53 = bf16[384,768]{1,0:T(8,128)(2,1)S(1)} collective-permute-done((bf16[384,768]{1,0:T(8,128)(2,1)S(1)}, bf16[384,768]{1,0:T(8,128)(2,1)S(1)}, u32[]{:S(2)}, u32[]{:S(2)}) %collective-permute-start.53) | collective-permute-done | bytes 589856 | tf_op jit(solution)/shard_map/ppermute | solution.py:344
  538.2 2.6 add_convert_fusion
  545.5 2.7 collective-permute-start.33
  549.1 7.3 %add_convert_fusion.2 = bf16[1024,768]{1,0:T(8,128)(2,1)S(1)} fusion(f32[1024,768]{1,0:T(8,128)} %copy-done.10, bf16[768,2304]{1,0:T(8,128)(2,1)} %all-gather.7.cloned.1.call-done, bf16[1024,768]{1,0:T(8,128)(2,1)S(1)} %get-tuple-element.113, bf16[1024,768]{1,0:T(8,128)(2,1)S(1)} %get-tuple-element.112, bf16[1024,768]{1,0:T(8,128)(2,1)} %get-tuple-element.22), kind=kOutput, calls=%fused_computation.36 | convolution fusion | flops 3639607296 | bytes 12976128 | tf_op jit(solution)/shard_map/dot_general | solution.py:313
  556.5 2.1 collective-permute-start.34
  559.6 2.2 collective-permute-start.21
  561.9 3.0 collective-permute-start.35
  564.9 3.8 fusion.6
  568.7 26.5 %collective-permute-done.35 = bf16[1,576]{1,0:T(2,128)(2,1)S(1)} collective-permute-done((bf16[1,576]{1,0:T(2,128)(2,1)S(1)}, bf16[1,576]{1,0:T(2,128)(2,1)S(1)}, u32[]{:S(2)}, u32[]{:S(2)}) %collective-permute-start.35) | collective-permute-done | bytes 1184 | tf_op jit(solution)/shard_map/ppermute | solution.py:341
  595.5 3.4 collective-permute-done.36
  601.3 2.9 collective-permute-start.49
  605.4 4.8 collective-permute-done.19
  612.2 12.7 %collective-permute-done.49 = bf16[48,3072]{1,0:T(8,128)(2,1)S(1)} collective-permute-done((bf16[48,3072]{1,0:T(8,128)(2,1)S(1)}, bf16[48,3072]{1,0:T(8,128)(2,1)S(1)}, u32[]{:S(2)}, u32[]{:S(2)}) %collective-permute-start.49) | collective-permute-done | bytes 294944 | tf_op jit(solution)/shard_map/ppermute | solution.py:341
  625.0 5.9 collective-permute-done.56
  631.7 2.5 collective-permute-start.26
  634.9 2.3 collective-permute-done.50
  639.0 6.7 collective-permute-done.26
  645.7 8.2 %collective-permute-done.25 = bf16[96,2304]{1,0:T(8,128)(2,1)S(1)} collective-permute-done((bf16[96,2304]{1,0:T(8,128)(2,1)S(1)}, bf16[96,2304]{1,0:T(8,128)(2,1)S(1)}, u32[]{:S(2)}, u32[]{:S(2)}) %collective-permute-start.25) | collective-permute-done | bytes 442400 | tf_op jit(solution)/shard_map/ppermute | solution.py:344
  657.1 4.5 collective-permute-done.27
  661.6 2.2 collective-permute-start.28
  665.0 8.8 %collective-permute-done.28 = bf16[48,2304]{1,0:T(8,128)(2,1)S(1)} collective-permute-done((bf16[48,2304]{1,0:T(8,128)(2,1)S(1)}, bf16[48,2304]{1,0:T(8,128)(2,1)S(1)}, u32[]{:S(2)}, u32[]{:S(2)}) %collective-permute-start.28) | collective-permute-done | bytes 221216 | tf_op jit(solution)/shard_map/ppermute | solution.py:341
  674.1 1.9 maximum_convert_fusion
  676.0 4.1 collective-permute-done.29
  (351 shorter events, 80.1 us)
Async XLA Ops:
  7.2 62.0 %all-gather.7.cloned.1.call-start = ((), (), s32[]{:S(2)}) async-start(), calls=%async_computation | async-start | bytes 3981312 | tf_op jit(solution)/shard_map/all_gather | solution.py:423
  9.8 202.7 %all-gather.9.cloned.1.call-start = ((), (), s32[]{:S(2)}) async-start(), calls=%async_computation.1 | async-start | bytes 1327104 | tf_op jit(solution)/shard_map/all_gather | solution.py:432
  10.5 206.2 %all-gather.11.cloned.1.call-start = ((), (), s32[]{:S(2)}) async-start(), calls=%async_computation.2 | async-start | bytes 5308416 | tf_op jit(solution)/shard_map/all_gather | solution.py:433
  11.2 217.6 %all-gather.13.cloned.1.call-start = ((), (), s32[]{:S(2)}) async-start(), calls=%async_computation.3 | async-start | bytes 5308416 | tf_op jit(solution)/shard_map/all_gather | solution.py:434
  12.4 15.2 %collective-permute-start = (bf16[2,256,768]{2,1,0:T(8,128)(2,1)}, bf16[2,256,768]{2,1,0:T(8,128)(2,1)S(1)}, u32[]{:S(2)}, u32[]{:S(2)}) collective-permute-start(bf16[2,256,768]{2,1,0:T(8,128)(2,1)} %get-tuple-element.153), channel_id=1, source_target_pairs={{0,1},{1,0},{2,3},{3,2},{4,5},{5,4},{6,7},{7,6},{8,9},{9,8},{10,11... | collective-permute-start | bytes 2359304 | tf_op jit(solution)/shard_map/ppermute | solution.py:338
  13.6 61.9 %collective-permute-start.4 = (s32[2,256,1]{1,2,0:T(1,128)}, s32[2,256,1]{1,2,0:T(1,128)}, u32[]{:S(2)}, u32[]{:S(2)}) collective-permute-start(s32[2,256,1]{1,2,0:T(1,128)} %get-tuple-element.200), channel_id=1, source_target_pairs={{0,1},{1,0},{2,3},{3,2},{4,5},{5,4},{6,7},{7,6},{8,9},{9,8},{10,11... | collective-permute-start | bytes 6152 | tf_op jit(solution)/shard_map/ppermute | solution.py:338
  15.9 69.7 %collective-permute-start.14 = (bf16[2,256,768]{2,1,0:T(8,128)(2,1)}, bf16[2,256,768]{2,1,0:T(8,128)(2,1)S(1)}, u32[]{:S(2)}, u32[]{:S(2)}) collective-permute-start(bf16[2,256,768]{2,1,0:T(8,128)(2,1)} %get-tuple-element.137), channel_id=1, source_target_pairs={{0,1},{1,0},{2,3},{3,2},{4,5},{5,4},{6,7},{7,6},{8,9},{9,8},{10,11... | collective-permute-start | bytes 2359304 | tf_op jit(solution)/shard_map/ppermute | solution.py:338
  29.0 14.1 %collective-permute-start.3 = (bf16[256,768]{1,0:T(8,128)(2,1)}, bf16[256,768]{1,0:T(8,128)(2,1)S(1)}, u32[]{:S(2)}, u32[]{:S(2)}) collective-permute-start(bf16[256,768]{1,0:T(8,128)(2,1)} %get-tuple-element.152), channel_id=1, source_target_pairs={{0,24},{8,16},{16,8},{24,0},{1,25},{9,17},{17,9},{25,1},{2,26},{10... | collective-permute-start | bytes 1179656 | tf_op jit(solution)/shard_map/ppermute | solution.py:341
  32.6 34.3 %collective-permute-start.2 = (bf16[256,768]{1,0:T(8,128)(2,1)}, bf16[256,768]{1,0:T(8,128)(2,1)S(1)}, u32[]{:S(2)}, u32[]{:S(2)}) collective-permute-start(bf16[256,768]{1,0:T(8,128)(2,1)} %get-tuple-element.151), channel_id=1, source_target_pairs={{0,16},{8,24},{16,0},{24,8},{1,17},{9,25},{17,1},{25,9},{2,18},{10... | collective-permute-start | bytes 1179656 | tf_op jit(solution)/shard_map/ppermute | solution.py:341
  32.6 34.3 %collective-permute-start.1 = (bf16[256,768]{1,0:T(8,128)(2,1)}, bf16[256,768]{1,0:T(8,128)(2,1)S(1)}, u32[]{:S(2)}, u32[]{:S(2)}) collective-permute-start(bf16[256,768]{1,0:T(8,128)(2,1)} %get-tuple-element.150), channel_id=1, source_target_pairs={{0,8},{8,0},{16,24},{24,16},{1,9},{9,1},{17,25},{25,17},{2,10},{10... | collective-permute-start | bytes 1179656 | tf_op jit(solution)/shard_map/ppermute | solution.py:341
  75.4 58.2 %collective-permute-start.9 = (bf16[1024,1536]{1,0:T(8,128)(2,1)}, bf16[1024,1536]{1,0:T(8,128)(2,1)}, u32[]{:S(2)}, u32[]{:S(2)}) collective-permute-start(bf16[1024,1536]{1,0:T(8,128)(2,1)} %add_convert_fusion.1.k_own.v_own), channel_id=1, source_target_pairs={{0,1},{1,0},{2,3},{3,2},{4,5},{5,4},{6,7},{7,6},{8,9},{9,8},{10,11... | collective-permute-start | bytes 9437192 | tf_op jit(solution)/shard_map/ppermute | solution.py:338
  76.1 6.6 collective-permute-start.7
  78.6 4.5 collective-permute-start.6
  78.7 4.5 collective-permute-start.5
  83.2 1.2 collective-permute-start.8
  88.3 14.0 %collective-permute-start.17 = (bf16[256,768]{1,0:T(8,128)(2,1)S(1)}, bf16[256,768]{1,0:T(8,128)(2,1)S(1)}, u32[]{:S(2)}, u32[]{:S(2)}) collective-permute-start(bf16[256,768]{1,0:T(8,128)(2,1)S(1)} %get-tuple-element.136), channel_id=1, source_target_pairs={{0,24},{8,16},{16,8},{24,0},{1,25},{9,17},{17,9},{25,1},{2,26},{10... | collective-permute-start | bytes 1179656 | tf_op jit(solution)/shard_map/ppermute | solution.py:341
  90.2 35.8 %collective-permute-start.16 = (bf16[256,768]{1,0:T(8,128)(2,1)S(1)}, bf16[256,768]{1,0:T(8,128)(2,1)S(1)}, u32[]{:S(2)}, u32[]{:S(2)}) collective-permute-start(bf16[256,768]{1,0:T(8,128)(2,1)S(1)} %get-tuple-element.135), channel_id=1, source_target_pairs={{0,16},{8,24},{16,0},{24,8},{1,17},{9,25},{17,1},{25,9},{2,18},{10... | collective-permute-start | bytes 1179656 | tf_op jit(solution)/shard_map/ppermute | solution.py:341
  91.3 34.7 %collective-permute-start.15 = (bf16[256,768]{1,0:T(8,128)(2,1)S(1)}, bf16[256,768]{1,0:T(8,128)(2,1)S(1)}, u32[]{:S(2)}, u32[]{:S(2)}) collective-permute-start(bf16[256,768]{1,0:T(8,128)(2,1)S(1)} %get-tuple-element.134), channel_id=1, source_target_pairs={{0,8},{8,0},{16,24},{24,16},{1,9},{9,1},{17,25},{25,17},{2,10},{10... | collective-permute-start | bytes 1179656 | tf_op jit(solution)/shard_map/ppermute | solution.py:341
  245.3 78.9 %collective-permute-start.12 = (bf16[256,768]{1,0:T(8,128)(2,1)}, bf16[256,768]{1,0:T(8,128)(2,1)S(1)}, u32[]{:S(2)}, u32[]{:S(2)}) collective-permute-start(bf16[256,768]{1,0:T(8,128)(2,1)} %get-tuple-element.146), channel_id=1, source_target_pairs={{0,24},{8,16},{16,8},{24,0},{1,25},{9,17},{17,9},{25,1},{2,26},{10... | collective-permute-start | bytes 1179656 | tf_op jit(solution)/shard_map/ppermute | solution.py:341
  251.4 81.5 %collective-permute-start.11 = (bf16[256,768]{1,0:T(8,128)(2,1)}, bf16[256,768]{1,0:T(8,128)(2,1)S(1)}, u32[]{:S(2)}, u32[]{:S(2)}) collective-permute-start(bf16[256,768]{1,0:T(8,128)(2,1)} %get-tuple-element.147), channel_id=1, source_target_pairs={{0,16},{8,24},{16,0},{24,8},{1,17},{9,25},{17,1},{25,9},{2,18},{10... | collective-permute-start | bytes 1179656 | tf_op jit(solution)/shard_map/ppermute | solution.py:341
  261.9 74.5 %collective-permute-start.10 = (bf16[256,768]{1,0:T(8,128)(2,1)S(1)}, bf16[256,768]{1,0:T(8,128)(2,1)S(1)}, u32[]{:S(2)}, u32[]{:S(2)}) collective-permute-start(bf16[256,768]{1,0:T(8,128)(2,1)S(1)} %get-tuple-element.148), channel_id=1, source_target_pairs={{0,8},{8,0},{16,24},{24,16},{1,9},{9,1},{17,25},{25,17},{2,10},{10... | collective-permute-start | bytes 1179656 | tf_op jit(solution)/shard_map/ppermute | solution.py:341
  307.0 16.5 %collective-permute-start.37 = (bf16[4,96,768]{2,1,0:T(8,128)(2,1)S(1)}, bf16[4,96,768]{2,1,0:T(8,128)(2,1)S(1)}, u32[]{:S(2)}, u32[]{:S(2)}) collective-permute-start(bf16[4,96,768]{2,1,0:T(8,128)(2,1)S(1)} %fusion.30), channel_id=1, source_target_pairs={{0,1},{1,0},{2,3},{3,2},{4,5},{5,4},{6,7},{7,6},{8,9},{9,8},{10,11... | collective-permute-start | bytes 1769480 | tf_op jit(solution)/shard_map/ppermute | solution.py:338
  316.8 129.6 %collective-permute-start.44 = (bf16[4,96,3072]{2,1,0:T(8,128)(2,1)}, bf16[4,96,3072]{2,1,0:T(8,128)(2,1)}, u32[]{:S(2)}, u32[]{:S(2)}) collective-permute-start(bf16[4,96,3072]{2,1,0:T(8,128)(2,1)} %fusion.16), channel_id=1, source_target_pairs={{0,1},{1,0},{2,3},{3,2},{4,5},{5,4},{6,7},{7,6},{8,9},{9,8},{10,11... | collective-permute-start | bytes 7077896 | tf_op jit(solution)/shard_map/ppermute | solution.py:338
  323.5 162.8 %collective-permute-start.51 = (bf16[4,384,768]{2,1,0:T(8,128)(2,1)}, bf16[4,384,768]{2,1,0:T(8,128)(2,1)}, u32[]{:S(2)}, u32[]{:S(2)}) collective-permute-start(bf16[4,384,768]{2,1,0:T(8,128)(2,1)} %fusion.17), channel_id=1, source_target_pairs={{0,1},{1,0},{2,3},{3,2},{4,5},{5,4},{6,7},{7,6},{8,9},{9,8},{10,11... | collective-permute-start | bytes 7077896 | tf_op jit(solution)/shard_map/ppermute | solution.py:338
  324.1 13.2 %collective-permute-start.40 = (bf16[96,768]{1,0:T(8,128)(2,1)S(1)}, bf16[96,768]{1,0:T(8,128)(2,1)S(1)}, u32[]{:S(2)}, u32[]{:S(2)}) collective-permute-start(bf16[96,768]{1,0:T(8,128)(2,1)S(1)} %get-tuple-element.160), channel_id=1, source_target_pairs={{0,6},{1,7},{2,4},{3,5},{4,2},{5,3},{6,0},{7,1},{8,14},{9,15},{10,... | collective-permute-start | bytes 442376 | tf_op jit(solution)/shard_map/ppermute | solution.py:344
  332.9 8.5 %collective-permute-start.39 = (bf16[96,768]{1,0:T(8,128)(2,1)S(1)}, bf16[96,768]{1,0:T(8,128)(2,1)S(1)}, u32[]{:S(2)}, u32[]{:S(2)}) collective-permute-start(bf16[96,768]{1,0:T(8,128)(2,1)S(1)} %get-tuple-element.161), channel_id=1, source_target_pairs={{0,4},{1,5},{2,6},{3,7},{4,0},{5,1},{6,2},{7,3},{8,12},{9,13},{10,... | collective-permute-start | bytes 442376 | tf_op jit(solution)/shard_map/ppermute | solution.py:344
  336.3 6.1 collective-permute-start.38
  342.5 4.4 collective-permute-start.41
  347.0 5.6 collective-permute-start.42
  347.7 97.3 %collective-permute-start.13 = (bf16[2,256,768]{2,1,0:T(8,128)(2,1)S(1)}, bf16[2,256,768]{2,1,0:T(8,128)(2,1)S(1)}, u32[]{:S(2)}, u32[]{:S(2)}) collective-permute-start(bf16[2,256,768]{2,1,0:T(8,128)(2,1)S(1)} %pad_maximum_fusion.7), channel_id=1, source_target_pairs={{0,1},{1,0},{2,3},{3,2},{4,5},{5,4},{6,7},{7,6},{8,9},{9,8},{10,11... | collective-permute-start | bytes 2359304 | tf_op jit(solution)/shard_map/ppermute | solution.py:338
  352.6 91.6 %collective-permute-start.43 = (bf16[48,768]{1,0:T(8,128)(2,1)S(1)}, bf16[48,768]{1,0:T(8,128)(2,1)S(1)}, u32[]{:S(2)}, u32[]{:S(2)}) collective-permute-start(bf16[48,768]{1,0:T(8,128)(2,1)S(1)} %add_convert_fusion.7), channel_id=1, source_target_pairs={{0,8},{8,0},{16,24},{24,16},{1,9},{9,1},{17,25},{25,17},{2,10},{10... | collective-permute-start | bytes 221192 | tf_op jit(solution)/shard_map/ppermute | solution.py:341
  352.7 90.9 %copy-start.33 = (f32[768]{0:T(1024)S(1)}, f32[768]{0:T(1024)}, u32[]{:S(2)}) copy-start(f32[768]{0:T(1024)} %get-tuple-element.87) | copy-start | bytes 9220
  352.7 91.5 %copy-start.35 = (f32[3072]{0:T(1024)S(1)}, f32[3072]{0:T(1024)}, u32[]{:S(2)}) copy-start(f32[3072]{0:T(1024)} %get-tuple-element.208) | copy-start | bytes 36868
  441.4 96.7 %collective-permute-start.18 = (bf16[2,1024,768]{2,1,0:T(8,128)(2,1)}, bf16[2,1024,768]{2,1,0:T(8,128)(2,1)}, u32[]{:S(2)}, u32[]{:S(2)}) collective-permute-start(bf16[2,1024,768]{2,1,0:T(8,128)(2,1)} %get-tuple-element.24), channel_id=1, source_target_pairs={{0,1},{1,0},{2,3},{3,2},{4,5},{5,4},{6,7},{7,6},{8,9},{9,8},{10,11... | collective-permute-start | bytes 9437192 | tf_op jit(solution)/shard_map/ppermute | solution.py:338
  451.9 38.5 %collective-permute-start.47 = (bf16[96,3072]{1,0:T(8,128)(2,1)}, bf16[96,3072]{1,0:T(8,128)(2,1)}, u32[]{:S(2)}, u32[]{:S(2)}) collective-permute-start(bf16[96,3072]{1,0:T(8,128)(2,1)} %get-tuple-element.118), channel_id=1, source_target_pairs={{0,6},{1,7},{2,4},{3,5},{4,2},{5,3},{6,0},{7,1},{8,14},{9,15},{10,... | collective-permute-start | bytes 1769480 | tf_op jit(solution)/shard_map/ppermute | solution.py:344
  454.5 56.2 %collective-permute-start.46 = (bf16[96,3072]{1,0:T(8,128)(2,1)S(1)}, bf16[96,3072]{1,0:T(8,128)(2,1)}, u32[]{:S(2)}, u32[]{:S(2)}) collective-permute-start(bf16[96,3072]{1,0:T(8,128)(2,1)S(1)} %get-tuple-element.119), channel_id=1, source_target_pairs={{0,4},{1,5},{2,6},{3,7},{4,0},{5,1},{6,2},{7,3},{8,12},{9,13},{10,... | collective-permute-start | bytes 1769480 | tf_op jit(solution)/shard_map/ppermute | solution.py:344
  486.3 27.5 %collective-permute-start.45 = (bf16[96,3072]{1,0:T(8,128)(2,1)S(1)}, bf16[96,3072]{1,0:T(8,128)(2,1)}, u32[]{:S(2)}, u32[]{:S(2)}) collective-permute-start(bf16[96,3072]{1,0:T(8,128)(2,1)S(1)} %get-tuple-element.117), channel_id=1, source_target_pairs={{0,2},{1,3},{2,0},{3,1},{4,6},{5,7},{6,4},{7,5},{8,10},{9,11},{10,... | collective-permute-start | bytes 1769480 | tf_op jit(solution)/shard_map/ppermute | solution.py:344
  489.0 27.4 %collective-permute-start.54 = (bf16[384,768]{1,0:T(8,128)(2,1)S(1)}, bf16[384,768]{1,0:T(8,128)(2,1)S(1)}, u32[]{:S(2)}, u32[]{:S(2)}) collective-permute-start(bf16[384,768]{1,0:T(8,128)(2,1)S(1)} %get-tuple-element.115), channel_id=1, source_target_pairs={{0,6},{1,7},{2,4},{3,5},{4,2},{5,3},{6,0},{7,1},{8,14},{9,15},{10,... | collective-permute-start | bytes 1769480 | tf_op jit(solution)/shard_map/ppermute | solution.py:344
  490.4 45.6 %collective-permute-start.53 = (bf16[384,768]{1,0:T(8,128)(2,1)S(1)}, bf16[384,768]{1,0:T(8,128)(2,1)S(1)}, u32[]{:S(2)}, u32[]{:S(2)}) collective-permute-start(bf16[384,768]{1,0:T(8,128)(2,1)S(1)} %get-tuple-element.116), channel_id=1, source_target_pairs={{0,4},{1,5},{2,6},{3,7},{4,0},{5,1},{6,2},{7,3},{8,12},{9,13},{10,... | collective-permute-start | bytes 1769480 | tf_op jit(solution)/shard_map/ppermute | solution.py:344
  510.7 26.3 %collective-permute-start.52 = (bf16[384,768]{1,0:T(8,128)(2,1)S(1)}, bf16[384,768]{1,0:T(8,128)(2,1)S(1)}, u32[]{:S(2)}, u32[]{:S(2)}) collective-permute-start(bf16[384,768]{1,0:T(8,128)(2,1)S(1)} %get-tuple-element.114), channel_id=1, source_target_pairs={{0,2},{1,3},{2,0},{3,1},{4,6},{5,7},{6,4},{7,5},{8,10},{9,11},{10,... | collective-permute-start | bytes 1769480 | tf_op jit(solution)/shard_map/ppermute | solution.py:344
  516.4 83.8 %collective-permute-start.48 = (bf16[48,3072]{1,0:T(8,128)(2,1)}, bf16[48,3072]{1,0:T(8,128)(2,1)}, u32[]{:S(2)}, u32[]{:S(2)}) collective-permute-start(bf16[48,3072]{1,0:T(8,128)(2,1)} %dynamic-slice_bitcast_fusion.14), channel_id=1, source_target_pairs={{0,8},{8,0},{16,24},{24,16},{1,9},{9,1},{17,25},{25,17},{2,10},{10... | collective-permute-start | bytes 884744 | tf_op jit(solution)/shard_map/ppermute | solution.py:341
  543.7 1.8 collective-permute-start.30
  545.5 55.9 %collective-permute-start.55 = (bf16[192,768]{1,0:T(8,128)(2,1)}, bf16[192,768]{1,0:T(8,128)(2,1)}, u32[]{:S(2)}, u32[]{:S(2)}) collective-permute-start(bf16[192,768]{1,0:T(8,128)(2,1)} %dynamic-slice_bitcast_fusion.13), channel_id=1, source_target_pairs={{0,8},{8,0},{16,24},{24,16},{1,9},{9,1},{17,25},{25,17},{2,10},{10... | collective-permute-start | bytes 884744 | tf_op jit(solution)/shard_map/ppermute | solution.py:341
  545.5 10.9 %collective-permute-start.33 = (bf16[2,576]{1,0:T(2,128)(2,1)S(1)}, bf16[2,576]{1,0:T(2,128)(2,1)S(1)}, u32[]{:S(2)}, u32[]{:S(2)}) collective-permute-start(bf16[2,576]{1,0:T(2,128)(2,1)S(1)} %get-tuple-element.177), channel_id=1, source_target_pairs={{0,6},{1,7},{2,4},{3,5},{4,2},{5,3},{6,0},{7,1},{8,14},{9,15},{10,... | collective-permute-start | bytes 6920 | tf_op jit(solution)/shard_map/ppermute | solution.py:344
  548.2 8.2 %collective-permute-start.32 = (bf16[2,576]{1,0:T(2,128)(2,1)S(1)}, bf16[2,576]{1,0:T(2,128)(2,1)S(1)}, u32[]{:S(2)}, u32[]{:S(2)}) collective-permute-start(bf16[2,576]{1,0:T(2,128)(2,1)S(1)} %get-tuple-element.178), channel_id=1, source_target_pairs={{0,4},{1,5},{2,6},{3,7},{4,0},{5,1},{6,2},{7,3},{8,12},{9,13},{10,... | collective-permute-start | bytes 6920 | tf_op jit(solution)/shard_map/ppermute | solution.py:344
  548.5 7.9 %collective-permute-start.31 = (bf16[2,576]{1,0:T(2,128)(2,1)S(1)}, bf16[2,576]{1,0:T(2,128)(2,1)S(1)}, u32[]{:S(2)}, u32[]{:S(2)}) collective-permute-start(bf16[2,576]{1,0:T(2,128)(2,1)S(1)} %get-tuple-element.176), channel_id=1, source_target_pairs={{0,2},{1,3},{2,0},{3,1},{4,6},{5,7},{6,4},{7,5},{8,10},{9,11},{10,... | collective-permute-start | bytes 6920 | tf_op jit(solution)/shard_map/ppermute | solution.py:344
  556.5 5.4 collective-permute-start.34
  559.6 45.6 %collective-permute-start.21 = (bf16[256,768]{1,0:T(8,128)(2,1)}, bf16[256,768]{1,0:T(8,128)(2,1)}, u32[]{:S(2)}, u32[]{:S(2)}) collective-permute-start(bf16[256,768]{1,0:T(8,128)(2,1)} %get-tuple-element.130), channel_id=1, source_target_pairs={{0,24},{8,16},{16,8},{24,0},{1,25},{9,17},{17,9},{25,1},{2,26},{10... | collective-permute-start | bytes 1179656 | tf_op jit(solution)/shard_map/ppermute | solution.py:341
  561.9 43.6 %collective-permute-start.20 = (bf16[256,768]{1,0:T(8,128)(2,1)}, bf16[256,768]{1,0:T(8,128)(2,1)}, u32[]{:S(2)}, u32[]{:S(2)}) collective-permute-start(bf16[256,768]{1,0:T(8,128)(2,1)} %get-tuple-element.131), channel_id=1, source_target_pairs={{0,16},{8,24},{16,0},{24,8},{1,17},{9,25},{17,1},{25,9},{2,18},{10... | collective-permute-start | bytes 1179656 | tf_op jit(solution)/shard_map/ppermute | solution.py:341
  561.9 33.3 %collective-permute-start.35 = (bf16[1,576]{1,0:T(2,128)(2,1)S(1)}, bf16[1,576]{1,0:T(2,128)(2,1)S(1)}, u32[]{:S(2)}, u32[]{:S(2)}) collective-permute-start(bf16[1,576]{1,0:T(2,128)(2,1)S(1)} %fusion.66), channel_id=1, source_target_pairs={{0,16},{8,24},{16,0},{24,8},{1,17},{9,25},{17,1},{25,9},{2,18},{10... | collective-permute-start | bytes 3464 | tf_op jit(solution)/shard_map/ppermute | solution.py:341
  595.2 3.7 collective-permute-start.36
  598.9 11.4 %collective-permute-start.19 = (bf16[256,768]{1,0:T(8,128)(2,1)}, bf16[256,768]{1,0:T(8,128)(2,1)}, u32[]{:S(2)}, u32[]{:S(2)}) collective-permute-start(bf16[256,768]{1,0:T(8,128)(2,1)} %get-tuple-element.132), channel_id=1, source_target_pairs={{0,8},{8,0},{16,24},{24,16},{1,9},{9,1},{17,25},{25,17},{2,10},{10... | collective-permute-start | bytes 1179656 | tf_op jit(solution)/shard_map/ppermute | solution.py:341
  600.2 30.9 %collective-permute-start.23 = (bf16[4,96,2304]{2,1,0:T(8,128)(2,1)S(1)}, bf16[4,96,2304]{2,1,0:T(8,128)(2,1)S(1)}, u32[]{:S(2)}, u32[]{:S(2)}) collective-permute-start(bf16[4,96,2304]{2,1,0:T(8,128)(2,1)S(1)} %fusion.19), channel_id=1, source_target_pairs={{0,1},{1,0},{2,3},{3,2},{4,5},{5,4},{6,7},{7,6},{8,9},{9,8},{10,11... | collective-permute-start | bytes 5308424 | tf_op jit(solution)/shard_map/ppermute | solution.py:338
  601.3 23.5 %collective-permute-start.49 = (bf16[48,3072]{1,0:T(8,128)(2,1)S(1)}, bf16[48,3072]{1,0:T(8,128)(2,1)S(1)}, u32[]{:S(2)}, u32[]{:S(2)}) collective-permute-start(bf16[48,3072]{1,0:T(8,128)(2,1)S(1)} %fusion.32), channel_id=1, source_target_pairs={{0,16},{8,24},{16,0},{24,8},{1,17},{9,25},{17,1},{25,9},{2,18},{10... | collective-permute-start | bytes 884744 | tf_op jit(solution)/shard_map/ppermute | solution.py:341
  605.2 25.7 %collective-permute-start.56 = (bf16[192,768]{1,0:T(8,128)(2,1)S(1)}, bf16[192,768]{1,0:T(8,128)(2,1)S(1)}, u32[]{:S(2)}, u32[]{:S(2)}) collective-permute-start(bf16[192,768]{1,0:T(8,128)(2,1)S(1)} %fusion.31), channel_id=1, source_target_pairs={{0,16},{8,24},{16,0},{24,8},{1,17},{9,25},{17,1},{25,9},{2,18},{10... | collective-permute-start | bytes 884744 | tf_op jit(solution)/shard_map/ppermute | solution.py:341
  612.1 61.9 %collective-permute-start.22 = (bf16[2,256,768]{2,1,0:T(8,128)(2,1)S(1)}, bf16[2,256,768]{2,1,0:T(8,128)(2,1)S(1)}, u32[]{:S(2)}, u32[]{:S(2)}) collective-permute-start(bf16[2,256,768]{2,1,0:T(8,128)(2,1)S(1)} %pad_maximum_fusion.9), channel_id=1, source_target_pairs={{0,1},{1,0},{2,3},{3,2},{4,5},{5,4},{6,7},{7,6},{8,9},{9,8},{10,11... | collective-permute-start | bytes 2359304 | tf_op jit(solution)/shard_map/ppermute | solution.py:338
  624.9 12.3 %collective-permute-start.50 = (bf16[48,3072]{1,0:T(8,128)(2,1)S(1)}, bf16[48,3072]{1,0:T(8,128)(2,1)S(1)}, u32[]{:S(2)}, u32[]{:S(2)}) collective-permute-start(bf16[48,3072]{1,0:T(8,128)(2,1)S(1)} %add_convert_fusion.5), channel_id=1, source_target_pairs={{0,8},{8,0},{16,24},{24,16},{1,9},{9,1},{17,25},{25,17},{2,10},{10... | collective-permute-start | bytes 884744 | tf_op jit(solution)/shard_map/ppermute | solution.py:341
  631.0 32.9 %collective-permute-start.57 = (bf16[192,768]{1,0:T(8,128)(2,1)S(1)}, bf16[192,768]{1,0:T(8,128)(2,1)S(1)}, u32[]{:S(2)}, u32[]{:S(2)}) collective-permute-start(bf16[192,768]{1,0:T(8,128)(2,1)S(1)} %add_convert_fusion.4), channel_id=1, source_target_pairs={{0,8},{8,0},{16,24},{24,16},{1,9},{9,1},{17,25},{25,17},{2,10},{10... | collective-permute-start | bytes 884744 | tf_op jit(solution)/shard_map/ppermute | solution.py:341
  631.7 14.0 %collective-permute-start.26 = (bf16[96,2304]{1,0:T(8,128)(2,1)S(1)}, bf16[96,2304]{1,0:T(8,128)(2,1)S(1)}, u32[]{:S(2)}, u32[]{:S(2)}) collective-permute-start(bf16[96,2304]{1,0:T(8,128)(2,1)S(1)} %get-tuple-element.121), channel_id=1, source_target_pairs={{0,6},{1,7},{2,4},{3,5},{4,2},{5,3},{6,0},{7,1},{8,14},{9,15},{10,... | collective-permute-start | bytes 1327112 | tf_op jit(solution)/shard_map/ppermute | solution.py:344
  634.2 19.8 %collective-permute-start.25 = (bf16[96,2304]{1,0:T(8,128)(2,1)S(1)}, bf16[96,2304]{1,0:T(8,128)(2,1)S(1)}, u32[]{:S(2)}, u32[]{:S(2)}) collective-permute-start(bf16[96,2304]{1,0:T(8,128)(2,1)S(1)} %get-tuple-element.122), channel_id=1, source_target_pairs={{0,4},{1,5},{2,6},{3,7},{4,0},{5,1},{6,2},{7,3},{8,12},{9,13},{10,... | collective-permute-start | bytes 1327112 | tf_op jit(solution)/shard_map/ppermute | solution.py:344
  637.3 16.7 %collective-permute-start.24 = (bf16[96,2304]{1,0:T(8,128)(2,1)S(1)}, bf16[96,2304]{1,0:T(8,128)(2,1)S(1)}, u32[]{:S(2)}, u32[]{:S(2)}) collective-permute-start(bf16[96,2304]{1,0:T(8,128)(2,1)S(1)} %get-tuple-element.120), channel_id=1, source_target_pairs={{0,2},{1,3},{2,0},{3,1},{4,6},{5,7},{6,4},{7,5},{8,10},{9,11},{10,... | collective-permute-start | bytes 1327112 | tf_op jit(solution)/shard_map/ppermute | solution.py:344
  654.2 7.4 %collective-permute-start.27 = (bf16[48,2304]{1,0:T(8,128)(2,1)S(1)}, bf16[48,2304]{1,0:T(8,128)(2,1)S(1)}, u32[]{:S(2)}, u32[]{:S(2)}) collective-permute-start(bf16[48,2304]{1,0:T(8,128)(2,1)S(1)} %dynamic-slice_bitcast_fusion.15), channel_id=1, source_target_pairs={{0,8},{8,0},{16,24},{24,16},{1,9},{9,1},{17,25},{25,17},{2,10},{10... | collective-permute-start | bytes 663560 | tf_op jit(solution)/shard_map/ppermute | solution.py:341
  661.6 12.2 %collective-permute-start.28 = (bf16[48,2304]{1,0:T(8,128)(2,1)S(1)}, bf16[48,2304]{1,0:T(8,128)(2,1)S(1)}, u32[]{:S(2)}, u32[]{:S(2)}) collective-permute-start(bf16[48,2304]{1,0:T(8,128)(2,1)S(1)} %fusion.33), channel_id=1, source_target_pairs={{0,16},{8,24},{16,0},{24,8},{1,17},{9,25},{17,1},{25,9},{2,18},{10... | collective-permute-start | bytes 663560 | tf_op jit(solution)/shard_map/ppermute | solution.py:341
  673.9 6.3 collective-permute-start.29
  (60 other events, 1164.6 us)
Sparse Core Ops, SparseCore 0:
  10.5 36.5 all-gather.6
  49.0 23.9 all-gather.8
  74.8 38.7 all-gather.10
  115.4 38.7 all-gather.12

commit v2 on v1

--- a/solution.py
+++ b/solution.py
@@ -42,7 +42,7 @@
             put(b, mate_ref[pl.ds(start, block), :])
 
 
-def forward_kernel(info, q_ref, k_own, k_mate, v_own, v_mate, qx_ref, kx_ref, out_ref, ext_ref, k_all, vt_all, *, size):
+def forward_kernel(info, q_ref, k_own, k_mate, v_own, v_mate, qx_ref, kx_ref, out_ref, ext_ref, k_all, vt_all, s_all, *, size):
     slot = pl.program_id(1)
     block = q_ref.shape[0]
     count = kx_ref.shape[0] // block
@@ -70,23 +70,46 @@
     qx = qx_ref[...]
     queries = [jnp.where(lane_head == h, rows, qx) for h in range(heads)]
 
+    part = block
+    lo, hi = info[2 + 2 * slot], info[3 + 2 * slot]
+
+    def score(h, kb, i, top):
+        at = pl.multiple_of(kb * block + i * part, part)
+        st = nt(k_all[h, pl.ds(at, part), :], queries[h])
+        s_all[h, i * part : (i + 1) * part, :] = st
+        return jnp.maximum(top, jnp.max(st.reshape(part // 8, 8, block), axis=0))
+
+    def weigh(h, kb, i, m, acc):
+        at = pl.multiple_of(kb * block + i * part, part)
+        p = jnp.exp2(s_all[h, i * part : (i + 1) * part, :] - m).astype(jnp.bfloat16)
+        return acc + nn(vt_all[h, :, pl.ds(at, part)], p)
+
+    least = jnp.full((8, block), -jnp.inf, jnp.float32)
+
     def step(kb, carry):
-        start = pl.multiple_of(kb * block, block)
-        fresh = []
+        tops, state = carry
+        tops, state = list(tops), list(state)
+        after = jnp.minimum(kb + 1, count - 1)
         for h in range(heads):
-            m, acc = carry[h]
-            st = nt(k_all[h, pl.ds(start, block), :], queries[h])
-            m_new = jnp.maximum(m, jnp.max(st, axis=0, keepdims=True))
-            p = jnp.exp2(st - m_new).astype(jnp.bfloat16)
-            acc = acc * jnp.exp2(m - m_new) + nn(vt_all[h, :, pl.ds(start, block)], p)
-            fresh.append((m_new, acc))
-        return tuple(fresh)
+            ahead = (h + 1) % heads
+            ahead_kb = kb if ahead else after
+            m, acc = state[h]
+            m_new = jnp.maximum(m, jnp.max(tops[h], axis=0, keepdims=True))
+            acc = acc * jnp.exp2(m - m_new)
+            top = least
+            for i in range(1):
+                top = score(ahead, ahead_kb, i, top)
+                acc = weigh(h, kb, i, m_new, acc)
+            tops[ahead] = top
+            state[h] = (m_new, acc)
+        return tuple(tops), tuple(state)
 
     start = tuple(
         (jnp.full((1, block), -jnp.inf, jnp.float32), jnp.zeros((vt_all.shape[1], block), jnp.float32))
         for _ in range(heads)
     )
-    done = lax.fori_loop(info[2 + 2 * slot], info[3 + 2 * slot], step, start)
+    first = score(0, lo, 0, least)
+    _, done = lax.fori_loop(lo, hi, step, ((first,) + (least,) * (heads - 1), start))
     sums = [acc[size : size + 1] for _, acc in done]
     out_t = jnp.concatenate([acc[:size] * (1.0 / l) for (_, acc), l in zip(done, sums)], axis=0)
     out_ref[...] = out_t.T.astype(out_ref.dtype)
@@ -126,6 +149,7 @@
             scratch_shapes=[
                 pltpu.VMEM((heads, length, LANES), jnp.bfloat16),
                 pltpu.VMEM((heads, size + 16, length), jnp.bfloat16),
+                pltpu.VMEM((heads, block, block), jnp.float32),
             ],
         ),
         out_shape=[jax.ShapeDtypeStruct((rows, width), jnp.bfloat16)] * 2,
@@ -218,29 +242,30 @@
                     mate_ref[j, pl.ds(spot, block), :] = (total[pl.ds(b * block, block), :] * factor).astype(mate_ref.dtype)
 
 
-def attention_backward(info, q, ext, grads, ctx, kv_own, kv_mate, kx, size):
+def attention_backward(info, q, ext, grads, ctx, kv_own, kv_mate, kx, size, first, some):
     rows, width = q.shape
     length = kx.shape[0]
     slots = (info.shape[0] - 2) // 2
     block = rows // slots
     pairs = width // LANES
     heads = LANES // size
-    tile = pl.BlockSpec((block, LANES), lambda p, s, i: (s, p))
+    tile = pl.BlockSpec((block, LANES), lambda p, s, i: (s, first + p))
+    out_tile = pl.BlockSpec((block, LANES), lambda p, s, i: (s, p))
     return pl.pallas_call(
         functools.partial(backward_kernel, size=size),
         grid_spec=pltpu.PrefetchScalarGridSpec(
             num_scalar_prefetch=1,
-            grid=(pairs, slots),
+            grid=(some, slots),
             in_specs=[
                 tile, tile, tile, tile,
-                pl.BlockSpec((rows, LANES), lambda p, s, i: (0, p)),
-                pl.BlockSpec((rows, LANES), lambda p, s, i: (0, p)),
-                pl.BlockSpec((rows, LANES), lambda p, s, i: (0, pairs + p)),
-                pl.BlockSpec((rows, LANES), lambda p, s, i: (0, pairs + p)),
+                pl.BlockSpec((rows, LANES), lambda p, s, i: (0, first + p)),
+                pl.BlockSpec((rows, LANES), lambda p, s, i: (0, first + p)),
+                pl.BlockSpec((rows, LANES), lambda p, s, i: (0, pairs + first + p)),
+                pl.BlockSpec((rows, LANES), lambda p, s, i: (0, pairs + first + p)),
                 pl.BlockSpec((length, LANES), lambda p, s, i: (0, 0)),
             ],
             out_specs=[
-                tile,
+                out_tile,
                 pl.BlockSpec((2, rows, LANES), lambda p, s, i: (0, 0, p)),
                 pl.BlockSpec((2, rows, LANES), lambda p, s, i: (0, 0, p)),
             ],
@@ -253,13 +278,15 @@
             ],
         ),
         out_shape=[
-            jax.ShapeDtypeStruct((rows, width), jnp.bfloat16),
-            jax.ShapeDtypeStruct((2, rows, width), jnp.float32),
-            jax.ShapeDtypeStruct((2, rows, width), jnp.bfloat16),
+            jax.ShapeDtypeStruct((rows, some * LANES), jnp.bfloat16),
+            jax.ShapeDtypeStruct((2, rows, some * LANES), jnp.float32),
+            jax.ShapeDtypeStruct((2, rows, some * LANES), jnp.bfloat16),
         ],
         compiler_params=pltpu.CompilerParams(dimension_semantics=("arbitrary", "arbitrary")),
         cost_estimate=pl.CostEstimate(
-            flops=5 * rows * length * width, bytes_accessed=12 * rows * width * 2, transcendentals=rows * length * pairs
+            flops=5 * rows * length * some * LANES,
+            bytes_accessed=24 * rows * some * LANES,
+            transcendentals=rows * length * some,
         ),
         name="attention_backward",
     )(info, q, ext, grads, ctx, kv_own, kv_mate, kv_own, kv_mate, kx)
@@ -280,6 +307,7 @@
 H = 12
 HD = 64
 LOG2E = 1.0 / LN2
+PARTS = 3
 eps_norm = 1e-06
 bf16 = jnp.bfloat16
 f32 = jnp.float32
@@ -325,14 +353,18 @@
     return lax.dynamic_index_in_dim(values, index, axis, keepdims=False)
 
 
+def after(values, *marks):
+    return lax.optimization_barrier((values, marks))[0]
+
+
 class Places:
     def __init__(self):
         self.columns = lax.axis_size("seq")
         self.shards = lax.axis_size("fsdp")
         self.column = lax.axis_index("seq")
-        shard = lax.axis_index("fsdp")
-        self.core = shard & 1
-        self.plane = shard >> 1
+        self.shard = lax.axis_index("fsdp")
+        self.core = self.shard & 1
+        self.plane = self.shard >> 1
 
     def mate(self, values):
         return lax.ppermute(values, "fsdp", xor_pairs(self.shards, 1))
@@ -355,11 +387,15 @@
         want = here.column ^ k
         part = pick(both, ((want // groups) ^ here.core) * groups + want % groups)
         slots.append(here.across(part, k) if k else part)
-    return jnp.stack(slots)
-
-
-def from_sequence(here, slots, groups):
-    rows = jnp.stack([here.across(slots[k], k) if k else slots[k] for k in range(here.columns)])
+    return slots
+
+
+def from_sequence_send(here, slots):
+    return [here.across(slots[k], k) if k else slots[k] for k in range(here.columns)]
+
+
+def from_sequence_end(here, slots, groups):
+    rows = jnp.stack(slots)
 
     def of(core):
         return jnp.stack([pick(rows, here.column ^ (core * groups + j)) for j in range(groups)])
@@ -370,26 +406,92 @@
     return jnp.concatenate([jnp.where(first, kept, other), jnp.where(first, other, kept)], axis=1)
 
 
-def reduce_share(here, partial):
+def place_kernel(info, *refs):
+    count = (len(refs) - 3) // 2
+    parts, out, buffers = refs[:count], refs[count], refs[count + 1 : 2 * count + 1]
+    in_sem, out_sem = refs[2 * count + 1 :]
+    reads = [pltpu.make_async_copy(parts[k], buffers[k], in_sem.at[k]) for k in range(count)]
+    writes = [pltpu.make_async_copy(buffers[k], out.at[info[k]], out_sem.at[k]) for k in range(count)]
+    for read in reads:
+        read.start()
+    for read, write in zip(reads, writes):
+        read.wait()
+        write.start()
+    for write in writes:
+        write.wait()
+
+
+def place(parts, spots):
+    count, (rows, width), kind = len(parts), parts[0].shape, parts[0].dtype
+    full = pl.pallas_call(
+        place_kernel,
+        grid_spec=pltpu.PrefetchScalarGridSpec(
+            num_scalar_prefetch=1,
+            grid=(),
+            in_specs=[pl.BlockSpec(memory_space=pl.ANY)] * count,
+            out_specs=pl.BlockSpec(memory_space=pl.ANY),
+            scratch_shapes=[pltpu.VMEM((rows, width), kind)] * count
+            + [pltpu.SemaphoreType.DMA((count,)), pltpu.SemaphoreType.DMA((count,))],
+        ),
+        out_shape=jax.ShapeDtypeStruct((count, rows, width), kind),
+        cost_estimate=pl.CostEstimate(flops=0, bytes_accessed=2 * count * rows * width * 2, transcendentals=0),
+        name="place_parts",
+    )(jnp.stack(spots).astype(jnp.int32), *parts)
+    return full.reshape(count * rows, width)
+
+
+def gather_shards(here, local):
+    if here.shards != 8:
+        return lax.all_gather(local, "fsdp", axis=0, tiled=True)
+    middle = local.shape[0] // 2
+    across_x, across_y = here.aside(local, 1), here.aside(local, 2)
+    corner = jnp.concatenate([here.aside(across_x[:middle], 2), here.aside(across_y[middle:], 1)], axis=0)
+    parts = [local, across_x, across_y, corner]
+    spots = [here.shard ^ (2 * k) for k in range(4)]
+    return place(parts + [here.mate(part) for part in parts], spots + [spot ^ 1 for spot in spots])
+
+
+def share_pair(here, partial):
     shards, rows, width = partial.shape
     pairs = partial.reshape(shards // 2, 2, rows, width)
-    total = pick(pairs, here.core, 1).astype(f32) + here.mate(pick(pairs, 1 - here.core, 1).astype(bf16)).astype(f32)
+    return pick(pairs, here.core, 1), here.mate(pick(pairs, 1 - here.core, 1).astype(bf16))
+
+
+def share_plane(here, kept, other):
+    total = kept.astype(f32) + other.astype(f32)
     low = total.astype(bf16)
-    share = pick(total, here.plane)
-    for k in range(1, shards // 2):
-        share = share + here.aside(pick(low, here.plane ^ k), k).astype(f32)
-    low = share.astype(bf16).reshape(2, rows // 2, width)
+    return pick(total, here.plane), [here.aside(pick(low, here.plane ^ k), k) for k in range(1, here.shards // 2)]
+
+
+def share_sum(share, others):
+    for other in others:
+        share = share + other.astype(f32)
+    return share.astype(bf16)
+
+
+def column_first(here, share):
+    low = share.reshape(2, share.shape[0] // 2, share.shape[1])
     side = here.column & 1
-    half = pick(low, side).astype(f32) + here.across(pick(low, 1 - side), 1).astype(f32)
-    step = 2
-    while step < here.columns:
-        low = half.astype(bf16)
-        half = low.astype(f32) + here.across(low, step).astype(f32)
+    return pick(low, side), here.across(pick(low, 1 - side), 1)
+
+
+def column_second(here, half, other):
+    low = (half.astype(f32) + other.astype(f32)).astype(bf16)
+    step, others = 2, []
+    while 2 * step < here.columns:
+        low = (low.astype(f32) + here.across(low, step).astype(f32)).astype(bf16)
         step *= 2
-    half = half.astype(bf16)
-    other = here.across(half, 1)
-    first = side == 0
-    return jnp.concatenate([jnp.where(first, half, other), jnp.where(first, other, half)], axis=0).astype(f32)
+    return low, here.across(low, step)
+
+
+def column_third(here, half, other):
+    half = (half.astype(f32) + other.astype(f32)).astype(bf16)
+    return half, here.across(half, 1)
+
+
+def column_last(here, half, other):
+    first = (here.column & 1) == 0
+    return jnp.concatenate([jnp.where(first, half, other), jnp.where(first, other, half)], axis=0)
 
 
 def per_device(
@@ -419,25 +521,27 @@
     rows = here.columns * half
     length = here.columns * piece
 
+    flat = jnp.concatenate(to_sequence(here, tokens), axis=0)
+
+    vectors = (query_bias, value_bias, merge_bias, first_gain, first_shift, down_bias, second_gain, second_shift)
+    columns = jnp.concatenate([jnp.stack(vectors, axis=1), up_bias.reshape(own, -1)], axis=1)
+    columns = jnp.pad(columns, ((0, 0), (0, LANES - columns.shape[1])))
     mix_local = mix_weight.reshape(own, H, 3, HD).transpose(0, 2, 1, 3).reshape(own, 3 * width)
-    mix_full = lax.all_gather(mix_local, "fsdp", axis=0, tiled=True)
-    small = (query_bias, value_bias, merge_bias, first_gain, first_shift, down_bias, second_gain, second_shift, up_bias)
-    packed = lax.all_gather(jnp.concatenate(small).reshape(1, -1), "fsdp", axis=0, tiled=True).astype(f32)
-
-    def vector(j):
-        return packed[:, j * own : (j + 1) * own].reshape(-1)
-
-    query_full, value_full, merge_bias_full, gain_one, shift_one, down_bias_full, gain_two, shift_two = map(vector, range(8))
-    up_bias_full = packed[:, 8 * own :].reshape(-1)
-    merge_full = lax.all_gather(merge_weight, "fsdp", axis=0, tiled=True)
-    up_full = lax.all_gather(up_weight, "fsdp", axis=0, tiled=True)
-    down_full = lax.all_gather(down_weight, "fsdp", axis=0, tiled=True)
-
-    ids_own = to_sequence(here, segment_ids.reshape(groups, piece, 1)).reshape(here.columns, half)
+    mix_all = gather_shards(here, jnp.concatenate([mix_local, columns], axis=1))
+    mix_full, columns_full = mix_all[:, : 3 * width], mix_all[:, 3 * width :].astype(f32)
+    merge_up = gather_shards(here, jnp.concatenate([merge_weight, up_weight], axis=1))
+    merge_full, up_full = merge_up[:, :width], merge_up[:, width:]
+    down_full = gather_shards(here, down_weight)
+    turned = columns_full[:, :8].T
+    query_full, value_full, merge_bias_full, gain_one, shift_one, down_bias_full, gain_two, shift_two = [
+        turned[j] for j in range(8)
+    ]
+    up_bias_full = columns_full[:, 8 : 8 + hidden_size // width].reshape(-1)
+
+    ids_own = jnp.concatenate(to_sequence(here, segment_ids.reshape(groups, piece, 1)), axis=0).reshape(here.columns, half)
     ids_mate = here.mate(ids_own)
     by_core = jnp.stack([jnp.where(here.core == 0, ids_own, ids_mate), jnp.where(here.core == 0, ids_mate, ids_own)], axis=1)
     ids = jnp.stack([pick(by_core, k ^ here.column) for k in range(here.columns)]).reshape(2 * here.columns, half)
-    blocks = 2 * (jnp.arange(here.columns) ^ here.column) + here.core
     first_id, last_id = ids[:, 0], ids[:, -1]
     low = jnp.sum(last_id[None, :] < ids_own[:, :1], axis=1)
     high = jnp.sum(first_id[None, :] <= ids_own[:, -1:], axis=1)
@@ -445,14 +549,16 @@
     key_ext = key_extension(ids.reshape(length))
     query_ext = query_extension(ids_own.reshape(rows))
 
-    flat = to_sequence(here, tokens).reshape(rows, width)
-    cotangent = to_sequence(here, output_grad).reshape(rows, width).astype(f32)
+    cotangent_slots = to_sequence(here, after(output_grad, flat))
 
     kv_bias = jnp.concatenate([jnp.zeros_like(value_full), value_full])
     key_value = (dot(flat, mix_full[:, width:]) + kv_bias).astype(bf16)
     query = ((dot(flat, mix_full[:, :width]) + query_full) * (LOG2E / math.sqrt(HD))).astype(bf16)
     key_value_mate = here.mate(key_value)
     context, ext = attention_forward(info, query, key_value, key_value_mate, query_ext, key_ext, HD)
+
+    cotangent = jnp.concatenate(after(cotangent_slots, context), axis=0).astype(f32)
+    merge_full, up_full, down_full = after((merge_full, up_full, down_full), context)
 
     attended = dot(context, merge_full) + merge_bias_full
     first_out, normed_one, factor_one = norm_forward(flat.astype(f32) + attended, gain_one, shift_one)
@@ -462,14 +568,16 @@
     active_low = active.astype(bf16)
     branch = dot(active_low, down_full) + down_bias_full
     result, normed_two, factor_two = norm_forward(first_out + branch, gain_two, shift_two)
-    output = from_sequence(here, result.astype(bf16).reshape(here.columns, half, width), groups)
+    output_slots = from_sequence_send(here, list(result.astype(bf16).reshape(here.columns, half, width)))
 
     grad_second, second_gain_grad, second_shift_grad = norm_backward(cotangent, normed_two, factor_two, gain_two)
     grad_branch = grad_second.astype(bf16)
     down_grad = dot(active_low.T, grad_branch)
+    down_kept, down_other = share_pair(here, down_grad.reshape(shards, -1, width))
     down_bias_grad = column_sums(grad_branch)
     grad_active = dot(grad_branch, down_full.T)
     grad_hidden = (grad_active * slope).astype(bf16)
+    down_share, down_others = share_plane(here, down_kept, after(down_other, grad_hidden))
     up_grad = dot(first_low.T, grad_hidden)
     up_bias_grad = column_sums(grad_hidden)
     grad_first = grad_second + dot(grad_hidden, up_full.T)
@@ -477,25 +585,55 @@
     grad_attended = grad_sum.astype(bf16)
     merge_grad = dot(context.T, grad_attended)
     merge_bias_grad = column_sums(grad_attended)
+    up_merge = jnp.concatenate([up_grad.reshape(shards, own, hidden_size), merge_grad.reshape(shards, own, width)], axis=2)
+    up_kept, up_other = share_pair(here, up_merge)
     grad_context = dot(grad_attended, merge_full.T).astype(bf16)
-
-    final_down = reduce_share(here, down_grad.reshape(shards, -1, width))
-    final_up = reduce_share(here, up_grad.reshape(shards, own, hidden_size))
-    final_merge = reduce_share(here, merge_grad.reshape(shards, own, width))
-
-    grad_query, grad_own, grad_mate = attention_backward(
-        info, query, ext, grad_context, context, key_value, key_value_mate, key_ext, HD
-    )
-    grad_kv = (grad_own + here.mate(grad_mate).astype(f32)).astype(bf16)
-    grad_mixed = jnp.concatenate([grad_query, grad_kv[0], grad_kv[1]], axis=1)
-    mix_grad = dot(flat.T, grad_mixed)
-    bias_sums = column_sums(grad_mixed)
-    query_grad, value_grad = bias_sums[:width], bias_sums[2 * width :]
-    input_grad = (grad_sum + dot(grad_mixed, mix_full.T)).astype(bf16)
-    final_input = from_sequence(here, input_grad.reshape(here.columns, half, width), groups).astype(f32)
-
-    final_mix = reduce_share(here, mix_grad.reshape(shards, own, 3 * width))
-    final_mix = final_mix.reshape(own, 3, H, HD).transpose(0, 2, 1, 3).reshape(own, 3 * width)
+    up_share, up_others = share_plane(here, up_kept, after(up_other, grad_context))
+
+    def backward(part, grads):
+        pairs = width // LANES // PARTS
+        dq, kept, other = attention_backward(
+            info, query, ext, grads, context, key_value, key_value_mate, key_ext, HD, part * pairs, pairs
+        )
+        return dq, kept, here.mate(other)
+
+    def mixed_part(pieces):
+        dq, kept, other = pieces
+        kv = (kept + other.astype(f32)).astype(bf16)
+        return jnp.concatenate([dq, kv[0], kv[1]], axis=1)
+
+    part_width = width // PARTS
+
+    def weight_part(part):
+        return jnp.concatenate(
+            [mix_full[:, j * width + part * part_width : j * width + (part + 1) * part_width] for j in range(3)], axis=1
+        )
+
+    one = backward(0, after(grad_context, down_share, up_share))
+    down_others, down_share = after((down_others, down_share), one[0])
+    down_half, down_other = column_first(here, share_sum(down_share, down_others))
+    up_others, up_share = after((up_others, up_share), one[0])
+    up_half, up_other = column_first(here, share_sum(up_share, up_others))
+    two = backward(1, after(grad_context, down_half, up_half))
+    down_half, down_other = column_second(here, *after((down_half, down_other), two[0]))
+    up_half, up_other = column_second(here, *after((up_half, up_other), two[0]))
+    mixed_one = mixed_part(after(one, two[0]))
+    mix_grad_one = dot(flat.T, mixed_one)
+    mix_kept_one, mix_other_one = share_pair(here, mix_grad_one.reshape(shards, own, -1))
+    input_part = dot(mixed_one, weight_part(0).T)
+    three = backward(2, after(grad_context, down_half, up_half, input_part, mix_kept_one))
+    down_half, down_other = column_third(here, *after((down_half, down_other), three[0]))
+    up_half, up_other = column_third(here, *after((up_half, up_other), three[0]))
+    mixed_two = mixed_part(after(two, three[0]))
+    mixed_three = mixed_part(three)
+    mixed_rest = jnp.concatenate([mixed_two, mixed_three], axis=1)
+    input_grad = grad_sum + input_part + dot(mixed_rest, jnp.concatenate([weight_part(1), weight_part(2)], axis=1).T)
+    input_slots = from_sequence_send(here, list(input_grad.astype(bf16).reshape(here.columns, half, width)))
+    mix_grad_rest = dot(flat.T, mixed_rest)
+
+    sums = [column_sums(m) for m in (mixed_one, mixed_two, mixed_three)]
+    query_grad = jnp.concatenate([s[:part_width] for s in sums])
+    value_grad = jnp.concatenate([s[2 * part_width :] for s in sums])
     vectors = (
         query_grad,
         value_grad,
@@ -505,11 +643,24 @@
         down_bias_grad,
         second_gain_grad,
         second_shift_grad,
-        up_bias_grad,
     )
-    packed_grad = jnp.concatenate([v.reshape(shards, -1) for v in vectors], axis=1)
-    final_packed = reduce_share(here, packed_grad.reshape(shards, 2, -1)).reshape(-1)
-    finals = [final_packed[j * own : (j + 1) * own] for j in range(8)] + [final_packed[8 * own :]]
+    columns_grad = jnp.concatenate([jnp.stack(vectors, axis=1), up_bias_grad.reshape(width, -1)], axis=1)
+    columns_grad = jnp.pad(columns_grad, ((0, 0), (0, LANES - columns_grad.shape[1])))
+    rest = jnp.concatenate([mix_grad_rest, columns_grad], axis=1).reshape(shards, own, -1)
+    rest_kept, rest_other = share_pair(here, rest)
+    mix_share_one, mix_others_one = share_plane(here, mix_kept_one, mix_other_one)
+    rest_share, rest_others = share_plane(here, rest_kept, rest_other)
+    mix_share = jnp.concatenate([share_sum(mix_share_one, mix_others_one), share_sum(rest_share, rest_others)], axis=1)
+    mix_last = column_last(here, *column_third(here, *column_second(here, *column_first(here, mix_share))))
+
+    output = from_sequence_end(here, after(output_slots, three[0]), groups)
+    final_input = from_sequence_end(here, input_slots, groups).astype(f32)
+    final_down = column_last(here, down_half, down_other).astype(f32)
+    final_up_merge = column_last(here, up_half, up_other).astype(f32)
+    final_mix = mix_last[:, : 3 * width].astype(f32).reshape(own, PARTS, 3, H // PARTS, HD)
+    final_mix = final_mix.transpose(0, 1, 3, 2, 4).reshape(own, 3 * width)
+    final_columns = mix_last[:, 3 * width :].astype(f32)
+    finals = final_columns[:, :8].T
     (
         final_query,
         final_value,
@@ -519,19 +670,19 @@
         final_down_bias,
         final_gain_two,
         final_shift_two,
-        final_up_bias,
-    ) = finals
+    ) = [finals[j] for j in range(8)]
+    final_up_bias = final_columns[:, 8 : 8 + hidden_size // width].reshape(-1)
     return (
         output,
         final_input,
         final_mix,
         final_query,
         final_value,
-        final_merge,
+        final_up_merge[:, hidden_size:],
         final_merge_bias,
         final_gain_one,
         final_shift_one,
-        final_up,
+        final_up_merge[:, :hidden_size],
         final_up_bias,
         final_down,
         final_down_bias,

time: 694 us -> 636 us (0.916)
  waiting for transfers between devices: 195 us -> 95.5 us
  local copies, waits for them, and re-layouts: 39.7 us -> 98.1 us
  other arithmetic: 46.1 us -> 72.9 us
  Pallas kernels: 168 us -> 153 us
  between operations: 15.3 us -> 2.47 us
  blocking collectives: 10.3 us -> 0 us
    ppermute x30 -> x24, waiting for transfers between devices: 142 us -> 71.4 us  [across(): return lax.ppermute(values, 'seq', xor_pairs(self.columns, bits))]
    pallas_call x1, Pallas kernels: 78.9 us -> 51 us  [attention_forward(): pl.pallas_call(functools.partial(forward_kernel, size=size), grid_spec=pl...]
    ppermute x15 -> x24, waiting for transfers between devices: 51.4 us -> 23.9 us  [aside(): return lax.ppermute(values, 'fsdp', xor_pairs(self.shards, 2 * bits))]
    ppermute x30 -> x24, starting transfers between devices: 46 us -> 68.9 us  [across(): return lax.ppermute(values, 'seq', xor_pairs(self.columns, bits))]
    ppermute x15 -> x24, starting transfers between devices: 70.1 us -> 47.6 us  [aside(): return lax.ppermute(values, 'fsdp', xor_pairs(self.shards, 2 * bits))]
    another operation x1 -> x19, local copies, waits for them, and re-layouts: 0.09 us -> 15.8 us  [the longest x16 14 us: per_device(): jnp.stack(vectors, axis=1)]
    unnamed x131 -> x168, local copies, waits for them, and re-layouts: 7.72 us -> 22.9 us
    pallas_call x0 -> x3, Pallas kernels: none -> 14.6 us  [place(): pl.pallas_call(place_kernel, grid_spec=pltpu.PrefetchScalarGridSpec(num_s...]
  transfers between devices with their start and end apart: 62 -> 74, of which waited for: 24 -> 14; matrix products, arithmetic and copies ran while one was open for 22% -> 28% of each run, Pallas kernels for 24% -> 24%
where the time goes in v2:
time: 636 us; the launch traced here: 628 us
  Pallas kernels  153 us (24%)
  starting transfers between devices  122 us (19%)
  local copies, waits for them, and re-layouts  98.1 us (15%)
  waiting for transfers between devices  95.5 us (15%)
  matrix products  85.2 us (13%)
  other arithmetic  72.9 us (11%)
    pallas_call x3, Pallas kernels, attention_backward(): pl.pallas_call(functools.partial(backward_kernel, size=size), grid_spec=p...  87 us
    dot_general x15, matrix products, dot(): return jnp.dot(a, b, preferred_element_type=f32)  85.2 us
    ppermute x24, waiting for transfers between devices, across(): return lax.ppermute(values, 'seq', xor_pairs(self.columns, bits))  71.4 us
    ppermute x24, starting transfers between devices, across(): return lax.ppermute(values, 'seq', xor_pairs(self.columns, bits))  68.9 us
    pallas_call x1, Pallas kernels, attention_forward(): pl.pallas_call(functools.partial(forward_kernel, size=size), grid_spec=pl...  51 us
    ppermute x24, starting transfers between devices, aside(): return lax.ppermute(values, 'fsdp', xor_pairs(self.shards, 2 * bits))  47.6 us
    ppermute x24, waiting for transfers between devices, aside(): return lax.ppermute(values, 'fsdp', xor_pairs(self.shards, 2 * bits))  23.9 us
    unnamed x168, local copies, waits for them, and re-layouts  22.9 us
  transfers between devices with their start and end apart: 74, of which 14 were waited for; matrix products, arithmetic and copies ran while one was open for 28% of the time, Pallas kernels for 24%

profile of v2, /device:TPU:0, one launch (start us, length us, event | category | flops | bytes accessed | tf_op | source)
XLA Modules:
  0.0 628.3 jit_solution(16179212085841222099)
XLA Ops:
  10.3 3.0 collective-permute-start.9
  16.6 2.9 constant_dynamic-slice_fusion.13
  20.1 4.1 collective-permute-done.9.refs_1_
  26.8 3.7 collective-permute-start.7
  41.6 5.6 collective-permute-done.12
  50.6 3.6 collective-permute-start.3
  58.0 3.8 place_parts.3
  66.2 22.1 %collective-permute-done.2 = bf16[256,768]{0,1:T(8,128)(2,1)S(1)} collective-permute-done((bf16[256,768]{0,1:T(8,128)(2,1)}, bf16[256,768]{0,1:T(8,128)(2,1)S(1)}, u32[]{:S(2)}, u32[]{:S(2)}) %collective-permute-start.2) | collective-permute-done | bytes 393248 | tf_op jit(solution)/shard_map/ppermute | solution.py:373
  89.5 4.8 add_convert_fusion.k_own.v_own
  96.3 7.1 %collective-permute-done.27.refs_2_ = bf16[384,768]{1,0:T(8,128)(2,1)} collective-permute-done((bf16[384,768]{1,0:T(8,128)(2,1)}, bf16[384,768]{1,0:T(8,128)(2,1)}, u32[]{:S(2)}, u32[]{:S(2)}) %collective-permute-start.27) | collective-permute-done | bytes 589856 | tf_op jit(solution)/shard_map/ppermute | solution.py:376
  113.0 2.0 collective-permute-start.21
  116.1 3.1 collective-permute-done.20
  119.2 2.3 collective-permute-done.21
  125.8 2.8 fusion.41
  132.1 4.6 multiply_convert_fusion.1.q_ref
  136.7 4.8 place_parts.5
  141.6 2.9 collective-permute-start.39
  146.0 6.0 place_parts.4
  152.0 2.4 slice.274
  154.4 4.7 slice.275
  159.2 51.0 %attention_forward.1 = (bf16[1024,768]{1,0:T(8,128)(2,1)}, bf16[1024,768]{1,0:T(8,128)(2,1)}) custom-call(s32[10]{0:T(128)} %pad_add_fusion.3.info, bf16[1024,768]{1,0:T(8,128)(2,1)} %multiply_convert_fusion.1.q_ref, bf16[1024,1536]{1,0:T(8,128)(2,1)} %copy-done, bf16[1024,1536]{1,0:T(8,128)(2,1)} %collective-permute-done.17.k_mate.v_mate, ...), custom_call_target="tpu_custom_call" | custom-call | flops 3221225472 | bytes 12582912 | tf_op jit(solution)/shard_map/attention_forward/pallas_call | solution.py:134
  210.3 3.2 fusion.96
  214.2 11.3 %multiply_convert_fusion = (bf16[1024,3072]{1,0:T(8,128)(2,1)}, f32[1024,3072]{1,0:T(8,128)}) fusion(f32[3072]{0:T(1024)S(1)} %copy-done.46, bf16[768,3072]{1,0:T(8,128)(2,1)S(1)} %bitcast.238, f32[1024,768]{0,1:T(8,128)S(1)} %get-tuple-element.317, f32[768]{0:T(1024)S(1)} %copy-done.49, f32[768]{0:T(1024)S(1)} %copy-done.43, ...), kind=kOutput, calls=%fused_computation.10 | convolution fusion | flops 4854644736 | bytes 26765312 | tf_op jit(solution)/shard_map/dot_general | solution.py:341
  225.5 7.7 %fusion.97 = (f32[1024]{0:T(1024)S(1)}, f32[1024,768]{0,1:T(8,128)S(1)}) fusion(f32[768]{0:T(1024)S(1)} %copy-done.50, bf16[1024,3072]{1,0:T(8,128)(2,1)} %get-tuple-element.318, bf16[3072,768]{1,0:T(8,128)(2,1)S(1)} %bitcast.235, f32[768]{0:T(1024)S(1)} %copy-done.49, f32[768]{0:T(1024)S(1)} %copy-done.43, f32[1024]{0:T(1024)S(1)} %add_rsqrt_fusion.1, ...), kind=kOutput, calls=%fused_computation.315 | convolution fusion | flops 4837342208 | bytes 17323008 | tf_op jit(solution)/shard_map/dot_general | solution.py:341
  233.6 2.8 fusion.17
  236.5 16.0 %convert_reduce_fusion.2 = (f32[768]{0:T(1024)}, bf16[1024,768]{0,1:T(8,128)(2,1)S(1)}, bf16[1024,768]{0,1:T(8,128)(2,1)S(1)}, f32[768]{0:T(1024)}) fusion(f32[1024]{0:T(1024)S(1)} %broadcast_multiply_fusion.2, f32[1024,768]{0,1:T(8,128)S(1)} %get-tuple-element.321, f32[1024]{0:T(1024)S(1)} %broadcast_multiply_fusion.4, ...), kind=kLoop, calls=%fused_computation.34 | loop fusion | flops 17299968 | bytes 7892992 | tf_op jit(solution)/shard_map/reduce_sum | solution.py:345
  252.5 7.6 %fusion.98 = f32[3072,768]{1,0:T(8,128)} fusion(bf16[1024,3072]{1,0:T(8,128)(2,1)S(1)} %bitcast.273, bf16[1024,768]{0,1:T(8,128)(2,1)S(1)} %get-tuple-element.223), kind=kOutput, calls=%fused_computation.316 | convolution fusion | flops 4831838208 | bytes 17301504 | tf_op jit(solution)/shard_map/dot_general | solution.py:341
  260.1 12.4 %convert_reduce_fusion = (f32[3072]{0:T(1024)}, bf16[1024,3072]{1,0:T(8,128)(2,1)S(1)}) fusion(f32[1024,3072]{1,0:T(8,128)} %get-tuple-element.319, f32[3072]{0:T(1024)S(1)} %copy-done.46, bf16[1024,768]{0,1:T(8,128)(2,1)S(1)} %get-tuple-element.223, bf16[3072,768]{1,0:T(8,128)(2,1)S(1)} %bitcast.236), kind=kOutput, calls=%fused_computation.9 | convolution fusion | flops 4872729600 | bytes 25190400 | tf_op jit(solution)/shard_map/dot_general | solution.py:341
  272.5 8.6 %multiply_reduce_fusion = (f32[768]{0:T(1024)}, f32[1024]{0:T(1024)S(1)}, f32[1024]{0:T(1024)S(1)}, f32[768]{0:T(1024)}, f32[1024,768]{0,1:T(8,128)S(1)}) fusion(f32[1024,768]{0,1:T(8,128)S(1)} %get-tuple-element.317, f32[1024]{0:T(1024)S(1)} %add_rsqrt_fusion.1, f32[1024]{0:T(1024)S(1)} %broadcast_multiply_fusion.5, f32[768]{0:T(1024)S(1)} %copy-done.43, ...), kind=kOutput, calls=%fused_computation.35 | convolution fusion | flops 4851494912 | bytes 22065152 | tf_op jit(solution)/shard_map/dot_general | solution.py:341
  281.1 5.3 fusion.80
  286.4 7.3 %fusion.20 = bf16[4,384,768]{2,1,0:T(8,128)(2,1)} fusion(f32[4,2,384,768]{3,2,1,0:T(8,128)} %bitcast.231, s32[]{:T(128)S(6)} %select_n.274), kind=kLoop, calls=%fused_computation.57 | loop fusion | bytes 4718596 | tf_op jit(solution)/shard_map/convert_element_type | solution.py:457
  297.1 2.2 fusion.18
  309.0 2.5 slice_dynamic-update-slice_fusion
  320.5 2.6 convolution_convert_fusion.do_ref
  323.1 3.9 fusion.90
  328.3 8.8 %collective-permute-start.42 = (bf16[384,768]{1,0:T(8,128)(2,1)}, bf16[384,768]{1,0:T(8,128)(2,1)}, u32[]{:S(2)}, u32[]{:S(2)}) collective-permute-start(bf16[384,768]{1,0:T(8,128)(2,1)} %get-tuple-element.242), channel_id=1, source_target_pairs={{0,2},{1,3},{2,0},{3,1},{4,6},{5,7},{6,4},{7,5},{8,10},{9,11},{10,... | collective-permute-start | bytes 1769480 | tf_op jit(solution)/shard_map/ppermute | solution.py:376
  337.1 7.8 %collective-permute-start.43 = (bf16[384,768]{1,0:T(8,128)(2,1)}, bf16[384,768]{1,0:T(8,128)(2,1)}, u32[]{:S(2)}, u32[]{:S(2)}) collective-permute-start(bf16[384,768]{1,0:T(8,128)(2,1)} %get-tuple-element.241), channel_id=1, source_target_pairs={{0,4},{1,5},{2,6},{3,7},{4,0},{5,1},{6,2},{7,3},{8,12},{9,13},{10,... | collective-permute-start | bytes 1769480 | tf_op jit(solution)/shard_map/ppermute | solution.py:376
  345.1 6.5 %fusion.88 = (bf16[4,96,3840]{2,1,0:T(8,128)(2,1)}, f32[4,96,3840]{2,1,0:T(8,128)}) fusion(bf16[4,96,3840]{2,1,0:T(8,128)(2,1)} %collective-permute-done.45, s32[]{:T(128)S(6)} %select_n.273, f32[4,2,96,768]{3,2,1,0:T(8,128)} %bitcast.230, f32[4,2,96,3072]{3,2,1,0:T(8,128)S(1)} %bitcast.215), kind=kLoop, calls=%fused_computation.307 | loop fusion | flops 5898240 | bytes 23592964 | tf_op jit(solution)/shard_map/convert_element_type | solution.py:462
  351.6 3.0 dynamic-slice_bitcast_fusion.3
  356.0 2.0 collective-permute-start.48
  358.0 2.9 collective-permute-start.49
  362.4 28.8 %attention_backward.3 = (bf16[1024,256]{1,0:T(8,128)(2,1)}, f32[2,1024,256]{2,1,0:T(8,128)}, bf16[2,1024,256]{2,1,0:T(8,128)(2,1)}) custom-call(s32[10]{0:T(128)} %pad_add_fusion.3.info, bf16[1024,768]{1,0:T(8,128)(2,1)} %multiply_convert_fusion.1.q_ref, bf16[1024,768]{1,0:T(8,128)(2,1)} %get-tuple-element.69.ext_ref, ...), custom_call_target="tpu_custom_call" | custom-call | flops 2684354560 | bytes 6291456 | tf_op jit(solution)/shard_map/attention_backward/pallas_call | solution.py:254
  391.3 18.4 %collective-permute-start.35 = (bf16[256,768]{0,1:T(8,128)(2,1)}, bf16[256,768]{0,1:T(8,128)(2,1)}, u32[]{:S(2)}, u32[]{:S(2)}) collective-permute-start(bf16[256,768]{0,1:T(8,128)(2,1)} %get-tuple-element.267), channel_id=1, source_target_pairs={{0,16},{8,24},{16,0},{24,8},{1,17},{9,25},{17,1},{25,9},{2,18},{10... | collective-permute-start | bytes 1179656 | tf_op jit(solution)/shard_map/ppermute | solution.py:373
  415.6 29.2 %attention_backward.4 = (bf16[1024,256]{1,0:T(8,128)(2,1)}, f32[2,1024,256]{2,1,0:T(8,128)}, bf16[2,1024,256]{2,1,0:T(8,128)(2,1)}) custom-call(s32[10]{0:T(128)} %pad_add_fusion.3.info, bf16[1024,768]{1,0:T(8,128)(2,1)} %multiply_convert_fusion.1.q_ref, bf16[1024,768]{1,0:T(8,128)(2,1)} %get-tuple-element.69.ext_ref, ...), custom_call_target="tpu_custom_call" | custom-call | flops 2684354560 | bytes 6291456 | tf_op jit(solution)/shard_map/attention_backward/pallas_call | solution.py:254
  447.2 14.3 %collective-permute-start.72 = (bf16[192,768]{1,0:T(8,128)(2,1)}, bf16[192,768]{1,0:T(8,128)(2,1)}, u32[]{:S(2)}, u32[]{:S(2)}) collective-permute-start(bf16[192,768]{1,0:T(8,128)(2,1)} %add_convert_fusion.11), channel_id=1, source_target_pairs={{0,16},{8,24},{16,0},{24,8},{1,17},{9,25},{17,1},{25,9},{2,18},{10... | collective-permute-start | bytes 884744 | tf_op jit(solution)/shard_map/ppermute | solution.py:373
  463.2 3.1 fusion.24
  466.3 2.8 fusion.79
  469.4 2.4 copy.172
  473.2 1.9 add_convert_fusion.9
  475.2 2.6 fusion.85
  477.9 29.0 %attention_backward.5 = (bf16[1024,256]{1,0:T(8,128)(2,1)}, f32[2,1024,256]{2,1,0:T(8,128)}, bf16[2,1024,256]{2,1,0:T(8,128)(2,1)}) custom-call(s32[10]{0:T(128)} %pad_add_fusion.3.info, bf16[1024,768]{1,0:T(8,128)(2,1)} %multiply_convert_fusion.1.q_ref, bf16[1024,768]{1,0:T(8,128)(2,1)} %get-tuple-element.69.ext_ref, ...), custom_call_target="tpu_custom_call" | custom-call | flops 2684354560 | bytes 6291456 | tf_op jit(solution)/shard_map/attention_backward/pallas_call | solution.py:254
  508.7 3.4 collective-permute-start.60
  518.5 4.9 collective-permute-start.73
  526.7 4.5 collective-permute-done.73
  535.6 2.8 concatenate.126
  538.4 5.0 fusion.84
  550.2 2.0 collective-permute-start.64
  552.3 4.4 add_convert_fusion.1
  556.8 13.4 %collective-permute-start.57 = (bf16[256,768]{0,1:T(8,128)(2,1)S(1)}, bf16[256,768]{0,1:T(8,128)(2,1)S(1)}, u32[]{:S(2)}, u32[]{:S(2)}) collective-permute-start(bf16[256,768]{0,1:T(8,128)(2,1)S(1)} %get-tuple-element.251), channel_id=1, source_target_pairs={{0,24},{8,16},{16,8},{24,0},{1,25},{9,17},{17,9},{25,1},{2,26},{10... | collective-permute-start | bytes 1179656 | tf_op jit(solution)/shard_map/ppermute | solution.py:373
  572.5 7.7 %collective-permute-done.57 = bf16[256,768]{0,1:T(8,128)(2,1)S(1)} collective-permute-done((bf16[256,768]{0,1:T(8,128)(2,1)S(1)}, bf16[256,768]{0,1:T(8,128)(2,1)S(1)}, u32[]{:S(2)}, u32[]{:S(2)}) %collective-permute-start.57) | collective-permute-done | bytes 393248 | tf_op jit(solution)/shard_map/ppermute | solution.py:373
  580.2 22.7 %collective-permute-done.56 = bf16[256,768]{0,1:T(8,128)(2,1)S(1)} collective-permute-done((bf16[256,768]{0,1:T(8,128)(2,1)S(1)}, bf16[256,768]{0,1:T(8,128)(2,1)S(1)}, u32[]{:S(2)}, u32[]{:S(2)}) %collective-permute-start.56) | collective-permute-done | bytes 393248 | tf_op jit(solution)/shard_map/ppermute | solution.py:373
  606.1 9.6 %collective-permute-done.68 = bf16[48,2432]{1,0:T(8,128)(2,1)S(1)} collective-permute-done((bf16[48,2432]{1,0:T(8,128)(2,1)S(1)}, bf16[48,2432]{1,0:T(8,128)(2,1)S(1)}, u32[]{:S(2)}, u32[]{:S(2)}) %collective-permute-start.68) | collective-permute-done | bytes 233504 | tf_op jit(solution)/shard_map/ppermute | solution.py:373
  617.6 2.4 copy.185
  619.9 3.6 collective-permute-done.69
  (438 shorter events, 135.2 us)
Async XLA Ops:
  10.3 13.9 %collective-permute-start.9 = (bf16[96,2432]{1,0:T(8,128)(2,1)}, bf16[96,2432]{1,0:T(8,128)(2,1)S(1)}, u32[]{:S(2)}, u32[]{:S(2)}) collective-permute-start(bf16[96,2432]{1,0:T(8,128)(2,1)} %fusion.36.refs_0_), channel_id=1, source_target_pairs={{0,2},{1,3},{2,0},{3,1},{4,6},{5,7},{6,4},{7,5},{8,10},{9,11},{10,... | collective-permute-start | bytes 1400840 | tf_op jit(solution)/shard_map/ppermute | solution.py:376
  13.3 25.3 %collective-permute-start.10 = (bf16[96,2432]{1,0:T(8,128)(2,1)}, bf16[96,2432]{1,0:T(8,128)(2,1)}, u32[]{:S(2)}, u32[]{:S(2)}) collective-permute-start(bf16[96,2432]{1,0:T(8,128)(2,1)} %fusion.36.refs_0_), channel_id=1, source_target_pairs={{0,4},{1,5},{2,6},{3,7},{4,0},{5,1},{6,2},{7,3},{8,12},{9,13},{10,... | collective-permute-start | bytes 1400840 | tf_op jit(solution)/shard_map/ppermute | solution.py:376
  14.8 11.9 %collective-permute-start.4 = (s32[2,256,1]{1,2,0:T(1,128)S(1)}, s32[2,256,1]{1,2,0:T(1,128)S(1)}, u32[]{:S(2)}, u32[]{:S(2)}) collective-permute-start(s32[2,256,1]{1,2,0:T(1,128)S(1)} %get-tuple-element.315), channel_id=1, source_target_pairs={{0,1},{1,0},{2,3},{3,2},{4,5},{5,4},{6,7},{7,6},{8,9},{9,8},{10,11... | collective-permute-start | bytes 6152 | tf_op jit(solution)/shard_map/ppermute | solution.py:370
  25.0 16.1 %collective-permute-start.11 = (bf16[48,2432]{1,0:T(8,128)(2,1)}, bf16[48,2432]{1,0:T(8,128)(2,1)S(1)}, u32[]{:S(2)}, u32[]{:S(2)}) collective-permute-start(bf16[48,2432]{1,0:T(8,128)(2,1)} %slice.264), channel_id=1, source_target_pairs={{0,4},{1,5},{2,6},{3,7},{4,0},{5,1},{6,2},{7,3},{8,12},{9,13},{10,... | collective-permute-start | bytes 700424 | tf_op jit(solution)/shard_map/ppermute | solution.py:376
  26.8 10.1 %collective-permute-start.7 = (s32[256,1]{0,1:T(1,128)S(1)}, s32[256,1]{0,1:T(1,128)S(1)}, u32[]{:S(2)}, u32[]{:S(2)}) collective-permute-start(s32[256,1]{0,1:T(1,128)S(1)} %fusion.71), channel_id=1, source_target_pairs={{0,24},{8,16},{16,8},{24,0},{1,25},{9,17},{17,9},{25,1},{2,26},{10... | collective-permute-start | bytes 3080 | tf_op jit(solution)/shard_map/ppermute | solution.py:373
  36.8 17.3 %collective-permute-start.13 = (bf16[96,2432]{1,0:T(8,128)(2,1)}, bf16[96,2432]{1,0:T(8,128)(2,1)S(1)}, u32[]{:S(2)}, u32[]{:S(2)}) collective-permute-start(bf16[96,2432]{1,0:T(8,128)(2,1)} %fusion.36.refs_0_), channel_id=1, source_target_pairs={{0,1},{1,0},{2,3},{3,2},{4,5},{5,4},{6,7},{7,6},{8,9},{9,8},{10,11... | collective-permute-start | bytes 1400840 | tf_op jit(solution)/shard_map/ppermute | solution.py:370
  36.8 12.1 %collective-permute-start = (bf16[2,256,768]{1,2,0:T(8,128)(2,1)}, bf16[2,256,768]{1,2,0:T(8,128)(2,1)S(1)}, u32[]{:S(2)}, u32[]{:S(2)}) collective-permute-start(bf16[2,256,768]{1,2,0:T(8,128)(2,1)} %bitcast.255), channel_id=1, source_target_pairs={{0,1},{1,0},{2,3},{3,2},{4,5},{5,4},{6,7},{7,6},{8,9},{9,8},{10,11... | collective-permute-start | bytes 2359304 | tf_op jit(solution)/shard_map/ppermute | solution.py:370
  41.1 13.1 %collective-permute-start.14 = (bf16[96,2432]{1,0:T(8,128)(2,1)S(1)}, bf16[96,2432]{1,0:T(8,128)(2,1)S(1)}, u32[]{:S(2)}, u32[]{:S(2)}) collective-permute-start(bf16[96,2432]{1,0:T(8,128)(2,1)S(1)} %copy-done.20), channel_id=1, source_target_pairs={{0,1},{1,0},{2,3},{3,2},{4,5},{5,4},{6,7},{7,6},{8,9},{9,8},{10,11... | collective-permute-start | bytes 1400840 | tf_op jit(solution)/shard_map/ppermute | solution.py:370
  41.1 14.1 %collective-permute-start.15 = (bf16[96,2432]{1,0:T(8,128)(2,1)}, bf16[96,2432]{1,0:T(8,128)(2,1)S(1)}, u32[]{:S(2)}, u32[]{:S(2)}) collective-permute-start(bf16[96,2432]{1,0:T(8,128)(2,1)} %collective-permute-done.10.refs_2_), channel_id=1, source_target_pairs={{0,1},{1,0},{2,3},{3,2},{4,5},{5,4},{6,7},{7,6},{8,9},{9,8},{10,11... | collective-permute-start | bytes 1400840 | tf_op jit(solution)/shard_map/ppermute | solution.py:370
  47.3 9.4 %collective-permute-start.16 = (bf16[96,2432]{1,0:T(8,128)(2,1)S(1)}, bf16[96,2432]{1,0:T(8,128)(2,1)S(1)}, u32[]{:S(2)}, u32[]{:S(2)}) collective-permute-start(bf16[96,2432]{1,0:T(8,128)(2,1)S(1)} %constant_dynamic-update-slice_fusion.refs_3_), channel_id=1, source_target_pairs={{0,1},{1,0},{2,3},{3,2},{4,5},{5,4},{6,7},{7,6},{8,9},{9,8},{10,11... | collective-permute-start | bytes 1400840 | tf_op jit(solution)/shard_map/ppermute | solution.py:370
  50.6 14.1 %collective-permute-start.3 = (bf16[256,768]{0,1:T(8,128)(2,1)}, bf16[256,768]{0,1:T(8,128)(2,1)S(1)}, u32[]{:S(2)}, u32[]{:S(2)}) collective-permute-start(bf16[256,768]{0,1:T(8,128)(2,1)} %get-tuple-element.273), channel_id=1, source_target_pairs={{0,24},{8,16},{16,8},{24,0},{1,25},{9,17},{17,9},{25,1},{2,26},{10... | collective-permute-start | bytes 1179656 | tf_op jit(solution)/shard_map/ppermute | solution.py:373
  54.2 34.1 %collective-permute-start.2 = (bf16[256,768]{0,1:T(8,128)(2,1)}, bf16[256,768]{0,1:T(8,128)(2,1)S(1)}, u32[]{:S(2)}, u32[]{:S(2)}) collective-permute-start(bf16[256,768]{0,1:T(8,128)(2,1)} %get-tuple-element.272), channel_id=1, source_target_pairs={{0,16},{8,24},{16,0},{24,8},{1,17},{9,25},{17,1},{25,9},{2,18},{10... | collective-permute-start | bytes 1179656 | tf_op jit(solution)/shard_map/ppermute | solution.py:373
  54.2 34.6 %collective-permute-start.1 = (bf16[256,768]{0,1:T(8,128)(2,1)}, bf16[256,768]{0,1:T(8,128)(2,1)S(1)}, u32[]{:S(2)}, u32[]{:S(2)}) collective-permute-start(bf16[256,768]{0,1:T(8,128)(2,1)} %get-tuple-element.271), channel_id=1, source_target_pairs={{0,8},{8,0},{16,24},{24,16},{1,9},{9,1},{17,25},{25,17},{2,10},{10... | collective-permute-start | bytes 1179656 | tf_op jit(solution)/shard_map/ppermute | solution.py:373
  55.2 51.0 %collective-permute-start.18 = (bf16[96,3840]{1,0:T(8,128)(2,1)}, bf16[96,3840]{1,0:T(8,128)(2,1)}, u32[]{:S(2)}, u32[]{:S(2)}) collective-permute-start(bf16[96,3840]{1,0:T(8,128)(2,1)} %constant_dynamic-update-slice_fusion.2.refs_0_), channel_id=1, source_target_pairs={{0,2},{1,3},{2,0},{3,1},{4,6},{5,7},{6,4},{7,5},{8,10},{9,11},{10,... | collective-permute-start | bytes 2211848 | tf_op jit(solution)/shard_map/ppermute | solution.py:376
  57.5 51.2 %collective-permute-start.19 = (bf16[96,3840]{1,0:T(8,128)(2,1)}, bf16[96,3840]{1,0:T(8,128)(2,1)}, u32[]{:S(2)}, u32[]{:S(2)}) collective-permute-start(bf16[96,3840]{1,0:T(8,128)(2,1)} %constant_dynamic-update-slice_fusion.2.refs_0_), channel_id=1, source_target_pairs={{0,4},{1,5},{2,6},{3,7},{4,0},{5,1},{6,2},{7,3},{8,12},{9,13},{10,... | collective-permute-start | bytes 2211848 | tf_op jit(solution)/shard_map/ppermute | solution.py:376
  64.7 29.8 %collective-permute-start.26 = (bf16[384,768]{1,0:T(8,128)(2,1)}, bf16[384,768]{1,0:T(8,128)(2,1)S(1)}, u32[]{:S(2)}, u32[]{:S(2)}) collective-permute-start(bf16[384,768]{1,0:T(8,128)(2,1)} %refs_0_.1), channel_id=1, source_target_pairs={{0,2},{1,3},{2,0},{3,1},{4,6},{5,7},{6,4},{7,5},{8,10},{9,11},{10,... | collective-permute-start | bytes 1769480 | tf_op jit(solution)/shard_map/ppermute | solution.py:376
  88.2 15.2 %collective-permute-start.27 = (bf16[384,768]{1,0:T(8,128)(2,1)}, bf16[384,768]{1,0:T(8,128)(2,1)}, u32[]{:S(2)}, u32[]{:S(2)}) collective-permute-start(bf16[384,768]{1,0:T(8,128)(2,1)} %refs_0_.1), channel_id=1, source_target_pairs={{0,4},{1,5},{2,6},{3,7},{4,0},{5,1},{6,2},{7,3},{8,12},{9,13},{10,... | collective-permute-start | bytes 1769480 | tf_op jit(solution)/shard_map/ppermute | solution.py:376
  94.3 64.8 %collective-permute-start.17 = (bf16[1024,1536]{1,0:T(8,128)(2,1)S(1)}, bf16[1024,1536]{1,0:T(8,128)(2,1)}, u32[]{:S(2)}, u32[]{:S(2)}) collective-permute-start(bf16[1024,1536]{1,0:T(8,128)(2,1)S(1)} %add_convert_fusion.k_own.v_own), channel_id=1, source_target_pairs={{0,1},{1,0},{2,3},{3,2},{4,5},{5,4},{6,7},{7,6},{8,9},{9,8},{10,11... | collective-permute-start | bytes 9437192 | tf_op jit(solution)/shard_map/ppermute | solution.py:370
  94.6 21.0 %collective-permute-start.30 = (bf16[384,768]{1,0:T(8,128)(2,1)}, bf16[384,768]{1,0:T(8,128)(2,1)}, u32[]{:S(2)}, u32[]{:S(2)}) collective-permute-start(bf16[384,768]{1,0:T(8,128)(2,1)} %refs_0_.1), channel_id=1, source_target_pairs={{0,1},{1,0},{2,3},{3,2},{4,5},{5,4},{6,7},{7,6},{8,9},{9,8},{10,11... | collective-permute-start | bytes 1769480 | tf_op jit(solution)/shard_map/ppermute | solution.py:370
  103.4 9.6 %collective-permute-start.28 = (bf16[192,768]{1,0:T(8,128)(2,1)}, bf16[192,768]{1,0:T(8,128)(2,1)S(1)}, u32[]{:S(2)}, u32[]{:S(2)}) collective-permute-start(bf16[192,768]{1,0:T(8,128)(2,1)} %slice.276), channel_id=1, source_target_pairs={{0,4},{1,5},{2,6},{3,7},{4,0},{5,1},{6,2},{7,3},{8,12},{9,13},{10,... | collective-permute-start | bytes 884744 | tf_op jit(solution)/shard_map/ppermute | solution.py:376
  106.1 9.3 %collective-permute-start.29 = (bf16[192,768]{1,0:T(8,128)(2,1)S(1)}, bf16[192,768]{1,0:T(8,128)(2,1)S(1)}, u32[]{:S(2)}, u32[]{:S(2)}) collective-permute-start(bf16[192,768]{1,0:T(8,128)(2,1)S(1)} %slice.277), channel_id=1, source_target_pairs={{0,2},{1,3},{2,0},{3,1},{4,6},{5,7},{6,4},{7,5},{8,10},{9,11},{10,... | collective-permute-start | bytes 884744 | tf_op jit(solution)/shard_map/ppermute | solution.py:376
  108.7 10.5 %collective-permute-start.20 = (bf16[48,3840]{1,0:T(8,128)(2,1)S(1)}, bf16[48,3840]{1,0:T(8,128)(2,1)S(1)}, u32[]{:S(2)}, u32[]{:S(2)}) collective-permute-start(bf16[48,3840]{1,0:T(8,128)(2,1)S(1)} %slice.272), channel_id=1, source_target_pairs={{0,4},{1,5},{2,6},{3,7},{4,0},{5,1},{6,2},{7,3},{8,12},{9,13},{10,... | collective-permute-start | bytes 1105928 | tf_op jit(solution)/shard_map/ppermute | solution.py:376
  113.0 8.5 %collective-permute-start.21 = (bf16[48,3840]{1,0:T(8,128)(2,1)S(1)}, bf16[48,3840]{1,0:T(8,128)(2,1)S(1)}, u32[]{:S(2)}, u32[]{:S(2)}) collective-permute-start(bf16[48,3840]{1,0:T(8,128)(2,1)S(1)} %slice.273), channel_id=1, source_target_pairs={{0,2},{1,3},{2,0},{3,1},{4,6},{5,7},{6,4},{7,5},{8,10},{9,11},{10,... | collective-permute-start | bytes 1105928 | tf_op jit(solution)/shard_map/ppermute | solution.py:376
  115.6 8.0 %collective-permute-start.31 = (bf16[384,768]{1,0:T(8,128)(2,1)S(1)}, bf16[384,768]{1,0:T(8,128)(2,1)S(1)}, u32[]{:S(2)}, u32[]{:S(2)}) collective-permute-start(bf16[384,768]{1,0:T(8,128)(2,1)S(1)} %copy-done.15), channel_id=1, source_target_pairs={{0,1},{1,0},{2,3},{3,2},{4,5},{5,4},{6,7},{7,6},{8,9},{9,8},{10,11... | collective-permute-start | bytes 1769480 | tf_op jit(solution)/shard_map/ppermute | solution.py:370
  123.0 18.5 %collective-permute-start.22 = (bf16[96,3840]{1,0:T(8,128)(2,1)}, bf16[96,3840]{1,0:T(8,128)(2,1)}, u32[]{:S(2)}, u32[]{:S(2)}) collective-permute-start(bf16[96,3840]{1,0:T(8,128)(2,1)} %constant_dynamic-update-slice_fusion.2.refs_0_), channel_id=1, source_target_pairs={{0,1},{1,0},{2,3},{3,2},{4,5},{5,4},{6,7},{7,6},{8,9},{9,8},{10,11... | collective-permute-start | bytes 2211848 | tf_op jit(solution)/shard_map/ppermute | solution.py:370
  123.6 18.1 %collective-permute-start.23 = (bf16[96,3840]{1,0:T(8,128)(2,1)}, bf16[96,3840]{1,0:T(8,128)(2,1)}, u32[]{:S(2)}, u32[]{:S(2)}) collective-permute-start(bf16[96,3840]{1,0:T(8,128)(2,1)} %collective-permute-done.18.refs_1_), channel_id=1, source_target_pairs={{0,1},{1,0},{2,3},{3,2},{4,5},{5,4},{6,7},{7,6},{8,9},{9,8},{10,11... | collective-permute-start | bytes 2211848 | tf_op jit(solution)/shard_map/ppermute | solution.py:370
  123.7 20.9 %collective-permute-start.24 = (bf16[96,3840]{1,0:T(8,128)(2,1)}, bf16[96,3840]{1,0:T(8,128)(2,1)}, u32[]{:S(2)}, u32[]{:S(2)}) collective-permute-start(bf16[96,3840]{1,0:T(8,128)(2,1)} %collective-permute-done.19.refs_2_), channel_id=1, source_target_pairs={{0,1},{1,0},{2,3},{3,2},{4,5},{5,4},{6,7},{7,6},{8,9},{9,8},{10,11... | collective-permute-start | bytes 2211848 | tf_op jit(solution)/shard_map/ppermute | solution.py:370
  124.1 21.9 %collective-permute-start.25 = (bf16[96,3840]{1,0:T(8,128)(2,1)}, bf16[96,3840]{1,0:T(8,128)(2,1)}, u32[]{:S(2)}, u32[]{:S(2)}) collective-permute-start(bf16[96,3840]{1,0:T(8,128)(2,1)} %constant_dynamic-update-slice_fusion.4.refs_3_), channel_id=1, source_target_pairs={{0,1},{1,0},{2,3},{3,2},{4,5},{5,4},{6,7},{7,6},{8,9},{9,8},{10,11... | collective-permute-start | bytes 2211848 | tf_op jit(solution)/shard_map/ppermute | solution.py:370
  141.5 92.1 %collective-permute-start.38 = (bf16[256,768]{0,1:T(8,128)(2,1)}, bf16[256,768]{0,1:T(8,128)(2,1)}, u32[]{:S(2)}, u32[]{:S(2)}) collective-permute-start(bf16[256,768]{0,1:T(8,128)(2,1)} %get-tuple-element.262), channel_id=1, source_target_pairs={{0,8},{8,0},{16,24},{24,16},{1,9},{9,1},{17,25},{25,17},{2,10},{10... | collective-permute-start | bytes 1179656 | tf_op jit(solution)/shard_map/ppermute | solution.py:373
  141.6 92.0 %collective-permute-start.39 = (bf16[256,768]{0,1:T(8,128)(2,1)}, bf16[256,768]{0,1:T(8,128)(2,1)}, u32[]{:S(2)}, u32[]{:S(2)}) collective-permute-start(bf16[256,768]{0,1:T(8,128)(2,1)} %get-tuple-element.263), channel_id=1, source_target_pairs={{0,16},{8,24},{16,0},{24,8},{1,17},{9,25},{17,1},{25,9},{2,18},{10... | collective-permute-start | bytes 1179656 | tf_op jit(solution)/shard_map/ppermute | solution.py:373
  144.5 89.1 %collective-permute-start.40 = (bf16[256,768]{0,1:T(8,128)(2,1)}, bf16[256,768]{0,1:T(8,128)(2,1)}, u32[]{:S(2)}, u32[]{:S(2)}) collective-permute-start(bf16[256,768]{0,1:T(8,128)(2,1)} %get-tuple-element.260), channel_id=1, source_target_pairs={{0,24},{8,16},{16,8},{24,0},{1,25},{9,17},{17,9},{25,1},{2,26},{10... | collective-permute-start | bytes 1179656 | tf_op jit(solution)/shard_map/ppermute | solution.py:373
  293.8 29.4 %collective-permute-start.41 = (bf16[4,384,768]{2,1,0:T(8,128)(2,1)}, bf16[4,384,768]{2,1,0:T(8,128)(2,1)}, u32[]{:S(2)}, u32[]{:S(2)}) collective-permute-start(bf16[4,384,768]{2,1,0:T(8,128)(2,1)} %fusion.20), channel_id=1, source_target_pairs={{0,1},{1,0},{2,3},{3,2},{4,5},{5,4},{6,7},{7,6},{8,9},{9,8},{10,11... | collective-permute-start | bytes 7077896 | tf_op jit(solution)/shard_map/ppermute | solution.py:370
  299.3 45.7 %collective-permute-start.45 = (bf16[4,96,3840]{2,1,0:T(8,128)(2,1)}, bf16[4,96,3840]{2,1,0:T(8,128)(2,1)}, u32[]{:S(2)}, u32[]{:S(2)}) collective-permute-start(bf16[4,96,3840]{2,1,0:T(8,128)(2,1)} %fusion.18), channel_id=1, source_target_pairs={{0,1},{1,0},{2,3},{3,2},{4,5},{5,4},{6,7},{7,6},{8,9},{9,8},{10,11... | collective-permute-start | bytes 8847368 | tf_op jit(solution)/shard_map/ppermute | solution.py:370
  328.3 29.7 %collective-permute-start.42 = (bf16[384,768]{1,0:T(8,128)(2,1)}, bf16[384,768]{1,0:T(8,128)(2,1)}, u32[]{:S(2)}, u32[]{:S(2)}) collective-permute-start(bf16[384,768]{1,0:T(8,128)(2,1)} %get-tuple-element.242), channel_id=1, source_target_pairs={{0,2},{1,3},{2,0},{3,1},{4,6},{5,7},{6,4},{7,5},{8,10},{9,11},{10,... | collective-permute-start | bytes 1769480 | tf_op jit(solution)/shard_map/ppermute | solution.py:376
  337.1 54.1 %collective-permute-start.43 = (bf16[384,768]{1,0:T(8,128)(2,1)}, bf16[384,768]{1,0:T(8,128)(2,1)}, u32[]{:S(2)}, u32[]{:S(2)}) collective-permute-start(bf16[384,768]{1,0:T(8,128)(2,1)} %get-tuple-element.241), channel_id=1, source_target_pairs={{0,4},{1,5},{2,6},{3,7},{4,0},{5,1},{6,2},{7,3},{8,12},{9,13},{10,... | collective-permute-start | bytes 1769480 | tf_op jit(solution)/shard_map/ppermute | solution.py:376
  344.9 46.3 %collective-permute-start.44 = (bf16[384,768]{1,0:T(8,128)(2,1)}, bf16[384,768]{1,0:T(8,128)(2,1)}, u32[]{:S(2)}, u32[]{:S(2)}) collective-permute-start(bf16[384,768]{1,0:T(8,128)(2,1)} %get-tuple-element.240), channel_id=1, source_target_pairs={{0,6},{1,7},{2,4},{3,5},{4,2},{5,3},{6,0},{7,1},{8,14},{9,15},{10,... | collective-permute-start | bytes 1769480 | tf_op jit(solution)/shard_map/ppermute | solution.py:376
  354.5 57.7 %collective-permute-start.47 = (bf16[96,3840]{1,0:T(8,128)(2,1)}, bf16[96,3840]{1,0:T(8,128)(2,1)}, u32[]{:S(2)}, u32[]{:S(2)}) collective-permute-start(bf16[96,3840]{1,0:T(8,128)(2,1)} %get-tuple-element.239), channel_id=1, source_target_pairs={{0,2},{1,3},{2,0},{3,1},{4,6},{5,7},{6,4},{7,5},{8,10},{9,11},{10,... | collective-permute-start | bytes 2211848 | tf_op jit(solution)/shard_map/ppermute | solution.py:376
  356.0 56.2 %collective-permute-start.48 = (bf16[96,3840]{1,0:T(8,128)(2,1)}, bf16[96,3840]{1,0:T(8,128)(2,1)}, u32[]{:S(2)}, u32[]{:S(2)}) collective-permute-start(bf16[96,3840]{1,0:T(8,128)(2,1)} %get-tuple-element.238), channel_id=1, source_target_pairs={{0,4},{1,5},{2,6},{3,7},{4,0},{5,1},{6,2},{7,3},{8,12},{9,13},{10,... | collective-permute-start | bytes 2211848 | tf_op jit(solution)/shard_map/ppermute | solution.py:376
  358.0 54.8 %collective-permute-start.49 = (bf16[96,3840]{1,0:T(8,128)(2,1)}, bf16[96,3840]{1,0:T(8,128)(2,1)}, u32[]{:S(2)}, u32[]{:S(2)}) collective-permute-start(bf16[96,3840]{1,0:T(8,128)(2,1)} %get-tuple-element.237), channel_id=1, source_target_pairs={{0,6},{1,7},{2,4},{3,5},{4,2},{5,3},{6,0},{7,1},{8,14},{9,15},{10,... | collective-permute-start | bytes 2211848 | tf_op jit(solution)/shard_map/ppermute | solution.py:376
  391.2 115.6 %collective-permute-start.34 = (bf16[256,768]{0,1:T(8,128)(2,1)}, bf16[256,768]{0,1:T(8,128)(2,1)}, u32[]{:S(2)}, u32[]{:S(2)}) collective-permute-start(bf16[256,768]{0,1:T(8,128)(2,1)} %get-tuple-element.268), channel_id=1, source_target_pairs={{0,8},{8,0},{16,24},{24,16},{1,9},{9,1},{17,25},{25,17},{2,10},{10... | collective-permute-start | bytes 1179656 | tf_op jit(solution)/shard_map/ppermute | solution.py:373
  391.3 116.0 %collective-permute-start.35 = (bf16[256,768]{0,1:T(8,128)(2,1)}, bf16[256,768]{0,1:T(8,128)(2,1)}, u32[]{:S(2)}, u32[]{:S(2)}) collective-permute-start(bf16[256,768]{0,1:T(8,128)(2,1)} %get-tuple-element.267), channel_id=1, source_target_pairs={{0,16},{8,24},{16,0},{24,8},{1,17},{9,25},{17,1},{25,9},{2,18},{10... | collective-permute-start | bytes 1179656 | tf_op jit(solution)/shard_map/ppermute | solution.py:373
  412.2 95.1 %collective-permute-start.36 = (bf16[256,768]{0,1:T(8,128)(2,1)}, bf16[256,768]{0,1:T(8,128)(2,1)}, u32[]{:S(2)}, u32[]{:S(2)}) collective-permute-start(bf16[256,768]{0,1:T(8,128)(2,1)} %get-tuple-element.266), channel_id=1, source_target_pairs={{0,24},{8,16},{16,8},{24,0},{1,25},{9,17},{17,9},{25,1},{2,26},{10... | collective-permute-start | bytes 1179656 | tf_op jit(solution)/shard_map/ppermute | solution.py:373
  412.2 32.6 %collective-permute-start.46 = (bf16[192,768]{1,0:T(8,128)(2,1)}, bf16[192,768]{1,0:T(8,128)(2,1)S(1)}, u32[]{:S(2)}, u32[]{:S(2)}) collective-permute-start(bf16[192,768]{1,0:T(8,128)(2,1)} %get-tuple-element.294), channel_id=1, source_target_pairs={{0,8},{8,0},{16,24},{24,16},{1,9},{9,1},{17,25},{25,17},{2,10},{10... | collective-permute-start | bytes 884744 | tf_op jit(solution)/shard_map/ppermute | solution.py:373
  412.8 34.4 %collective-permute-start.51 = (bf16[2,1024,256]{2,1,0:T(8,128)(2,1)}, bf16[2,1024,256]{2,1,0:T(8,128)(2,1)}, u32[]{:S(2)}, u32[]{:S(2)}) collective-permute-start(bf16[2,1024,256]{2,1,0:T(8,128)(2,1)} %get-tuple-element.94), channel_id=1, source_target_pairs={{0,1},{1,0},{2,3},{3,2},{4,5},{5,4},{6,7},{7,6},{8,9},{9,8},{10,11... | collective-permute-start | bytes 3145736 | tf_op jit(solution)/shard_map/ppermute | solution.py:370
  444.8 28.3 %collective-permute-start.50 = (bf16[48,3840]{1,0:T(8,128)(2,1)}, bf16[48,3840]{1,0:T(8,128)(2,1)}, u32[]{:S(2)}, u32[]{:S(2)}) collective-permute-start(bf16[48,3840]{1,0:T(8,128)(2,1)} %get-tuple-element.287), channel_id=1, source_target_pairs={{0,8},{8,0},{16,24},{24,16},{1,9},{9,1},{17,25},{25,17},{2,10},{10... | collective-permute-start | bytes 1105928 | tf_op jit(solution)/shard_map/ppermute | solution.py:373
  447.2 61.5 %collective-permute-start.72 = (bf16[192,768]{1,0:T(8,128)(2,1)}, bf16[192,768]{1,0:T(8,128)(2,1)}, u32[]{:S(2)}, u32[]{:S(2)}) collective-permute-start(bf16[192,768]{1,0:T(8,128)(2,1)} %add_convert_fusion.11), channel_id=1, source_target_pairs={{0,16},{8,24},{16,0},{24,8},{1,17},{9,25},{17,1},{25,9},{2,18},{10... | collective-permute-start | bytes 884744 | tf_op jit(solution)/shard_map/ppermute | solution.py:373
  475.2 33.4 %collective-permute-start.70 = (bf16[48,3840]{1,0:T(8,128)(2,1)}, bf16[48,3840]{1,0:T(8,128)(2,1)}, u32[]{:S(2)}, u32[]{:S(2)}) collective-permute-start(bf16[48,3840]{1,0:T(8,128)(2,1)} %add_convert_fusion.9), channel_id=1, source_target_pairs={{0,16},{8,24},{16,0},{24,8},{1,17},{9,25},{17,1},{25,9},{2,18},{10... | collective-permute-start | bytes 1105928 | tf_op jit(solution)/shard_map/ppermute | solution.py:373
  506.8 11.7 %collective-permute-start.53 = (bf16[2,1024,256]{2,1,0:T(8,128)(2,1)}, bf16[2,1024,256]{2,1,0:T(8,128)(2,1)S(1)}, u32[]{:S(2)}, u32[]{:S(2)}) collective-permute-start(bf16[2,1024,256]{2,1,0:T(8,128)(2,1)} %get-tuple-element.105), channel_id=1, source_target_pairs={{0,1},{1,0},{2,3},{3,2},{4,5},{5,4},{6,7},{7,6},{8,9},{9,8},{10,11... | collective-permute-start | bytes 3145736 | tf_op jit(solution)/shard_map/ppermute | solution.py:370
  507.3 25.1 %collective-permute-start.54 = (bf16[2,1024,256]{2,1,0:T(8,128)(2,1)}, bf16[2,1024,256]{2,1,0:T(8,128)(2,1)S(1)}, u32[]{:S(2)}, u32[]{:S(2)}) collective-permute-start(bf16[2,1024,256]{2,1,0:T(8,128)(2,1)} %get-tuple-element.110), channel_id=1, source_target_pairs={{0,1},{1,0},{2,3},{3,2},{4,5},{5,4},{6,7},{7,6},{8,9},{9,8},{10,11... | collective-permute-start | bytes 3145736 | tf_op jit(solution)/shard_map/ppermute | solution.py:370
  508.5 16.3 %collective-permute-start.62 = (bf16[96,768]{1,0:T(8,128)(2,1)S(1)}, bf16[96,768]{1,0:T(8,128)(2,1)S(1)}, u32[]{:S(2)}, u32[]{:S(2)}) collective-permute-start(bf16[96,768]{1,0:T(8,128)(2,1)S(1)} %get-tuple-element.292), channel_id=1, source_target_pairs={{0,6},{1,7},{2,4},{3,5},{4,2},{5,3},{6,0},{7,1},{8,14},{9,15},{10,... | collective-permute-start | bytes 442376 | tf_op jit(solution)/shard_map/ppermute | solution.py:376
  508.6 16.3 %collective-permute-start.61 = (bf16[96,768]{1,0:T(8,128)(2,1)S(1)}, bf16[96,768]{1,0:T(8,128)(2,1)S(1)}, u32[]{:S(2)}, u32[]{:S(2)}) collective-permute-start(bf16[96,768]{1,0:T(8,128)(2,1)S(1)} %get-tuple-element.293), channel_id=1, source_target_pairs={{0,4},{1,5},{2,6},{3,7},{4,0},{5,1},{6,2},{7,3},{8,12},{9,13},{10,... | collective-permute-start | bytes 442376 | tf_op jit(solution)/shard_map/ppermute | solution.py:376
  508.7 16.3 %collective-permute-start.60 = (bf16[96,768]{1,0:T(8,128)(2,1)S(1)}, bf16[96,768]{1,0:T(8,128)(2,1)S(1)}, u32[]{:S(2)}, u32[]{:S(2)}) collective-permute-start(bf16[96,768]{1,0:T(8,128)(2,1)S(1)} %get-tuple-element.291), channel_id=1, source_target_pairs={{0,2},{1,3},{2,0},{3,1},{4,6},{5,7},{6,4},{7,5},{8,10},{9,11},{10,... | collective-permute-start | bytes 442376 | tf_op jit(solution)/shard_map/ppermute | solution.py:376
  518.5 12.7 %collective-permute-start.73 = (bf16[192,768]{1,0:T(8,128)(2,1)S(1)}, bf16[192,768]{1,0:T(8,128)(2,1)S(1)}, u32[]{:S(2)}, u32[]{:S(2)}) collective-permute-start(bf16[192,768]{1,0:T(8,128)(2,1)S(1)} %add_convert_fusion.10), channel_id=1, source_target_pairs={{0,8},{8,0},{16,24},{24,16},{1,9},{9,1},{17,25},{25,17},{2,10},{10... | collective-permute-start | bytes 884744 | tf_op jit(solution)/shard_map/ppermute | solution.py:373
  524.8 22.2 %collective-permute-start.52 = (bf16[2,256,768]{1,2,0:T(8,128)(2,1)}, bf16[2,256,768]{1,2,0:T(8,128)(2,1)}, u32[]{:S(2)}, u32[]{:S(2)}) collective-permute-start(bf16[2,256,768]{1,2,0:T(8,128)(2,1)} %pad_maximum_fusion.7), channel_id=1, source_target_pairs={{0,1},{1,0},{2,3},{3,2},{4,5},{5,4},{6,7},{7,6},{8,9},{9,8},{10,11... | collective-permute-start | bytes 2359304 | tf_op jit(solution)/shard_map/ppermute | solution.py:370
  524.9 19.0 %collective-permute-start.71 = (bf16[48,3840]{1,0:T(8,128)(2,1)}, bf16[48,3840]{1,0:T(8,128)(2,1)}, u32[]{:S(2)}, u32[]{:S(2)}) collective-permute-start(bf16[48,3840]{1,0:T(8,128)(2,1)} %add_convert_fusion.8), channel_id=1, source_target_pairs={{0,8},{8,0},{16,24},{24,16},{1,9},{9,1},{17,25},{25,17},{2,10},{10... | collective-permute-start | bytes 1105928 | tf_op jit(solution)/shard_map/ppermute | solution.py:373
  548.7 21.5 %collective-permute-start.66 = (bf16[96,1664]{1,0:T(8,128)(2,1)S(1)}, bf16[96,1664]{1,0:T(8,128)(2,1)S(1)}, u32[]{:S(2)}, u32[]{:S(2)}) collective-permute-start(bf16[96,1664]{1,0:T(8,128)(2,1)S(1)} %get-tuple-element.277), channel_id=1, source_target_pairs={{0,6},{1,7},{2,4},{3,5},{4,2},{5,3},{6,0},{7,1},{8,14},{9,15},{10,... | collective-permute-start | bytes 958472 | tf_op jit(solution)/shard_map/ppermute | solution.py:376
  548.9 22.0 %collective-permute-start.65 = (bf16[96,1664]{1,0:T(8,128)(2,1)S(1)}, bf16[96,1664]{1,0:T(8,128)(2,1)S(1)}, u32[]{:S(2)}, u32[]{:S(2)}) collective-permute-start(bf16[96,1664]{1,0:T(8,128)(2,1)S(1)} %get-tuple-element.278), channel_id=1, source_target_pairs={{0,4},{1,5},{2,6},{3,7},{4,0},{5,1},{6,2},{7,3},{8,12},{9,13},{10,... | collective-permute-start | bytes 958472 | tf_op jit(solution)/shard_map/ppermute | solution.py:376
  550.2 20.6 %collective-permute-start.64 = (bf16[96,1664]{1,0:T(8,128)(2,1)S(1)}, bf16[96,1664]{1,0:T(8,128)(2,1)S(1)}, u32[]{:S(2)}, u32[]{:S(2)}) collective-permute-start(bf16[96,1664]{1,0:T(8,128)(2,1)S(1)} %get-tuple-element.276), channel_id=1, source_target_pairs={{0,2},{1,3},{2,0},{3,1},{4,6},{5,7},{6,4},{7,5},{8,10},{9,11},{10,... | collective-permute-start | bytes 958472 | tf_op jit(solution)/shard_map/ppermute | solution.py:376
  556.8 23.4 %collective-permute-start.57 = (bf16[256,768]{0,1:T(8,128)(2,1)S(1)}, bf16[256,768]{0,1:T(8,128)(2,1)S(1)}, u32[]{:S(2)}, u32[]{:S(2)}) collective-permute-start(bf16[256,768]{0,1:T(8,128)(2,1)S(1)} %get-tuple-element.251), channel_id=1, source_target_pairs={{0,24},{8,16},{16,8},{24,0},{1,25},{9,17},{17,9},{25,1},{2,26},{10... | collective-permute-start | bytes 1179656 | tf_op jit(solution)/shard_map/ppermute | solution.py:373
  570.2 32.8 %collective-permute-start.56 = (bf16[256,768]{0,1:T(8,128)(2,1)S(1)}, bf16[256,768]{0,1:T(8,128)(2,1)S(1)}, u32[]{:S(2)}, u32[]{:S(2)}) collective-permute-start(bf16[256,768]{0,1:T(8,128)(2,1)S(1)} %get-tuple-element.252), channel_id=1, source_target_pairs={{0,16},{8,24},{16,0},{24,8},{1,17},{9,25},{17,1},{25,9},{2,18},{10... | collective-permute-start | bytes 1179656 | tf_op jit(solution)/shard_map/ppermute | solution.py:373
  570.2 32.8 %collective-permute-start.55 = (bf16[256,768]{0,1:T(8,128)(2,1)S(1)}, bf16[256,768]{0,1:T(8,128)(2,1)S(1)}, u32[]{:S(2)}, u32[]{:S(2)}) collective-permute-start(bf16[256,768]{0,1:T(8,128)(2,1)S(1)} %get-tuple-element.253), channel_id=1, source_target_pairs={{0,8},{8,0},{16,24},{24,16},{1,9},{9,1},{17,25},{25,17},{2,10},{10... | collective-permute-start | bytes 1179656 | tf_op jit(solution)/shard_map/ppermute | solution.py:373
  571.1 32.2 %collective-permute-start.67 = (bf16[48,2432]{1,0:T(8,128)(2,1)S(1)}, bf16[48,2432]{1,0:T(8,128)(2,1)S(1)}, u32[]{:S(2)}, u32[]{:S(2)}) collective-permute-start(bf16[48,2432]{1,0:T(8,128)(2,1)S(1)} %dynamic-slice_bitcast_fusion.16), channel_id=1, source_target_pairs={{0,8},{8,0},{16,24},{24,16},{1,9},{9,1},{17,25},{25,17},{2,10},{10... | collective-permute-start | bytes 700424 | tf_op jit(solution)/shard_map/ppermute | solution.py:373
  603.4 12.4 %collective-permute-start.68 = (bf16[48,2432]{1,0:T(8,128)(2,1)S(1)}, bf16[48,2432]{1,0:T(8,128)(2,1)S(1)}, u32[]{:S(2)}, u32[]{:S(2)}) collective-permute-start(bf16[48,2432]{1,0:T(8,128)(2,1)S(1)} %fusion.37), channel_id=1, source_target_pairs={{0,16},{8,24},{16,0},{24,8},{1,17},{9,25},{17,1},{25,9},{2,18},{10... | collective-permute-start | bytes 700424 | tf_op jit(solution)/shard_map/ppermute | solution.py:373
  604.4 11.5 %collective-permute-start.58 = (bf16[2,256,768]{1,2,0:T(8,128)(2,1)}, bf16[2,256,768]{1,2,0:T(8,128)(2,1)}, u32[]{:S(2)}, u32[]{:S(2)}) collective-permute-start(bf16[2,256,768]{1,2,0:T(8,128)(2,1)} %pad_maximum_fusion.9), channel_id=1, source_target_pairs={{0,1},{1,0},{2,3},{3,2},{4,5},{5,4},{6,7},{7,6},{8,9},{9,8},{10,11... | collective-permute-start | bytes 2359304 | tf_op jit(solution)/shard_map/ppermute | solution.py:370
  (84 other events, 947.4 us)

commit v3 on v2

--- a/solution.py
+++ b/solution.py
@@ -124,8 +124,8 @@
     ext_ref[...] = (jnp.concatenate(parts[::-1], axis=0).T + qx.astype(jnp.float32)).astype(ext_ref.dtype)
 
 
-def attention_forward(info, q, kv_own, kv_mate, qx, kx, size):
-    rows, width = q.shape
+def attention_forward(info, own, mate, qx, kx, size):
+    rows, width = own.shape[0], own.shape[1] // 3
     length = kx.shape[0]
     slots = (info.shape[0] - 2) // 2
     block = rows // slots
@@ -138,10 +138,10 @@
             grid=(pairs, slots),
             in_specs=[
                 pl.BlockSpec((block, LANES), lambda p, s, i: (s, p)),
-                pl.BlockSpec((rows, LANES), lambda p, s, i: (0, p)),
-                pl.BlockSpec((rows, LANES), lambda p, s, i: (0, p)),
                 pl.BlockSpec((rows, LANES), lambda p, s, i: (0, pairs + p)),
                 pl.BlockSpec((rows, LANES), lambda p, s, i: (0, pairs + p)),
+                pl.BlockSpec((rows, LANES), lambda p, s, i: (0, 2 * pairs + p)),
+                pl.BlockSpec((rows, LANES), lambda p, s, i: (0, 2 * pairs + p)),
                 pl.BlockSpec((block, LANES), lambda p, s, i: (s, 0)),
                 pl.BlockSpec((length, LANES), lambda p, s, i: (0, 0)),
             ],
@@ -158,7 +158,7 @@
             flops=2 * rows * length * width, bytes_accessed=8 * rows * width * 2, transcendentals=rows * length * pairs
         ),
         name="attention_forward",
-    )(info, q, kv_own, kv_mate, kv_own, kv_mate, qx, kx)
+    )(info, own, own, mate, own, mate, qx, kx)
 
 
 def backward_kernel(
@@ -242,30 +242,32 @@
                     mate_ref[j, pl.ds(spot, block), :] = (total[pl.ds(b * block, block), :] * factor).astype(mate_ref.dtype)
 
 
-def attention_backward(info, q, ext, grads, ctx, kv_own, kv_mate, kx, size, first, some):
-    rows, width = q.shape
+def attention_backward(info, own, mate, ext, grads, ctx, kx, size, first):
+    rows, width = ctx.shape
     length = kx.shape[0]
     slots = (info.shape[0] - 2) // 2
     block = rows // slots
     pairs = width // LANES
     heads = LANES // size
-    tile = pl.BlockSpec((block, LANES), lambda p, s, i: (s, first + p))
-    out_tile = pl.BlockSpec((block, LANES), lambda p, s, i: (s, p))
+    tile = pl.BlockSpec((block, LANES), lambda p, s, i: (s, p))
     return pl.pallas_call(
         functools.partial(backward_kernel, size=size),
         grid_spec=pltpu.PrefetchScalarGridSpec(
             num_scalar_prefetch=1,
-            grid=(some, slots),
+            grid=(pairs, slots),
             in_specs=[
-                tile, tile, tile, tile,
-                pl.BlockSpec((rows, LANES), lambda p, s, i: (0, first + p)),
-                pl.BlockSpec((rows, LANES), lambda p, s, i: (0, first + p)),
-                pl.BlockSpec((rows, LANES), lambda p, s, i: (0, pairs + first + p)),
-                pl.BlockSpec((rows, LANES), lambda p, s, i: (0, pairs + first + p)),
+                tile,
+                tile,
+                pl.BlockSpec((block, LANES), lambda p, s, i: (s, first + p)),
+                tile,
+                pl.BlockSpec((rows, LANES), lambda p, s, i: (0, pairs + p)),
+                pl.BlockSpec((rows, LANES), lambda p, s, i: (0, pairs + p)),
+                pl.BlockSpec((rows, LANES), lambda p, s, i: (0, 2 * pairs + p)),
+                pl.BlockSpec((rows, LANES), lambda p, s, i: (0, 2 * pairs + p)),
                 pl.BlockSpec((length, LANES), lambda p, s, i: (0, 0)),
             ],
             out_specs=[
-                out_tile,
+                tile,
                 pl.BlockSpec((2, rows, LANES), lambda p, s, i: (0, 0, p)),
                 pl.BlockSpec((2, rows, LANES), lambda p, s, i: (0, 0, p)),
             ],
@@ -278,18 +280,16 @@
             ],
         ),
         out_shape=[
-            jax.ShapeDtypeStruct((rows, some * LANES), jnp.bfloat16),
-            jax.ShapeDtypeStruct((2, rows, some * LANES), jnp.float32),
-            jax.ShapeDtypeStruct((2, rows, some * LANES), jnp.bfloat16),
+            jax.ShapeDtypeStruct((rows, width), jnp.bfloat16),
+            jax.ShapeDtypeStruct((2, rows, width), jnp.float32),
+            jax.ShapeDtypeStruct((2, rows, width), jnp.bfloat16),
         ],
         compiler_params=pltpu.CompilerParams(dimension_semantics=("arbitrary", "arbitrary")),
         cost_estimate=pl.CostEstimate(
-            flops=5 * rows * length * some * LANES,
-            bytes_accessed=24 * rows * some * LANES,
-            transcendentals=rows * length * some,
+            flops=5 * rows * length * width, bytes_accessed=24 * rows * width, transcendentals=rows * length * pairs
         ),
         name="attention_backward",
-    )(info, q, ext, grads, ctx, kv_own, kv_mate, kv_own, kv_mate, kx)
+    )(info, own, ext, grads, ctx, own, mate, own, mate, kx)
 
 
 def key_extension(ids):
@@ -376,18 +376,18 @@
         return lax.ppermute(values, "fsdp", xor_pairs(self.shards, 2 * bits))
 
 
-def to_sequence(here, values):
+def to_sequence_parts(here, values):
     groups, piece, width = values.shape
     halves = values.reshape(groups, 2, piece // 2, width)
     kept = pick(halves, here.core, 1)
     other = here.mate(pick(halves, 1 - here.core, 1))
-    both = jnp.concatenate([kept, other], axis=0)
-    slots = []
+    parts = []
     for k in range(here.columns):
         want = here.column ^ k
-        part = pick(both, ((want // groups) ^ here.core) * groups + want % groups)
-        slots.append(here.across(part, k) if k else part)
-    return slots
+        same = lax.div(want, groups) == here.core
+        spot = lax.rem(want, groups)
+        parts.append(jnp.where(same, pick(kept, spot), pick(other, spot)))
+    return parts
 
 
 def from_sequence_send(here, slots):
@@ -406,49 +406,84 @@
     return jnp.concatenate([jnp.where(first, kept, other), jnp.where(first, other, kept)], axis=1)
 
 
-def place_kernel(info, *refs):
-    count = (len(refs) - 3) // 2
-    parts, out, buffers = refs[:count], refs[count], refs[count + 1 : 2 * count + 1]
-    in_sem, out_sem = refs[2 * count + 1 :]
+def place_kernel(info, *refs, count, cuts, outs):
+    parts, full, buffers = refs[:count], refs[count : count + outs], refs[count + outs : 2 * count + outs]
+    in_sem, out_sem = refs[2 * count + outs :]
     reads = [pltpu.make_async_copy(parts[k], buffers[k], in_sem.at[k]) for k in range(count)]
-    writes = [pltpu.make_async_copy(buffers[k], out.at[info[k]], out_sem.at[k]) for k in range(count)]
     for read in reads:
         read.start()
-    for read, write in zip(reads, writes):
-        read.wait()
-        write.start()
+    writes = []
+    for k in range(count):
+        reads[k].wait()
+        for j, (row, rows, col, cols, out, out_col) in enumerate(cuts):
+            write = pltpu.make_async_copy(
+                buffers[k].at[pl.ds(row, rows), pl.ds(col, cols)],
+                full[out].at[info[k], :, pl.ds(out_col, cols)],
+                out_sem.at[k, j],
+            )
+            write.start()
+            writes.append(write)
     for write in writes:
         write.wait()
 
 
-def place(parts, spots):
+def out_shapes(cuts):
+    shapes = {}
+    for row, rows, col, cols, out, out_col in cuts:
+        shapes[out] = (rows, max(shapes.get(out, (0, 0))[1], out_col + cols))
+    return [shapes[out] for out in sorted(shapes)]
+
+
+def place(parts, spots, cuts):
     count, (rows, width), kind = len(parts), parts[0].shape, parts[0].dtype
-    full = pl.pallas_call(
-        place_kernel,
+    shapes = out_shapes(cuts)
+    return pl.pallas_call(
+        functools.partial(place_kernel, count=count, cuts=cuts, outs=len(shapes)),
         grid_spec=pltpu.PrefetchScalarGridSpec(
             num_scalar_prefetch=1,
             grid=(),
             in_specs=[pl.BlockSpec(memory_space=pl.ANY)] * count,
-            out_specs=pl.BlockSpec(memory_space=pl.ANY),
+            out_specs=[pl.BlockSpec(memory_space=pl.ANY)] * len(shapes),
             scratch_shapes=[pltpu.VMEM((rows, width), kind)] * count
-            + [pltpu.SemaphoreType.DMA((count,)), pltpu.SemaphoreType.DMA((count,))],
+            + [pltpu.SemaphoreType.DMA((count,)), pltpu.SemaphoreType.DMA((count, len(cuts)))],
         ),
-        out_shape=jax.ShapeDtypeStruct((count, rows, width), kind),
+        out_shape=[jax.ShapeDtypeStruct((count,) + shape, kind) for shape in shapes],
         cost_estimate=pl.CostEstimate(flops=0, bytes_accessed=2 * count * rows * width * 2, transcendentals=0),
         name="place_parts",
     )(jnp.stack(spots).astype(jnp.int32), *parts)
-    return full.reshape(count * rows, width)
-
-
-def gather_shards(here, local):
-    if here.shards != 8:
-        return lax.all_gather(local, "fsdp", axis=0, tiled=True)
-    middle = local.shape[0] // 2
-    across_x, across_y = here.aside(local, 1), here.aside(local, 2)
-    corner = jnp.concatenate([here.aside(across_x[:middle], 2), here.aside(across_y[middle:], 1)], axis=0)
-    parts = [local, across_x, across_y, corner]
-    spots = [here.shard ^ (2 * k) for k in range(4)]
-    return place(parts + [here.mate(part) for part in parts], spots + [spot ^ 1 for spot in spots])
+
+
+class Gather:
+    def __init__(self, here, local, cuts):
+        self.here, self.local, self.cuts = here, local, cuts
+        self.direct = here.shards == 8
+        if self.direct:
+            self.parts = [local, here.aside(local, 1), here.aside(local, 2)]
+        else:
+            self.full = lax.all_gather(local, "fsdp", axis=0, tiled=False)
+
+    def corner(self, *marks):
+        if self.direct:
+            here = self.here
+            middle = self.local.shape[0] // 32 * 16
+            _, across_x, across_y = self.parts = after(self.parts, *marks)
+            self.mates = [here.mate(part) for part in self.parts]
+            self.last = [here.aside(across_x[:middle], 2), here.aside(across_y[middle:], 1)]
+
+    def finish(self, *marks):
+        here = self.here
+        if not self.direct:
+            shapes = out_shapes(self.cuts)
+            full = [[] for _ in shapes]
+            for row, rows, col, cols, out, out_col in self.cuts:
+                full[out].append(self.full[:, row : row + rows, col : col + cols])
+            whole = [jnp.concatenate(pieces, axis=2) for pieces in full]
+        else:
+            corner = jnp.concatenate(after(self.last, *marks), axis=0)
+            spots = [here.shard ^ (2 * k) for k in range(4)]
+            mates = self.mates + [here.mate(corner)]
+            whole = place(self.parts + [corner] + mates, spots + [spot ^ 1 for spot in spots], self.cuts)
+        return [w.reshape(-1, w.shape[2]) for w in whole]
 
 
 def share_pair(here, partial):
@@ -458,9 +493,11 @@
 
 
 def share_plane(here, kept, other):
-    total = kept.astype(f32) + other.astype(f32)
-    low = total.astype(bf16)
-    return pick(total, here.plane), [here.aside(pick(low, here.plane ^ k), k) for k in range(1, here.shards // 2)]
+    def total(k):
+        spot = here.plane ^ k
+        return pick(kept, spot).astype(f32) + pick(other, spot).astype(f32)
+
+    return total(0), [here.aside(total(k).astype(bf16), k) for k in range(1, here.shards // 2)]
 
 
 def share_sum(share, others):
@@ -521,24 +558,31 @@
     rows = here.columns * half
     length = here.columns * piece
 
-    flat = jnp.concatenate(to_sequence(here, tokens), axis=0)
+    def sequence(values):
+        return from_sequence_send(here, to_sequence_parts(here, values))
+
+    ups = hidden_size // width
+    part_width = width // PARTS
+    token_parts = to_sequence_parts(here, tokens)
+    flat = jnp.concatenate(from_sequence_send(here, token_parts), axis=0)
 
     vectors = (query_bias, value_bias, merge_bias, first_gain, first_shift, down_bias, second_gain, second_shift)
-    columns = jnp.concatenate([jnp.stack(vectors, axis=1), up_bias.reshape(own, -1)], axis=1)
-    columns = jnp.pad(columns, ((0, 0), (0, LANES - columns.shape[1])))
-    mix_local = mix_weight.reshape(own, H, 3, HD).transpose(0, 2, 1, 3).reshape(own, 3 * width)
-    mix_all = gather_shards(here, jnp.concatenate([mix_local, columns], axis=1))
-    mix_full, columns_full = mix_all[:, : 3 * width], mix_all[:, 3 * width :].astype(f32)
-    merge_up = gather_shards(here, jnp.concatenate([merge_weight, up_weight], axis=1))
-    merge_full, up_full = merge_up[:, :width], merge_up[:, width:]
-    down_full = gather_shards(here, down_weight)
-    turned = columns_full[:, :8].T
+    lines = jnp.concatenate([jnp.stack(vectors), up_bias.reshape(ups, own)], axis=0)
+    columns = jnp.pad(lines, ((0, LANES - lines.shape[0]), (0, 0))).T
+    mix_local = mix_weight.reshape(own, PARTS, H // PARTS, 3, HD).transpose(0, 1, 3, 2, 4).reshape(own, 3 * width)
+    mix_local = jnp.concatenate([mix_local, columns], axis=1)
+    mix_cuts = [(0, own, p * width, width, p, 0) for p in range(PARTS)] + [(0, own, 3 * width, LANES, PARTS, 0)]
+    mix_gather = Gather(here, after(mix_local, token_parts), mix_cuts)
+    mix_gather.corner()
+    *mix_parts, columns_full = mix_gather.finish()
+    lines_full = columns_full.T.astype(f32)
     query_full, value_full, merge_bias_full, gain_one, shift_one, down_bias_full, gain_two, shift_two = [
-        turned[j] for j in range(8)
+        lines_full[j] for j in range(8)
     ]
-    up_bias_full = columns_full[:, 8 : 8 + hidden_size // width].reshape(-1)
-
-    ids_own = jnp.concatenate(to_sequence(here, segment_ids.reshape(groups, piece, 1)), axis=0).reshape(here.columns, half)
+    up_bias_full = lines_full[8 : 8 + ups].reshape(ups, shards, own).transpose(1, 0, 2).reshape(-1)
+
+    ids_local = after(segment_ids, token_parts).reshape(groups, piece, 1)
+    ids_own = jnp.concatenate(sequence(ids_local), axis=0).reshape(here.columns, half)
     ids_mate = here.mate(ids_own)
     by_core = jnp.stack([jnp.where(here.core == 0, ids_own, ids_mate), jnp.where(here.core == 0, ids_mate, ids_own)], axis=1)
     ids = jnp.stack([pick(by_core, k ^ here.column) for k in range(here.columns)]).reshape(2 * here.columns, half)
@@ -549,16 +593,36 @@
     key_ext = key_extension(ids.reshape(length))
     query_ext = query_extension(ids_own.reshape(rows))
 
-    cotangent_slots = to_sequence(here, after(output_grad, flat))
-
-    kv_bias = jnp.concatenate([jnp.zeros_like(value_full), value_full])
-    key_value = (dot(flat, mix_full[:, width:]) + kv_bias).astype(bf16)
-    query = ((dot(flat, mix_full[:, :width]) + query_full) * (LOG2E / math.sqrt(HD))).astype(bf16)
-    key_value_mate = here.mate(key_value)
-    context, ext = attention_forward(info, query, key_value, key_value_mate, query_ext, key_ext, HD)
-
-    cotangent = jnp.concatenate(after(cotangent_slots, context), axis=0).astype(f32)
-    merge_full, up_full, down_full = after((merge_full, up_full, down_full), context)
+    packed = jnp.concatenate(
+        [merge_weight] + [up_weight[:, j * width : (j + 1) * width] for j in range(ups)] + [down_weight], axis=0
+    )
+    cuts = [(0, own, 0, width, 0, 0)] + [((1 + j) * own, own, 0, width, 1, j * width) for j in range(ups)]
+    cuts.append(((1 + ups) * own, ups * own, 0, width, 2, 0))
+    weight_gather = Gather(here, after(packed, flat), cuts)
+    cotangent_slots = sequence(after(output_grad, flat))
+
+    column_scale = jnp.where(jnp.arange(width) < part_width, LOG2E / math.sqrt(HD), 1.0)
+    mixed, mixed_mate = [], []
+    for p in range(PARTS):
+        of_part = slice(p * part_width, (p + 1) * part_width)
+        bias = jnp.concatenate([query_full[of_part], jnp.zeros((part_width,), f32), value_full[of_part]])
+        mixed.append(((dot(flat, mix_parts[p]) + bias) * column_scale).astype(bf16))
+        mixed_mate.append(here.mate(mixed[p]))
+
+    contexts, exts = [], []
+    for p in range(PARTS):
+        if p:
+            mixed[p], mixed_mate[p] = after((mixed[p], mixed_mate[p]), contexts[-1])
+        if p == 1:
+            weight_gather.corner(contexts[-1])
+        context, ext = attention_forward(info, mixed[p], mixed_mate[p], query_ext, key_ext, HD)
+        contexts.append(context)
+        exts.append(ext)
+    context = jnp.concatenate(contexts, axis=1)
+
+    cotangent = jnp.concatenate(after(cotangent_slots, contexts[-1]), axis=0).astype(f32)
+    merge_full, up_full, down_full = weight_gather.finish(contexts[-2])
+    merge_full, up_full, down_full = after((merge_full, up_full, down_full), contexts[-1])
 
     attended = dot(context, merge_full) + merge_bias_full
     first_out, normed_one, factor_one = norm_forward(flat.astype(f32) + attended, gain_one, shift_one)
@@ -591,9 +655,8 @@
     up_share, up_others = share_plane(here, up_kept, after(up_other, grad_context))
 
     def backward(part, grads):
-        pairs = width // LANES // PARTS
         dq, kept, other = attention_backward(
-            info, query, ext, grads, context, key_value, key_value_mate, key_ext, HD, part * pairs, pairs
+            info, mixed[part], mixed_mate[part], exts[part], grads, contexts[part], key_ext, HD, part * part_width // LANES
         )
         return dq, kept, here.mate(other)
 
@@ -601,13 +664,6 @@
         dq, kept, other = pieces
         kv = (kept + other.astype(f32)).astype(bf16)
         return jnp.concatenate([dq, kv[0], kv[1]], axis=1)
-
-    part_width = width // PARTS
-
-    def weight_part(part):
-        return jnp.concatenate(
-            [mix_full[:, j * width + part * part_width : j * width + (part + 1) * part_width] for j in range(3)], axis=1
-        )
 
     one = backward(0, after(grad_context, down_share, up_share))
     down_others, down_share = after((down_others, down_share), one[0])
@@ -620,15 +676,17 @@
     mixed_one = mixed_part(after(one, two[0]))
     mix_grad_one = dot(flat.T, mixed_one)
     mix_kept_one, mix_other_one = share_pair(here, mix_grad_one.reshape(shards, own, -1))
-    input_part = dot(mixed_one, weight_part(0).T)
-    three = backward(2, after(grad_context, down_half, up_half, input_part, mix_kept_one))
+    input_part = grad_sum + dot(mixed_one, mix_parts[0].T)
+    mix_share_one, mix_others_one = share_plane(here, mix_kept_one, after(mix_other_one, input_part))
+    three = backward(2, after(grad_context, down_half, up_half, mix_share_one))
     down_half, down_other = column_third(here, *after((down_half, down_other), three[0]))
     up_half, up_other = column_third(here, *after((up_half, up_other), three[0]))
     mixed_two = mixed_part(after(two, three[0]))
-    mixed_three = mixed_part(three)
-    mixed_rest = jnp.concatenate([mixed_two, mixed_three], axis=1)
-    input_grad = grad_sum + input_part + dot(mixed_rest, jnp.concatenate([weight_part(1), weight_part(2)], axis=1).T)
-    input_slots = from_sequence_send(here, list(input_grad.astype(bf16).reshape(here.columns, half, width)))
+    input_part = input_part + dot(mixed_two, mix_parts[1].T)
+    mixed_three = mixed_part(after(three, input_part))
+    input_low = (input_part + dot(mixed_three, mix_parts[2].T)).astype(bf16)
+    input_slots = from_sequence_send(here, list(input_low.reshape(here.columns, half, width)))
+    mixed_rest = after(jnp.concatenate([mixed_two, mixed_three], axis=1), input_low)
     mix_grad_rest = dot(flat.T, mixed_rest)
 
     sums = [column_sums(m) for m in (mixed_one, mixed_two, mixed_three)]
@@ -644,11 +702,11 @@
         second_gain_grad,
         second_shift_grad,
     )
-    columns_grad = jnp.concatenate([jnp.stack(vectors, axis=1), up_bias_grad.reshape(width, -1)], axis=1)
-    columns_grad = jnp.pad(columns_grad, ((0, 0), (0, LANES - columns_grad.shape[1])))
+    up_lines = up_bias_grad.reshape(shards, ups, own).transpose(1, 0, 2).reshape(ups, width)
+    lines_grad = jnp.concatenate([jnp.stack(vectors), up_lines], axis=0)
+    columns_grad = jnp.pad(lines_grad, ((0, LANES - lines_grad.shape[0]), (0, 0))).T
     rest = jnp.concatenate([mix_grad_rest, columns_grad], axis=1).reshape(shards, own, -1)
     rest_kept, rest_other = share_pair(here, rest)
-    mix_share_one, mix_others_one = share_plane(here, mix_kept_one, mix_other_one)
     rest_share, rest_others = share_plane(here, rest_kept, rest_other)
     mix_share = jnp.concatenate([share_sum(mix_share_one, mix_others_one), share_sum(rest_share, rest_others)], axis=1)
     mix_last = column_last(here, *column_third(here, *column_second(here, *column_first(here, mix_share))))
@@ -660,7 +718,7 @@
     final_mix = mix_last[:, : 3 * width].astype(f32).reshape(own, PARTS, 3, H // PARTS, HD)
     final_mix = final_mix.transpose(0, 1, 3, 2, 4).reshape(own, 3 * width)
     final_columns = mix_last[:, 3 * width :].astype(f32)
-    finals = final_columns[:, :8].T
+    finals = final_columns.T
     (
         final_query,
         final_value,
@@ -671,7 +729,7 @@
         final_gain_two,
         final_shift_two,
     ) = [finals[j] for j in range(8)]
-    final_up_bias = final_columns[:, 8 : 8 + hidden_size // width].reshape(-1)
+    final_up_bias = finals[8 : 8 + ups].reshape(-1)
     return (
         output,
         final_input,

time: 636 us -> 586 us (0.921)
  local copies, waits for them, and re-layouts: 98.1 us -> 68.2 us
  other arithmetic: 72.9 us -> 49.2 us
  starting transfers between devices: 122 us -> 103 us
  Pallas kernels: 153 us -> 171 us
  matrix products: 85.2 us -> 95.6 us
    ppermute x24 -> x20, starting transfers between devices: 47.6 us -> 23.7 us  [aside(): return lax.ppermute(values, 'fsdp', xor_pairs(self.shards, 2 * bits))]
    ppermute x26 -> x24, starting transfers between devices: 5.08 us -> 27.7 us  [mate(): return lax.ppermute(values, 'fsdp', xor_pairs(self.shards, 1))]
    ppermute x24, starting transfers between devices: 68.9 us -> 51.8 us  [across(): return lax.ppermute(values, 'seq', xor_pairs(self.columns, bits))]
    reduce_sum x5, other arithmetic: 18 us -> 6.03 us  [column_sums(): return jnp.sum(values.astype(f32), axis=0)]
    another operation x18 -> x11, local copies, waits for them, and re-layouts: 14.2 us -> 2.49 us  [the longest x8 2.37 us: per_device(): lines_grad = jnp.concatenate([jnp.stack(vectors), up_lines], axis=0)]
    pallas_call x1 -> x3, Pallas kernels: 51 us -> 61.5 us  [attention_forward(): pl.pallas_call(functools.partial(forward_kernel, size=size), grid_spec=pl...]
    dot_general x15 -> x17, matrix products: 85.2 us -> 95.6 us  [dot(): return jnp.dot(a, b, preferred_element_type=f32)]
    slice x13 -> x9, local copies, waits for them, and re-layouts: 16 us -> 6.03 us  [the longest x2 2.11 us: corner(): across_x[:middle]]
  transfers between devices with their start and end apart: 74 -> 68, of which waited for: 14 -> 18; matrix products, arithmetic and copies ran while one was open for 28% -> 22% of each run, Pallas kernels for 24% -> 28%
where the time goes in v3:
time: 586 us; the launch traced here: 580 us
  Pallas kernels  171 us (29%)
  starting transfers between devices  103 us (18%)
  matrix products  95.6 us (16%)
  waiting for transfers between devices  89.5 us (15%)
  local copies, waits for them, and re-layouts  68.2 us (12%)
  other arithmetic  49.2 us (8%)
    pallas_call x3, Pallas kernels, attention_backward(): pl.pallas_call(functools.partial(backward_kernel, size=size), grid_spec=p...  96.4 us
    dot_general x17, matrix products, dot(): return jnp.dot(a, b, preferred_element_type=f32)  95.6 us
    ppermute x24, waiting for transfers between devices, across(): return lax.ppermute(values, 'seq', xor_pairs(self.columns, bits))  63.3 us
    pallas_call x3, Pallas kernels, attention_forward(): pl.pallas_call(functools.partial(forward_kernel, size=size), grid_spec=pl...  61.5 us
    ppermute x24, starting transfers between devices, across(): return lax.ppermute(values, 'seq', xor_pairs(self.columns, bits))  51.8 us
    unnamed x201, local copies, waits for them, and re-layouts  32.1 us
    ppermute x24, starting transfers between devices, mate(): return lax.ppermute(values, 'fsdp', xor_pairs(self.shards, 1))  27.7 us
    ppermute x20, waiting for transfers between devices, aside(): return lax.ppermute(values, 'fsdp', xor_pairs(self.shards, 2 * bits))  25 us
  transfers between devices with their start and end apart: 68, of which 18 were waited for; matrix products, arithmetic and copies ran while one was open for 22% of the time, Pallas kernels for 28%

profile of v3, /device:TPU:0, one launch (start us, length us, event | category | flops | bytes accessed | tf_op | source)
XLA Modules:
  0.0 580.0 jit_solution(8286933054070067771)
XLA Ops:
  19.2 1.9 constant_dynamic-update-slice_fusion.5.refs_0_
  23.6 4.8 collective-permute-start.7
  32.9 3.6 collective-permute-start.3
  39.7 2.4 collective-permute-done.9.refs_1_
  45.6 4.0 collective-permute-done.11
  53.3 15.8 %collective-permute-done.2 = bf16[256,768]{0,1:T(8,128)(2,1)} collective-permute-done((bf16[256,768]{0,1:T(8,128)(2,1)}, bf16[256,768]{0,1:T(8,128)(2,1)}, u32[]{:S(2)}, u32[]{:S(2)}) %collective-permute-start.2) | collective-permute-done | bytes 393248 | tf_op jit(solution)/shard_map/ppermute | solution.py:373
  72.3 4.0 place_parts.2
  77.5 4.4 multiply_convert_fusion.3.q_ref.k_own.v_own
  82.0 2.8 multiply_convert_fusion.2.q_ref.k_own.v_own
  88.5 3.1 multiply_convert_fusion.1.q_ref.k_own.v_own
  92.0 20.6 %attention_forward.3 = (bf16[1024,256]{1,0:T(8,128)(2,1)}, bf16[1024,256]{1,0:T(8,128)(2,1)}) custom-call(s32[10]{0:T(128)} %pad_add_fusion.3.info, bf16[1024,768]{1,0:T(8,128)(2,1)} %multiply_convert_fusion.3.q_ref.k_own.v_own, bf16[1024,768]{1,0:T(8,128)(2,1)} %multiply_convert_fusion.3.q_ref.k_own.v_own, ...), custom_call_target="tpu_custom_call" | custom-call | flops 1073741824 | bytes 4194304 | tf_op jit(solution)/shard_map/attention_forward/pallas_call | solution.py:134
  112.6 2.1 slice.206
  116.3 2.0 slice.207
  120.8 1.9 copy.292
  127.4 2.9 bitcast_select_fusion
  130.9 6.7 %collective-permute-start.33 = (bf16[256,768]{0,1:T(8,128)(2,1)}, bf16[256,768]{0,1:T(8,128)(2,1)}, u32[]{:S(2)}, u32[]{:S(2)}) collective-permute-start(bf16[256,768]{0,1:T(8,128)(2,1)} %get-tuple-element.355), channel_id=1, source_target_pairs={{0,16},{8,24},{16,0},{24,8},{1,17},{9,25},{17,1},{25,9},{2,18},{10... | collective-permute-start | bytes 1179656 | tf_op jit(solution)/shard_map/ppermute | solution.py:373
  137.5 20.4 %attention_forward.4 = (bf16[1024,256]{1,0:T(8,128)(2,1)}, bf16[1024,256]{1,0:T(8,128)(2,1)}) custom-call(s32[10]{0:T(128)} %pad_add_fusion.3.info, bf16[1024,768]{1,0:T(8,128)(2,1)} %copy-done.1, bf16[1024,768]{1,0:T(8,128)(2,1)} %copy-done.1, bf16[1024,768]{1,0:T(8,128)(2,1)} %collective-permute-done.18.k_mate.v_mate, bf16[1024,768]{1,0:T(8,128)(2,1)} %copy-done.1, ...), custom_call_target="tpu_custom_call" | custom-call | flops 1073741824 | bytes 4194304 | tf_op jit(solution)/shard_map/attention_forward/pallas_call | solution.py:134
  157.9 2.3 collective-permute-start.25
  163.3 3.7 collective-permute-start.34
  169.0 20.5 %attention_forward.5 = (bf16[1024,256]{1,0:T(8,128)(2,1)}, bf16[1024,256]{1,0:T(8,128)(2,1)}) custom-call(s32[10]{0:T(128)} %pad_add_fusion.3.info, bf16[1024,768]{1,0:T(8,128)(2,1)} %copy-done, bf16[1024,768]{1,0:T(8,128)(2,1)} %copy-done, bf16[1024,768]{1,0:T(8,128)(2,1)} %collective-permute-done.19.k_mate.v_mate, bf16[1024,768]{1,0:T(8,128)(2,1)} %copy-done, ...), custom_call_target="tpu_custom_call" | custom-call | flops 1073741824 | bytes 4194304 | tf_op jit(solution)/shard_map/attention_forward/pallas_call | solution.py:134
  191.3 1.9 constant_dynamic-update-slice_fusion.2
  193.3 9.5 %place_parts.3 = (bf16[8,96,768]{2,1,0:T(8,128)(2,1)}, bf16[8,96,3072]{2,1,0:T(8,128)(2,1)}, bf16[8,384,768]{2,1,0:T(8,128)(2,1)}) custom-call(s32[8]{0:T(128)} %stack.179.info, bf16[864,768]{1,0:T(8,128)(2,1)} %constant_dynamic-update-slice_fusion.5.refs_0_, bf16[864,768]{1,0:T(8,128)(2,1)} %collective-permute-done.20.refs_1_, ...), custom_call_target="tpu_custom_call" | custom-call | bytes 21233664 | tf_op jit(solution)/shard_map/place_parts/pallas_call | solution.py:440
  202.8 3.9 fusion.88
  207.1 11.6 %multiply_convert_fusion = (bf16[1024,3072]{1,0:T(8,128)(2,1)}, f32[1024,3072]{1,0:T(8,128)}) fusion(f32[3072]{0:T(1024)S(1)} %add.552, bf16[768,3072]{1,0:T(8,128)(2,1)S(1)} %bitcast.381, f32[1024,768]{0,1:T(8,128)S(1)} %get-tuple-element.399, f32[768]{0:T(1024)S(1)} %get-tuple-element.281, f32[768]{0:T(1024)S(1)} %get-tuple-element.282, ...), kind=kOutput, calls=%fused_computation.18 | convolution fusion | flops 4854644736 | bytes 26765312 | tf_op jit(solution)/shard_map/dot_general | solution.py:341
  218.7 7.7 %fusion.89 = (f32[1024]{0:T(1024)S(1)}, f32[1024,768]{0,1:T(8,128)S(1)}) fusion(f32[768]{0:T(1024)S(1)} %get-tuple-element.280, bf16[1024,3072]{1,0:T(8,128)(2,1)} %get-tuple-element.400, bf16[3072,768]{1,0:T(8,128)(2,1)S(1)} %bitcast.385, f32[768]{0:T(1024)S(1)} %get-tuple-element.281, f32[768]{0:T(1024)S(1)} %get-tuple-element.282, ...), kind=kOutput, calls=%fused_computation.316 | convolution fusion | flops 4837342208 | bytes 17323008 | tf_op jit(solution)/shard_map/dot_general | solution.py:341
  226.8 2.6 fusion.14
  229.4 4.1 convert_reduce_fusion.2
  233.4 7.4 %fusion.90 = f32[3072,768]{1,0:T(8,128)S(1)} fusion(bf16[1024,3072]{1,0:T(8,128)(2,1)} %get-tuple-element.400, bf16[1024,768]{0,1:T(8,128)(2,1)S(1)} %get-tuple-element.299), kind=kOutput, calls=%fused_computation.317 | convolution fusion | flops 4831838208 | bytes 17301504 | tf_op jit(solution)/shard_map/dot_general | solution.py:341
  240.9 16.4 %convert_reduce_fusion = (f32[3072]{0:T(1024)}, bf16[1024,3072]{1,0:T(8,128)(2,1)}) fusion(f32[1024,3072]{1,0:T(8,128)} %get-tuple-element.401, f32[3072]{0:T(1024)S(1)} %add.552, bf16[1024,768]{0,1:T(8,128)(2,1)S(1)} %get-tuple-element.299, bf16[3072,768]{1,0:T(8,128)(2,1)S(1)} %bitcast.388), kind=kOutput, calls=%fused_computation.17 | convolution fusion | flops 4872729600 | bytes 25190400 | tf_op jit(solution)/shard_map/dot_general | solution.py:341
  257.3 10.5 %multiply_reduce_fusion = (f32[768]{0:T(1024)}, f32[1024]{0:T(1024)S(1)}, f32[1024]{0:T(1024)S(1)}, f32[768]{0:T(1024)}, f32[1024,768]{0,1:T(8,128)S(1)}) fusion(f32[1024,768]{0,1:T(8,128)S(1)} %get-tuple-element.399, f32[1024]{0:T(1024)S(1)} %add_rsqrt_fusion.1, f32[1024]{0:T(1024)S(1)} %broadcast_multiply_fusion.5, f32[768]{0:T(1024)S(1)} %get-tuple-element.282, ...), kind=kOutput, calls=%fused_computation.35 | convolution fusion | flops 4851494912 | bytes 22065152 | tf_op jit(solution)/shard_map/dot_general | solution.py:341
  267.8 7.6 %fusion.76 = f32[768,3072]{1,0:T(8,128)S(1)} fusion(bf16[1024,3072]{1,0:T(8,128)(2,1)} %get-tuple-element.406, f32[1024,768]{0,1:T(8,128)S(1)} %get-tuple-element.399, f32[768]{0:T(1024)S(1)} %get-tuple-element.281, f32[768]{0:T(1024)S(1)} %get-tuple-element.282, f32[1024]{0:T(1024)S(1)} %add_rsqrt_fusion.1, f32[1024]{0:T(1024)S(1)} %broadcast_multiply_fusion.5), kind=kOutput, calls=%fused_computation.306 | convolution fusion | flops 4835770368 | bytes 18888704 | tf_op jit(solution)/shard_map/dot_general | solution.py:341
  275.5 1.9 fusion.17
  277.4 5.1 collective-permute-start.35
  283.7 4.0 fusion.72
  287.7 2.0 fusion.15
  289.7 4.7 convert_add_fusion
  294.4 2.6 convolution_convert_fusion.do_ref
  297.0 3.5 collective-permute-start.38
  300.5 3.9 fusion.21
  305.2 5.4 collective-permute-done.36
  315.1 31.9 %attention_backward.3 = (bf16[1024,256]{1,0:T(8,128)(2,1)}, f32[2,1024,256]{2,1,0:T(8,128)}, bf16[2,1024,256]{2,1,0:T(8,128)(2,1)}) custom-call(s32[10]{0:T(128)} %pad_add_fusion.3.info, bf16[1024,768]{1,0:T(8,128)(2,1)} %multiply_convert_fusion.3.q_ref.k_own.v_own, bf16[1024,256]{1,0:T(8,128)(2,1)} %get-tuple-element.135.ext_ref, ...), custom_call_target="tpu_custom_call" | custom-call | flops 2684354560 | bytes 6291456 | tf_op jit(solution)/shard_map/attention_backward/pallas_call | solution.py:253
  349.0 2.0 collective-permute-start.40
  350.9 7.6 %collective-permute-start.45 = (bf16[2,1024,256]{2,1,0:T(8,128)(2,1)}, bf16[2,1024,256]{2,1,0:T(8,128)(2,1)}, u32[]{:S(2)}, u32[]{:S(2)}) collective-permute-start(bf16[2,1024,256]{2,1,0:T(8,128)(2,1)} %get-tuple-element.155), channel_id=1, source_target_pairs={{0,1},{1,0},{2,3},{3,2},{4,5},{5,4},{6,7},{7,6},{8,9},{9,8},{10,11... | collective-permute-start | bytes 3145736 | tf_op jit(solution)/shard_map/ppermute | solution.py:370
  359.7 32.3 %attention_backward.4 = (bf16[1024,256]{1,0:T(8,128)(2,1)}, f32[2,1024,256]{2,1,0:T(8,128)}, bf16[2,1024,256]{2,1,0:T(8,128)(2,1)}) custom-call(s32[10]{0:T(128)} %pad_add_fusion.3.info, bf16[1024,768]{1,0:T(8,128)(2,1)} %copy-done.1, bf16[1024,256]{1,0:T(8,128)(2,1)} %get-tuple-element.143.ext_ref, bf16[1024,768]{1,0:T(8,128)(2,1)} %convolution_convert_fusion.do_ref, ...), custom_call_target="tpu_custom_call" | custom-call | flops 2684354560 | bytes 6291456 | tf_op jit(solution)/shard_map/attention_backward/pallas_call | solution.py:253
  392.1 9.0 %collective-permute-start.48 = (bf16[2,1024,256]{2,1,0:T(8,128)(2,1)}, bf16[2,1024,256]{2,1,0:T(8,128)(2,1)}, u32[]{:S(2)}, u32[]{:S(2)}) collective-permute-start(bf16[2,1024,256]{2,1,0:T(8,128)(2,1)} %get-tuple-element.167), channel_id=1, source_target_pairs={{0,1},{1,0},{2,3},{3,2},{4,5},{5,4},{6,7},{7,6},{8,9},{9,8},{10,11... | collective-permute-start | bytes 3145736 | tf_op jit(solution)/shard_map/ppermute | solution.py:370
  403.1 2.8 fusion.75
  406.7 3.1 convolution_add_fusion.1
  409.9 2.6 collective-permute-start.56
  412.5 3.0 collective-permute-start.55
  417.2 6.5 %collective-permute-start.29 = (bf16[256,768]{0,1:T(8,128)(2,1)S(1)}, bf16[256,768]{0,1:T(8,128)(2,1)S(1)}, u32[]{:S(2)}, u32[]{:S(2)}) collective-permute-start(bf16[256,768]{0,1:T(8,128)(2,1)S(1)} %copy-done.41), channel_id=1, source_target_pairs={{0,16},{8,24},{16,0},{24,8},{1,17},{9,25},{17,1},{25,9},{2,18},{10... | collective-permute-start | bytes 1179656 | tf_op jit(solution)/shard_map/ppermute | solution.py:373
  423.7 2.7 collective-permute-start.30
  427.9 32.3 %attention_backward.5 = (bf16[1024,256]{1,0:T(8,128)(2,1)}, f32[2,1024,256]{2,1,0:T(8,128)}, bf16[2,1024,256]{2,1,0:T(8,128)(2,1)}) custom-call(s32[10]{0:T(128)} %pad_add_fusion.3.info, bf16[1024,768]{1,0:T(8,128)(2,1)} %copy-done, bf16[1024,256]{1,0:T(8,128)(2,1)} %get-tuple-element.128.ext_ref, bf16[1024,768]{1,0:T(8,128)(2,1)} %convolution_convert_fusion.do_ref, ...), custom_call_target="tpu_custom_call" | custom-call | flops 2684354560 | bytes 6291456 | tf_op jit(solution)/shard_map/attention_backward/pallas_call | solution.py:253
  460.1 12.7 %collective-permute-start.64 = (bf16[48,3840]{1,0:T(8,128)(2,1)S(1)}, bf16[48,3840]{1,0:T(8,128)(2,1)S(1)}, u32[]{:S(2)}, u32[]{:S(2)}) collective-permute-start(bf16[48,3840]{1,0:T(8,128)(2,1)S(1)} %add_convert_fusion.8), channel_id=1, source_target_pairs={{0,16},{8,24},{16,0},{24,8},{1,17},{9,25},{17,1},{25,9},{2,18},{10... | collective-permute-start | bytes 1105928 | tf_op jit(solution)/shard_map/ppermute | solution.py:373
  478.2 6.7 %collective-permute-done.64 = bf16[48,3840]{1,0:T(8,128)(2,1)S(1)} collective-permute-done((bf16[48,3840]{1,0:T(8,128)(2,1)S(1)}, bf16[48,3840]{1,0:T(8,128)(2,1)S(1)}, u32[]{:S(2)}, u32[]{:S(2)}) %collective-permute-start.64) | collective-permute-done | bytes 368672 | tf_op jit(solution)/shard_map/ppermute | solution.py:373
  489.8 5.2 collective-permute-done.67
  504.3 4.9 fusion.80
  513.6 2.3 collective-permute-start.59
  518.4 3.2 collective-permute-start.52
  521.6 2.8 collective-permute-done.60
  525.1 5.5 collective-permute-done.59
  532.3 22.0 %collective-permute-done.51 = bf16[256,768]{0,1:T(8,128)(2,1)S(1)} collective-permute-done((bf16[256,768]{0,1:T(8,128)(2,1)S(1)}, bf16[256,768]{0,1:T(8,128)(2,1)S(1)}, u32[]{:S(2)}, u32[]{:S(2)}) %collective-permute-start.51) | collective-permute-done | bytes 393248 | tf_op jit(solution)/shard_map/ppermute | solution.py:373
  557.5 9.6 %collective-permute-done.62 = bf16[48,2432]{1,0:T(8,128)(2,1)S(1)} collective-permute-done((bf16[48,2432]{1,0:T(8,128)(2,1)S(1)}, bf16[48,2432]{1,0:T(8,128)(2,1)S(1)}, u32[]{:S(2)}, u32[]{:S(2)}) %collective-permute-start.62) | collective-permute-done | bytes 233504 | tf_op jit(solution)/shard_map/ppermute | solution.py:373
  569.0 2.4 copy.274
  571.3 3.6 collective-permute-done.63
  (450 shorter events, 114.4 us)
Async XLA Ops:
  3.3 17.9 %collective-permute-start = (bf16[2,256,768]{1,2,0:T(8,128)(2,1)}, bf16[2,256,768]{1,2,0:T(8,128)(2,1)S(1)}, u32[]{:S(2)}, u32[]{:S(2)}) collective-permute-start(bf16[2,256,768]{1,2,0:T(8,128)(2,1)} %bitcast.2), channel_id=1, source_target_pairs={{0,1},{1,0},{2,3},{3,2},{4,5},{5,4},{6,7},{7,6},{8,9},{9,8},{10,11... | collective-permute-start | bytes 2359304 | tf_op jit(solution)/shard_map/ppermute | solution.py:370
  23.6 9.2 %collective-permute-start.7 = (s32[256,1]{0,1:T(1,128)S(1)}, s32[256,1]{0,1:T(1,128)S(1)}, u32[]{:S(2)}, u32[]{:S(2)}) collective-permute-start(s32[256,1]{0,1:T(1,128)S(1)} %get-tuple-element.388), channel_id=1, source_target_pairs={{0,24},{8,16},{16,8},{24,0},{1,25},{9,17},{17,9},{25,1},{2,26},{10... | collective-permute-start | bytes 3080 | tf_op jit(solution)/shard_map/ppermute | solution.py:373
  28.5 8.0 %collective-permute-start.6 = (s32[256,1]{0,1:T(1,128)S(1)}, s32[256,1]{0,1:T(1,128)S(1)}, u32[]{:S(2)}, u32[]{:S(2)}) collective-permute-start(s32[256,1]{0,1:T(1,128)S(1)} %get-tuple-element.386), channel_id=1, source_target_pairs={{0,16},{8,24},{16,0},{24,8},{1,17},{9,25},{17,1},{25,9},{2,18},{10... | collective-permute-start | bytes 3080 | tf_op jit(solution)/shard_map/ppermute | solution.py:373
  28.5 8.0 %collective-permute-start.5 = (s32[256,1]{0,1:T(1,128)S(1)}, s32[256,1]{0,1:T(1,128)S(1)}, u32[]{:S(2)}, u32[]{:S(2)}) collective-permute-start(s32[256,1]{0,1:T(1,128)S(1)} %get-tuple-element.387), channel_id=1, source_target_pairs={{0,8},{8,0},{16,24},{24,16},{1,9},{9,1},{17,25},{25,17},{2,10},{10... | collective-permute-start | bytes 3080 | tf_op jit(solution)/shard_map/ppermute | solution.py:373
  29.7 12.4 %collective-permute-start.9 = (bf16[96,2432]{1,0:T(8,128)(2,1)S(1)}, bf16[96,2432]{1,0:T(8,128)(2,1)S(1)}, u32[]{:S(2)}, u32[]{:S(2)}) collective-permute-start(bf16[96,2432]{1,0:T(8,128)(2,1)S(1)} %pad_maximum_fusion.16.refs_0_), channel_id=1, source_target_pairs={{0,2},{1,3},{2,0},{3,1},{4,6},{5,7},{6,4},{7,5},{8,10},{9,11},{10,... | collective-permute-start | bytes 1400840 | tf_op jit(solution)/shard_map/ppermute | solution.py:376
  31.3 12.0 %collective-permute-start.10 = (bf16[96,2432]{1,0:T(8,128)(2,1)S(1)}, bf16[96,2432]{1,0:T(8,128)(2,1)S(1)}, u32[]{:S(2)}, u32[]{:S(2)}) collective-permute-start(bf16[96,2432]{1,0:T(8,128)(2,1)S(1)} %pad_maximum_fusion.16.refs_0_), channel_id=1, source_target_pairs={{0,4},{1,5},{2,6},{3,7},{4,0},{5,1},{6,2},{7,3},{8,12},{9,13},{10,... | collective-permute-start | bytes 1400840 | tf_op jit(solution)/shard_map/ppermute | solution.py:376
  32.9 19.9 %collective-permute-start.3 = (bf16[256,768]{0,1:T(8,128)(2,1)S(1)}, bf16[256,768]{0,1:T(8,128)(2,1)}, u32[]{:S(2)}, u32[]{:S(2)}) collective-permute-start(bf16[256,768]{0,1:T(8,128)(2,1)S(1)} %get-tuple-element.359), channel_id=1, source_target_pairs={{0,24},{8,16},{16,8},{24,0},{1,25},{9,17},{17,9},{25,1},{2,26},{10... | collective-permute-start | bytes 1179656 | tf_op jit(solution)/shard_map/ppermute | solution.py:373
  36.5 32.7 %collective-permute-start.2 = (bf16[256,768]{0,1:T(8,128)(2,1)}, bf16[256,768]{0,1:T(8,128)(2,1)}, u32[]{:S(2)}, u32[]{:S(2)}) collective-permute-start(bf16[256,768]{0,1:T(8,128)(2,1)} %get-tuple-element.360), channel_id=1, source_target_pairs={{0,16},{8,24},{16,0},{24,8},{1,17},{9,25},{17,1},{25,9},{2,18},{10... | collective-permute-start | bytes 1179656 | tf_op jit(solution)/shard_map/ppermute | solution.py:373
  38.9 31.4 %collective-permute-start.1 = (bf16[256,768]{0,1:T(8,128)(2,1)}, bf16[256,768]{0,1:T(8,128)(2,1)}, u32[]{:S(2)}, u32[]{:S(2)}) collective-permute-start(bf16[256,768]{0,1:T(8,128)(2,1)} %get-tuple-element.361), channel_id=1, source_target_pairs={{0,8},{8,0},{16,24},{24,16},{1,9},{9,1},{17,25},{25,17},{2,10},{10... | collective-permute-start | bytes 1179656 | tf_op jit(solution)/shard_map/ppermute | solution.py:373
  43.3 6.3 %collective-permute-start.11 = (bf16[48,2432]{1,0:T(8,128)(2,1)S(1)}, bf16[48,2432]{1,0:T(8,128)(2,1)S(1)}, u32[]{:S(2)}, u32[]{:S(2)}) collective-permute-start(bf16[48,2432]{1,0:T(8,128)(2,1)S(1)} %slice.188), channel_id=1, source_target_pairs={{0,4},{1,5},{2,6},{3,7},{4,0},{5,1},{6,2},{7,3},{8,12},{9,13},{10,... | collective-permute-start | bytes 700424 | tf_op jit(solution)/shard_map/ppermute | solution.py:376
  44.9 6.1 %collective-permute-start.12 = (bf16[48,2432]{1,0:T(8,128)(2,1)S(1)}, bf16[48,2432]{1,0:T(8,128)(2,1)S(1)}, u32[]{:S(2)}, u32[]{:S(2)}) collective-permute-start(bf16[48,2432]{1,0:T(8,128)(2,1)S(1)} %slice.189), channel_id=1, source_target_pairs={{0,2},{1,3},{2,0},{3,1},{4,6},{5,7},{6,4},{7,5},{8,10},{9,11},{10,... | collective-permute-start | bytes 700424 | tf_op jit(solution)/shard_map/ppermute | solution.py:376
  49.6 21.8 %collective-permute-start.14 = (bf16[96,2432]{1,0:T(8,128)(2,1)S(1)}, bf16[96,2432]{1,0:T(8,128)(2,1)S(1)}, u32[]{:S(2)}, u32[]{:S(2)}) collective-permute-start(bf16[96,2432]{1,0:T(8,128)(2,1)S(1)} %collective-permute-done.9.refs_1_), channel_id=1, source_target_pairs={{0,1},{1,0},{2,3},{3,2},{4,5},{5,4},{6,7},{7,6},{8,9},{9,8},{10,11... | collective-permute-start | bytes 1400840 | tf_op jit(solution)/shard_map/ppermute | solution.py:370
  51.8 19.7 %collective-permute-start.15 = (bf16[96,2432]{1,0:T(8,128)(2,1)S(1)}, bf16[96,2432]{1,0:T(8,128)(2,1)S(1)}, u32[]{:S(2)}, u32[]{:S(2)}) collective-permute-start(bf16[96,2432]{1,0:T(8,128)(2,1)S(1)} %collective-permute-done.10.refs_2_), channel_id=1, source_target_pairs={{0,1},{1,0},{2,3},{3,2},{4,5},{5,4},{6,7},{7,6},{8,9},{9,8},{10,11... | collective-permute-start | bytes 1400840 | tf_op jit(solution)/shard_map/ppermute | solution.py:370
  52.8 18.1 %collective-permute-start.13 = (bf16[96,2432]{1,0:T(8,128)(2,1)S(1)}, bf16[96,2432]{1,0:T(8,128)(2,1)S(1)}, u32[]{:S(2)}, u32[]{:S(2)}) collective-permute-start(bf16[96,2432]{1,0:T(8,128)(2,1)S(1)} %pad_maximum_fusion.16.refs_0_), channel_id=1, source_target_pairs={{0,1},{1,0},{2,3},{3,2},{4,5},{5,4},{6,7},{7,6},{8,9},{9,8},{10,11... | collective-permute-start | bytes 1400840 | tf_op jit(solution)/shard_map/ppermute | solution.py:370
  70.3 42.3 %collective-permute-start.20 = (bf16[864,768]{1,0:T(8,128)(2,1)}, bf16[864,768]{1,0:T(8,128)(2,1)}, u32[]{:S(2)}, u32[]{:S(2)}) collective-permute-start(bf16[864,768]{1,0:T(8,128)(2,1)} %constant_dynamic-update-slice_fusion.5.refs_0_), channel_id=1, source_target_pairs={{0,2},{1,3},{2,0},{3,1},{4,6},{5,7},{6,4},{7,5},{8,10},{9,11},{10,... | collective-permute-start | bytes 3981320 | tf_op jit(solution)/shard_map/ppermute | solution.py:376
  70.9 41.7 %collective-permute-start.21 = (bf16[864,768]{1,0:T(8,128)(2,1)}, bf16[864,768]{1,0:T(8,128)(2,1)}, u32[]{:S(2)}, u32[]{:S(2)}) collective-permute-start(bf16[864,768]{1,0:T(8,128)(2,1)} %constant_dynamic-update-slice_fusion.5.refs_0_), channel_id=1, source_target_pairs={{0,4},{1,5},{2,6},{3,7},{4,0},{5,1},{6,2},{7,3},{8,12},{9,13},{10,... | collective-permute-start | bytes 3981320 | tf_op jit(solution)/shard_map/ppermute | solution.py:376
  82.0 9.6 %collective-permute-start.17 = (bf16[1024,768]{1,0:T(8,128)(2,1)}, bf16[1024,768]{1,0:T(8,128)(2,1)}, u32[]{:S(2)}, u32[]{:S(2)}) collective-permute-start(bf16[1024,768]{1,0:T(8,128)(2,1)} %multiply_convert_fusion.3.q_ref.k_own.v_own), channel_id=1, source_target_pairs={{0,1},{1,0},{2,3},{3,2},{4,5},{5,4},{6,7},{7,6},{8,9},{9,8},{10,11... | collective-permute-start | bytes 4718600 | tf_op jit(solution)/shard_map/ppermute | solution.py:370
  84.9 46.0 %collective-permute-start.18 = (bf16[1024,768]{1,0:T(8,128)(2,1)S(1)}, bf16[1024,768]{1,0:T(8,128)(2,1)}, u32[]{:S(2)}, u32[]{:S(2)}) collective-permute-start(bf16[1024,768]{1,0:T(8,128)(2,1)S(1)} %multiply_convert_fusion.2.q_ref.k_own.v_own), channel_id=1, source_target_pairs={{0,1},{1,0},{2,3},{3,2},{4,5},{5,4},{6,7},{7,6},{8,9},{9,8},{10,11... | collective-permute-start | bytes 4718600 | tf_op jit(solution)/shard_map/ppermute | solution.py:370
  87.8 39.7 %collective-permute-start.31 = (bf16[2,256,768]{1,2,0:T(8,128)(2,1)}, bf16[2,256,768]{1,2,0:T(8,128)(2,1)}, u32[]{:S(2)}, u32[]{:S(2)}) collective-permute-start(bf16[2,256,768]{1,2,0:T(8,128)(2,1)} %bitcast.63), channel_id=1, source_target_pairs={{0,1},{1,0},{2,3},{3,2},{4,5},{5,4},{6,7},{7,6},{8,9},{9,8},{10,11... | collective-permute-start | bytes 2359304 | tf_op jit(solution)/shard_map/ppermute | solution.py:370
  91.6 71.7 %collective-permute-start.19 = (bf16[1024,768]{1,0:T(8,128)(2,1)S(1)}, bf16[1024,768]{1,0:T(8,128)(2,1)}, u32[]{:S(2)}, u32[]{:S(2)}) collective-permute-start(bf16[1024,768]{1,0:T(8,128)(2,1)S(1)} %multiply_convert_fusion.1.q_ref.k_own.v_own), channel_id=1, source_target_pairs={{0,1},{1,0},{2,3},{3,2},{4,5},{5,4},{6,7},{7,6},{8,9},{9,8},{10,11... | collective-permute-start | bytes 4718600 | tf_op jit(solution)/shard_map/ppermute | solution.py:370
  114.7 43.2 %collective-permute-start.22 = (bf16[432,768]{1,0:T(8,128)(2,1)}, bf16[432,768]{1,0:T(8,128)(2,1)}, u32[]{:S(2)}, u32[]{:S(2)}) collective-permute-start(bf16[432,768]{1,0:T(8,128)(2,1)} %slice.206), channel_id=1, source_target_pairs={{0,4},{1,5},{2,6},{3,7},{4,0},{5,1},{6,2},{7,3},{8,12},{9,13},{10,... | collective-permute-start | bytes 1990664 | tf_op jit(solution)/shard_map/ppermute | solution.py:376
  118.2 42.0 %collective-permute-start.23 = (bf16[432,768]{1,0:T(8,128)(2,1)}, bf16[432,768]{1,0:T(8,128)(2,1)}, u32[]{:S(2)}, u32[]{:S(2)}) collective-permute-start(bf16[432,768]{1,0:T(8,128)(2,1)} %slice.207), channel_id=1, source_target_pairs={{0,2},{1,3},{2,0},{3,1},{4,6},{5,7},{6,4},{7,5},{8,10},{9,11},{10,... | collective-permute-start | bytes 1990664 | tf_op jit(solution)/shard_map/ppermute | solution.py:376
  130.3 32.3 %collective-permute-start.32 = (bf16[256,768]{0,1:T(8,128)(2,1)}, bf16[256,768]{0,1:T(8,128)(2,1)}, u32[]{:S(2)}, u32[]{:S(2)}) collective-permute-start(bf16[256,768]{0,1:T(8,128)(2,1)} %get-tuple-element.356), channel_id=1, source_target_pairs={{0,8},{8,0},{16,24},{24,16},{1,9},{9,1},{17,25},{25,17},{2,10},{10... | collective-permute-start | bytes 1179656 | tf_op jit(solution)/shard_map/ppermute | solution.py:373
  130.9 32.3 %collective-permute-start.33 = (bf16[256,768]{0,1:T(8,128)(2,1)}, bf16[256,768]{0,1:T(8,128)(2,1)}, u32[]{:S(2)}, u32[]{:S(2)}) collective-permute-start(bf16[256,768]{0,1:T(8,128)(2,1)} %get-tuple-element.355), channel_id=1, source_target_pairs={{0,16},{8,24},{16,0},{24,8},{1,17},{9,25},{17,1},{25,9},{2,18},{10... | collective-permute-start | bytes 1179656 | tf_op jit(solution)/shard_map/ppermute | solution.py:373
  157.9 35.3 %collective-permute-start.25 = (bf16[864,768]{1,0:T(8,128)(2,1)}, bf16[864,768]{1,0:T(8,128)(2,1)}, u32[]{:S(2)}, u32[]{:S(2)}) collective-permute-start(bf16[864,768]{1,0:T(8,128)(2,1)} %collective-permute-done.20.refs_1_), channel_id=1, source_target_pairs={{0,1},{1,0},{2,3},{3,2},{4,5},{5,4},{6,7},{7,6},{8,9},{9,8},{10,11... | collective-permute-start | bytes 3981320 | tf_op jit(solution)/shard_map/ppermute | solution.py:370
  160.3 33.0 %collective-permute-start.24 = (bf16[864,768]{1,0:T(8,128)(2,1)}, bf16[864,768]{1,0:T(8,128)(2,1)}, u32[]{:S(2)}, u32[]{:S(2)}) collective-permute-start(bf16[864,768]{1,0:T(8,128)(2,1)} %constant_dynamic-update-slice_fusion.5.refs_0_), channel_id=1, source_target_pairs={{0,1},{1,0},{2,3},{3,2},{4,5},{5,4},{6,7},{7,6},{8,9},{9,8},{10,11... | collective-permute-start | bytes 3981320 | tf_op jit(solution)/shard_map/ppermute | solution.py:370
  162.7 30.6 %collective-permute-start.26 = (bf16[864,768]{1,0:T(8,128)(2,1)}, bf16[864,768]{1,0:T(8,128)(2,1)}, u32[]{:S(2)}, u32[]{:S(2)}) collective-permute-start(bf16[864,768]{1,0:T(8,128)(2,1)} %collective-permute-done.21.refs_2_), channel_id=1, source_target_pairs={{0,1},{1,0},{2,3},{3,2},{4,5},{5,4},{6,7},{7,6},{8,9},{9,8},{10,11... | collective-permute-start | bytes 3981320 | tf_op jit(solution)/shard_map/ppermute | solution.py:370
  163.2 30.1 %collective-permute-start.27 = (bf16[864,768]{1,0:T(8,128)(2,1)S(1)}, bf16[864,768]{1,0:T(8,128)(2,1)}, u32[]{:S(2)}, u32[]{:S(2)}) collective-permute-start(bf16[864,768]{1,0:T(8,128)(2,1)S(1)} %constant_dynamic-update-slice_fusion.7.refs_3_), channel_id=1, source_target_pairs={{0,1},{1,0},{2,3},{3,2},{4,5},{5,4},{6,7},{7,6},{8,9},{9,8},{10,11... | collective-permute-start | bytes 3981320 | tf_op jit(solution)/shard_map/ppermute | solution.py:370
  163.3 26.2 %collective-permute-start.34 = (bf16[256,768]{0,1:T(8,128)(2,1)}, bf16[256,768]{0,1:T(8,128)(2,1)S(1)}, u32[]{:S(2)}, u32[]{:S(2)}) collective-permute-start(bf16[256,768]{0,1:T(8,128)(2,1)} %get-tuple-element.354), channel_id=1, source_target_pairs={{0,24},{8,16},{16,8},{24,0},{1,25},{9,17},{17,9},{25,1},{2,26},{10... | collective-permute-start | bytes 1179656 | tf_op jit(solution)/shard_map/ppermute | solution.py:373
  277.4 12.3 %collective-permute-start.35 = (bf16[4,384,768]{2,1,0:T(8,128)(2,1)}, bf16[4,384,768]{2,1,0:T(8,128)(2,1)}, u32[]{:S(2)}, u32[]{:S(2)}) collective-permute-start(bf16[4,384,768]{2,1,0:T(8,128)(2,1)} %fusion.17), channel_id=1, source_target_pairs={{0,1},{1,0},{2,3},{3,2},{4,5},{5,4},{6,7},{7,6},{8,9},{9,8},{10,11... | collective-permute-start | bytes 7077896 | tf_op jit(solution)/shard_map/ppermute | solution.py:370
  289.7 10.8 %collective-permute-start.39 = (bf16[4,96,3840]{2,1,0:T(8,128)(2,1)}, bf16[4,96,3840]{2,1,0:T(8,128)(2,1)}, u32[]{:S(2)}, u32[]{:S(2)}) collective-permute-start(bf16[4,96,3840]{2,1,0:T(8,128)(2,1)} %fusion.15), channel_id=1, source_target_pairs={{0,1},{1,0},{2,3},{3,2},{4,5},{5,4},{6,7},{7,6},{8,9},{9,8},{10,11... | collective-permute-start | bytes 8847368 | tf_op jit(solution)/shard_map/ppermute | solution.py:370
  294.4 16.2 %collective-permute-start.36 = (bf16[384,768]{1,0:T(8,128)(2,1)S(1)}, bf16[384,768]{1,0:T(8,128)(2,1)S(1)}, u32[]{:S(2)}, u32[]{:S(2)}) collective-permute-start(bf16[384,768]{1,0:T(8,128)(2,1)S(1)} %get-tuple-element.311), channel_id=1, source_target_pairs={{0,2},{1,3},{2,0},{3,1},{4,6},{5,7},{6,4},{7,5},{8,10},{9,11},{10,... | collective-permute-start | bytes 1769480 | tf_op jit(solution)/shard_map/ppermute | solution.py:376
  297.0 50.0 %collective-permute-start.37 = (bf16[384,768]{1,0:T(8,128)(2,1)}, bf16[384,768]{1,0:T(8,128)(2,1)}, u32[]{:S(2)}, u32[]{:S(2)}) collective-permute-start(bf16[384,768]{1,0:T(8,128)(2,1)} %get-tuple-element.310), channel_id=1, source_target_pairs={{0,4},{1,5},{2,6},{3,7},{4,0},{5,1},{6,2},{7,3},{8,12},{9,13},{10,... | collective-permute-start | bytes 1769480 | tf_op jit(solution)/shard_map/ppermute | solution.py:376
  297.0 50.1 %collective-permute-start.38 = (bf16[384,768]{1,0:T(8,128)(2,1)}, bf16[384,768]{1,0:T(8,128)(2,1)}, u32[]{:S(2)}, u32[]{:S(2)}) collective-permute-start(bf16[384,768]{1,0:T(8,128)(2,1)} %get-tuple-element.309), channel_id=1, source_target_pairs={{0,6},{1,7},{2,4},{3,5},{4,2},{5,3},{6,0},{7,1},{8,14},{9,15},{10,... | collective-permute-start | bytes 1769480 | tf_op jit(solution)/shard_map/ppermute | solution.py:376
  304.4 46.5 %collective-permute-start.41 = (bf16[96,3840]{1,0:T(8,128)(2,1)}, bf16[96,3840]{1,0:T(8,128)(2,1)S(1)}, u32[]{:S(2)}, u32[]{:S(2)}) collective-permute-start(bf16[96,3840]{1,0:T(8,128)(2,1)} %get-tuple-element.306), channel_id=1, source_target_pairs={{0,2},{1,3},{2,0},{3,1},{4,6},{5,7},{6,4},{7,5},{8,10},{9,11},{10,... | collective-permute-start | bytes 2211848 | tf_op jit(solution)/shard_map/ppermute | solution.py:376
  304.5 54.1 %collective-permute-start.42 = (bf16[96,3840]{1,0:T(8,128)(2,1)}, bf16[96,3840]{1,0:T(8,128)(2,1)S(1)}, u32[]{:S(2)}, u32[]{:S(2)}) collective-permute-start(bf16[96,3840]{1,0:T(8,128)(2,1)} %get-tuple-element.307), channel_id=1, source_target_pairs={{0,4},{1,5},{2,6},{3,7},{4,0},{5,1},{6,2},{7,3},{8,12},{9,13},{10,... | collective-permute-start | bytes 2211848 | tf_op jit(solution)/shard_map/ppermute | solution.py:376
  310.6 48.0 %collective-permute-start.43 = (bf16[96,3840]{1,0:T(8,128)(2,1)}, bf16[96,3840]{1,0:T(8,128)(2,1)S(1)}, u32[]{:S(2)}, u32[]{:S(2)}) collective-permute-start(bf16[96,3840]{1,0:T(8,128)(2,1)} %get-tuple-element.304), channel_id=1, source_target_pairs={{0,6},{1,7},{2,4},{3,5},{4,2},{5,3},{6,0},{7,1},{8,14},{9,15},{10,... | collective-permute-start | bytes 2211848 | tf_op jit(solution)/shard_map/ppermute | solution.py:376
  347.0 113.1 %collective-permute-start.28 = (bf16[256,768]{0,1:T(8,128)(2,1)}, bf16[256,768]{0,1:T(8,128)(2,1)}, u32[]{:S(2)}, u32[]{:S(2)}) collective-permute-start(bf16[256,768]{0,1:T(8,128)(2,1)} %get-tuple-element.342), channel_id=1, source_target_pairs={{0,8},{8,0},{16,24},{24,16},{1,9},{9,1},{17,25},{25,17},{2,10},{10... | collective-permute-start | bytes 1179656 | tf_op jit(solution)/shard_map/ppermute | solution.py:373
  349.0 43.0 %collective-permute-start.40 = (bf16[192,768]{1,0:T(8,128)(2,1)S(1)}, bf16[192,768]{1,0:T(8,128)(2,1)S(1)}, u32[]{:S(2)}, u32[]{:S(2)}) collective-permute-start(bf16[192,768]{1,0:T(8,128)(2,1)S(1)} %get-tuple-element.368), channel_id=1, source_target_pairs={{0,8},{8,0},{16,24},{24,16},{1,9},{9,1},{17,25},{25,17},{2,10},{10... | collective-permute-start | bytes 884744 | tf_op jit(solution)/shard_map/ppermute | solution.py:373
  350.9 50.2 %collective-permute-start.45 = (bf16[2,1024,256]{2,1,0:T(8,128)(2,1)}, bf16[2,1024,256]{2,1,0:T(8,128)(2,1)}, u32[]{:S(2)}, u32[]{:S(2)}) collective-permute-start(bf16[2,1024,256]{2,1,0:T(8,128)(2,1)} %get-tuple-element.155), channel_id=1, source_target_pairs={{0,1},{1,0},{2,3},{3,2},{4,5},{5,4},{6,7},{7,6},{8,9},{9,8},{10,11... | collective-permute-start | bytes 3145736 | tf_op jit(solution)/shard_map/ppermute | solution.py:370
  392.0 17.8 %collective-permute-start.44 = (bf16[48,3840]{1,0:T(8,128)(2,1)}, bf16[48,3840]{1,0:T(8,128)(2,1)S(1)}, u32[]{:S(2)}, u32[]{:S(2)}) collective-permute-start(bf16[48,3840]{1,0:T(8,128)(2,1)} %get-tuple-element.364), channel_id=1, source_target_pairs={{0,8},{8,0},{16,24},{24,16},{1,9},{9,1},{17,25},{25,17},{2,10},{10... | collective-permute-start | bytes 1105928 | tf_op jit(solution)/shard_map/ppermute | solution.py:373
  392.1 84.0 %collective-permute-start.48 = (bf16[2,1024,256]{2,1,0:T(8,128)(2,1)}, bf16[2,1024,256]{2,1,0:T(8,128)(2,1)}, u32[]{:S(2)}, u32[]{:S(2)}) collective-permute-start(bf16[2,1024,256]{2,1,0:T(8,128)(2,1)} %get-tuple-element.167), channel_id=1, source_target_pairs={{0,1},{1,0},{2,3},{3,2},{4,5},{5,4},{6,7},{7,6},{8,9},{9,8},{10,11... | collective-permute-start | bytes 3145736 | tf_op jit(solution)/shard_map/ppermute | solution.py:370
  406.0 3.8 collective-permute-start.46
  409.9 7.3 %collective-permute-start.56 = (bf16[96,768]{1,0:T(8,128)(2,1)S(1)}, bf16[96,768]{1,0:T(8,128)(2,1)S(1)}, u32[]{:S(2)}, u32[]{:S(2)}) collective-permute-start(bf16[96,768]{1,0:T(8,128)(2,1)S(1)} %get-tuple-element.317), channel_id=1, source_target_pairs={{0,6},{1,7},{2,4},{3,5},{4,2},{5,3},{6,0},{7,1},{8,14},{9,15},{10,... | collective-permute-start | bytes 442376 | tf_op jit(solution)/shard_map/ppermute | solution.py:376
  412.5 11.2 %collective-permute-start.55 = (bf16[96,768]{1,0:T(8,128)(2,1)S(1)}, bf16[96,768]{1,0:T(8,128)(2,1)S(1)}, u32[]{:S(2)}, u32[]{:S(2)}) collective-permute-start(bf16[96,768]{1,0:T(8,128)(2,1)S(1)} %get-tuple-element.318), channel_id=1, source_target_pairs={{0,4},{1,5},{2,6},{3,7},{4,0},{5,1},{6,2},{7,3},{8,12},{9,13},{10,... | collective-permute-start | bytes 442376 | tf_op jit(solution)/shard_map/ppermute | solution.py:376
  415.4 11.0 %collective-permute-start.54 = (bf16[96,768]{1,0:T(8,128)(2,1)S(1)}, bf16[96,768]{1,0:T(8,128)(2,1)S(1)}, u32[]{:S(2)}, u32[]{:S(2)}) collective-permute-start(bf16[96,768]{1,0:T(8,128)(2,1)S(1)} %get-tuple-element.316), channel_id=1, source_target_pairs={{0,2},{1,3},{2,0},{3,1},{4,6},{5,7},{6,4},{7,5},{8,10},{9,11},{10,... | collective-permute-start | bytes 442376 | tf_op jit(solution)/shard_map/ppermute | solution.py:376
  417.2 55.6 %collective-permute-start.29 = (bf16[256,768]{0,1:T(8,128)(2,1)S(1)}, bf16[256,768]{0,1:T(8,128)(2,1)S(1)}, u32[]{:S(2)}, u32[]{:S(2)}) collective-permute-start(bf16[256,768]{0,1:T(8,128)(2,1)S(1)} %copy-done.41), channel_id=1, source_target_pairs={{0,16},{8,24},{16,0},{24,8},{1,17},{9,25},{17,1},{25,9},{2,18},{10... | collective-permute-start | bytes 1179656 | tf_op jit(solution)/shard_map/ppermute | solution.py:373
  423.7 49.1 %collective-permute-start.30 = (bf16[256,768]{0,1:T(8,128)(2,1)S(1)}, bf16[256,768]{0,1:T(8,128)(2,1)S(1)}, u32[]{:S(2)}, u32[]{:S(2)}) collective-permute-start(bf16[256,768]{0,1:T(8,128)(2,1)S(1)} %copy-done.40), channel_id=1, source_target_pairs={{0,24},{8,16},{16,8},{24,0},{1,25},{9,17},{17,9},{25,1},{2,26},{10... | collective-permute-start | bytes 1179656 | tf_op jit(solution)/shard_map/ppermute | solution.py:373
  426.4 58.6 %collective-permute-start.66 = (bf16[192,768]{1,0:T(8,128)(2,1)S(1)}, bf16[192,768]{1,0:T(8,128)(2,1)S(1)}, u32[]{:S(2)}, u32[]{:S(2)}) collective-permute-start(bf16[192,768]{1,0:T(8,128)(2,1)S(1)} %add_convert_fusion.10), channel_id=1, source_target_pairs={{0,16},{8,24},{16,0},{24,8},{1,17},{9,25},{17,1},{25,9},{2,18},{10... | collective-permute-start | bytes 884744 | tf_op jit(solution)/shard_map/ppermute | solution.py:373
  460.1 24.8 %collective-permute-start.64 = (bf16[48,3840]{1,0:T(8,128)(2,1)S(1)}, bf16[48,3840]{1,0:T(8,128)(2,1)S(1)}, u32[]{:S(2)}, u32[]{:S(2)}) collective-permute-start(bf16[48,3840]{1,0:T(8,128)(2,1)S(1)} %add_convert_fusion.8), channel_id=1, source_target_pairs={{0,16},{8,24},{16,0},{24,8},{1,17},{9,25},{17,1},{25,9},{2,18},{10... | collective-permute-start | bytes 1105928 | tf_op jit(solution)/shard_map/ppermute | solution.py:373
  476.0 40.9 %collective-permute-start.47 = (bf16[2,256,768]{1,2,0:T(8,128)(2,1)}, bf16[2,256,768]{1,2,0:T(8,128)(2,1)}, u32[]{:S(2)}, u32[]{:S(2)}) collective-permute-start(bf16[2,256,768]{1,2,0:T(8,128)(2,1)} %pad_maximum_fusion.10), channel_id=1, source_target_pairs={{0,1},{1,0},{2,3},{3,2},{4,5},{5,4},{6,7},{7,6},{8,9},{9,8},{10,11... | collective-permute-start | bytes 2359304 | tf_op jit(solution)/shard_map/ppermute | solution.py:370
  476.1 20.1 %collective-permute-start.49 = (bf16[2,1024,256]{2,1,0:T(8,128)(2,1)S(1)}, bf16[2,1024,256]{2,1,0:T(8,128)(2,1)S(1)}, u32[]{:S(2)}, u32[]{:S(2)}) collective-permute-start(bf16[2,1024,256]{2,1,0:T(8,128)(2,1)S(1)} %copy-done.79), channel_id=1, source_target_pairs={{0,1},{1,0},{2,3},{3,2},{4,5},{5,4},{6,7},{7,6},{8,9},{9,8},{10,11... | collective-permute-start | bytes 3145736 | tf_op jit(solution)/shard_map/ppermute | solution.py:370
  485.1 9.9 %collective-permute-start.67 = (bf16[192,768]{1,0:T(8,128)(2,1)S(1)}, bf16[192,768]{1,0:T(8,128)(2,1)S(1)}, u32[]{:S(2)}, u32[]{:S(2)}) collective-permute-start(bf16[192,768]{1,0:T(8,128)(2,1)S(1)} %add_convert_fusion.9), channel_id=1, source_target_pairs={{0,8},{8,0},{16,24},{24,16},{1,9},{9,1},{17,25},{25,17},{2,10},{10... | collective-permute-start | bytes 884744 | tf_op jit(solution)/shard_map/ppermute | solution.py:373
  488.4 21.3 %collective-permute-start.65 = (bf16[48,3840]{1,0:T(8,128)(2,1)}, bf16[48,3840]{1,0:T(8,128)(2,1)}, u32[]{:S(2)}, u32[]{:S(2)}) collective-permute-start(bf16[48,3840]{1,0:T(8,128)(2,1)} %add_convert_fusion.7), channel_id=1, source_target_pairs={{0,8},{8,0},{16,24},{24,16},{1,9},{9,1},{17,25},{25,17},{2,10},{10... | collective-permute-start | bytes 1105928 | tf_op jit(solution)/shard_map/ppermute | solution.py:373
  513.0 11.4 %collective-permute-start.60 = (bf16[96,1664]{1,0:T(8,128)(2,1)S(1)}, bf16[96,1664]{1,0:T(8,128)(2,1)S(1)}, u32[]{:S(2)}, u32[]{:S(2)}) collective-permute-start(bf16[96,1664]{1,0:T(8,128)(2,1)S(1)} %get-tuple-element.313), channel_id=1, source_target_pairs={{0,6},{1,7},{2,4},{3,5},{4,2},{5,3},{6,0},{7,1},{8,14},{9,15},{10,... | collective-permute-start | bytes 958472 | tf_op jit(solution)/shard_map/ppermute | solution.py:376
  513.6 17.0 %collective-permute-start.59 = (bf16[96,1664]{1,0:T(8,128)(2,1)S(1)}, bf16[96,1664]{1,0:T(8,128)(2,1)S(1)}, u32[]{:S(2)}, u32[]{:S(2)}) collective-permute-start(bf16[96,1664]{1,0:T(8,128)(2,1)S(1)} %get-tuple-element.314), channel_id=1, source_target_pairs={{0,4},{1,5},{2,6},{3,7},{4,0},{5,1},{6,2},{7,3},{8,12},{9,13},{10,... | collective-permute-start | bytes 958472 | tf_op jit(solution)/shard_map/ppermute | solution.py:376
  515.8 15.8 %collective-permute-start.58 = (bf16[96,1664]{1,0:T(8,128)(2,1)S(1)}, bf16[96,1664]{1,0:T(8,128)(2,1)S(1)}, u32[]{:S(2)}, u32[]{:S(2)}) collective-permute-start(bf16[96,1664]{1,0:T(8,128)(2,1)S(1)} %get-tuple-element.312), channel_id=1, source_target_pairs={{0,2},{1,3},{2,0},{3,1},{4,6},{5,7},{6,4},{7,5},{8,10},{9,11},{10,... | collective-permute-start | bytes 958472 | tf_op jit(solution)/shard_map/ppermute | solution.py:376
  518.4 14.0 %collective-permute-start.52 = (bf16[256,768]{0,1:T(8,128)(2,1)S(1)}, bf16[256,768]{0,1:T(8,128)(2,1)S(1)}, u32[]{:S(2)}, u32[]{:S(2)}) collective-permute-start(bf16[256,768]{0,1:T(8,128)(2,1)S(1)} %get-tuple-element.327), channel_id=1, source_target_pairs={{0,24},{8,16},{16,8},{24,0},{1,25},{9,17},{17,9},{25,1},{2,26},{10... | collective-permute-start | bytes 1179656 | tf_op jit(solution)/shard_map/ppermute | solution.py:373
  521.6 32.7 %collective-permute-start.51 = (bf16[256,768]{0,1:T(8,128)(2,1)S(1)}, bf16[256,768]{0,1:T(8,128)(2,1)S(1)}, u32[]{:S(2)}, u32[]{:S(2)}) collective-permute-start(bf16[256,768]{0,1:T(8,128)(2,1)S(1)} %get-tuple-element.328), channel_id=1, source_target_pairs={{0,16},{8,24},{16,0},{24,8},{1,17},{9,25},{17,1},{25,9},{2,18},{10... | collective-permute-start | bytes 1179656 | tf_op jit(solution)/shard_map/ppermute | solution.py:373
  524.4 30.0 %collective-permute-start.50 = (bf16[256,768]{0,1:T(8,128)(2,1)S(1)}, bf16[256,768]{0,1:T(8,128)(2,1)S(1)}, u32[]{:S(2)}, u32[]{:S(2)}) collective-permute-start(bf16[256,768]{0,1:T(8,128)(2,1)S(1)} %get-tuple-element.329), channel_id=1, source_target_pairs={{0,8},{8,0},{16,24},{24,16},{1,9},{9,1},{17,25},{25,17},{2,10},{10... | collective-permute-start | bytes 1179656 | tf_op jit(solution)/shard_map/ppermute | solution.py:373
  532.0 22.7 %collective-permute-start.61 = (bf16[48,2432]{1,0:T(8,128)(2,1)S(1)}, bf16[48,2432]{1,0:T(8,128)(2,1)S(1)}, u32[]{:S(2)}, u32[]{:S(2)}) collective-permute-start(bf16[48,2432]{1,0:T(8,128)(2,1)S(1)} %dynamic-slice_bitcast_fusion.4), channel_id=1, source_target_pairs={{0,8},{8,0},{16,24},{24,16},{1,9},{9,1},{17,25},{25,17},{2,10},{10... | collective-permute-start | bytes 700424 | tf_op jit(solution)/shard_map/ppermute | solution.py:373
  554.8 12.4 %collective-permute-start.62 = (bf16[48,2432]{1,0:T(8,128)(2,1)S(1)}, bf16[48,2432]{1,0:T(8,128)(2,1)S(1)}, u32[]{:S(2)}, u32[]{:S(2)}) collective-permute-start(bf16[48,2432]{1,0:T(8,128)(2,1)S(1)} %fusion.46), channel_id=1, source_target_pairs={{0,16},{8,24},{16,0},{24,8},{1,17},{9,25},{17,1},{25,9},{2,18},{10... | collective-permute-start | bytes 700424 | tf_op jit(solution)/shard_map/ppermute | solution.py:373
  555.8 11.5 %collective-permute-start.53 = (bf16[2,256,768]{1,2,0:T(8,128)(2,1)}, bf16[2,256,768]{1,2,0:T(8,128)(2,1)}, u32[]{:S(2)}, u32[]{:S(2)}) collective-permute-start(bf16[2,256,768]{1,2,0:T(8,128)(2,1)} %pad_maximum_fusion.12), channel_id=1, source_target_pairs={{0,1},{1,0},{2,3},{3,2},{4,5},{5,4},{6,7},{7,6},{8,9},{9,8},{10,11... | collective-permute-start | bytes 2359304 | tf_op jit(solution)/shard_map/ppermute | solution.py:370
  567.2 7.8 %collective-permute-start.63 = (bf16[48,2432]{1,0:T(8,128)(2,1)S(1)}, bf16[48,2432]{1,0:T(8,128)(2,1)}, u32[]{:S(2)}, u32[]{:S(2)}) collective-permute-start(bf16[48,2432]{1,0:T(8,128)(2,1)S(1)} %add_convert_fusion.11), channel_id=1, source_target_pairs={{0,8},{8,0},{16,24},{24,16},{1,9},{9,1},{17,25},{25,17},{2,10},{10... | collective-permute-start | bytes 700424 | tf_op jit(solution)/shard_map/ppermute | solution.py:373
  (91 other events, 800.0 us)

commit v4 on v3

--- a/solution.py
+++ b/solution.py
@@ -2,6 +2,7 @@
 import jax, jax.numpy as jnp
 from jax import lax
 from jax.experimental import pallas as pl
+from jax.experimental.layout import Layout, with_layout_constraint
 from jax.experimental.pallas import tpu as pltpu
 from jax.sharding import PartitionSpec as P
 
@@ -42,8 +43,28 @@
             put(b, mate_ref[pl.ds(start, block), :])
 
 
-def forward_kernel(info, q_ref, k_own, k_mate, v_own, v_mate, qx_ref, kx_ref, out_ref, ext_ref, k_all, vt_all, s_all, *, size):
+def forward_kernel(info, q_ref, k_own, k_mate, v_own, v_mate, qx_ref, kx_ref, *refs, size, plan):
+    pieces, moves, outs = plan
+    count = len(pieces)
+    beside, (out_ref, ext_ref), full = refs[:count], refs[count : count + 2], refs[count + 2 : count + 2 + len(outs)]
+    k_all, vt_all, s_all, *sems = refs[count + 2 + len(outs) :]
     slot = pl.program_id(1)
+    if count:
+        copies = [
+            pltpu.make_async_copy(beside[j], full[out].at[info[info.shape[0] - count + j]], sems[0].at[j])
+            for j, out in enumerate(moves)
+        ]
+
+        @pl.when((pl.program_id(0) == 0) & (slot == 0))
+        def _():
+            for copy in copies:
+                copy.start()
+
+        @pl.when((pl.program_id(0) == pl.num_programs(0) - 1) & (slot == pl.num_programs(1) - 1))
+        def _():
+            for copy in copies:
+                copy.wait()
+
     block = q_ref.shape[0]
     count = kx_ref.shape[0] // block
     heads = LANES // size
@@ -124,15 +145,22 @@
     ext_ref[...] = (jnp.concatenate(parts[::-1], axis=0).T + qx.astype(jnp.float32)).astype(ext_ref.dtype)
 
 
-def attention_forward(info, own, mate, qx, kx, size):
+NOTHING = ((), (), ())
+
+
+def attention_forward(info, own, mate, qx, kx, size, plan=NOTHING, spots=()):
     rows, width = own.shape[0], own.shape[1] // 3
     length = kx.shape[0]
     slots = (info.shape[0] - 2) // 2
     block = rows // slots
     pairs = width // LANES
     heads = LANES // size
+    pieces, moves, outs = plan
+    if pieces:
+        info = jnp.concatenate([info, jnp.stack(spots).astype(jnp.int32)])
+    anywhere = pl.BlockSpec(memory_space=pl.ANY)
     return pl.pallas_call(
-        functools.partial(forward_kernel, size=size),
+        functools.partial(forward_kernel, size=size, plan=(moves, moves, outs)),
         grid_spec=pltpu.PrefetchScalarGridSpec(
             num_scalar_prefetch=1,
             grid=(pairs, slots),
@@ -144,21 +172,24 @@
                 pl.BlockSpec((rows, LANES), lambda p, s, i: (0, 2 * pairs + p)),
                 pl.BlockSpec((block, LANES), lambda p, s, i: (s, 0)),
                 pl.BlockSpec((length, LANES), lambda p, s, i: (0, 0)),
-            ],
-            out_specs=[pl.BlockSpec((block, LANES), lambda p, s, i: (s, p))] * 2,
+            ]
+            + [anywhere] * len(pieces),
+            out_specs=[pl.BlockSpec((block, LANES), lambda p, s, i: (s, p))] * 2 + [anywhere] * len(outs),
             scratch_shapes=[
                 pltpu.VMEM((heads, length, LANES), jnp.bfloat16),
                 pltpu.VMEM((heads, size + 16, length), jnp.bfloat16),
                 pltpu.VMEM((heads, block, block), jnp.float32),
-            ],
+            ]
+            + [pltpu.SemaphoreType.DMA((len(pieces),))] * bool(pieces),
         ),
-        out_shape=[jax.ShapeDtypeStruct((rows, width), jnp.bfloat16)] * 2,
+        out_shape=[jax.ShapeDtypeStruct((rows, width), jnp.bfloat16)] * 2
+        + [jax.ShapeDtypeStruct(shape, jnp.bfloat16) for shape in outs],
         compiler_params=pltpu.CompilerParams(dimension_semantics=("arbitrary", "arbitrary")),
         cost_estimate=pl.CostEstimate(
             flops=2 * rows * length * width, bytes_accessed=8 * rows * width * 2, transcendentals=rows * length * pairs
         ),
         name="attention_forward",
-    )(info, own, own, mate, own, mate, qx, kx)
+    )(info, own, own, mate, own, mate, qx, kx, *pieces)
 
 
 def backward_kernel(
@@ -349,6 +380,10 @@
     return [(i, i ^ bits) for i in range(size)]
 
 
+def straight(values):
+    return with_layout_constraint(values, Layout(tuple(range(values.ndim))))
+
+
 def pick(values, index, axis=0):
     return lax.dynamic_index_in_dim(values, index, axis, keepdims=False)
 
@@ -379,14 +414,14 @@
 def to_sequence_parts(here, values):
     groups, piece, width = values.shape
     halves = values.reshape(groups, 2, piece // 2, width)
-    kept = pick(halves, here.core, 1)
-    other = here.mate(pick(halves, 1 - here.core, 1))
+    kept = straight(pick(halves, here.core, 1))
+    other = straight(here.mate(straight(pick(halves, 1 - here.core, 1))))
     parts = []
     for k in range(here.columns):
         want = here.column ^ k
         same = lax.div(want, groups) == here.core
         spot = lax.rem(want, groups)
-        parts.append(jnp.where(same, pick(kept, spot), pick(other, spot)))
+        parts.append(straight(jnp.where(same, pick(kept, spot), pick(other, spot))))
     return parts
 
 
@@ -406,7 +441,8 @@
     return jnp.concatenate([jnp.where(first, kept, other), jnp.where(first, other, kept)], axis=1)
 
 
-def place_kernel(info, *refs, count, cuts, outs):
+def place_kernel(info, *refs, moves, outs):
+    count = len(moves)
     parts, full, buffers = refs[:count], refs[count : count + outs], refs[count + outs : 2 * count + outs]
     in_sem, out_sem = refs[2 * count + outs :]
     reads = [pltpu.make_async_copy(parts[k], buffers[k], in_sem.at[k]) for k in range(count)]
@@ -415,10 +451,10 @@
     writes = []
     for k in range(count):
         reads[k].wait()
-        for j, (row, rows, col, cols, out, out_col) in enumerate(cuts):
+        for j, (row, rows, cut_row, col, cols, out) in enumerate(moves[k]):
             write = pltpu.make_async_copy(
-                buffers[k].at[pl.ds(row, rows), pl.ds(col, cols)],
-                full[out].at[info[k], :, pl.ds(out_col, cols)],
+                buffers[k].at[pl.ds(cut_row, rows), pl.ds(col, cols)],
+                full[out].at[info[k], pl.ds(row, rows), :],
                 out_sem.at[k, j],
             )
             write.start()
@@ -427,63 +463,71 @@
         write.wait()
 
 
-def out_shapes(cuts):
-    shapes = {}
-    for row, rows, col, cols, out, out_col in cuts:
-        shapes[out] = (rows, max(shapes.get(out, (0, 0))[1], out_col + cols))
-    return [shapes[out] for out in sorted(shapes)]
-
-
-def place(parts, spots, cuts):
-    count, (rows, width), kind = len(parts), parts[0].shape, parts[0].dtype
-    shapes = out_shapes(cuts)
-    return pl.pallas_call(
-        functools.partial(place_kernel, count=count, cuts=cuts, outs=len(shapes)),
+def place(parts, spots, firsts, rows, cuts):
+    kind = parts[0].dtype
+    shards = sum(part.shape[0] for part in parts) // rows
+    moves = [
+        [(first, part.shape[0], 0, col, cols, out) for out, (col, cols) in enumerate(cuts)] for first, part in zip(firsts, parts)
+    ]
+    full = pl.pallas_call(
+        functools.partial(place_kernel, moves=moves, outs=len(cuts)),
         grid_spec=pltpu.PrefetchScalarGridSpec(
             num_scalar_prefetch=1,
             grid=(),
-            in_specs=[pl.BlockSpec(memory_space=pl.ANY)] * count,
-            out_specs=[pl.BlockSpec(memory_space=pl.ANY)] * len(shapes),
-            scratch_shapes=[pltpu.VMEM((rows, width), kind)] * count
-            + [pltpu.SemaphoreType.DMA((count,)), pltpu.SemaphoreType.DMA((count, len(cuts)))],
+            in_specs=[pl.BlockSpec(memory_space=pl.ANY)] * len(parts),
+            out_specs=[pl.BlockSpec(memory_space=pl.ANY)] * len(cuts),
+            scratch_shapes=[pltpu.VMEM(part.shape, kind) for part in parts]
+            + [pltpu.SemaphoreType.DMA((len(parts),)), pltpu.SemaphoreType.DMA((len(parts), len(cuts)))],
         ),
-        out_shape=[jax.ShapeDtypeStruct((count,) + shape, kind) for shape in shapes],
-        cost_estimate=pl.CostEstimate(flops=0, bytes_accessed=2 * count * rows * width * 2, transcendentals=0),
+        out_shape=[jax.ShapeDtypeStruct((shards, rows, cols), kind) for _, cols in cuts],
+        cost_estimate=pl.CostEstimate(flops=0, bytes_accessed=0, transcendentals=0),
         name="place_parts",
     )(jnp.stack(spots).astype(jnp.int32), *parts)
-
-
-class Gather:
-    def __init__(self, here, local, cuts):
-        self.here, self.local, self.cuts = here, local, cuts
-        self.direct = here.shards == 8
-        if self.direct:
-            self.parts = [local, here.aside(local, 1), here.aside(local, 2)]
-        else:
-            self.full = lax.all_gather(local, "fsdp", axis=0, tiled=False)
-
-    def corner(self, *marks):
-        if self.direct:
-            here = self.here
-            middle = self.local.shape[0] // 32 * 16
-            _, across_x, across_y = self.parts = after(self.parts, *marks)
-            self.mates = [here.mate(part) for part in self.parts]
-            self.last = [here.aside(across_x[:middle], 2), here.aside(across_y[middle:], 1)]
-
-    def finish(self, *marks):
-        here = self.here
-        if not self.direct:
-            shapes = out_shapes(self.cuts)
-            full = [[] for _ in shapes]
-            for row, rows, col, cols, out, out_col in self.cuts:
-                full[out].append(self.full[:, row : row + rows, col : col + cols])
-            whole = [jnp.concatenate(pieces, axis=2) for pieces in full]
-        else:
-            corner = jnp.concatenate(after(self.last, *marks), axis=0)
-            spots = [here.shard ^ (2 * k) for k in range(4)]
-            mates = self.mates + [here.mate(corner)]
-            whole = place(self.parts + [corner] + mates, spots + [spot ^ 1 for spot in spots], self.cuts)
-        return [w.reshape(-1, w.shape[2]) for w in whole]
+    return [f.reshape(-1, f.shape[2]) for f in full]
+
+
+def gather_cut(here, local, cuts, mark):
+    if here.shards != 8:
+        full = lax.all_gather(local, "fsdp", axis=0, tiled=True)
+        return [full[:, col : col + cols] for col, cols in cuts]
+    rows = local.shape[0]
+    middle = rows // 2
+    across_x, across_y = here.aside(local, 1), here.aside(local, 2)
+    across_x, across_y = after((across_x, across_y), mark)
+    low, high = here.aside(across_x[:middle], 2), here.aside(across_y[middle:], 1)
+    parts = [local, across_x, across_y, low, high]
+    spots = [here.shard ^ (2 * k) for k in (0, 1, 2, 3, 3)]
+    parts, spots = parts + [here.mate(part) for part in parts], spots + [spot ^ 1 for spot in spots]
+    return place(parts, spots, [0, 0, 0, 0, middle] * 2, rows, cuts)
+
+
+def pack_kernel(mix_ref, merge_ref, columns_ref, out_ref, *, size, parts):
+    rows, width = merge_ref.shape
+    per = LANES // size
+    lane_low = lane_of(rows) < size
+    pairs = width // LANES // parts
+    for pair in range(width // LANES):
+        part, spot = pair // pairs, pair % pairs
+        for j in range(3):
+            one, two = [((3 * (per * pair + k) + j) * size) // LANES * LANES for k in range(2)]
+            one, two = mix_ref[:, one : one + LANES].astype(jnp.float32), mix_ref[:, two : two + LANES].astype(jnp.float32)
+            if j % 2:
+                joined = pltpu.roll(jnp.where(lane_low, two, one), size, 1)
+            else:
+                joined = jnp.where(lane_low, one, two)
+            at = (part * 3 + j) * pairs * LANES + spot * LANES
+            out_ref[:, at : at + LANES] = joined.astype(out_ref.dtype)
+    out_ref[:, 3 * width : 4 * width] = merge_ref[...]
+    out_ref[:, 4 * width :] = columns_ref[...]
+
+
+def pack(mix, merge, columns, size, parts):
+    rows, width = merge.shape
+    return pl.pallas_call(
+        functools.partial(pack_kernel, size=size, parts=parts),
+        out_shape=jax.ShapeDtypeStruct((rows, 4 * width + LANES), mix.dtype),
+        name="pack_projection",
+    )(mix, merge, columns)
 
 
 def share_pair(here, partial):
@@ -558,31 +602,30 @@
     rows = here.columns * half
     length = here.columns * piece
 
-    def sequence(values):
-        return from_sequence_send(here, to_sequence_parts(here, values))
+    def send(parts):
+        return [straight(part) for part in from_sequence_send(here, parts)]
 
     ups = hidden_size // width
     part_width = width // PARTS
     token_parts = to_sequence_parts(here, tokens)
-    flat = jnp.concatenate(from_sequence_send(here, token_parts), axis=0)
+    token_slots = send(token_parts)
 
     vectors = (query_bias, value_bias, merge_bias, first_gain, first_shift, down_bias, second_gain, second_shift)
-    lines = jnp.concatenate([jnp.stack(vectors), up_bias.reshape(ups, own)], axis=0)
+    local_weights = after((vectors, up_bias, mix_weight, merge_weight), token_parts)
+    lines = jnp.concatenate([jnp.stack(local_weights[0]), local_weights[1].reshape(ups, own)], axis=0)
     columns = jnp.pad(lines, ((0, LANES - lines.shape[0]), (0, 0))).T
-    mix_local = mix_weight.reshape(own, PARTS, H // PARTS, 3, HD).transpose(0, 1, 3, 2, 4).reshape(own, 3 * width)
-    mix_local = jnp.concatenate([mix_local, columns], axis=1)
-    mix_cuts = [(0, own, p * width, width, p, 0) for p in range(PARTS)] + [(0, own, 3 * width, LANES, PARTS, 0)]
-    mix_gather = Gather(here, after(mix_local, token_parts), mix_cuts)
-    mix_gather.corner()
-    *mix_parts, columns_full = mix_gather.finish()
+    mix_local = pack(local_weights[2], local_weights[3], columns, HD, PARTS)
+    *mix_parts, merge_full, columns_full = gather_cut(
+        here, mix_local, [(p * width, width) for p in range(PARTS + 1)] + [(4 * width, LANES)], token_slots[2]
+    )
     lines_full = columns_full.T.astype(f32)
     query_full, value_full, merge_bias_full, gain_one, shift_one, down_bias_full, gain_two, shift_two = [
         lines_full[j] for j in range(8)
     ]
     up_bias_full = lines_full[8 : 8 + ups].reshape(ups, shards, own).transpose(1, 0, 2).reshape(-1)
 
-    ids_local = after(segment_ids, token_parts).reshape(groups, piece, 1)
-    ids_own = jnp.concatenate(sequence(ids_local), axis=0).reshape(here.columns, half)
+    ids_parts = to_sequence_parts(here, after(segment_ids, token_parts).reshape(groups, piece, 1))
+    ids_own = jnp.concatenate(send(ids_parts), axis=0).reshape(here.columns, half)
     ids_mate = here.mate(ids_own)
     by_core = jnp.stack([jnp.where(here.core == 0, ids_own, ids_mate), jnp.where(here.core == 0, ids_mate, ids_own)], axis=1)
     ids = jnp.stack([pick(by_core, k ^ here.column) for k in range(here.columns)]).reshape(2 * here.columns, half)
@@ -593,13 +636,20 @@
     key_ext = key_extension(ids.reshape(length))
     query_ext = query_extension(ids_own.reshape(rows))
 
-    packed = jnp.concatenate(
-        [merge_weight] + [up_weight[:, j * width : (j + 1) * width] for j in range(ups)] + [down_weight], axis=0
+    cotangent_parts = to_sequence_parts(here, after(output_grad, token_parts))
+    ready = (cotangent_parts, mix_parts, merge_full, lines_full, info, key_ext, query_ext)
+    token_slots, (cotangent_parts, mix_parts, merge_full, lines_full, info, key_ext, query_ext) = lax.optimization_barrier(
+        (token_slots, ready)
     )
-    cuts = [(0, own, 0, width, 0, 0)] + [((1 + j) * own, own, 0, width, 1, j * width) for j in range(ups)]
-    cuts.append(((1 + ups) * own, ups * own, 0, width, 2, 0))
-    weight_gather = Gather(here, after(packed, flat), cuts)
-    cotangent_slots = sequence(after(output_grad, flat))
+    flat = straight(jnp.concatenate(token_slots, axis=0))
+    cotangent_slots = send(after(cotangent_parts, flat))
+    direct = shards == 8
+    up_local, down_local = after((up_weight, down_weight), mix_parts[0])
+    if direct:
+        up_parts = [up_local, here.aside(up_local, 1), here.aside(up_local, 2)]
+        down_parts = [down_local, here.aside(down_local, 1), here.aside(down_local, 2)]
+    else:
+        up_full, down_full = [lax.all_gather(w, "fsdp", axis=0, tiled=True) for w in (up_local, down_local)]
 
     column_scale = jnp.where(jnp.arange(width) < part_width, LOG2E / math.sqrt(HD), 1.0)
     mixed, mixed_mate = [], []
@@ -610,26 +660,37 @@
         mixed_mate.append(here.mate(mixed[p]))
 
     contexts, exts = [], []
+    plan, spots = NOTHING, ()
     for p in range(PARTS):
         if p:
             mixed[p], mixed_mate[p] = after((mixed[p], mixed_mate[p]), contexts[-1])
-        if p == 1:
-            weight_gather.corner(contexts[-1])
-        context, ext = attention_forward(info, mixed[p], mixed_mate[p], query_ext, key_ext, HD)
+        if p == 1 and direct:
+            up_parts, down_parts = after((up_parts, down_parts), contexts[-1])
+            up_parts.append(here.aside(up_parts[1], 2))
+            down_parts.append(here.aside(down_parts[2], 1))
+            mates = [[here.mate(w) for w in parts] for parts in (up_parts, down_parts)]
+        if p == PARTS - 1:
+            mixed[p], cotangent_slots = after((mixed[p], cotangent_slots), cotangent_slots)
+            if direct:
+                pieces = up_parts + mates[0] + down_parts + mates[1]
+                outs = [(shards,) + up_weight.shape, (shards,) + down_weight.shape]
+                spots = [here.shard ^ (2 * k) for k in range(4)]
+                spots = (spots + [spot ^ 1 for spot in spots]) * 2
+                plan = (tuple(after(pieces, contexts[-1])), (0,) * 8 + (1,) * 8, tuple(outs))
+        context, ext, *placed = attention_forward(info, mixed[p], mixed_mate[p], query_ext, key_ext, HD, plan, spots)
         contexts.append(context)
         exts.append(ext)
+    if direct:
+        up_full, down_full = [full.reshape(-1, full.shape[2]) for full in placed]
     context = jnp.concatenate(contexts, axis=1)
-
     cotangent = jnp.concatenate(after(cotangent_slots, contexts[-1]), axis=0).astype(f32)
-    merge_full, up_full, down_full = weight_gather.finish(contexts[-2])
-    merge_full, up_full, down_full = after((merge_full, up_full, down_full), contexts[-1])
 
     attended = dot(context, merge_full) + merge_bias_full
     first_out, normed_one, factor_one = norm_forward(flat.astype(f32) + attended, gain_one, shift_one)
     first_low = first_out.astype(bf16)
     hidden = dot(first_low, up_full) + up_bias_full
     active, slope = gelu_parts(hidden)
-    active_low = active.astype(bf16)
+    active_low, slope_low = lax.optimization_barrier((active.astype(bf16), slope.astype(bf16)))
     branch = dot(active_low, down_full) + down_bias_full
     result, normed_two, factor_two = norm_forward(first_out + branch, gain_two, shift_two)
     output_slots = from_sequence_send(here, list(result.astype(bf16).reshape(here.columns, half, width)))
@@ -640,7 +701,7 @@
     down_kept, down_other = share_pair(here, down_grad.reshape(shards, -1, width))
     down_bias_grad = column_sums(grad_branch)
     grad_active = dot(grad_branch, down_full.T)
-    grad_hidden = (grad_active * slope).astype(bf16)
+    grad_hidden = (grad_active * slope_low.astype(f32)).astype(bf16)
     down_share, down_others = share_plane(here, down_kept, after(down_other, grad_hidden))
     up_grad = dot(first_low.T, grad_hidden)
     up_bias_grad = column_sums(grad_hidden)
@@ -665,13 +726,13 @@
         kv = (kept + other.astype(f32)).astype(bf16)
         return jnp.concatenate([dq, kv[0], kv[1]], axis=1)
 
-    one = backward(0, after(grad_context, down_share, up_share))
-    down_others, down_share = after((down_others, down_share), one[0])
     down_half, down_other = column_first(here, share_sum(down_share, down_others))
+    one = backward(0, after(grad_context, down_half, up_share, output_slots))
+    down_half, down_other = column_second(here, *after((down_half, down_other), one[0]))
     up_others, up_share = after((up_others, up_share), one[0])
     up_half, up_other = column_first(here, share_sum(up_share, up_others))
     two = backward(1, after(grad_context, down_half, up_half))
-    down_half, down_other = column_second(here, *after((down_half, down_other), two[0]))
+    down_half, down_other = column_third(here, *after((down_half, down_other), two[0]))
     up_half, up_other = column_second(here, *after((up_half, up_other), two[0]))
     mixed_one = mixed_part(after(one, two[0]))
     mix_grad_one = dot(flat.T, mixed_one)
@@ -679,15 +740,18 @@
     input_part = grad_sum + dot(mixed_one, mix_parts[0].T)
     mix_share_one, mix_others_one = share_plane(here, mix_kept_one, after(mix_other_one, input_part))
     three = backward(2, after(grad_context, down_half, up_half, mix_share_one))
-    down_half, down_other = column_third(here, *after((down_half, down_other), three[0]))
+    down_half, down_other = after((down_half, down_other), three[0])
     up_half, up_other = column_third(here, *after((up_half, up_other), three[0]))
     mixed_two = mixed_part(after(two, three[0]))
+    mix_grad_two = dot(flat.T, mixed_two)
+    mix_kept_two, mix_other_two = share_pair(here, mix_grad_two.reshape(shards, own, -1))
     input_part = input_part + dot(mixed_two, mix_parts[1].T)
-    mixed_three = mixed_part(after(three, input_part))
+    mixed_three = mixed_part(after(three, input_part, mix_kept_two))
     input_low = (input_part + dot(mixed_three, mix_parts[2].T)).astype(bf16)
     input_slots = from_sequence_send(here, list(input_low.reshape(here.columns, half, width)))
-    mixed_rest = after(jnp.concatenate([mixed_two, mixed_three], axis=1), input_low)
-    mix_grad_rest = dot(flat.T, mixed_rest)
+    mixed_three, mix_other_two, down_other, up_other = after((mixed_three, mix_other_two, down_other, up_other), input_low)
+    mix_share_two, mix_others_two = share_plane(here, mix_kept_two, mix_other_two)
+    mix_grad_rest = dot(flat.T, mixed_three)
 
     sums = [column_sums(m) for m in (mixed_one, mixed_two, mixed_three)]
     query_grad = jnp.concatenate([s[:part_width] for s in sums])
@@ -707,11 +771,18 @@
     columns_grad = jnp.pad(lines_grad, ((0, LANES - lines_grad.shape[0]), (0, 0))).T
     rest = jnp.concatenate([mix_grad_rest, columns_grad], axis=1).reshape(shards, own, -1)
     rest_kept, rest_other = share_pair(here, rest)
-    rest_share, rest_others = share_plane(here, rest_kept, rest_other)
-    mix_share = jnp.concatenate([share_sum(mix_share_one, mix_others_one), share_sum(rest_share, rest_others)], axis=1)
+    rest_share, rest_others = share_plane(here, rest_kept, after(rest_other, input_slots[1]))
+    mix_share = jnp.concatenate(
+        [
+            share_sum(mix_share_one, mix_others_one),
+            share_sum(mix_share_two, mix_others_two),
+            share_sum(rest_share, rest_others),
+        ],
+        axis=1,
+    )
     mix_last = column_last(here, *column_third(here, *column_second(here, *column_first(here, mix_share))))
 
-    output = from_sequence_end(here, after(output_slots, three[0]), groups)
+    output = from_sequence_end(here, after(output_slots, input_low), groups)
     final_input = from_sequence_end(here, input_slots, groups).astype(f32)
     final_down = column_last(here, down_half, down_other).astype(f32)
     final_up_merge = column_last(here, up_half, up_other).astype(f32)

time: 586 us -> 861 us (1.47)
  Pallas kernels: 171 us -> 425 us
  starting transfers between devices: 103 us -> 142 us
  local copies, waits for them, and re-layouts: 68.2 us -> 40.7 us
  waiting for transfers between devices: 89.5 us -> 110 us
  matrix products: 95.6 us -> 78.6 us
    pallas_call x5, Pallas kernels: 74.9 us -> 337 us  [the longest x3 330 us: attention_forward(): pl.pallas_call(functools.partial(forward_kernel, size=size, plan=(moves,...]
    ppermute x20 -> x25, starting transfers between devices: 23.7 us -> 67.1 us  [aside(): return lax.ppermute(values, 'fsdp', xor_pairs(self.shards, 2 * bits))]
    ppermute x20 -> x25, waiting for transfers between devices: 25 us -> 47 us  [aside(): return lax.ppermute(values, 'fsdp', xor_pairs(self.shards, 2 * bits))]
    unnamed x201 -> x165, local copies, waits for them, and re-layouts: 32.1 us -> 11.7 us
    dot_general x17 -> x18, matrix products: 95.6 us -> 78.6 us  [dot(): return jnp.dot(a, b, preferred_element_type=f32)]
    ppermute x24 -> x30, starting transfers between devices: 27.7 us -> 15.3 us  [mate(): return lax.ppermute(values, 'fsdp', xor_pairs(self.shards, 1))]
    pallas_call x3, Pallas kernels: 96.4 us -> 87.6 us  [attention_backward(): pl.pallas_call(functools.partial(backward_kernel, size=size), grid_spec=p...]
  transfers between devices with their start and end apart: 68 -> 79, of which waited for: 18 -> 30; matrix products, arithmetic and copies ran while one was open for 22% -> 10% of each run, Pallas kernels for 28% -> 15%
where the time goes in v4:
time: 861 us; the launch traced here: 853 us
  Pallas kernels  425 us (49%)
  starting transfers between devices  142 us (16%)
  waiting for transfers between devices  110 us (13%)
  matrix products  78.6 us (9%)
  other arithmetic  53.7 us (6%)
  local copies, waits for them, and re-layouts  40.7 us (5%)
    pallas_call x3, Pallas kernels, attention_forward(): pl.pallas_call(functools.partial(forward_kernel, size=size, plan=(moves,...  330 us
    pallas_call x3, Pallas kernels, attention_backward(): pl.pallas_call(functools.partial(backward_kernel, size=size), grid_spec=p...  87.6 us
    dot_general x18, matrix products, dot(): return jnp.dot(a, b, preferred_element_type=f32)  78.6 us
    ppermute x25, starting transfers between devices, aside(): return lax.ppermute(values, 'fsdp', xor_pairs(self.shards, 2 * bits))  67.1 us
    ppermute x24, waiting for transfers between devices, across(): return lax.ppermute(values, 'seq', xor_pairs(self.columns, bits))  60.9 us
    ppermute x24, starting transfers between devices, across(): return lax.ppermute(values, 'seq', xor_pairs(self.columns, bits))  59.8 us
    ppermute x25, waiting for transfers between devices, aside(): return lax.ppermute(values, 'fsdp', xor_pairs(self.shards, 2 * bits))  47 us
  transfers between devices with their start and end apart: 79, of which 30 were waited for; matrix products, arithmetic and copies ran while one was open for 10% of the time, Pallas kernels for 15%

profile of v4, /device:TPU:0, one launch (start us, length us, event | category | flops | bytes accessed | tf_op | source)
XLA Modules:
  0.0 852.9 jit_solution(16120953919002359342)
XLA Ops:
  6.7 2.0 pack_projection.1.refs_0_
  8.8 2.8 collective-permute-start.5
  15.0 3.7 collective-permute-start.17
  19.4 2.4 dynamic-slice_bitcast_fusion.1
  23.3 6.3 collective-permute-start.2
  29.7 9.6 %collective-permute-done.16 = s32[256,1]{1,0:T(8,128)S(1)} collective-permute-done((s32[256,1]{1,0:T(8,128)S(1)}, s32[256,1]{1,0:T(8,128)S(1)}, u32[]{:S(2)}, u32[]{:S(2)}) %collective-permute-start.16) | collective-permute-done | bytes 1056 | tf_op jit(solution)/shard_map/ppermute | solution.py:408
  53.5 6.8 collective-permute-done.7.refs_3_
  62.7 2.6 collective-permute-start.3
  65.3 5.2 place_parts.1
  71.7 2.6 collective-permute-done.1
  74.3 9.3 %collective-permute-done.3 = bf16[256,768]{1,0:T(8,128)(2,1)S(1)} collective-permute-done((bf16[256,768]{1,0:T(8,128)(2,1)}, bf16[256,768]{1,0:T(8,128)(2,1)S(1)}, u32[]{:S(2)}, u32[]{:S(2)}) %collective-permute-start.3) | collective-permute-done | bytes 393248 | tf_op jit(solution)/shard_map/ppermute | solution.py:408
  85.8 2.5 multiply_convert_fusion.2.q_ref.k_own.v_own
  91.9 6.8 collective-permute-done.25.refs_1_
  101.0 11.8 %collective-permute-done.27.refs_9_ = bf16[384,768]{1,0:T(8,128)(2,1)S(1)} collective-permute-done((bf16[384,768]{1,0:T(8,128)(2,1)S(1)}, bf16[384,768]{1,0:T(8,128)(2,1)S(1)}, u32[]{:S(2)}, u32[]{:S(2)}) %collective-permute-start.27) | collective-permute-done | bytes 589856 | tf_op jit(solution)/shard_map/ppermute | solution.py:411
  115.5 2.8 collective-permute-start.24
  118.4 18.9 %attention_forward.3 = (bf16[1024,256]{1,0:T(8,128)(2,1)}, bf16[1024,256]{1,0:T(8,128)(2,1)}) custom-call(s32[10]{0:T(128)} %pad_add_fusion.3.info, bf16[1024,768]{1,0:T(8,128)(2,1)} %copy-done.2, bf16[1024,768]{1,0:T(8,128)(2,1)} %copy-done.2, bf16[1024,768]{1,0:T(8,128)(2,1)} %copy-done.3, bf16[1024,768]{1,0:T(8,128)(2,1)} %copy-done.2, ...), custom_call_target="tpu_custom_call" | custom-call | flops 1073741824 | bytes 4194304 | tf_op jit(solution)/shard_map/attention_forward/pallas_call | solution.py:162
  137.3 3.6 collective-permute-start.29
  140.9 2.2 collective-permute-done.23
  145.0 8.8 %collective-permute-done.29.refs_3_ = bf16[96,3072]{1,0:T(8,128)(2,1)} collective-permute-done((bf16[96,3072]{1,0:T(8,128)(2,1)}, bf16[96,3072]{1,0:T(8,128)(2,1)}, u32[]{:S(2)}, u32[]{:S(2)}) %collective-permute-start.29) | collective-permute-done | bytes 589856 | tf_op jit(solution)/shard_map/ppermute | solution.py:411
  156.0 3.6 collective-permute-done.34.refs_11_
  160.6 18.9 %attention_forward.4 = (bf16[1024,256]{1,0:T(8,128)(2,1)}, bf16[1024,256]{1,0:T(8,128)(2,1)}) custom-call(s32[10]{0:T(128)} %pad_add_fusion.3.info, bf16[1024,768]{1,0:T(8,128)(2,1)} %copy-done.1, bf16[1024,768]{1,0:T(8,128)(2,1)} %copy-done.1, bf16[1024,768]{1,0:T(8,128)(2,1)} %collective-permute-done.20.k_mate.v_mate, bf16[1024,768]{1,0:T(8,128)(2,1)} %copy-done.1, ...), custom_call_target="tpu_custom_call" | custom-call | flops 1073741824 | bytes 4194304 | tf_op jit(solution)/shard_map/attention_forward/pallas_call | solution.py:162
  182.5 291.9 %attention_forward.5 = (bf16[1024,256]{1,0:T(8,128)(2,1)}, bf16[1024,256]{1,0:T(8,128)(2,1)}, bf16[8,96,3072]{2,1,0:T(8,128)(2,1)}, bf16[8,384,768]{2,1,0:T(8,128)(2,1)}) custom-call(s32[26]{0:T(128)} %concatenate.83.info, bf16[1024,768]{1,0:T(8,128)(2,1)} %multiply_convert_fusion.2.q_ref.k_own.v_own, ...), custom_call_target="tpu_custom_call" | custom-call | flops 1073741824 | bytes 4194304 | tf_op jit(solution)/shard_map/attention_forward/pallas_call | solution.py:162
  476.3 3.9 fusion.92
  480.9 13.9 %fusion.4 = (bf16[1024,3072]{1,0:T(8,128)(2,1)}, bf16[1024,3072]{1,0:T(8,128)(2,1)S(1)}) fusion(f32[3072]{0:T(1024)S(1)} %add.551, bf16[768,3072]{1,0:T(8,128)(2,1)S(1)} %bitcast.367, f32[1024,768]{1,0:T(8,128)S(1)} %get-tuple-element.475, f32[768]{0:T(1024)S(1)} %get-tuple-element.351, f32[768]{0:T(1024)S(1)} %get-tuple-element.352, ...), kind=kOutput, calls=%fused_computation.15 | convolution fusion | flops 4873519104 | bytes 20473856 | tf_op jit(solution)/shard_map/dot_general | solution.py:372
  494.8 5.5 fusion.93
  501.3 3.3 fusion.13
  504.6 4.0 convert_reduce_fusion.2
  508.5 7.8 fusion.76
  516.4 9.7 %convert_reduce_fusion = (f32[3072]{0:T(1024)}, bf16[1024,3072]{1,0:T(8,128)(2,1)S(1)}) fusion(bf16[1024,3072]{1,0:T(8,128)(2,1)} %get-tuple-element.230, bf16[3072,768]{1,0:T(8,128)(2,1)} %bitcast.368, f32[1024,768]{1,0:T(8,128)S(1)} %get-tuple-element.369), kind=kOutput, calls=%fused_computation.16 | convolution fusion | flops 4848350208 | bytes 20459520 | tf_op jit(solution)/shard_map/dot_general | solution.py:372
  526.1 9.0 %multiply_reduce_fusion = (f32[768]{0:T(1024)}, f32[1024]{0:T(1024)S(1)}, f32[1024]{0:T(1024)S(1)}, f32[768]{0:T(1024)}, f32[1024,768]{1,0:T(8,128)S(1)}) fusion(f32[1024,768]{1,0:T(8,128)S(1)} %get-tuple-element.475, f32[1024]{0:T(1024)S(1)} %add_rsqrt_fusion.1, f32[1024]{0:T(1024)S(1)} %broadcast_multiply_fusion.5, f32[768]{0:T(1024)S(1)} %get-tuple-element.352, ...), kind=kOutput, calls=%fused_computation.34 | convolution fusion | flops 4839698432 | bytes 20472832 | tf_op jit(solution)/shard_map/dot_general | solution.py:372
  535.0 5.6 fusion.81
  547.3 2.1 collective-permute-start.46
  549.3 4.0 fusion.16
  553.5 4.6 convolution_convert_fusion.do_ref
  558.3 3.0 fusion.34
  561.3 7.2 collective-permute-start.45
  569.3 7.1 collective-permute-start.39
  577.9 3.9 fusion.20
  581.8 11.9 %collective-permute-done.39 = bf16[256,768]{1,0:T(8,128)(2,1)S(1)} collective-permute-done((bf16[256,768]{1,0:T(8,128)(2,1)S(1)}, bf16[256,768]{1,0:T(8,128)(2,1)S(1)}, u32[]{:S(2)}, u32[]{:S(2)}) %collective-permute-start.39) | collective-permute-done | bytes 393248 | tf_op jit(solution)/shard_map/ppermute | solution.py:408
  601.0 5.5 collective-permute-start.48
  607.6 29.1 %attention_backward.3 = (bf16[1024,256]{1,0:T(8,128)(2,1)}, f32[2,1024,256]{2,1,0:T(8,128)}, bf16[2,1024,256]{2,1,0:T(8,128)(2,1)}) custom-call(s32[10]{0:T(128)} %pad_add_fusion.3.info, bf16[1024,768]{1,0:T(8,128)(2,1)} %copy-done.2, bf16[1024,256]{1,0:T(8,128)(2,1)} %get-tuple-element.231.ext_ref, bf16[1024,768]{1,0:T(8,128)(2,1)} %convolution_convert_fusion.do_ref, ...), custom_call_target="tpu_custom_call" | custom-call | flops 2684354560 | bytes 6291456 | tf_op jit(solution)/shard_map/attention_backward/pallas_call | solution.py:284
  636.7 2.1 collective-permute-start.47
  639.9 10.6 %collective-permute-start.53 = (bf16[192,768]{1,0:T(8,128)(2,1)S(1)}, bf16[192,768]{1,0:T(8,128)(2,1)}, u32[]{:S(2)}, u32[]{:S(2)}) collective-permute-start(bf16[192,768]{1,0:T(8,128)(2,1)S(1)} %add_convert_fusion.9), channel_id=1, source_target_pairs={{0,16},{8,24},{16,0},{24,8},{1,17},{9,25},{17,1},{25,9},{2,18},{10... | collective-permute-start | bytes 884744 | tf_op jit(solution)/shard_map/ppermute | solution.py:408
  652.9 29.3 %attention_backward.4 = (bf16[1024,256]{1,0:T(8,128)(2,1)}, f32[2,1024,256]{2,1,0:T(8,128)}, bf16[2,1024,256]{2,1,0:T(8,128)(2,1)}) custom-call(s32[10]{0:T(128)} %pad_add_fusion.3.info, bf16[1024,768]{1,0:T(8,128)(2,1)} %copy-done.1, bf16[1024,256]{1,0:T(8,128)(2,1)} %get-tuple-element.238.ext_ref, bf16[1024,768]{1,0:T(8,128)(2,1)} %convolution_convert_fusion.do_ref, ...), custom_call_target="tpu_custom_call" | custom-call | flops 2684354560 | bytes 6291456 | tf_op jit(solution)/shard_map/attention_backward/pallas_call | solution.py:284
  682.3 3.2 collective-permute-start.52
  687.2 2.0 collective-permute-start.66
  693.3 3.1 convolution_add_fusion.1
  697.2 14.8 %collective-permute-start.64 = (bf16[96,768]{1,0:T(8,128)(2,1)S(1)}, bf16[96,768]{1,0:T(8,128)(2,1)S(1)}, u32[]{:S(2)}, u32[]{:S(2)}) collective-permute-start(bf16[96,768]{1,0:T(8,128)(2,1)S(1)} %get-tuple-element.391), channel_id=1, source_target_pairs={{0,6},{1,7},{2,4},{3,5},{4,2},{5,3},{6,0},{7,1},{8,14},{9,15},{10,... | collective-permute-start | bytes 442376 | tf_op jit(solution)/shard_map/ppermute | solution.py:411
  712.0 3.0 collective-permute-start.63
  718.3 2.6 collective-permute-done.63
  723.5 29.3 %attention_backward.5 = (bf16[1024,256]{1,0:T(8,128)(2,1)}, f32[2,1024,256]{2,1,0:T(8,128)}, bf16[2,1024,256]{2,1,0:T(8,128)(2,1)}) custom-call(s32[10]{0:T(128)} %pad_add_fusion.3.info, bf16[1024,768]{1,0:T(8,128)(2,1)} %multiply_convert_fusion.2.q_ref.k_own.v_own, bf16[1024,256]{1,0:T(8,128)(2,1)} %get-tuple-element.252.ext_ref, ...), custom_call_target="tpu_custom_call" | custom-call | flops 2684354560 | bytes 6291456 | tf_op jit(solution)/shard_map/attention_backward/pallas_call | solution.py:284
  767.8 3.3 collective-permute-done.68
  771.4 2.9 fusion.94
  774.2 4.4 collective-permute-start.60
  781.5 2.4 copy.165
  787.0 8.5 collective-permute-start.71
  800.3 3.7 collective-permute-done.58
  804.0 8.9 %collective-permute-start.70 = (bf16[96,768]{1,0:T(8,128)(2,1)S(1)}, bf16[96,768]{1,0:T(8,128)(2,1)S(1)}, u32[]{:S(2)}, u32[]{:S(2)}) collective-permute-start(bf16[96,768]{1,0:T(8,128)(2,1)S(1)} %get-tuple-element.389), channel_id=1, source_target_pairs={{0,4},{1,5},{2,6},{3,7},{4,0},{5,1},{6,2},{7,3},{8,12},{9,13},{10,... | collective-permute-start | bytes 442376 | tf_op jit(solution)/shard_map/ppermute | solution.py:411
  816.5 2.9 collective-permute-start.74
  825.2 2.9 collective-permute-start.76
  828.3 3.8 collective-permute-done.76
  832.1 2.7 collective-permute-start.77
  836.2 6.4 collective-permute-done.77
  844.8 4.1 collective-permute-done.78
  (435 shorter events, 127.1 us)
Async XLA Ops:
  8.8 38.1 %collective-permute-start.5 = (bf16[96,3200]{1,0:T(8,128)(2,1)}, bf16[96,3200]{1,0:T(8,128)(2,1)}, u32[]{:S(2)}, u32[]{:S(2)}) collective-permute-start(bf16[96,3200]{1,0:T(8,128)(2,1)} %pack_projection.1.refs_0_), channel_id=1, source_target_pairs={{0,2},{1,3},{2,0},{3,1},{4,6},{5,7},{6,4},{7,5},{8,10},{9,11},{10,... | collective-permute-start | bytes 1843208 | tf_op jit(solution)/shard_map/ppermute | solution.py:411
  11.6 35.2 %collective-permute-start.6 = (bf16[96,3200]{1,0:T(8,128)(2,1)}, bf16[96,3200]{1,0:T(8,128)(2,1)}, u32[]{:S(2)}, u32[]{:S(2)}) collective-permute-start(bf16[96,3200]{1,0:T(8,128)(2,1)} %pack_projection.1.refs_0_), channel_id=1, source_target_pairs={{0,4},{1,5},{2,6},{3,7},{4,0},{5,1},{6,2},{7,3},{8,12},{9,13},{10,... | collective-permute-start | bytes 1843208 | tf_op jit(solution)/shard_map/ppermute | solution.py:411
  18.6 20.6 %collective-permute-start.16 = (s32[256,1]{1,0:T(8,128)S(1)}, s32[256,1]{1,0:T(8,128)S(1)}, u32[]{:S(2)}, u32[]{:S(2)}) collective-permute-start(s32[256,1]{1,0:T(8,128)S(1)} %get-tuple-element.449), channel_id=1, source_target_pairs={{0,16},{8,24},{16,0},{24,8},{1,17},{9,25},{17,1},{25,9},{2,18},{10... | collective-permute-start | bytes 3080 | tf_op jit(solution)/shard_map/ppermute | solution.py:408
  18.6 22.3 %collective-permute-start.15 = (s32[256,1]{1,0:T(8,128)S(1)}, s32[256,1]{1,0:T(8,128)}, u32[]{:S(2)}, u32[]{:S(2)}) collective-permute-start(s32[256,1]{1,0:T(8,128)S(1)} %get-tuple-element.450), channel_id=1, source_target_pairs={{0,8},{8,0},{16,24},{24,16},{1,9},{9,1},{17,25},{25,17},{2,10},{10... | collective-permute-start | bytes 3080 | tf_op jit(solution)/shard_map/ppermute | solution.py:408
  23.3 23.6 %collective-permute-start.2 = (bf16[256,768]{1,0:T(8,128)(2,1)S(1)}, bf16[256,768]{1,0:T(8,128)(2,1)S(1)}, u32[]{:S(2)}, u32[]{:S(2)}) collective-permute-start(bf16[256,768]{1,0:T(8,128)(2,1)S(1)} %get-tuple-element.421), channel_id=1, source_target_pairs={{0,16},{8,24},{16,0},{24,8},{1,17},{9,25},{17,1},{25,9},{2,18},{10... | collective-permute-start | bytes 1179656 | tf_op jit(solution)/shard_map/ppermute | solution.py:408
  39.9 11.5 %collective-permute-start.4 = (bf16[2,256,768]{2,1,0:T(8,128)(2,1)}, bf16[2,256,768]{2,1,0:T(8,128)(2,1)S(1)}, u32[]{:S(2)}, u32[]{:S(2)}) collective-permute-start(bf16[2,256,768]{2,1,0:T(8,128)(2,1)} %get-tuple-element.419), channel_id=1, source_target_pairs={{0,1},{1,0},{2,3},{3,2},{4,5},{5,4},{6,7},{7,6},{8,9},{9,8},{10,11... | collective-permute-start | bytes 2359304 | tf_op jit(solution)/shard_map/ppermute | solution.py:405
  44.8 17.9 %collective-permute-start.9 = (bf16[96,3200]{1,0:T(8,128)(2,1)S(1)}, bf16[96,3200]{1,0:T(8,128)(2,1)}, u32[]{:S(2)}, u32[]{:S(2)}) collective-permute-start(bf16[96,3200]{1,0:T(8,128)(2,1)S(1)} %copy-done.9), channel_id=1, source_target_pairs={{0,1},{1,0},{2,3},{3,2},{4,5},{5,4},{6,7},{7,6},{8,9},{9,8},{10,11... | collective-permute-start | bytes 1843208 | tf_op jit(solution)/shard_map/ppermute | solution.py:405
  48.7 14.0 %collective-permute-start.10 = (bf16[96,3200]{1,0:T(8,128)(2,1)}, bf16[96,3200]{1,0:T(8,128)(2,1)}, u32[]{:S(2)}, u32[]{:S(2)}) collective-permute-start(bf16[96,3200]{1,0:T(8,128)(2,1)} %collective-permute-done.5.refs_1_), channel_id=1, source_target_pairs={{0,1},{1,0},{2,3},{3,2},{4,5},{5,4},{6,7},{7,6},{8,9},{9,8},{10,11... | collective-permute-start | bytes 1843208 | tf_op jit(solution)/shard_map/ppermute | solution.py:405
  50.4 14.9 %collective-permute-start.11 = (bf16[96,3200]{1,0:T(8,128)(2,1)}, bf16[96,3200]{1,0:T(8,128)(2,1)}, u32[]{:S(2)}, u32[]{:S(2)}) collective-permute-start(bf16[96,3200]{1,0:T(8,128)(2,1)} %collective-permute-done.6.refs_2_), channel_id=1, source_target_pairs={{0,1},{1,0},{2,3},{3,2},{4,5},{5,4},{6,7},{7,6},{8,9},{9,8},{10,11... | collective-permute-start | bytes 1843208 | tf_op jit(solution)/shard_map/ppermute | solution.py:405
  50.9 9.4 %collective-permute-start.7 = (bf16[48,3200]{1,0:T(8,128)(2,1)}, bf16[48,3200]{1,0:T(8,128)(2,1)S(1)}, u32[]{:S(2)}, u32[]{:S(2)}) collective-permute-start(bf16[48,3200]{1,0:T(8,128)(2,1)} %slice.166), channel_id=1, source_target_pairs={{0,4},{1,5},{2,6},{3,7},{4,0},{5,1},{6,2},{7,3},{8,12},{9,13},{10,... | collective-permute-start | bytes 921608 | tf_op jit(solution)/shard_map/ppermute | solution.py:411
  51.4 9.2 %collective-permute-start.8 = (bf16[48,3200]{1,0:T(8,128)(2,1)}, bf16[48,3200]{1,0:T(8,128)(2,1)}, u32[]{:S(2)}, u32[]{:S(2)}) collective-permute-start(bf16[48,3200]{1,0:T(8,128)(2,1)} %slice.167), channel_id=1, source_target_pairs={{0,2},{1,3},{2,0},{3,1},{4,6},{5,7},{6,4},{7,5},{8,10},{9,11},{10,... | collective-permute-start | bytes 921608 | tf_op jit(solution)/shard_map/ppermute | solution.py:411
  62.7 11.6 %collective-permute-start.1 = (bf16[256,768]{1,0:T(8,128)(2,1)}, bf16[256,768]{1,0:T(8,128)(2,1)S(1)}, u32[]{:S(2)}, u32[]{:S(2)}) collective-permute-start(bf16[256,768]{1,0:T(8,128)(2,1)} %get-tuple-element.422), channel_id=1, source_target_pairs={{0,8},{8,0},{16,24},{24,16},{1,9},{9,1},{17,25},{25,17},{2,10},{10... | collective-permute-start | bytes 1179656 | tf_op jit(solution)/shard_map/ppermute | solution.py:408
  62.7 20.8 %collective-permute-start.3 = (bf16[256,768]{1,0:T(8,128)(2,1)}, bf16[256,768]{1,0:T(8,128)(2,1)S(1)}, u32[]{:S(2)}, u32[]{:S(2)}) collective-permute-start(bf16[256,768]{1,0:T(8,128)(2,1)} %get-tuple-element.420), channel_id=1, source_target_pairs={{0,24},{8,16},{16,8},{24,0},{1,25},{9,17},{17,9},{25,1},{2,26},{10... | collective-permute-start | bytes 1179656 | tf_op jit(solution)/shard_map/ppermute | solution.py:408
  83.6 15.1 %collective-permute-start.25 = (bf16[96,3072]{1,0:T(8,128)(2,1)}, bf16[96,3072]{1,0:T(8,128)(2,1)S(1)}, u32[]{:S(2)}, u32[]{:S(2)}) collective-permute-start(bf16[96,3072]{1,0:T(8,128)(2,1)} %refs_0_), channel_id=1, source_target_pairs={{0,2},{1,3},{2,0},{3,1},{4,6},{5,7},{6,4},{7,5},{8,10},{9,11},{10,... | collective-permute-start | bytes 1769480 | tf_op jit(solution)/shard_map/ppermute | solution.py:411
  84.1 15.1 %collective-permute-start.26 = (bf16[96,3072]{1,0:T(8,128)(2,1)}, bf16[96,3072]{1,0:T(8,128)(2,1)S(1)}, u32[]{:S(2)}, u32[]{:S(2)}) collective-permute-start(bf16[96,3072]{1,0:T(8,128)(2,1)} %refs_0_), channel_id=1, source_target_pairs={{0,4},{1,5},{2,6},{3,7},{4,0},{5,1},{6,2},{7,3},{8,12},{9,13},{10,... | collective-permute-start | bytes 1769480 | tf_op jit(solution)/shard_map/ppermute | solution.py:411
  88.4 55.3 %collective-permute-start.21 = (bf16[1024,768]{1,0:T(8,128)(2,1)}, bf16[1024,768]{1,0:T(8,128)(2,1)}, u32[]{:S(2)}, u32[]{:S(2)}) collective-permute-start(bf16[1024,768]{1,0:T(8,128)(2,1)} %multiply_convert_fusion.2.q_ref.k_own.v_own), channel_id=1, source_target_pairs={{0,1},{1,0},{2,3},{3,2},{4,5},{5,4},{6,7},{7,6},{8,9},{9,8},{10,11... | collective-permute-start | bytes 4718600 | tf_op jit(solution)/shard_map/ppermute | solution.py:405
  89.8 24.5 %collective-permute-start.19 = (bf16[1024,768]{1,0:T(8,128)(2,1)S(1)}, bf16[1024,768]{1,0:T(8,128)(2,1)S(1)}, u32[]{:S(2)}, u32[]{:S(2)}) collective-permute-start(bf16[1024,768]{1,0:T(8,128)(2,1)S(1)} %multiply_convert_fusion.4.q_ref.k_own.v_own), channel_id=1, source_target_pairs={{0,1},{1,0},{2,3},{3,2},{4,5},{5,4},{6,7},{7,6},{8,9},{9,8},{10,11... | collective-permute-start | bytes 4718600 | tf_op jit(solution)/shard_map/ppermute | solution.py:405
  91.8 51.9 %collective-permute-start.20 = (bf16[1024,768]{1,0:T(8,128)(2,1)S(1)}, bf16[1024,768]{1,0:T(8,128)(2,1)}, u32[]{:S(2)}, u32[]{:S(2)}) collective-permute-start(bf16[1024,768]{1,0:T(8,128)(2,1)S(1)} %multiply_convert_fusion.3.q_ref.k_own.v_own), channel_id=1, source_target_pairs={{0,1},{1,0},{2,3},{3,2},{4,5},{5,4},{6,7},{7,6},{8,9},{9,8},{10,11... | collective-permute-start | bytes 4718600 | tf_op jit(solution)/shard_map/ppermute | solution.py:405
  98.7 14.1 %collective-permute-start.27 = (bf16[384,768]{1,0:T(8,128)(2,1)S(1)}, bf16[384,768]{1,0:T(8,128)(2,1)S(1)}, u32[]{:S(2)}, u32[]{:S(2)}) collective-permute-start(bf16[384,768]{1,0:T(8,128)(2,1)S(1)} %copy-done.21), channel_id=1, source_target_pairs={{0,2},{1,3},{2,0},{3,1},{4,6},{5,7},{6,4},{7,5},{8,10},{9,11},{10,... | collective-permute-start | bytes 1769480 | tf_op jit(solution)/shard_map/ppermute | solution.py:411
  99.3 13.9 %collective-permute-start.28 = (bf16[384,768]{1,0:T(8,128)(2,1)S(1)}, bf16[384,768]{1,0:T(8,128)(2,1)S(1)}, u32[]{:S(2)}, u32[]{:S(2)}) collective-permute-start(bf16[384,768]{1,0:T(8,128)(2,1)S(1)} %copy-done.21), channel_id=1, source_target_pairs={{0,4},{1,5},{2,6},{3,7},{4,0},{5,1},{6,2},{7,3},{8,12},{9,13},{10,... | collective-permute-start | bytes 1769480 | tf_op jit(solution)/shard_map/ppermute | solution.py:411
  112.8 24.5 %collective-permute-start.22 = (bf16[256,768]{1,0:T(8,128)(2,1)}, bf16[256,768]{1,0:T(8,128)(2,1)S(1)}, u32[]{:S(2)}, u32[]{:S(2)}) collective-permute-start(bf16[256,768]{1,0:T(8,128)(2,1)} %get-tuple-element.188), channel_id=1, source_target_pairs={{0,8},{8,0},{16,24},{24,16},{1,9},{9,1},{17,25},{25,17},{2,10},{10... | collective-permute-start | bytes 1179656 | tf_op jit(solution)/shard_map/ppermute | solution.py:408
  113.2 29.9 %collective-permute-start.23 = (bf16[256,768]{1,0:T(8,128)(2,1)}, bf16[256,768]{1,0:T(8,128)(2,1)S(1)}, u32[]{:S(2)}, u32[]{:S(2)}) collective-permute-start(bf16[256,768]{1,0:T(8,128)(2,1)} %get-tuple-element.189), channel_id=1, source_target_pairs={{0,16},{8,24},{16,0},{24,8},{1,17},{9,25},{17,1},{25,9},{2,18},{10... | collective-permute-start | bytes 1179656 | tf_op jit(solution)/shard_map/ppermute | solution.py:408
  115.5 27.6 %collective-permute-start.24 = (bf16[256,768]{1,0:T(8,128)(2,1)}, bf16[256,768]{1,0:T(8,128)(2,1)S(1)}, u32[]{:S(2)}, u32[]{:S(2)}) collective-permute-start(bf16[256,768]{1,0:T(8,128)(2,1)} %get-tuple-element.190), channel_id=1, source_target_pairs={{0,24},{8,16},{16,8},{24,0},{1,25},{9,17},{17,9},{25,1},{2,26},{10... | collective-permute-start | bytes 1179656 | tf_op jit(solution)/shard_map/ppermute | solution.py:408
  137.3 16.5 %collective-permute-start.29 = (bf16[96,3072]{1,0:T(8,128)(2,1)}, bf16[96,3072]{1,0:T(8,128)(2,1)}, u32[]{:S(2)}, u32[]{:S(2)}) collective-permute-start(bf16[96,3072]{1,0:T(8,128)(2,1)} %copy-done.22), channel_id=1, source_target_pairs={{0,4},{1,5},{2,6},{3,7},{4,0},{5,1},{6,2},{7,3},{8,12},{9,13},{10,... | collective-permute-start | bytes 1769480 | tf_op jit(solution)/shard_map/ppermute | solution.py:411
  143.1 12.3 %collective-permute-start.30 = (bf16[96,3072]{1,0:T(8,128)(2,1)}, bf16[96,3072]{1,0:T(8,128)(2,1)}, u32[]{:S(2)}, u32[]{:S(2)}) collective-permute-start(bf16[96,3072]{1,0:T(8,128)(2,1)} %refs_0_), channel_id=1, source_target_pairs={{0,1},{1,0},{2,3},{3,2},{4,5},{5,4},{6,7},{7,6},{8,9},{9,8},{10,11... | collective-permute-start | bytes 1769480 | tf_op jit(solution)/shard_map/ppermute | solution.py:405
  143.1 12.3 %collective-permute-start.31 = (bf16[96,3072]{1,0:T(8,128)(2,1)}, bf16[96,3072]{1,0:T(8,128)(2,1)}, u32[]{:S(2)}, u32[]{:S(2)}) collective-permute-start(bf16[96,3072]{1,0:T(8,128)(2,1)} %copy-done.22), channel_id=1, source_target_pairs={{0,1},{1,0},{2,3},{3,2},{4,5},{5,4},{6,7},{7,6},{8,9},{9,8},{10,11... | collective-permute-start | bytes 1769480 | tf_op jit(solution)/shard_map/ppermute | solution.py:405
  143.7 12.3 %collective-permute-start.32 = (bf16[96,3072]{1,0:T(8,128)(2,1)}, bf16[96,3072]{1,0:T(8,128)(2,1)}, u32[]{:S(2)}, u32[]{:S(2)}) collective-permute-start(bf16[96,3072]{1,0:T(8,128)(2,1)} %copy-done.23), channel_id=1, source_target_pairs={{0,1},{1,0},{2,3},{3,2},{4,5},{5,4},{6,7},{7,6},{8,9},{9,8},{10,11... | collective-permute-start | bytes 1769480 | tf_op jit(solution)/shard_map/ppermute | solution.py:405
  143.7 15.9 %collective-permute-start.34 = (bf16[384,768]{1,0:T(8,128)(2,1)}, bf16[384,768]{1,0:T(8,128)(2,1)S(1)}, u32[]{:S(2)}, u32[]{:S(2)}) collective-permute-start(bf16[384,768]{1,0:T(8,128)(2,1)} %copy-done.25), channel_id=1, source_target_pairs={{0,2},{1,3},{2,0},{3,1},{4,6},{5,7},{6,4},{7,5},{8,10},{9,11},{10,... | collective-permute-start | bytes 1769480 | tf_op jit(solution)/shard_map/ppermute | solution.py:411
  153.8 26.8 %collective-permute-start.37 = (bf16[384,768]{1,0:T(8,128)(2,1)}, bf16[384,768]{1,0:T(8,128)(2,1)S(1)}, u32[]{:S(2)}, u32[]{:S(2)}) collective-permute-start(bf16[384,768]{1,0:T(8,128)(2,1)} %copy-done.25), channel_id=1, source_target_pairs={{0,1},{1,0},{2,3},{3,2},{4,5},{5,4},{6,7},{7,6},{8,9},{9,8},{10,11... | collective-permute-start | bytes 1769480 | tf_op jit(solution)/shard_map/ppermute | solution.py:405
  155.4 25.2 %collective-permute-start.35 = (bf16[384,768]{1,0:T(8,128)(2,1)}, bf16[384,768]{1,0:T(8,128)(2,1)}, u32[]{:S(2)}, u32[]{:S(2)}) collective-permute-start(bf16[384,768]{1,0:T(8,128)(2,1)} %refs_8_), channel_id=1, source_target_pairs={{0,1},{1,0},{2,3},{3,2},{4,5},{5,4},{6,7},{7,6},{8,9},{9,8},{10,11... | collective-permute-start | bytes 1769480 | tf_op jit(solution)/shard_map/ppermute | solution.py:405
  155.4 25.2 %collective-permute-start.36 = (bf16[384,768]{1,0:T(8,128)(2,1)}, bf16[384,768]{1,0:T(8,128)(2,1)}, u32[]{:S(2)}, u32[]{:S(2)}) collective-permute-start(bf16[384,768]{1,0:T(8,128)(2,1)} %copy-done.24), channel_id=1, source_target_pairs={{0,1},{1,0},{2,3},{3,2},{4,5},{5,4},{6,7},{7,6},{8,9},{9,8},{10,11... | collective-permute-start | bytes 1769480 | tf_op jit(solution)/shard_map/ppermute | solution.py:405
  155.9 25.8 %collective-permute-start.33 = (bf16[96,3072]{1,0:T(8,128)(2,1)}, bf16[96,3072]{1,0:T(8,128)(2,1)}, u32[]{:S(2)}, u32[]{:S(2)}) collective-permute-start(bf16[96,3072]{1,0:T(8,128)(2,1)} %collective-permute-done.29.refs_3_), channel_id=1, source_target_pairs={{0,1},{1,0},{2,3},{3,2},{4,5},{5,4},{6,7},{7,6},{8,9},{9,8},{10,11... | collective-permute-start | bytes 1769480 | tf_op jit(solution)/shard_map/ppermute | solution.py:405
  159.6 22.1 %collective-permute-start.38 = (bf16[384,768]{1,0:T(8,128)(2,1)S(1)}, bf16[384,768]{1,0:T(8,128)(2,1)}, u32[]{:S(2)}, u32[]{:S(2)}) collective-permute-start(bf16[384,768]{1,0:T(8,128)(2,1)S(1)} %collective-permute-done.34.refs_11_), channel_id=1, source_target_pairs={{0,1},{1,0},{2,3},{3,2},{4,5},{5,4},{6,7},{7,6},{8,9},{9,8},{10,11... | collective-permute-start | bytes 1769480 | tf_op jit(solution)/shard_map/ppermute | solution.py:405
  547.3 29.1 %collective-permute-start.46 = (bf16[4,96,3840]{2,1,0:T(8,128)(2,1)}, bf16[4,96,3840]{2,1,0:T(8,128)(2,1)}, u32[]{:S(2)}, u32[]{:S(2)}) collective-permute-start(bf16[4,96,3840]{2,1,0:T(8,128)(2,1)} %fusion.14), channel_id=1, source_target_pairs={{0,1},{1,0},{2,3},{3,2},{4,5},{5,4},{6,7},{7,6},{8,9},{9,8},{10,11... | collective-permute-start | bytes 8847368 | tf_op jit(solution)/shard_map/ppermute | solution.py:405
  561.3 33.7 %collective-permute-start.45 = (bf16[384,768]{1,0:T(8,128)(2,1)S(1)}, bf16[384,768]{1,0:T(8,128)(2,1)S(1)}, u32[]{:S(2)}, u32[]{:S(2)}) collective-permute-start(bf16[384,768]{1,0:T(8,128)(2,1)S(1)} %get-tuple-element.381), channel_id=1, source_target_pairs={{0,6},{1,7},{2,4},{3,5},{4,2},{5,3},{6,0},{7,1},{8,14},{9,15},{10,... | collective-permute-start | bytes 1769480 | tf_op jit(solution)/shard_map/ppermute | solution.py:411
  568.5 27.2 %collective-permute-start.44 = (bf16[384,768]{1,0:T(8,128)(2,1)S(1)}, bf16[384,768]{1,0:T(8,128)(2,1)S(1)}, u32[]{:S(2)}, u32[]{:S(2)}) collective-permute-start(bf16[384,768]{1,0:T(8,128)(2,1)S(1)} %get-tuple-element.382), channel_id=1, source_target_pairs={{0,4},{1,5},{2,6},{3,7},{4,0},{5,1},{6,2},{7,3},{8,12},{9,13},{10,... | collective-permute-start | bytes 1769480 | tf_op jit(solution)/shard_map/ppermute | solution.py:411
  568.5 29.0 %collective-permute-start.43 = (bf16[384,768]{1,0:T(8,128)(2,1)S(1)}, bf16[384,768]{1,0:T(8,128)(2,1)S(1)}, u32[]{:S(2)}, u32[]{:S(2)}) collective-permute-start(bf16[384,768]{1,0:T(8,128)(2,1)S(1)} %get-tuple-element.380), channel_id=1, source_target_pairs={{0,2},{1,3},{2,0},{3,1},{4,6},{5,7},{6,4},{7,5},{8,10},{9,11},{10,... | collective-permute-start | bytes 1769480 | tf_op jit(solution)/shard_map/ppermute | solution.py:411
  569.3 24.5 %collective-permute-start.39 = (bf16[256,768]{1,0:T(8,128)(2,1)S(1)}, bf16[256,768]{1,0:T(8,128)(2,1)S(1)}, u32[]{:S(2)}, u32[]{:S(2)}) collective-permute-start(bf16[256,768]{1,0:T(8,128)(2,1)S(1)} %get-tuple-element.412), channel_id=1, source_target_pairs={{0,8},{8,0},{16,24},{24,16},{1,9},{9,1},{17,25},{25,17},{2,10},{10... | collective-permute-start | bytes 1179656 | tf_op jit(solution)/shard_map/ppermute | solution.py:408
  576.4 24.7 %collective-permute-start.40 = (bf16[256,768]{1,0:T(8,128)(2,1)S(1)}, bf16[256,768]{1,0:T(8,128)(2,1)}, u32[]{:S(2)}, u32[]{:S(2)}) collective-permute-start(bf16[256,768]{1,0:T(8,128)(2,1)S(1)} %get-tuple-element.411), channel_id=1, source_target_pairs={{0,16},{8,24},{16,0},{24,8},{1,17},{9,25},{17,1},{25,9},{2,18},{10... | collective-permute-start | bytes 1179656 | tf_op jit(solution)/shard_map/ppermute | solution.py:408
  593.7 13.1 %collective-permute-start.41 = (bf16[256,768]{1,0:T(8,128)(2,1)S(1)}, bf16[256,768]{1,0:T(8,128)(2,1)S(1)}, u32[]{:S(2)}, u32[]{:S(2)}) collective-permute-start(bf16[256,768]{1,0:T(8,128)(2,1)S(1)} %get-tuple-element.410), channel_id=1, source_target_pairs={{0,24},{8,16},{16,8},{24,0},{1,25},{9,17},{17,9},{25,1},{2,26},{10... | collective-permute-start | bytes 1179656 | tf_op jit(solution)/shard_map/ppermute | solution.py:408
  595.0 55.5 %collective-permute-start.49 = (bf16[96,3840]{1,0:T(8,128)(2,1)}, bf16[96,3840]{1,0:T(8,128)(2,1)S(1)}, u32[]{:S(2)}, u32[]{:S(2)}) collective-permute-start(bf16[96,3840]{1,0:T(8,128)(2,1)} %get-tuple-element.376), channel_id=1, source_target_pairs={{0,2},{1,3},{2,0},{3,1},{4,6},{5,7},{6,4},{7,5},{8,10},{9,11},{10,... | collective-permute-start | bytes 2211848 | tf_op jit(solution)/shard_map/ppermute | solution.py:411
  595.7 54.7 %collective-permute-start.50 = (bf16[96,3840]{1,0:T(8,128)(2,1)}, bf16[96,3840]{1,0:T(8,128)(2,1)}, u32[]{:S(2)}, u32[]{:S(2)}) collective-permute-start(bf16[96,3840]{1,0:T(8,128)(2,1)} %get-tuple-element.377), channel_id=1, source_target_pairs={{0,4},{1,5},{2,6},{3,7},{4,0},{5,1},{6,2},{7,3},{8,12},{9,13},{10,... | collective-permute-start | bytes 2211848 | tf_op jit(solution)/shard_map/ppermute | solution.py:411
  597.5 53.0 %collective-permute-start.51 = (bf16[96,3840]{1,0:T(8,128)(2,1)}, bf16[96,3840]{1,0:T(8,128)(2,1)}, u32[]{:S(2)}, u32[]{:S(2)}) collective-permute-start(bf16[96,3840]{1,0:T(8,128)(2,1)} %get-tuple-element.374), channel_id=1, source_target_pairs={{0,6},{1,7},{2,4},{3,5},{4,2},{5,3},{6,0},{7,1},{8,14},{9,15},{10,... | collective-permute-start | bytes 2211848 | tf_op jit(solution)/shard_map/ppermute | solution.py:411
  601.0 37.8 %collective-permute-start.48 = (bf16[192,768]{1,0:T(8,128)(2,1)}, bf16[192,768]{1,0:T(8,128)(2,1)}, u32[]{:S(2)}, u32[]{:S(2)}) collective-permute-start(bf16[192,768]{1,0:T(8,128)(2,1)} %get-tuple-element.438), channel_id=1, source_target_pairs={{0,8},{8,0},{16,24},{24,16},{1,9},{9,1},{17,25},{25,17},{2,10},{10... | collective-permute-start | bytes 884744 | tf_op jit(solution)/shard_map/ppermute | solution.py:408
  636.7 52.5 %collective-permute-start.47 = (bf16[2,1024,256]{2,1,0:T(8,128)(2,1)}, bf16[2,1024,256]{2,1,0:T(8,128)(2,1)}, u32[]{:S(2)}, u32[]{:S(2)}) collective-permute-start(bf16[2,1024,256]{2,1,0:T(8,128)(2,1)} %get-tuple-element.237), channel_id=1, source_target_pairs={{0,1},{1,0},{2,3},{3,2},{4,5},{5,4},{6,7},{7,6},{8,9},{9,8},{10,11... | collective-permute-start | bytes 3145736 | tf_op jit(solution)/shard_map/ppermute | solution.py:405
  639.9 45.6 %collective-permute-start.53 = (bf16[192,768]{1,0:T(8,128)(2,1)S(1)}, bf16[192,768]{1,0:T(8,128)(2,1)}, u32[]{:S(2)}, u32[]{:S(2)}) collective-permute-start(bf16[192,768]{1,0:T(8,128)(2,1)S(1)} %add_convert_fusion.9), channel_id=1, source_target_pairs={{0,16},{8,24},{16,0},{24,8},{1,17},{9,25},{17,1},{25,9},{2,18},{10... | collective-permute-start | bytes 884744 | tf_op jit(solution)/shard_map/ppermute | solution.py:408
  682.3 70.6 %collective-permute-start.52 = (bf16[2,1024,256]{2,1,0:T(8,128)(2,1)}, bf16[2,1024,256]{2,1,0:T(8,128)(2,1)}, u32[]{:S(2)}, u32[]{:S(2)}) collective-permute-start(bf16[2,1024,256]{2,1,0:T(8,128)(2,1)} %get-tuple-element.251), channel_id=1, source_target_pairs={{0,1},{1,0},{2,3},{3,2},{4,5},{5,4},{6,7},{7,6},{8,9},{9,8},{10,11... | collective-permute-start | bytes 3145736 | tf_op jit(solution)/shard_map/ppermute | solution.py:405
  685.4 11.7 %collective-permute-start.54 = (bf16[48,3840]{1,0:T(8,128)(2,1)}, bf16[48,3840]{1,0:T(8,128)(2,1)S(1)}, u32[]{:S(2)}, u32[]{:S(2)}) collective-permute-start(bf16[48,3840]{1,0:T(8,128)(2,1)} %get-tuple-element.434), channel_id=1, source_target_pairs={{0,8},{8,0},{16,24},{24,16},{1,9},{9,1},{17,25},{25,17},{2,10},{10... | collective-permute-start | bytes 1105928 | tf_op jit(solution)/shard_map/ppermute | solution.py:408
  687.2 72.9 %collective-permute-start.66 = (bf16[192,768]{1,0:T(8,128)(2,1)}, bf16[192,768]{1,0:T(8,128)(2,1)}, u32[]{:S(2)}, u32[]{:S(2)}) collective-permute-start(bf16[192,768]{1,0:T(8,128)(2,1)} %add_convert_fusion.8), channel_id=1, source_target_pairs={{0,8},{8,0},{16,24},{24,16},{1,9},{9,1},{17,25},{25,17},{2,10},{10... | collective-permute-start | bytes 884744 | tf_op jit(solution)/shard_map/ppermute | solution.py:408
  697.2 19.2 %collective-permute-start.64 = (bf16[96,768]{1,0:T(8,128)(2,1)S(1)}, bf16[96,768]{1,0:T(8,128)(2,1)S(1)}, u32[]{:S(2)}, u32[]{:S(2)}) collective-permute-start(bf16[96,768]{1,0:T(8,128)(2,1)S(1)} %get-tuple-element.391), channel_id=1, source_target_pairs={{0,6},{1,7},{2,4},{3,5},{4,2},{5,3},{6,0},{7,1},{8,14},{9,15},{10,... | collective-permute-start | bytes 442376 | tf_op jit(solution)/shard_map/ppermute | solution.py:411
  712.0 8.9 %collective-permute-start.63 = (bf16[96,768]{1,0:T(8,128)(2,1)S(1)}, bf16[96,768]{1,0:T(8,128)(2,1)S(1)}, u32[]{:S(2)}, u32[]{:S(2)}) collective-permute-start(bf16[96,768]{1,0:T(8,128)(2,1)S(1)} %get-tuple-element.392), channel_id=1, source_target_pairs={{0,4},{1,5},{2,6},{3,7},{4,0},{5,1},{6,2},{7,3},{8,12},{9,13},{10,... | collective-permute-start | bytes 442376 | tf_op jit(solution)/shard_map/ppermute | solution.py:411
  716.4 41.9 %collective-permute-start.67 = (bf16[48,3840]{1,0:T(8,128)(2,1)S(1)}, bf16[48,3840]{1,0:T(8,128)(2,1)}, u32[]{:S(2)}, u32[]{:S(2)}) collective-permute-start(bf16[48,3840]{1,0:T(8,128)(2,1)S(1)} %add_convert_fusion.7), channel_id=1, source_target_pairs={{0,16},{8,24},{16,0},{24,8},{1,17},{9,25},{17,1},{25,9},{2,18},{10... | collective-permute-start | bytes 1105928 | tf_op jit(solution)/shard_map/ppermute | solution.py:408
  754.6 9.1 %collective-permute-start.56 = (bf16[2,1024,256]{2,1,0:T(8,128)(2,1)S(1)}, bf16[2,1024,256]{2,1,0:T(8,128)(2,1)S(1)}, u32[]{:S(2)}, u32[]{:S(2)}) collective-permute-start(bf16[2,1024,256]{2,1,0:T(8,128)(2,1)S(1)} %copy-done.68), channel_id=1, source_target_pairs={{0,1},{1,0},{2,3},{3,2},{4,5},{5,4},{6,7},{7,6},{8,9},{9,8},{10,11... | collective-permute-start | bytes 3145736 | tf_op jit(solution)/shard_map/ppermute | solution.py:405
  757.9 13.2 %collective-permute-start.65 = (bf16[4,96,768]{2,1,0:T(8,128)(2,1)S(1)}, bf16[4,96,768]{2,1,0:T(8,128)(2,1)S(1)}, u32[]{:S(2)}, u32[]{:S(2)}) collective-permute-start(bf16[4,96,768]{2,1,0:T(8,128)(2,1)S(1)} %fusion.41), channel_id=1, source_target_pairs={{0,1},{1,0},{2,3},{3,2},{4,5},{5,4},{6,7},{7,6},{8,9},{9,8},{10,11... | collective-permute-start | bytes 1769480 | tf_op jit(solution)/shard_map/ppermute | solution.py:405
  760.1 11.0 %collective-permute-start.68 = (bf16[48,3840]{1,0:T(8,128)(2,1)S(1)}, bf16[48,3840]{1,0:T(8,128)(2,1)S(1)}, u32[]{:S(2)}, u32[]{:S(2)}) collective-permute-start(bf16[48,3840]{1,0:T(8,128)(2,1)S(1)} %add_convert_fusion.6), channel_id=1, source_target_pairs={{0,8},{8,0},{16,24},{24,16},{1,9},{9,1},{17,25},{25,17},{2,10},{10... | collective-permute-start | bytes 1105928 | tf_op jit(solution)/shard_map/ppermute | solution.py:408
  774.2 46.5 %collective-permute-start.60 = (bf16[256,768]{1,0:T(8,128)(2,1)}, bf16[256,768]{1,0:T(8,128)(2,1)}, u32[]{:S(2)}, u32[]{:S(2)}) collective-permute-start(bf16[256,768]{1,0:T(8,128)(2,1)} %get-tuple-element.401), channel_id=1, source_target_pairs={{0,24},{8,16},{16,8},{24,0},{1,25},{9,17},{17,9},{25,1},{2,26},{10... | collective-permute-start | bytes 1179656 | tf_op jit(solution)/shard_map/ppermute | solution.py:408
  778.6 42.2 %collective-permute-start.59 = (bf16[256,768]{1,0:T(8,128)(2,1)}, bf16[256,768]{1,0:T(8,128)(2,1)}, u32[]{:S(2)}, u32[]{:S(2)}) collective-permute-start(bf16[256,768]{1,0:T(8,128)(2,1)} %get-tuple-element.402), channel_id=1, source_target_pairs={{0,16},{8,24},{16,0},{24,8},{1,17},{9,25},{17,1},{25,9},{2,18},{10... | collective-permute-start | bytes 1179656 | tf_op jit(solution)/shard_map/ppermute | solution.py:408
  779.0 25.0 %collective-permute-start.58 = (bf16[256,768]{1,0:T(8,128)(2,1)}, bf16[256,768]{1,0:T(8,128)(2,1)}, u32[]{:S(2)}, u32[]{:S(2)}) collective-permute-start(bf16[256,768]{1,0:T(8,128)(2,1)} %get-tuple-element.403), channel_id=1, source_target_pairs={{0,8},{8,0},{16,24},{24,16},{1,9},{9,1},{17,25},{25,17},{2,10},{10... | collective-permute-start | bytes 1179656 | tf_op jit(solution)/shard_map/ppermute | solution.py:408
  785.5 27.3 %collective-permute-start.72 = (bf16[4,96,896]{2,1,0:T(8,128)(2,1)S(1)}, bf16[4,96,896]{2,1,0:T(8,128)(2,1)S(1)}, u32[]{:S(2)}, u32[]{:S(2)}) collective-permute-start(bf16[4,96,896]{2,1,0:T(8,128)(2,1)S(1)} %fusion.39), channel_id=1, source_target_pairs={{0,1},{1,0},{2,3},{3,2},{4,5},{5,4},{6,7},{7,6},{8,9},{9,8},{10,11... | collective-permute-start | bytes 2064392 | tf_op jit(solution)/shard_map/ppermute | solution.py:405
  787.0 26.9 %collective-permute-start.71 = (bf16[96,768]{1,0:T(8,128)(2,1)S(1)}, bf16[96,768]{1,0:T(8,128)(2,1)S(1)}, u32[]{:S(2)}, u32[]{:S(2)}) collective-permute-start(bf16[96,768]{1,0:T(8,128)(2,1)S(1)} %get-tuple-element.388), channel_id=1, source_target_pairs={{0,6},{1,7},{2,4},{3,5},{4,2},{5,3},{6,0},{7,1},{8,14},{9,15},{10,... | collective-permute-start | bytes 442376 | tf_op jit(solution)/shard_map/ppermute | solution.py:411
  804.0 12.6 %collective-permute-start.70 = (bf16[96,768]{1,0:T(8,128)(2,1)S(1)}, bf16[96,768]{1,0:T(8,128)(2,1)S(1)}, u32[]{:S(2)}, u32[]{:S(2)}) collective-permute-start(bf16[96,768]{1,0:T(8,128)(2,1)S(1)} %get-tuple-element.389), channel_id=1, source_target_pairs={{0,4},{1,5},{2,6},{3,7},{4,0},{5,1},{6,2},{7,3},{8,12},{9,13},{10,... | collective-permute-start | bytes 442376 | tf_op jit(solution)/shard_map/ppermute | solution.py:411
  820.8 14.1 %collective-permute-start.57 = (bf16[2,256,768]{2,1,0:T(8,128)(2,1)S(1)}, bf16[2,256,768]{2,1,0:T(8,128)(2,1)S(1)}, u32[]{:S(2)}, u32[]{:S(2)}) collective-permute-start(bf16[2,256,768]{2,1,0:T(8,128)(2,1)S(1)} %pad_maximum_fusion.9), channel_id=1, source_target_pairs={{0,1},{1,0},{2,3},{3,2},{4,5},{5,4},{6,7},{7,6},{8,9},{9,8},{10,11... | collective-permute-start | bytes 2359304 | tf_op jit(solution)/shard_map/ppermute | solution.py:405
  828.2 14.5 %collective-permute-start.61 = (bf16[2,256,768]{2,1,0:T(8,128)(2,1)S(1)}, bf16[2,256,768]{2,1,0:T(8,128)(2,1)S(1)}, u32[]{:S(2)}, u32[]{:S(2)}) collective-permute-start(bf16[2,256,768]{2,1,0:T(8,128)(2,1)S(1)} %pad_maximum_fusion.11), channel_id=1, source_target_pairs={{0,1},{1,0},{2,3},{3,2},{4,5},{5,4},{6,7},{7,6},{8,9},{9,8},{10,11... | collective-permute-start | bytes 2359304 | tf_op jit(solution)/shard_map/ppermute | solution.py:405
  832.1 10.4 %collective-permute-start.77 = (bf16[48,2432]{1,0:T(8,128)(2,1)S(1)}, bf16[48,2432]{1,0:T(8,128)(2,1)S(1)}, u32[]{:S(2)}, u32[]{:S(2)}) collective-permute-start(bf16[48,2432]{1,0:T(8,128)(2,1)S(1)} %fusion.43), channel_id=1, source_target_pairs={{0,16},{8,24},{16,0},{24,8},{1,17},{9,25},{17,1},{25,9},{2,18},{10... | collective-permute-start | bytes 700424 | tf_op jit(solution)/shard_map/ppermute | solution.py:408
  (92 other events, 887.6 us)

commit v5 on v4

--- a/solution.py
+++ b/solution.py
@@ -44,26 +44,40 @@
 
 
 def forward_kernel(info, q_ref, k_own, k_mate, v_own, v_mate, qx_ref, kx_ref, *refs, size, plan):
-    pieces, moves, outs = plan
-    count = len(pieces)
+    count, moves, outs = plan
     beside, (out_ref, ext_ref), full = refs[:count], refs[count : count + 2], refs[count + 2 : count + 2 + len(outs)]
-    k_all, vt_all, s_all, *sems = refs[count + 2 + len(outs) :]
+    k_all, vt_all, s_all, *buffers = refs[count + 2 + len(outs) :]
     slot = pl.program_id(1)
     if count:
-        copies = [
-            pltpu.make_async_copy(beside[j], full[out].at[info[info.shape[0] - count + j]], sems[0].at[j])
-            for j, out in enumerate(moves)
+        in_sem, out_sem = buffers[count:]
+        reads = [pltpu.make_async_copy(beside[j], buffers[j], in_sem.at[j]) for j in range(count)]
+        writes = [
+            pltpu.make_async_copy(
+                buffers[j].at[pl.ds(row, rows), :],
+                full[out].at[info[info.shape[0] - count + j], :, pl.ds(col, buffers[j].shape[1])],
+                out_sem.at[j, k],
+            )
+            for j in range(count)
+            for k, (row, rows, out, col) in enumerate(moves)
         ]
-
-        @pl.when((pl.program_id(0) == 0) & (slot == 0))
+        at = pl.program_id(0) * pl.num_programs(1) + slot
+
+        @pl.when(at == 0)
         def _():
-            for copy in copies:
-                copy.start()
-
-        @pl.when((pl.program_id(0) == pl.num_programs(0) - 1) & (slot == pl.num_programs(1) - 1))
+            for read in reads:
+                read.start()
+
+        @pl.when(at == 2)
         def _():
-            for copy in copies:
-                copy.wait()
+            for read in reads:
+                read.wait()
+            for write in writes:
+                write.start()
+
+        @pl.when(at == pl.num_programs(0) * pl.num_programs(1) - 1)
+        def _():
+            for write in writes:
+                write.wait()
 
     block = q_ref.shape[0]
     count = kx_ref.shape[0] // block
@@ -160,7 +174,7 @@
         info = jnp.concatenate([info, jnp.stack(spots).astype(jnp.int32)])
     anywhere = pl.BlockSpec(memory_space=pl.ANY)
     return pl.pallas_call(
-        functools.partial(forward_kernel, size=size, plan=(moves, moves, outs)),
+        functools.partial(forward_kernel, size=size, plan=(len(pieces), moves, outs)),
         grid_spec=pltpu.PrefetchScalarGridSpec(
             num_scalar_prefetch=1,
             grid=(pairs, slots),
@@ -180,7 +194,8 @@
                 pltpu.VMEM((heads, size + 16, length), jnp.bfloat16),
                 pltpu.VMEM((heads, block, block), jnp.float32),
             ]
-            + [pltpu.SemaphoreType.DMA((len(pieces),))] * bool(pieces),
+            + [pltpu.VMEM(piece.shape, piece.dtype) for piece in pieces]
+            + [pltpu.SemaphoreType.DMA((len(pieces),)), pltpu.SemaphoreType.DMA((len(pieces), len(moves)))] * bool(pieces),
         ),
         out_shape=[jax.ShapeDtypeStruct((rows, width), jnp.bfloat16)] * 2
         + [jax.ShapeDtypeStruct(shape, jnp.bfloat16) for shape in outs],
@@ -425,8 +440,8 @@
     return parts
 
 
-def from_sequence_send(here, slots):
-    return [here.across(slots[k], k) if k else slots[k] for k in range(here.columns)]
+def from_sequence_send(here, slots, first=0):
+    return [here.across(part, k) if k else part for k, part in enumerate(slots, first)]
 
 
 def from_sequence_end(here, slots, groups):
@@ -486,19 +501,21 @@
     return [f.reshape(-1, f.shape[2]) for f in full]
 
 
+def gather_direct(here, local):
+    return [local] + [here.aside(local, k) for k in range(1, 4)]
+
+
+def with_mates(here, parts):
+    spots = [here.shard ^ (2 * k) for k in range(4)]
+    return parts + [here.mate(part) for part in parts], spots + [spot ^ 1 for spot in spots]
+
+
 def gather_cut(here, local, cuts, mark):
     if here.shards != 8:
         full = lax.all_gather(local, "fsdp", axis=0, tiled=True)
         return [full[:, col : col + cols] for col, cols in cuts]
-    rows = local.shape[0]
-    middle = rows // 2
-    across_x, across_y = here.aside(local, 1), here.aside(local, 2)
-    across_x, across_y = after((across_x, across_y), mark)
-    low, high = here.aside(across_x[:middle], 2), here.aside(across_y[middle:], 1)
-    parts = [local, across_x, across_y, low, high]
-    spots = [here.shard ^ (2 * k) for k in (0, 1, 2, 3, 3)]
-    parts, spots = parts + [here.mate(part) for part in parts], spots + [spot ^ 1 for spot in spots]
-    return place(parts, spots, [0, 0, 0, 0, middle] * 2, rows, cuts)
+    parts, spots = with_mates(here, after(gather_direct(here, local), mark))
+    return place(parts, spots, [0] * 8, local.shape[0], cuts)
 
 
 def pack_kernel(mix_ref, merge_ref, columns_ref, out_ref, *, size, parts):
@@ -602,12 +619,25 @@
     rows = here.columns * half
     length = here.columns * piece
 
-    def send(parts):
-        return [straight(part) for part in from_sequence_send(here, parts)]
+    def send(parts, first=0):
+        return [straight(part) for part in from_sequence_send(here, parts, first)]
 
     ups = hidden_size // width
     part_width = width // PARTS
-    token_parts = to_sequence_parts(here, tokens)
+    ids_sent = [segment_ids] + [here.across(segment_ids, k) for k in range(1, here.columns)]
+    ids_slots = jnp.stack([pick(i, lax.rem(here.column, groups)) for i in ids_sent])
+    ids_other = here.mate(ids_slots)
+    ids_slots = jnp.where(lax.div(here.column, groups) == here.core, ids_slots, ids_other)
+    ids_own = pick(ids_slots.reshape(here.columns, 2, half), here.core, 1)
+    ids = jnp.stack([pick(ids_slots, here.column ^ k) for k in range(here.columns)]).reshape(2 * here.columns, half)
+    first_id, last_id = ids[:, 0], ids[:, -1]
+    low = jnp.sum(last_id[None, :] < ids_own[:, :1], axis=1)
+    high = jnp.sum(first_id[None, :] <= ids_own[:, -1:], axis=1)
+    info = jnp.concatenate([jnp.stack([here.core, here.column]), jnp.stack([low, high], axis=1).reshape(-1)]).astype(jnp.int32)
+    key_ext = key_extension(ids.reshape(length))
+    query_ext = query_extension(ids_own.reshape(rows))
+
+    token_parts, ids_sent = lax.optimization_barrier((to_sequence_parts(here, tokens), ids_sent))
     token_slots = send(token_parts)
 
     vectors = (query_bias, value_bias, merge_bias, first_gain, first_shift, down_bias, second_gain, second_shift)
@@ -624,30 +654,19 @@
     ]
     up_bias_full = lines_full[8 : 8 + ups].reshape(ups, shards, own).transpose(1, 0, 2).reshape(-1)
 
-    ids_parts = to_sequence_parts(here, after(segment_ids, token_parts).reshape(groups, piece, 1))
-    ids_own = jnp.concatenate(send(ids_parts), axis=0).reshape(here.columns, half)
-    ids_mate = here.mate(ids_own)
-    by_core = jnp.stack([jnp.where(here.core == 0, ids_own, ids_mate), jnp.where(here.core == 0, ids_mate, ids_own)], axis=1)
-    ids = jnp.stack([pick(by_core, k ^ here.column) for k in range(here.columns)]).reshape(2 * here.columns, half)
-    first_id, last_id = ids[:, 0], ids[:, -1]
-    low = jnp.sum(last_id[None, :] < ids_own[:, :1], axis=1)
-    high = jnp.sum(first_id[None, :] <= ids_own[:, -1:], axis=1)
-    info = jnp.concatenate([jnp.stack([here.core, here.column]), jnp.stack([low, high], axis=1).reshape(-1)]).astype(jnp.int32)
-    key_ext = key_extension(ids.reshape(length))
-    query_ext = query_extension(ids_own.reshape(rows))
-
     cotangent_parts = to_sequence_parts(here, after(output_grad, token_parts))
     ready = (cotangent_parts, mix_parts, merge_full, lines_full, info, key_ext, query_ext)
     token_slots, (cotangent_parts, mix_parts, merge_full, lines_full, info, key_ext, query_ext) = lax.optimization_barrier(
         (token_slots, ready)
     )
     flat = straight(jnp.concatenate(token_slots, axis=0))
-    cotangent_slots = send(after(cotangent_parts, flat))
+    cotangent_parts = after(cotangent_parts, flat)
+    cotangent_two = send(cotangent_parts[2:3], 2)
     direct = shards == 8
     up_local, down_local = after((up_weight, down_weight), mix_parts[0])
     if direct:
-        up_parts = [up_local, here.aside(up_local, 1), here.aside(up_local, 2)]
-        down_parts = [down_local, here.aside(down_local, 1), here.aside(down_local, 2)]
+        packed = jnp.concatenate([up_local[:, j * width : (j + 1) * width] for j in range(ups)] + [down_local], axis=0)
+        packed_parts = gather_direct(here, after(packed, flat))
     else:
         up_full, down_full = [lax.all_gather(w, "fsdp", axis=0, tiled=True) for w in (up_local, down_local)]
 
@@ -659,24 +678,21 @@
         mixed.append(((dot(flat, mix_parts[p]) + bias) * column_scale).astype(bf16))
         mixed_mate.append(here.mate(mixed[p]))
 
+    mixed, mixed_mate = lax.optimization_barrier((mixed, mixed_mate))
     contexts, exts = [], []
     plan, spots = NOTHING, ()
     for p in range(PARTS):
         if p:
             mixed[p], mixed_mate[p] = after((mixed[p], mixed_mate[p]), contexts[-1])
-        if p == 1 and direct:
-            up_parts, down_parts = after((up_parts, down_parts), contexts[-1])
-            up_parts.append(here.aside(up_parts[1], 2))
-            down_parts.append(here.aside(down_parts[2], 1))
-            mates = [[here.mate(w) for w in parts] for parts in (up_parts, down_parts)]
-        if p == PARTS - 1:
-            mixed[p], cotangent_slots = after((mixed[p], cotangent_slots), cotangent_slots)
-            if direct:
-                pieces = up_parts + mates[0] + down_parts + mates[1]
-                outs = [(shards,) + up_weight.shape, (shards,) + down_weight.shape]
-                spots = [here.shard ^ (2 * k) for k in range(4)]
-                spots = (spots + [spot ^ 1 for spot in spots]) * 2
-                plan = (tuple(after(pieces, contexts[-1])), (0,) * 8 + (1,) * 8, tuple(outs))
+        if p == 1:
+            mixed[p], cotangent_two = lax.optimization_barrier((mixed[p], cotangent_two))
+            later = after(cotangent_parts, contexts[-1])
+            cotangent_slots = send(later[:2]) + cotangent_two + send(later[3:], 3)
+        if p == PARTS - 1 and direct:
+            pieces, spots = with_mates(here, after(packed_parts, contexts[-1]))
+            moves = [(j * own, own, 0, j * width) for j in range(ups)] + [(ups * own, ups * own, 1, 0)]
+            outs = [(shards,) + up_weight.shape, (shards,) + down_weight.shape]
+            plan = (pieces, tuple(moves), tuple(outs))
         context, ext, *placed = attention_forward(info, mixed[p], mixed_mate[p], query_ext, key_ext, HD, plan, spots)
         contexts.append(context)
         exts.append(ext)
@@ -693,7 +709,7 @@
     active_low, slope_low = lax.optimization_barrier((active.astype(bf16), slope.astype(bf16)))
     branch = dot(active_low, down_full) + down_bias_full
     result, normed_two, factor_two = norm_forward(first_out + branch, gain_two, shift_two)
-    output_slots = from_sequence_send(here, list(result.astype(bf16).reshape(here.columns, half, width)))
+    result_low = result.astype(bf16)
 
     grad_second, second_gain_grad, second_shift_grad = norm_backward(cotangent, normed_two, factor_two, gain_two)
     grad_branch = grad_second.astype(bf16)
@@ -726,32 +742,31 @@
         kv = (kept + other.astype(f32)).astype(bf16)
         return jnp.concatenate([dq, kv[0], kv[1]], axis=1)
 
+    one = backward(0, after(grad_context, down_share, up_share))
+    down_others, down_share = after((down_others, down_share), one[0])
     down_half, down_other = column_first(here, share_sum(down_share, down_others))
-    one = backward(0, after(grad_context, down_half, up_share, output_slots))
-    down_half, down_other = column_second(here, *after((down_half, down_other), one[0]))
     up_others, up_share = after((up_others, up_share), one[0])
     up_half, up_other = column_first(here, share_sum(up_share, up_others))
+    output_slots = from_sequence_send(here, list(after(result_low, one[0]).reshape(here.columns, half, width)))
     two = backward(1, after(grad_context, down_half, up_half))
-    down_half, down_other = column_third(here, *after((down_half, down_other), two[0]))
+    down_half, down_other = column_second(here, *after((down_half, down_other), two[0]))
     up_half, up_other = column_second(here, *after((up_half, up_other), two[0]))
     mixed_one = mixed_part(after(one, two[0]))
     mix_grad_one = dot(flat.T, mixed_one)
     mix_kept_one, mix_other_one = share_pair(here, mix_grad_one.reshape(shards, own, -1))
     input_part = grad_sum + dot(mixed_one, mix_parts[0].T)
     mix_share_one, mix_others_one = share_plane(here, mix_kept_one, after(mix_other_one, input_part))
-    three = backward(2, after(grad_context, down_half, up_half, mix_share_one))
-    down_half, down_other = after((down_half, down_other), three[0])
-    up_half, up_other = column_third(here, *after((up_half, up_other), three[0]))
+    three = backward(2, after(grad_context, down_half, up_half, mix_share_one, output_slots[:3]))
+    down_half, down_other, up_half, up_other = after((down_half, down_other, up_half, up_other), three[0])
     mixed_two = mixed_part(after(two, three[0]))
-    mix_grad_two = dot(flat.T, mixed_two)
-    mix_kept_two, mix_other_two = share_pair(here, mix_grad_two.reshape(shards, own, -1))
     input_part = input_part + dot(mixed_two, mix_parts[1].T)
-    mixed_three = mixed_part(after(three, input_part, mix_kept_two))
+    mixed_three = mixed_part(after(three, input_part))
     input_low = (input_part + dot(mixed_three, mix_parts[2].T)).astype(bf16)
     input_slots = from_sequence_send(here, list(input_low.reshape(here.columns, half, width)))
-    mixed_three, mix_other_two, down_other, up_other = after((mixed_three, mix_other_two, down_other, up_other), input_low)
-    mix_share_two, mix_others_two = share_plane(here, mix_kept_two, mix_other_two)
-    mix_grad_rest = dot(flat.T, mixed_three)
+    mixed_rest = after(jnp.concatenate([mixed_two, mixed_three], axis=1), input_low)
+    mix_grad_rest = dot(flat.T, mixed_rest)
+    down_half, down_other = column_third(here, *after((down_half, down_other), mix_grad_rest))
+    up_half, up_other = column_third(here, *after((up_half, up_other), mix_grad_rest))
 
     sums = [column_sums(m) for m in (mixed_one, mixed_two, mixed_three)]
     query_grad = jnp.concatenate([s[:part_width] for s in sums])
@@ -771,11 +786,10 @@
     columns_grad = jnp.pad(lines_grad, ((0, LANES - lines_grad.shape[0]), (0, 0))).T
     rest = jnp.concatenate([mix_grad_rest, columns_grad], axis=1).reshape(shards, own, -1)
     rest_kept, rest_other = share_pair(here, rest)
-    rest_share, rest_others = share_plane(here, rest_kept, after(rest_other, input_slots[1]))
+    rest_share, rest_others = share_plane(here, rest_kept, rest_other)
     mix_share = jnp.concatenate(
         [
             share_sum(mix_share_one, mix_others_one),
-            share_sum(mix_share_two, mix_others_two),
             share_sum(rest_share, rest_others),
         ],
         axis=1,

time: 861 us -> 557 us (0.65)
  Pallas kernels: 425 us -> 166 us
  starting transfers between devices: 142 us -> 88.9 us
  local copies, waits for them, and re-layouts: 40.7 us -> 58.4 us
    pallas_call x3, Pallas kernels: 330 us -> 62.9 us  [attention_forward(): pl.pallas_call(functools.partial(forward_kernel, size=size, plan=(len(pie...]
    ppermute x25 -> x18, starting transfers between devices: 67.1 us -> 31.7 us  [aside(): return lax.ppermute(values, 'fsdp', xor_pairs(self.shards, 2 * bits))]
    ppermute x24, waiting for transfers between devices: 60.9 us -> 79.2 us  [across(): return lax.ppermute(values, 'seq', xor_pairs(self.columns, bits))]
    ppermute x25 -> x18, waiting for transfers between devices: 47 us -> 30.1 us  [aside(): return lax.ppermute(values, 'fsdp', xor_pairs(self.shards, 2 * bits))]
    ppermute x24, starting transfers between devices: 59.8 us -> 50.5 us  [across(): return lax.ppermute(values, 'seq', xor_pairs(self.columns, bits))]
    ppermute x30 -> x23, starting transfers between devices: 15.3 us -> 6.58 us  [mate(): return lax.ppermute(values, 'fsdp', xor_pairs(self.shards, 1))]
    unnamed x165 -> x148, local copies, waits for them, and re-layouts: 11.7 us -> 17.6 us
    dot_general x18 -> x17, matrix products: 78.6 us -> 75 us  [dot(): return jnp.dot(a, b, preferred_element_type=f32)]
  transfers between devices with their start and end apart: 79 -> 65, of which waited for: 30 -> 19; matrix products, arithmetic and copies ran while one was open for 10% -> 22% of each run, Pallas kernels for 15% -> 30%
where the time goes in v5:
time: 557 us; the launch traced here: 550 us
  Pallas kernels  166 us (30%)
  waiting for transfers between devices  109 us (20%)
  starting transfers between devices  88.9 us (16%)
  matrix products  75 us (13%)
  local copies, waits for them, and re-layouts  58.4 us (10%)
  other arithmetic  50.1 us (9%)
    pallas_call x3, Pallas kernels, attention_backward(): pl.pallas_call(functools.partial(backward_kernel, size=size), grid_spec=p...  96.2 us
    ppermute x24, waiting for transfers between devices, across(): return lax.ppermute(values, 'seq', xor_pairs(self.columns, bits))  79.2 us
    dot_general x17, matrix products, dot(): return jnp.dot(a, b, preferred_element_type=f32)  75 us
    pallas_call x3, Pallas kernels, attention_forward(): pl.pallas_call(functools.partial(forward_kernel, size=size, plan=(len(pie...  62.9 us
    ppermute x24, starting transfers between devices, across(): return lax.ppermute(values, 'seq', xor_pairs(self.columns, bits))  50.5 us
    ppermute x18, starting transfers between devices, aside(): return lax.ppermute(values, 'fsdp', xor_pairs(self.shards, 2 * bits))  31.7 us
    ppermute x18, waiting for transfers between devices, aside(): return lax.ppermute(values, 'fsdp', xor_pairs(self.shards, 2 * bits))  30.1 us
    unnamed x148, local copies, waits for them, and re-layouts  17.6 us
  transfers between devices with their start and end apart: 65, of which 19 were waited for; matrix products, arithmetic and copies ran while one was open for 22% of the time, Pallas kernels for 30%

profile of v5, /device:TPU:0, one launch (start us, length us, event | category | flops | bytes accessed | tf_op | source)
XLA Modules:
  0.0 550.1 jit_solution(1339357927452037613)
XLA Ops:
  0.7 3.1 collective-permute-start.1
  3.8 2.6 collective-permute-start.2
  6.4 2.4 dynamic-slice_bitcast_fusion.3
  9.9 2.1 collective-permute-done.3
  18.2 2.0 pack_projection.1.refs_0_
  27.2 17.7 %collective-permute-done.5 = bf16[256,768]{1,0:T(8,128)(2,1)S(1)} collective-permute-done((bf16[256,768]{1,0:T(8,128)(2,1)}, bf16[256,768]{1,0:T(8,128)(2,1)S(1)}, u32[]{:S(2)}, u32[]{:S(2)}) %collective-permute-start.5) | collective-permute-done | bytes 393248 | tf_op jit(solution)/shard_map/ppermute | solution.py:423
  44.9 6.3 %collective-permute-done.9.refs_2_ = bf16[96,3200]{1,0:T(8,128)(2,1)} collective-permute-done((bf16[96,3200]{1,0:T(8,128)(2,1)}, bf16[96,3200]{1,0:T(8,128)(2,1)}, u32[]{:S(2)}, u32[]{:S(2)}) %collective-permute-start.9) | collective-permute-done | bytes 614432 | tf_op jit(solution)/shard_map/ppermute | solution.py:426
  52.8 1.8 or_convert_fusion.kx_ref
  58.5 5.2 place_parts.1
  66.5 8.0 %collective-permute-done.6 = bf16[256,768]{1,0:T(8,128)(2,1)} collective-permute-done((bf16[256,768]{1,0:T(8,128)(2,1)}, bf16[256,768]{1,0:T(8,128)(2,1)}, u32[]{:S(2)}, u32[]{:S(2)}) %collective-permute-start.6) | collective-permute-done | bytes 393248 | tf_op jit(solution)/shard_map/ppermute | solution.py:423
  90.2 3.1 collective-permute-start.19
  93.3 20.9 %attention_forward.3 = (bf16[1024,256]{1,0:T(8,128)(2,1)}, bf16[1024,256]{1,0:T(8,128)(2,1)}) custom-call(s32[10]{0:T(128)} %pad_add_fusion.3.info, bf16[1024,768]{1,0:T(8,128)(2,1)} %copy-done.2, bf16[1024,768]{1,0:T(8,128)(2,1)} %copy-done.2, bf16[1024,768]{1,0:T(8,128)(2,1)} %copy-done.5, bf16[1024,768]{1,0:T(8,128)(2,1)} %copy-done.2, ...), custom_call_target="tpu_custom_call" | custom-call | flops 1073741824 | bytes 4194304 | tf_op jit(solution)/shard_map/attention_forward/pallas_call | solution.py:176
  114.3 20.5 %attention_forward.4 = (bf16[1024,256]{1,0:T(8,128)(2,1)}, bf16[1024,256]{1,0:T(8,128)(2,1)}) custom-call(s32[10]{0:T(128)} %pad_add_fusion.3.info, bf16[1024,768]{1,0:T(8,128)(2,1)} %copy-done.1, bf16[1024,768]{1,0:T(8,128)(2,1)} %copy-done.1, bf16[1024,768]{1,0:T(8,128)(2,1)} %copy-done.4, bf16[1024,768]{1,0:T(8,128)(2,1)} %copy-done.1, ...), custom_call_target="tpu_custom_call" | custom-call | flops 1073741824 | bytes 4194304 | tf_op jit(solution)/shard_map/attention_forward/pallas_call | solution.py:176
  134.8 5.0 collective-permute-done.21.refs_2_
  145.0 2.7 collective-permute-start.27
  150.0 3.8 collective-permute-start.28
  153.8 21.4 %attention_forward.5 = (bf16[1024,256]{1,0:T(8,128)(2,1)}, bf16[1024,256]{1,0:T(8,128)(2,1)}, bf16[8,96,3072]{2,1,0:T(8,128)(2,1)}, bf16[8,384,768]{2,1,0:T(8,128)(2,1)}) custom-call(s32[18]{0:T(128)} %concatenate.87.info, bf16[1024,768]{1,0:T(8,128)(2,1)} %copy-done.3, bf16[1024,768]{1,0:T(8,128)(2,1)} %copy-done.3, ...), custom_call_target="tpu_custom_call" | custom-call | flops 1073741824 | bytes 4194304 | tf_op jit(solution)/shard_map/attention_forward/pallas_call | solution.py:176
  175.2 1.9 constant_dynamic-update-slice_fusion.5
  177.2 3.4 fusion.76
  181.2 13.9 %fusion.4 = (bf16[1024,3072]{1,0:T(8,128)(2,1)}, bf16[1024,3072]{1,0:T(8,128)(2,1)S(1)}) fusion(f32[3072]{0:T(1024)S(1)} %add.499, bf16[768,3072]{1,0:T(8,128)(2,1)S(1)} %bitcast.331, f32[1024,768]{1,0:T(8,128)S(1)} %get-tuple-element.469, f32[768]{0:T(1024)S(1)} %get-tuple-element.360, f32[768]{0:T(1024)S(1)} %get-tuple-element.361, ...), kind=kOutput, calls=%fused_computation.15 | convolution fusion | flops 4873519104 | bytes 20473856 | tf_op jit(solution)/shard_map/dot_general | solution.py:387
  195.2 5.5 fusion.77
  201.2 3.3 fusion.13
  204.6 3.3 convert_reduce_fusion.2
  207.9 7.7 %fusion.60 = f32[3072,768]{1,0:T(8,128)} fusion(bf16[1024,3072]{1,0:T(8,128)(2,1)S(1)} %get-tuple-element.208, f32[1024,768]{1,0:T(8,128)S(1)} %get-tuple-element.374), kind=kOutput, calls=%fused_computation.266 | convolution fusion | flops 4832624640 | bytes 18874368 | tf_op jit(solution)/shard_map/dot_general | solution.py:387
  215.6 9.5 %convert_reduce_fusion = (f32[3072]{0:T(1024)}, bf16[1024,3072]{1,0:T(8,128)(2,1)S(1)}) fusion(bf16[1024,3072]{1,0:T(8,128)(2,1)} %get-tuple-element.222, bf16[3072,768]{1,0:T(8,128)(2,1)} %bitcast.332, f32[1024,768]{1,0:T(8,128)S(1)} %get-tuple-element.374), kind=kOutput, calls=%fused_computation.16 | convolution fusion | flops 4848350208 | bytes 20459520 | tf_op jit(solution)/shard_map/dot_general | solution.py:387
  225.1 9.0 %multiply_reduce_fusion = (f32[768]{0:T(1024)}, f32[1024]{0:T(1024)S(1)}, f32[1024]{0:T(1024)S(1)}, f32[768]{0:T(1024)}, f32[1024,768]{1,0:T(8,128)S(1)}) fusion(f32[1024,768]{1,0:T(8,128)S(1)} %get-tuple-element.469, f32[1024]{0:T(1024)S(1)} %add_rsqrt_fusion.1, f32[1024]{0:T(1024)S(1)} %broadcast_multiply_fusion.5, f32[768]{0:T(1024)S(1)} %get-tuple-element.361, ...), kind=kOutput, calls=%fused_computation.35 | convolution fusion | flops 4839698432 | bytes 20472832 | tf_op jit(solution)/shard_map/dot_general | solution.py:387
  234.1 5.6 %fusion.65 = f32[768,3072]{1,0:T(8,128)S(1)} fusion(bf16[1024,3072]{1,0:T(8,128)(2,1)S(1)} %get-tuple-element.474, f32[1024,768]{1,0:T(8,128)S(1)} %get-tuple-element.469, f32[768]{0:T(1024)S(1)} %get-tuple-element.360, f32[768]{0:T(1024)S(1)} %get-tuple-element.361, f32[1024]{0:T(1024)S(1)} %add_rsqrt_fusion.1, f32[1024]{0:T(1024)S(1)} %broadcast_multiply_fusion.5), kind=kOutput, calls=%fused_computation.271 | convolution fusion | flops 4835770368 | bytes 18888704 | tf_op jit(solution)/shard_map/dot_general | solution.py:387
  239.8 7.5 %fusion.16 = bf16[4,384,768]{2,1,0:T(8,128)(2,1)} fusion(f32[4,2,384,768]{3,2,1,0:T(8,128)} %bitcast.288, s32[]{:T(128)S(6)} %select_n.329), kind=kLoop, calls=%fused_computation.58 | loop fusion | bytes 4718596 | tf_op jit(solution)/shard_map/convert_element_type | solution.py:553
  250.4 2.0 fusion.14
  252.9 4.7 fusion.33
  258.8 2.6 convolution_convert_fusion.do_ref
  267.2 5.8 %collective-permute-start.36 = (bf16[384,768]{1,0:T(8,128)(2,1)}, bf16[384,768]{1,0:T(8,128)(2,1)}, u32[]{:S(2)}, u32[]{:S(2)}) collective-permute-start(bf16[384,768]{1,0:T(8,128)(2,1)} %get-tuple-element.384), channel_id=1, source_target_pairs={{0,4},{1,5},{2,6},{3,7},{4,0},{5,1},{6,2},{7,3},{8,12},{9,13},{10,... | collective-permute-start | bytes 1769480 | tf_op jit(solution)/shard_map/ppermute | solution.py:426
  272.9 5.3 fusion.20
  279.8 1.9 collective-permute-start.39
  281.7 32.1 %attention_backward.3 = (bf16[1024,256]{1,0:T(8,128)(2,1)}, f32[2,1024,256]{2,1,0:T(8,128)}, bf16[2,1024,256]{2,1,0:T(8,128)(2,1)}) custom-call(s32[10]{0:T(128)} %pad_add_fusion.3.info, bf16[1024,768]{1,0:T(8,128)(2,1)} %copy-done.2, bf16[1024,256]{1,0:T(8,128)(2,1)} %get-tuple-element.210.ext_ref, bf16[1024,768]{1,0:T(8,128)(2,1)} %convolution_convert_fusion.do_ref, ...), custom_call_target="tpu_custom_call" | custom-call | flops 2684354560 | bytes 6291456 | tf_op jit(solution)/shard_map/attention_backward/pallas_call | solution.py:299
  315.0 9.3 %collective-permute-start.31 = (bf16[256,768]{1,0:T(8,128)(2,1)}, bf16[256,768]{1,0:T(8,128)(2,1)}, u32[]{:S(2)}, u32[]{:S(2)}) collective-permute-start(bf16[256,768]{1,0:T(8,128)(2,1)} %get-tuple-element.413), channel_id=1, source_target_pairs={{0,8},{8,0},{16,24},{24,16},{1,9},{9,1},{17,25},{25,17},{2,10},{10... | collective-permute-start | bytes 1179656 | tf_op jit(solution)/shard_map/ppermute | solution.py:423
  326.0 2.7 collective-permute-start.34
  328.7 2.0 collective-permute-done.39
  330.7 2.1 collective-permute-start.42
  332.8 1.9 add_convert_fusion.5
  335.6 32.1 %attention_backward.4 = (bf16[1024,256]{1,0:T(8,128)(2,1)}, f32[2,1024,256]{2,1,0:T(8,128)}, bf16[2,1024,256]{2,1,0:T(8,128)(2,1)}) custom-call(s32[10]{0:T(128)} %pad_add_fusion.3.info, bf16[1024,768]{1,0:T(8,128)(2,1)} %copy-done.1, bf16[1024,256]{1,0:T(8,128)(2,1)} %get-tuple-element.230.ext_ref, bf16[1024,768]{1,0:T(8,128)(2,1)} %convolution_convert_fusion.do_ref, ...), custom_call_target="tpu_custom_call" | custom-call | flops 2684354560 | bytes 6291456 | tf_op jit(solution)/shard_map/attention_backward/pallas_call | solution.py:299
  367.8 6.0 %collective-permute-start.43 = (bf16[48,3840]{1,0:T(8,128)(2,1)}, bf16[48,3840]{1,0:T(8,128)(2,1)S(1)}, u32[]{:S(2)}, u32[]{:S(2)}) collective-permute-start(bf16[48,3840]{1,0:T(8,128)(2,1)} %get-tuple-element.435), channel_id=1, source_target_pairs={{0,8},{8,0},{16,24},{24,16},{1,9},{9,1},{17,25},{25,17},{2,10},{10... | collective-permute-start | bytes 1105928 | tf_op jit(solution)/shard_map/ppermute | solution.py:423
  373.8 2.0 add_convert_fusion.4
  378.3 3.1 convolution_add_fusion.1
  381.8 6.6 %collective-permute-start.53 = (bf16[96,768]{1,0:T(8,128)(2,1)S(1)}, bf16[96,768]{1,0:T(8,128)(2,1)S(1)}, u32[]{:S(2)}, u32[]{:S(2)}) collective-permute-start(bf16[96,768]{1,0:T(8,128)(2,1)S(1)} %get-tuple-element.392), channel_id=1, source_target_pairs={{0,6},{1,7},{2,4},{3,5},{4,2},{5,3},{6,0},{7,1},{8,14},{9,15},{10,... | collective-permute-start | bytes 442376 | tf_op jit(solution)/shard_map/ppermute | solution.py:426
  389.4 3.5 collective-permute-done.53
  393.9 2.1 collective-permute-done.52
  396.0 3.1 collective-permute-start.33
  402.7 32.1 %attention_backward.5 = (bf16[1024,256]{1,0:T(8,128)(2,1)}, f32[2,1024,256]{2,1,0:T(8,128)}, bf16[2,1024,256]{2,1,0:T(8,128)(2,1)}) custom-call(s32[10]{0:T(128)} %pad_add_fusion.3.info, bf16[1024,768]{1,0:T(8,128)(2,1)} %copy-done.3, bf16[1024,256]{1,0:T(8,128)(2,1)} %get-tuple-element.246.ext_ref, bf16[1024,768]{1,0:T(8,128)(2,1)} %convolution_convert_fusion.do_ref, ...), custom_call_target="tpu_custom_call" | custom-call | flops 2684354560 | bytes 6291456 | tf_op jit(solution)/shard_map/attention_backward/pallas_call | solution.py:299
  434.8 2.2 add_convert_fusion.3
  437.6 7.1 %collective-permute-done.62 = bf16[48,3840]{1,0:T(8,128)(2,1)S(1)} collective-permute-done((bf16[48,3840]{1,0:T(8,128)(2,1)S(1)}, bf16[48,3840]{1,0:T(8,128)(2,1)S(1)}, u32[]{:S(2)}, u32[]{:S(2)}) %collective-permute-start.62) | collective-permute-done | bytes 368672 | tf_op jit(solution)/shard_map/ppermute | solution.py:423
  453.3 2.6 collective-permute-start.49
  458.9 2.0 concatenate.102
  466.3 4.6 fusion.78
  474.1 13.0 %collective-permute-done.64 = bf16[192,768]{1,0:T(8,128)(2,1)S(1)} collective-permute-done((bf16[192,768]{1,0:T(8,128)(2,1)S(1)}, bf16[192,768]{1,0:T(8,128)(2,1)S(1)}, u32[]{:S(2)}, u32[]{:S(2)}) %collective-permute-start.64) | collective-permute-done | bytes 294944 | tf_op jit(solution)/shard_map/ppermute | solution.py:423
  487.1 2.5 collective-permute-start.63
  490.7 7.9 %collective-permute-done.63 = bf16[48,3840]{1,0:T(8,128)(2,1)S(1)} collective-permute-done((bf16[48,3840]{1,0:T(8,128)(2,1)S(1)}, bf16[48,3840]{1,0:T(8,128)(2,1)S(1)}, u32[]{:S(2)}, u32[]{:S(2)}) %collective-permute-start.63) | collective-permute-done | bytes 368672 | tf_op jit(solution)/shard_map/ppermute | solution.py:423
  499.0 5.6 %collective-permute-start.57 = (bf16[96,1664]{1,0:T(8,128)(2,1)S(1)}, bf16[96,1664]{1,0:T(8,128)(2,1)S(1)}, u32[]{:S(2)}, u32[]{:S(2)}) collective-permute-start(bf16[96,1664]{1,0:T(8,128)(2,1)S(1)} %get-tuple-element.388), channel_id=1, source_target_pairs={{0,6},{1,7},{2,4},{3,5},{4,2},{5,3},{6,0},{7,1},{8,14},{9,15},{10,... | collective-permute-start | bytes 958472 | tf_op jit(solution)/shard_map/ppermute | solution.py:426
  508.7 4.3 collective-permute-done.57
  512.9 5.2 collective-permute-done.56
  519.8 6.4 %collective-permute-done.58 = bf16[48,2432]{1,0:T(8,128)(2,1)S(1)} collective-permute-done((bf16[48,2432]{1,0:T(8,128)(2,1)S(1)}, bf16[48,2432]{1,0:T(8,128)(2,1)S(1)}, u32[]{:S(2)}, u32[]{:S(2)}) %collective-permute-start.58) | collective-permute-done | bytes 233504 | tf_op jit(solution)/shard_map/ppermute | solution.py:423
  528.9 9.6 %collective-permute-done.59 = bf16[48,2432]{1,0:T(8,128)(2,1)S(1)} collective-permute-done((bf16[48,2432]{1,0:T(8,128)(2,1)S(1)}, bf16[48,2432]{1,0:T(8,128)(2,1)S(1)}, u32[]{:S(2)}, u32[]{:S(2)}) %collective-permute-start.59) | collective-permute-done | bytes 233504 | tf_op jit(solution)/shard_map/ppermute | solution.py:423
  538.8 1.9 maximum_convert_fusion
  540.7 5.6 %collective-permute-done.60 = bf16[48,2432]{1,0:T(8,128)(2,1)S(1)} collective-permute-done((bf16[48,2432]{1,0:T(8,128)(2,1)S(1)}, bf16[48,2432]{1,0:T(8,128)(2,1)S(1)}, u32[]{:S(2)}, u32[]{:S(2)}) %collective-permute-start.60) | collective-permute-done | bytes 233504 | tf_op jit(solution)/shard_map/ppermute | solution.py:423
  (379 shorter events, 105.4 us)
Async XLA Ops:
  0.7 11.4 %collective-permute-start.1 = (s32[2,512]{1,0:T(2,128)}, s32[2,512]{1,0:T(2,128)S(1)}, u32[]{:S(2)}, u32[]{:S(2)}) collective-permute-start(s32[2,512]{1,0:T(2,128)} %param.17), channel_id=1, source_target_pairs={{0,8},{8,0},{16,24},{24,16},{1,9},{9,1},{17,25},{25,17},{2,10},{10... | collective-permute-start | bytes 12296 | tf_op jit(solution)/shard_map/ppermute | solution.py:423
  3.8 8.2 %collective-permute-start.2 = (s32[2,512]{1,0:T(2,128)}, s32[2,512]{1,0:T(2,128)S(1)}, u32[]{:S(2)}, u32[]{:S(2)}) collective-permute-start(s32[2,512]{1,0:T(2,128)} %param.17), channel_id=1, source_target_pairs={{0,16},{8,24},{16,0},{24,8},{1,17},{9,25},{17,1},{25,9},{2,18},{10... | collective-permute-start | bytes 12296 | tf_op jit(solution)/shard_map/ppermute | solution.py:423
  6.4 5.6 %collective-permute-start.3 = (s32[2,512]{1,0:T(2,128)}, s32[2,512]{1,0:T(2,128)S(1)}, u32[]{:S(2)}, u32[]{:S(2)}) collective-permute-start(s32[2,512]{1,0:T(2,128)} %param.17), channel_id=1, source_target_pairs={{0,24},{8,16},{16,8},{24,0},{1,25},{9,17},{17,9},{25,1},{2,26},{10... | collective-permute-start | bytes 12296 | tf_op jit(solution)/shard_map/ppermute | solution.py:423
  8.7 6.1 %collective-permute-start = (bf16[2,256,768]{2,1,0:T(8,128)(2,1)}, bf16[2,256,768]{2,1,0:T(8,128)(2,1)S(1)}, u32[]{:S(2)}, u32[]{:S(2)}) collective-permute-start(bf16[2,256,768]{2,1,0:T(8,128)(2,1)} %get-tuple-element.426), channel_id=1, source_target_pairs={{0,1},{1,0},{2,3},{3,2},{4,5},{5,4},{6,7},{7,6},{8,9},{9,8},{10,11... | collective-permute-start | bytes 2359304 | tf_op jit(solution)/shard_map/ppermute | solution.py:420
  20.3 24.7 %collective-permute-start.8 = (bf16[96,3200]{1,0:T(8,128)(2,1)}, bf16[96,3200]{1,0:T(8,128)(2,1)}, u32[]{:S(2)}, u32[]{:S(2)}) collective-permute-start(bf16[96,3200]{1,0:T(8,128)(2,1)} %pack_projection.1.refs_0_), channel_id=1, source_target_pairs={{0,2},{1,3},{2,0},{3,1},{4,6},{5,7},{6,4},{7,5},{8,10},{9,11},{10,... | collective-permute-start | bytes 1843208 | tf_op jit(solution)/shard_map/ppermute | solution.py:426
  21.8 29.4 %collective-permute-start.9 = (bf16[96,3200]{1,0:T(8,128)(2,1)}, bf16[96,3200]{1,0:T(8,128)(2,1)}, u32[]{:S(2)}, u32[]{:S(2)}) collective-permute-start(bf16[96,3200]{1,0:T(8,128)(2,1)} %pack_projection.1.refs_0_), channel_id=1, source_target_pairs={{0,4},{1,5},{2,6},{3,7},{4,0},{5,1},{6,2},{7,3},{8,12},{9,13},{10,... | collective-permute-start | bytes 1843208 | tf_op jit(solution)/shard_map/ppermute | solution.py:426
  23.3 27.9 %collective-permute-start.10 = (bf16[96,3200]{1,0:T(8,128)(2,1)}, bf16[96,3200]{1,0:T(8,128)(2,1)}, u32[]{:S(2)}, u32[]{:S(2)}) collective-permute-start(bf16[96,3200]{1,0:T(8,128)(2,1)} %pack_projection.1.refs_0_), channel_id=1, source_target_pairs={{0,6},{1,7},{2,4},{3,5},{4,2},{5,3},{6,0},{7,1},{8,14},{9,15},{10,... | collective-permute-start | bytes 1843208 | tf_op jit(solution)/shard_map/ppermute | solution.py:426
  25.5 19.4 %collective-permute-start.5 = (bf16[256,768]{1,0:T(8,128)(2,1)}, bf16[256,768]{1,0:T(8,128)(2,1)S(1)}, u32[]{:S(2)}, u32[]{:S(2)}) collective-permute-start(bf16[256,768]{1,0:T(8,128)(2,1)} %get-tuple-element.147), channel_id=1, source_target_pairs={{0,16},{8,24},{16,0},{24,8},{1,17},{9,25},{17,1},{25,9},{2,18},{10... | collective-permute-start | bytes 1179656 | tf_op jit(solution)/shard_map/ppermute | solution.py:423
  26.2 28.4 %collective-permute-start.7 = (bf16[2,256,768]{2,1,0:T(8,128)(2,1)S(1)}, bf16[2,256,768]{2,1,0:T(8,128)(2,1)S(1)}, u32[]{:S(2)}, u32[]{:S(2)}) collective-permute-start(bf16[2,256,768]{2,1,0:T(8,128)(2,1)S(1)} %get-tuple-element.420), channel_id=1, source_target_pairs={{0,1},{1,0},{2,3},{3,2},{4,5},{5,4},{6,7},{7,6},{8,9},{9,8},{10,11... | collective-permute-start | bytes 2359304 | tf_op jit(solution)/shard_map/ppermute | solution.py:420
  51.2 4.5 collective-permute-start.11
  51.2 6.3 %collective-permute-start.12 = (bf16[96,3200]{1,0:T(8,128)(2,1)}, bf16[96,3200]{1,0:T(8,128)(2,1)S(1)}, u32[]{:S(2)}, u32[]{:S(2)}) collective-permute-start(bf16[96,3200]{1,0:T(8,128)(2,1)} %collective-permute-done.8.refs_1_), channel_id=1, source_target_pairs={{0,1},{1,0},{2,3},{3,2},{4,5},{5,4},{6,7},{7,6},{8,9},{9,8},{10,11... | collective-permute-start | bytes 1843208 | tf_op jit(solution)/shard_map/ppermute | solution.py:420
  51.7 5.8 %collective-permute-start.13 = (bf16[96,3200]{1,0:T(8,128)(2,1)}, bf16[96,3200]{1,0:T(8,128)(2,1)S(1)}, u32[]{:S(2)}, u32[]{:S(2)}) collective-permute-start(bf16[96,3200]{1,0:T(8,128)(2,1)} %collective-permute-done.9.refs_2_), channel_id=1, source_target_pairs={{0,1},{1,0},{2,3},{3,2},{4,5},{5,4},{6,7},{7,6},{8,9},{9,8},{10,11... | collective-permute-start | bytes 1843208 | tf_op jit(solution)/shard_map/ppermute | solution.py:420
  51.8 5.7 %collective-permute-start.14 = (bf16[96,3200]{1,0:T(8,128)(2,1)}, bf16[96,3200]{1,0:T(8,128)(2,1)}, u32[]{:S(2)}, u32[]{:S(2)}) collective-permute-start(bf16[96,3200]{1,0:T(8,128)(2,1)} %collective-permute-done.10.refs_3_), channel_id=1, source_target_pairs={{0,1},{1,0},{2,3},{3,2},{4,5},{5,4},{6,7},{7,6},{8,9},{9,8},{10,11... | collective-permute-start | bytes 1843208 | tf_op jit(solution)/shard_map/ppermute | solution.py:420
  54.6 12.0 %collective-permute-start.4 = (bf16[256,768]{1,0:T(8,128)(2,1)}, bf16[256,768]{1,0:T(8,128)(2,1)}, u32[]{:S(2)}, u32[]{:S(2)}) collective-permute-start(bf16[256,768]{1,0:T(8,128)(2,1)} %get-tuple-element.146), channel_id=1, source_target_pairs={{0,8},{8,0},{16,24},{24,16},{1,9},{9,1},{17,25},{25,17},{2,10},{10... | collective-permute-start | bytes 1179656 | tf_op jit(solution)/shard_map/ppermute | solution.py:423
  55.7 18.9 %collective-permute-start.6 = (bf16[256,768]{1,0:T(8,128)(2,1)}, bf16[256,768]{1,0:T(8,128)(2,1)}, u32[]{:S(2)}, u32[]{:S(2)}) collective-permute-start(bf16[256,768]{1,0:T(8,128)(2,1)} %get-tuple-element.148), channel_id=1, source_target_pairs={{0,24},{8,16},{16,8},{24,0},{1,25},{9,17},{17,9},{25,1},{2,26},{10... | collective-permute-start | bytes 1179656 | tf_op jit(solution)/shard_map/ppermute | solution.py:423
  79.2 9.6 %collective-permute-start.16 = (bf16[1024,768]{1,0:T(8,128)(2,1)S(1)}, bf16[1024,768]{1,0:T(8,128)(2,1)S(1)}, u32[]{:S(2)}, u32[]{:S(2)}) collective-permute-start(bf16[1024,768]{1,0:T(8,128)(2,1)S(1)} %multiply_convert_fusion.4.q_ref.k_own.v_own), channel_id=1, source_target_pairs={{0,1},{1,0},{2,3},{3,2},{4,5},{5,4},{6,7},{7,6},{8,9},{9,8},{10,11... | collective-permute-start | bytes 4718600 | tf_op jit(solution)/shard_map/ppermute | solution.py:420
  81.0 9.3 %collective-permute-start.17 = (bf16[1024,768]{1,0:T(8,128)(2,1)S(1)}, bf16[1024,768]{1,0:T(8,128)(2,1)S(1)}, u32[]{:S(2)}, u32[]{:S(2)}) collective-permute-start(bf16[1024,768]{1,0:T(8,128)(2,1)S(1)} %multiply_convert_fusion.3.q_ref.k_own.v_own), channel_id=1, source_target_pairs={{0,1},{1,0},{2,3},{3,2},{4,5},{5,4},{6,7},{7,6},{8,9},{9,8},{10,11... | collective-permute-start | bytes 4718600 | tf_op jit(solution)/shard_map/ppermute | solution.py:420
  82.7 10.6 %collective-permute-start.18 = (bf16[1024,768]{1,0:T(8,128)(2,1)S(1)}, bf16[1024,768]{1,0:T(8,128)(2,1)}, u32[]{:S(2)}, u32[]{:S(2)}) collective-permute-start(bf16[1024,768]{1,0:T(8,128)(2,1)S(1)} %multiply_convert_fusion.2.q_ref.k_own.v_own), channel_id=1, source_target_pairs={{0,1},{1,0},{2,3},{3,2},{4,5},{5,4},{6,7},{7,6},{8,9},{9,8},{10,11... | collective-permute-start | bytes 4718600 | tf_op jit(solution)/shard_map/ppermute | solution.py:420
  86.7 48.1 %collective-permute-start.20 = (bf16[768,768]{1,0:T(8,128)(2,1)}, bf16[768,768]{1,0:T(8,128)(2,1)}, u32[]{:S(2)}, u32[]{:S(2)}) collective-permute-start(bf16[768,768]{1,0:T(8,128)(2,1)} %constant_dynamic-update-slice_fusion.4.refs_0_), channel_id=1, source_target_pairs={{0,2},{1,3},{2,0},{3,1},{4,6},{5,7},{6,4},{7,5},{8,10},{9,11},{10,... | collective-permute-start | bytes 3538952 | tf_op jit(solution)/shard_map/ppermute | solution.py:426
  87.9 51.9 %collective-permute-start.21 = (bf16[768,768]{1,0:T(8,128)(2,1)}, bf16[768,768]{1,0:T(8,128)(2,1)}, u32[]{:S(2)}, u32[]{:S(2)}) collective-permute-start(bf16[768,768]{1,0:T(8,128)(2,1)} %constant_dynamic-update-slice_fusion.4.refs_0_), channel_id=1, source_target_pairs={{0,4},{1,5},{2,6},{3,7},{4,0},{5,1},{6,2},{7,3},{8,12},{9,13},{10,... | collective-permute-start | bytes 3538952 | tf_op jit(solution)/shard_map/ppermute | solution.py:426
  88.8 52.7 %collective-permute-start.22 = (bf16[768,768]{1,0:T(8,128)(2,1)}, bf16[768,768]{1,0:T(8,128)(2,1)}, u32[]{:S(2)}, u32[]{:S(2)}) collective-permute-start(bf16[768,768]{1,0:T(8,128)(2,1)} %constant_dynamic-update-slice_fusion.4.refs_0_), channel_id=1, source_target_pairs={{0,6},{1,7},{2,4},{3,5},{4,2},{5,3},{6,0},{7,1},{8,14},{9,15},{10,... | collective-permute-start | bytes 3538952 | tf_op jit(solution)/shard_map/ppermute | solution.py:426
  90.2 24.0 %collective-permute-start.19 = (bf16[256,768]{1,0:T(8,128)(2,1)S(1)}, bf16[256,768]{1,0:T(8,128)(2,1)S(1)}, u32[]{:S(2)}, u32[]{:S(2)}) collective-permute-start(bf16[256,768]{1,0:T(8,128)(2,1)S(1)} %copy-done.33), channel_id=1, source_target_pairs={{0,16},{8,24},{16,0},{24,8},{1,17},{9,25},{17,1},{25,9},{2,18},{10... | collective-permute-start | bytes 1179656 | tf_op jit(solution)/shard_map/ppermute | solution.py:423
  141.5 8.6 %collective-permute-start.23 = (bf16[768,768]{1,0:T(8,128)(2,1)}, bf16[768,768]{1,0:T(8,128)(2,1)}, u32[]{:S(2)}, u32[]{:S(2)}) collective-permute-start(bf16[768,768]{1,0:T(8,128)(2,1)} %constant_dynamic-update-slice_fusion.4.refs_0_), channel_id=1, source_target_pairs={{0,1},{1,0},{2,3},{3,2},{4,5},{5,4},{6,7},{7,6},{8,9},{9,8},{10,11... | collective-permute-start | bytes 3538952 | tf_op jit(solution)/shard_map/ppermute | solution.py:420
  141.5 12.4 %collective-permute-start.24 = (bf16[768,768]{1,0:T(8,128)(2,1)}, bf16[768,768]{1,0:T(8,128)(2,1)}, u32[]{:S(2)}, u32[]{:S(2)}) collective-permute-start(bf16[768,768]{1,0:T(8,128)(2,1)} %collective-permute-done.20.refs_1_), channel_id=1, source_target_pairs={{0,1},{1,0},{2,3},{3,2},{4,5},{5,4},{6,7},{7,6},{8,9},{9,8},{10,11... | collective-permute-start | bytes 3538952 | tf_op jit(solution)/shard_map/ppermute | solution.py:420
  142.0 11.9 %collective-permute-start.25 = (bf16[768,768]{1,0:T(8,128)(2,1)}, bf16[768,768]{1,0:T(8,128)(2,1)}, u32[]{:S(2)}, u32[]{:S(2)}) collective-permute-start(bf16[768,768]{1,0:T(8,128)(2,1)} %collective-permute-done.21.refs_2_), channel_id=1, source_target_pairs={{0,1},{1,0},{2,3},{3,2},{4,5},{5,4},{6,7},{7,6},{8,9},{9,8},{10,11... | collective-permute-start | bytes 3538952 | tf_op jit(solution)/shard_map/ppermute | solution.py:420
  142.0 11.9 %collective-permute-start.26 = (bf16[768,768]{1,0:T(8,128)(2,1)}, bf16[768,768]{1,0:T(8,128)(2,1)}, u32[]{:S(2)}, u32[]{:S(2)}) collective-permute-start(bf16[768,768]{1,0:T(8,128)(2,1)} %collective-permute-done.22.refs_3_), channel_id=1, source_target_pairs={{0,1},{1,0},{2,3},{3,2},{4,5},{5,4},{6,7},{7,6},{8,9},{9,8},{10,11... | collective-permute-start | bytes 3538952 | tf_op jit(solution)/shard_map/ppermute | solution.py:420
  145.0 56.2 %collective-permute-start.27 = (bf16[256,768]{1,0:T(8,128)(2,1)}, bf16[256,768]{1,0:T(8,128)(2,1)S(1)}, u32[]{:S(2)}, u32[]{:S(2)}) collective-permute-start(bf16[256,768]{1,0:T(8,128)(2,1)} %get-tuple-element.215), channel_id=1, source_target_pairs={{0,8},{8,0},{16,24},{24,16},{1,9},{9,1},{17,25},{25,17},{2,10},{10... | collective-permute-start | bytes 1179656 | tf_op jit(solution)/shard_map/ppermute | solution.py:423
  150.0 51.2 %collective-permute-start.28 = (bf16[256,768]{1,0:T(8,128)(2,1)}, bf16[256,768]{1,0:T(8,128)(2,1)S(1)}, u32[]{:S(2)}, u32[]{:S(2)}) collective-permute-start(bf16[256,768]{1,0:T(8,128)(2,1)} %get-tuple-element.217), channel_id=1, source_target_pairs={{0,24},{8,16},{16,8},{24,0},{1,25},{9,17},{17,9},{25,1},{2,26},{10... | collective-permute-start | bytes 1179656 | tf_op jit(solution)/shard_map/ppermute | solution.py:423
  247.3 5.7 %collective-permute-start.29 = (bf16[4,384,768]{2,1,0:T(8,128)(2,1)}, bf16[4,384,768]{2,1,0:T(8,128)(2,1)}, u32[]{:S(2)}, u32[]{:S(2)}) collective-permute-start(bf16[4,384,768]{2,1,0:T(8,128)(2,1)} %fusion.16), channel_id=1, source_target_pairs={{0,1},{1,0},{2,3},{3,2},{4,5},{5,4},{6,7},{7,6},{8,9},{9,8},{10,11... | collective-permute-start | bytes 7077896 | tf_op jit(solution)/shard_map/ppermute | solution.py:420
  252.4 20.5 %collective-permute-start.30 = (bf16[4,96,3840]{2,1,0:T(8,128)(2,1)}, bf16[4,96,3840]{2,1,0:T(8,128)(2,1)}, u32[]{:S(2)}, u32[]{:S(2)}) collective-permute-start(bf16[4,96,3840]{2,1,0:T(8,128)(2,1)} %fusion.14), channel_id=1, source_target_pairs={{0,1},{1,0},{2,3},{3,2},{4,5},{5,4},{6,7},{7,6},{8,9},{9,8},{10,11... | collective-permute-start | bytes 8847368 | tf_op jit(solution)/shard_map/ppermute | solution.py:420
  257.6 24.1 %collective-permute-start.35 = (bf16[384,768]{1,0:T(8,128)(2,1)}, bf16[384,768]{1,0:T(8,128)(2,1)}, u32[]{:S(2)}, u32[]{:S(2)}) collective-permute-start(bf16[384,768]{1,0:T(8,128)(2,1)} %get-tuple-element.385), channel_id=1, source_target_pairs={{0,2},{1,3},{2,0},{3,1},{4,6},{5,7},{6,4},{7,5},{8,10},{9,11},{10,... | collective-permute-start | bytes 1769480 | tf_op jit(solution)/shard_map/ppermute | solution.py:426
  267.2 47.8 %collective-permute-start.36 = (bf16[384,768]{1,0:T(8,128)(2,1)}, bf16[384,768]{1,0:T(8,128)(2,1)}, u32[]{:S(2)}, u32[]{:S(2)}) collective-permute-start(bf16[384,768]{1,0:T(8,128)(2,1)} %get-tuple-element.384), channel_id=1, source_target_pairs={{0,4},{1,5},{2,6},{3,7},{4,0},{5,1},{6,2},{7,3},{8,12},{9,13},{10,... | collective-permute-start | bytes 1769480 | tf_op jit(solution)/shard_map/ppermute | solution.py:426
  272.9 51.3 %collective-permute-start.37 = (bf16[384,768]{1,0:T(8,128)(2,1)}, bf16[384,768]{1,0:T(8,128)(2,1)}, u32[]{:S(2)}, u32[]{:S(2)}) collective-permute-start(bf16[384,768]{1,0:T(8,128)(2,1)} %get-tuple-element.383), channel_id=1, source_target_pairs={{0,6},{1,7},{2,4},{3,5},{4,2},{5,3},{6,0},{7,1},{8,14},{9,15},{10,... | collective-permute-start | bytes 1769480 | tf_op jit(solution)/shard_map/ppermute | solution.py:426
  278.2 47.8 %collective-permute-start.38 = (bf16[96,3840]{1,0:T(8,128)(2,1)}, bf16[96,3840]{1,0:T(8,128)(2,1)}, u32[]{:S(2)}, u32[]{:S(2)}) collective-permute-start(bf16[96,3840]{1,0:T(8,128)(2,1)} %get-tuple-element.379), channel_id=1, source_target_pairs={{0,2},{1,3},{2,0},{3,1},{4,6},{5,7},{6,4},{7,5},{8,10},{9,11},{10,... | collective-permute-start | bytes 2211848 | tf_op jit(solution)/shard_map/ppermute | solution.py:426
  279.8 51.0 %collective-permute-start.39 = (bf16[96,3840]{1,0:T(8,128)(2,1)}, bf16[96,3840]{1,0:T(8,128)(2,1)}, u32[]{:S(2)}, u32[]{:S(2)}) collective-permute-start(bf16[96,3840]{1,0:T(8,128)(2,1)} %get-tuple-element.380), channel_id=1, source_target_pairs={{0,4},{1,5},{2,6},{3,7},{4,0},{5,1},{6,2},{7,3},{8,12},{9,13},{10,... | collective-permute-start | bytes 2211848 | tf_op jit(solution)/shard_map/ppermute | solution.py:426
  281.7 51.1 %collective-permute-start.40 = (bf16[96,3840]{1,0:T(8,128)(2,1)}, bf16[96,3840]{1,0:T(8,128)(2,1)}, u32[]{:S(2)}, u32[]{:S(2)}) collective-permute-start(bf16[96,3840]{1,0:T(8,128)(2,1)} %get-tuple-element.377), channel_id=1, source_target_pairs={{0,6},{1,7},{2,4},{3,5},{4,2},{5,3},{6,0},{7,1},{8,14},{9,15},{10,... | collective-permute-start | bytes 2211848 | tf_op jit(solution)/shard_map/ppermute | solution.py:426
  315.0 86.2 %collective-permute-start.31 = (bf16[256,768]{1,0:T(8,128)(2,1)}, bf16[256,768]{1,0:T(8,128)(2,1)}, u32[]{:S(2)}, u32[]{:S(2)}) collective-permute-start(bf16[256,768]{1,0:T(8,128)(2,1)} %get-tuple-element.413), channel_id=1, source_target_pairs={{0,8},{8,0},{16,24},{24,16},{1,9},{9,1},{17,25},{25,17},{2,10},{10... | collective-permute-start | bytes 1179656 | tf_op jit(solution)/shard_map/ppermute | solution.py:423
  324.3 78.5 %collective-permute-start.32 = (bf16[256,768]{1,0:T(8,128)(2,1)}, bf16[256,768]{1,0:T(8,128)(2,1)}, u32[]{:S(2)}, u32[]{:S(2)}) collective-permute-start(bf16[256,768]{1,0:T(8,128)(2,1)} %get-tuple-element.412), channel_id=1, source_target_pairs={{0,16},{8,24},{16,0},{24,8},{1,17},{9,25},{17,1},{25,9},{2,18},{10... | collective-permute-start | bytes 1179656 | tf_op jit(solution)/shard_map/ppermute | solution.py:423
  326.0 47.8 %collective-permute-start.34 = (bf16[2,1024,256]{2,1,0:T(8,128)(2,1)}, bf16[2,1024,256]{2,1,0:T(8,128)(2,1)S(1)}, u32[]{:S(2)}, u32[]{:S(2)}) collective-permute-start(bf16[2,1024,256]{2,1,0:T(8,128)(2,1)} %get-tuple-element.229), channel_id=1, source_target_pairs={{0,1},{1,0},{2,3},{3,2},{4,5},{5,4},{6,7},{7,6},{8,9},{9,8},{10,11... | collective-permute-start | bytes 3145736 | tf_op jit(solution)/shard_map/ppermute | solution.py:420
  330.7 37.0 %collective-permute-start.42 = (bf16[192,768]{1,0:T(8,128)(2,1)S(1)}, bf16[192,768]{1,0:T(8,128)(2,1)S(1)}, u32[]{:S(2)}, u32[]{:S(2)}) collective-permute-start(bf16[192,768]{1,0:T(8,128)(2,1)S(1)} %get-tuple-element.439), channel_id=1, source_target_pairs={{0,8},{8,0},{16,24},{24,16},{1,9},{9,1},{17,25},{25,17},{2,10},{10... | collective-permute-start | bytes 884744 | tf_op jit(solution)/shard_map/ppermute | solution.py:423
  367.7 67.1 %collective-permute-start.41 = (bf16[2,1024,256]{2,1,0:T(8,128)(2,1)}, bf16[2,1024,256]{2,1,0:T(8,128)(2,1)}, u32[]{:S(2)}, u32[]{:S(2)}) collective-permute-start(bf16[2,1024,256]{2,1,0:T(8,128)(2,1)} %get-tuple-element.245), channel_id=1, source_target_pairs={{0,1},{1,0},{2,3},{3,2},{4,5},{5,4},{6,7},{7,6},{8,9},{9,8},{10,11... | collective-permute-start | bytes 3145736 | tf_op jit(solution)/shard_map/ppermute | solution.py:420
  367.8 21.1 %collective-permute-start.43 = (bf16[48,3840]{1,0:T(8,128)(2,1)}, bf16[48,3840]{1,0:T(8,128)(2,1)S(1)}, u32[]{:S(2)}, u32[]{:S(2)}) collective-permute-start(bf16[48,3840]{1,0:T(8,128)(2,1)} %get-tuple-element.435), channel_id=1, source_target_pairs={{0,8},{8,0},{16,24},{24,16},{1,9},{9,1},{17,25},{25,17},{2,10},{10... | collective-permute-start | bytes 1105928 | tf_op jit(solution)/shard_map/ppermute | solution.py:423
  377.5 4.2 collective-permute-start.44
  381.8 11.2 %collective-permute-start.53 = (bf16[96,768]{1,0:T(8,128)(2,1)S(1)}, bf16[96,768]{1,0:T(8,128)(2,1)S(1)}, u32[]{:S(2)}, u32[]{:S(2)}) collective-permute-start(bf16[96,768]{1,0:T(8,128)(2,1)S(1)} %get-tuple-element.392), channel_id=1, source_target_pairs={{0,6},{1,7},{2,4},{3,5},{4,2},{5,3},{6,0},{7,1},{8,14},{9,15},{10,... | collective-permute-start | bytes 442376 | tf_op jit(solution)/shard_map/ppermute | solution.py:426
  388.9 7.1 %collective-permute-start.52 = (bf16[96,768]{1,0:T(8,128)(2,1)S(1)}, bf16[96,768]{1,0:T(8,128)(2,1)S(1)}, u32[]{:S(2)}, u32[]{:S(2)}) collective-permute-start(bf16[96,768]{1,0:T(8,128)(2,1)S(1)} %get-tuple-element.393), channel_id=1, source_target_pairs={{0,4},{1,5},{2,6},{3,7},{4,0},{5,1},{6,2},{7,3},{8,12},{9,13},{10,... | collective-permute-start | bytes 442376 | tf_op jit(solution)/shard_map/ppermute | solution.py:426
  392.9 6.1 %collective-permute-start.51 = (bf16[96,768]{1,0:T(8,128)(2,1)S(1)}, bf16[96,768]{1,0:T(8,128)(2,1)S(1)}, u32[]{:S(2)}, u32[]{:S(2)}) collective-permute-start(bf16[96,768]{1,0:T(8,128)(2,1)S(1)} %get-tuple-element.391), channel_id=1, source_target_pairs={{0,2},{1,3},{2,0},{3,1},{4,6},{5,7},{6,4},{7,5},{8,10},{9,11},{10,... | collective-permute-start | bytes 442376 | tf_op jit(solution)/shard_map/ppermute | solution.py:426
  396.0 57.3 %collective-permute-start.33 = (bf16[256,768]{1,0:T(8,128)(2,1)}, bf16[256,768]{1,0:T(8,128)(2,1)}, u32[]{:S(2)}, u32[]{:S(2)}) collective-permute-start(bf16[256,768]{1,0:T(8,128)(2,1)} %get-tuple-element.411), channel_id=1, source_target_pairs={{0,24},{8,16},{16,8},{24,0},{1,25},{9,17},{17,9},{25,1},{2,26},{10... | collective-permute-start | bytes 1179656 | tf_op jit(solution)/shard_map/ppermute | solution.py:423
  399.1 38.6 %collective-permute-start.61 = (bf16[192,768]{1,0:T(8,128)(2,1)S(1)}, bf16[192,768]{1,0:T(8,128)(2,1)S(1)}, u32[]{:S(2)}, u32[]{:S(2)}) collective-permute-start(bf16[192,768]{1,0:T(8,128)(2,1)S(1)} %add_convert_fusion.10), channel_id=1, source_target_pairs={{0,16},{8,24},{16,0},{24,8},{1,17},{9,25},{17,1},{25,9},{2,18},{10... | collective-permute-start | bytes 884744 | tf_op jit(solution)/shard_map/ppermute | solution.py:423
  401.2 43.5 %collective-permute-start.62 = (bf16[48,3840]{1,0:T(8,128)(2,1)S(1)}, bf16[48,3840]{1,0:T(8,128)(2,1)S(1)}, u32[]{:S(2)}, u32[]{:S(2)}) collective-permute-start(bf16[48,3840]{1,0:T(8,128)(2,1)S(1)} %add_convert_fusion.8), channel_id=1, source_target_pairs={{0,16},{8,24},{16,0},{24,8},{1,17},{9,25},{17,1},{25,9},{2,18},{10... | collective-permute-start | bytes 1105928 | tf_op jit(solution)/shard_map/ppermute | solution.py:423
  437.2 11.8 %collective-permute-start.45 = (bf16[2,1024,256]{2,1,0:T(8,128)(2,1)S(1)}, bf16[2,1024,256]{2,1,0:T(8,128)(2,1)S(1)}, u32[]{:S(2)}, u32[]{:S(2)}) collective-permute-start(bf16[2,1024,256]{2,1,0:T(8,128)(2,1)S(1)} %copy-done.59), channel_id=1, source_target_pairs={{0,1},{1,0},{2,3},{3,2},{4,5},{5,4},{6,7},{7,6},{8,9},{9,8},{10,11... | collective-permute-start | bytes 3145736 | tf_op jit(solution)/shard_map/ppermute | solution.py:420
  453.3 52.1 %collective-permute-start.49 = (bf16[256,768]{1,0:T(8,128)(2,1)}, bf16[256,768]{1,0:T(8,128)(2,1)}, u32[]{:S(2)}, u32[]{:S(2)}) collective-permute-start(bf16[256,768]{1,0:T(8,128)(2,1)} %get-tuple-element.402), channel_id=1, source_target_pairs={{0,24},{8,16},{16,8},{24,0},{1,25},{9,17},{17,9},{25,1},{2,26},{10... | collective-permute-start | bytes 1179656 | tf_op jit(solution)/shard_map/ppermute | solution.py:423
  456.0 51.3 %collective-permute-start.48 = (bf16[256,768]{1,0:T(8,128)(2,1)}, bf16[256,768]{1,0:T(8,128)(2,1)}, u32[]{:S(2)}, u32[]{:S(2)}) collective-permute-start(bf16[256,768]{1,0:T(8,128)(2,1)} %get-tuple-element.403), channel_id=1, source_target_pairs={{0,16},{8,24},{16,0},{24,8},{1,17},{9,25},{17,1},{25,9},{2,18},{10... | collective-permute-start | bytes 1179656 | tf_op jit(solution)/shard_map/ppermute | solution.py:423
  456.0 51.2 %collective-permute-start.47 = (bf16[256,768]{1,0:T(8,128)(2,1)}, bf16[256,768]{1,0:T(8,128)(2,1)}, u32[]{:S(2)}, u32[]{:S(2)}) collective-permute-start(bf16[256,768]{1,0:T(8,128)(2,1)} %get-tuple-element.404), channel_id=1, source_target_pairs={{0,8},{8,0},{16,24},{24,16},{1,9},{9,1},{17,25},{25,17},{2,10},{10... | collective-permute-start | bytes 1179656 | tf_op jit(solution)/shard_map/ppermute | solution.py:423
  471.4 27.3 %collective-permute-start.54 = (bf16[4,96,1664]{2,1,0:T(8,128)(2,1)S(1)}, bf16[4,96,1664]{2,1,0:T(8,128)(2,1)S(1)}, u32[]{:S(2)}, u32[]{:S(2)}) collective-permute-start(bf16[4,96,1664]{2,1,0:T(8,128)(2,1)S(1)} %fusion.32), channel_id=1, source_target_pairs={{0,1},{1,0},{2,3},{3,2},{4,5},{5,4},{6,7},{7,6},{8,9},{9,8},{10,11... | collective-permute-start | bytes 3833864 | tf_op jit(solution)/shard_map/ppermute | solution.py:420
  472.0 15.1 %collective-permute-start.64 = (bf16[192,768]{1,0:T(8,128)(2,1)S(1)}, bf16[192,768]{1,0:T(8,128)(2,1)S(1)}, u32[]{:S(2)}, u32[]{:S(2)}) collective-permute-start(bf16[192,768]{1,0:T(8,128)(2,1)S(1)} %add_convert_fusion.9), channel_id=1, source_target_pairs={{0,8},{8,0},{16,24},{24,16},{1,9},{9,1},{17,25},{25,17},{2,10},{10... | collective-permute-start | bytes 884744 | tf_op jit(solution)/shard_map/ppermute | solution.py:423
  487.1 11.5 %collective-permute-start.63 = (bf16[48,3840]{1,0:T(8,128)(2,1)S(1)}, bf16[48,3840]{1,0:T(8,128)(2,1)S(1)}, u32[]{:S(2)}, u32[]{:S(2)}) collective-permute-start(bf16[48,3840]{1,0:T(8,128)(2,1)S(1)} %add_convert_fusion.7), channel_id=1, source_target_pairs={{0,8},{8,0},{16,24},{24,16},{1,9},{9,1},{17,25},{25,17},{2,10},{10... | collective-permute-start | bytes 1105928 | tf_op jit(solution)/shard_map/ppermute | solution.py:423
  499.0 14.0 %collective-permute-start.57 = (bf16[96,1664]{1,0:T(8,128)(2,1)S(1)}, bf16[96,1664]{1,0:T(8,128)(2,1)S(1)}, u32[]{:S(2)}, u32[]{:S(2)}) collective-permute-start(bf16[96,1664]{1,0:T(8,128)(2,1)S(1)} %get-tuple-element.388), channel_id=1, source_target_pairs={{0,6},{1,7},{2,4},{3,5},{4,2},{5,3},{6,0},{7,1},{8,14},{9,15},{10,... | collective-permute-start | bytes 958472 | tf_op jit(solution)/shard_map/ppermute | solution.py:426
  504.5 13.6 %collective-permute-start.56 = (bf16[96,1664]{1,0:T(8,128)(2,1)S(1)}, bf16[96,1664]{1,0:T(8,128)(2,1)S(1)}, u32[]{:S(2)}, u32[]{:S(2)}) collective-permute-start(bf16[96,1664]{1,0:T(8,128)(2,1)S(1)} %get-tuple-element.389), channel_id=1, source_target_pairs={{0,4},{1,5},{2,6},{3,7},{4,0},{5,1},{6,2},{7,3},{8,12},{9,13},{10,... | collective-permute-start | bytes 958472 | tf_op jit(solution)/shard_map/ppermute | solution.py:426
  505.4 12.8 %collective-permute-start.55 = (bf16[96,1664]{1,0:T(8,128)(2,1)S(1)}, bf16[96,1664]{1,0:T(8,128)(2,1)S(1)}, u32[]{:S(2)}, u32[]{:S(2)}) collective-permute-start(bf16[96,1664]{1,0:T(8,128)(2,1)S(1)} %get-tuple-element.387), channel_id=1, source_target_pairs={{0,2},{1,3},{2,0},{3,1},{4,6},{5,7},{6,4},{7,5},{8,10},{9,11},{10,... | collective-permute-start | bytes 958472 | tf_op jit(solution)/shard_map/ppermute | solution.py:426
  507.2 20.3 %collective-permute-start.46 = (bf16[2,256,768]{2,1,0:T(8,128)(2,1)S(1)}, bf16[2,256,768]{2,1,0:T(8,128)(2,1)S(1)}, u32[]{:S(2)}, u32[]{:S(2)}) collective-permute-start(bf16[2,256,768]{2,1,0:T(8,128)(2,1)S(1)} %pad_maximum_fusion.9), channel_id=1, source_target_pairs={{0,1},{1,0},{2,3},{3,2},{4,5},{5,4},{6,7},{7,6},{8,9},{9,8},{10,11... | collective-permute-start | bytes 2359304 | tf_op jit(solution)/shard_map/ppermute | solution.py:420
  518.5 7.7 %collective-permute-start.58 = (bf16[48,2432]{1,0:T(8,128)(2,1)S(1)}, bf16[48,2432]{1,0:T(8,128)(2,1)S(1)}, u32[]{:S(2)}, u32[]{:S(2)}) collective-permute-start(bf16[48,2432]{1,0:T(8,128)(2,1)S(1)} %dynamic-slice_bitcast_fusion.8), channel_id=1, source_target_pairs={{0,8},{8,0},{16,24},{24,16},{1,9},{9,1},{17,25},{25,17},{2,10},{10... | collective-permute-start | bytes 700424 | tf_op jit(solution)/shard_map/ppermute | solution.py:423
  519.7 19.0 %collective-permute-start.50 = (bf16[2,256,768]{2,1,0:T(8,128)(2,1)S(1)}, bf16[2,256,768]{2,1,0:T(8,128)(2,1)S(1)}, u32[]{:S(2)}, u32[]{:S(2)}) collective-permute-start(bf16[2,256,768]{2,1,0:T(8,128)(2,1)S(1)} %pad_maximum_fusion.11), channel_id=1, source_target_pairs={{0,1},{1,0},{2,3},{3,2},{4,5},{5,4},{6,7},{7,6},{8,9},{9,8},{10,11... | collective-permute-start | bytes 2359304 | tf_op jit(solution)/shard_map/ppermute | solution.py:420
  526.2 12.3 %collective-permute-start.59 = (bf16[48,2432]{1,0:T(8,128)(2,1)S(1)}, bf16[48,2432]{1,0:T(8,128)(2,1)S(1)}, u32[]{:S(2)}, u32[]{:S(2)}) collective-permute-start(bf16[48,2432]{1,0:T(8,128)(2,1)S(1)} %fusion.45), channel_id=1, source_target_pairs={{0,16},{8,24},{16,0},{24,8},{1,17},{9,25},{17,1},{25,9},{2,18},{10... | collective-permute-start | bytes 700424 | tf_op jit(solution)/shard_map/ppermute | solution.py:423
  538.6 7.7 %collective-permute-start.60 = (bf16[48,2432]{1,0:T(8,128)(2,1)S(1)}, bf16[48,2432]{1,0:T(8,128)(2,1)S(1)}, u32[]{:S(2)}, u32[]{:S(2)}) collective-permute-start(bf16[48,2432]{1,0:T(8,128)(2,1)S(1)} %add_convert_fusion.11), channel_id=1, source_target_pairs={{0,8},{8,0},{16,24},{24,16},{1,9},{9,1},{17,25},{25,17},{2,10},{10... | collective-permute-start | bytes 700424 | tf_op jit(solution)/shard_map/ppermute | solution.py:423
  (66 other events, 606.1 us)

commit v6 on v5

--- a/solution.py
+++ b/solution.py
@@ -558,7 +558,14 @@
         spot = here.plane ^ k
         return pick(kept, spot).astype(f32) + pick(other, spot).astype(f32)
 
-    return total(0), [here.aside(total(k).astype(bf16), k) for k in range(1, here.shards // 2)]
+    return total(0), [total(k).astype(bf16) for k in range(1, here.shards // 2)]
+
+
+def share_send(here, lows):
+    others = []
+    for k, low in enumerate(lows, 1):
+        others.append(here.aside(after(low, others[k - 3]) if k > 2 else low, k))
+    return others
 
 
 def share_sum(share, others):
@@ -641,12 +648,12 @@
     token_slots = send(token_parts)
 
     vectors = (query_bias, value_bias, merge_bias, first_gain, first_shift, down_bias, second_gain, second_shift)
-    local_weights = after((vectors, up_bias, mix_weight, merge_weight), token_parts)
+    local_weights = after((vectors, up_bias, mix_weight, merge_weight), ids_sent)
     lines = jnp.concatenate([jnp.stack(local_weights[0]), local_weights[1].reshape(ups, own)], axis=0)
     columns = jnp.pad(lines, ((0, LANES - lines.shape[0]), (0, 0))).T
     mix_local = pack(local_weights[2], local_weights[3], columns, HD, PARTS)
     *mix_parts, merge_full, columns_full = gather_cut(
-        here, mix_local, [(p * width, width) for p in range(PARTS + 1)] + [(4 * width, LANES)], token_slots[2]
+        here, mix_local, [(p * width, width) for p in range(PARTS + 1)] + [(4 * width, LANES)], token_slots[2:]
     )
     lines_full = columns_full.T.astype(f32)
     query_full, value_full, merge_bias_full, gain_one, shift_one, down_bias_full, gain_two, shift_two = [
@@ -709,27 +716,31 @@
     active_low, slope_low = lax.optimization_barrier((active.astype(bf16), slope.astype(bf16)))
     branch = dot(active_low, down_full) + down_bias_full
     result, normed_two, factor_two = norm_forward(first_out + branch, gain_two, shift_two)
-    result_low = result.astype(bf16)
+    result_low = list(result.astype(bf16).reshape(here.columns, half, width))
+    output_far = from_sequence_send(here, result_low[3:], 3)
 
     grad_second, second_gain_grad, second_shift_grad = norm_backward(cotangent, normed_two, factor_two, gain_two)
     grad_branch = grad_second.astype(bf16)
-    down_grad = dot(active_low.T, grad_branch)
+    down_grad = dot(active_low.T, grad_branch).astype(bf16)
     down_kept, down_other = share_pair(here, down_grad.reshape(shards, -1, width))
     down_bias_grad = column_sums(grad_branch)
     grad_active = dot(grad_branch, down_full.T)
     grad_hidden = (grad_active * slope_low.astype(f32)).astype(bf16)
-    down_share, down_others = share_plane(here, down_kept, after(down_other, grad_hidden))
-    up_grad = dot(first_low.T, grad_hidden)
+    down_share, down_lows = share_plane(here, down_kept, after(down_other, grad_hidden))
+    grad_hidden, down_lows = lax.optimization_barrier((grad_hidden, down_lows))
+    down_others = share_send(here, down_lows)
+    up_grad = dot(first_low.T, grad_hidden).astype(bf16)
     up_bias_grad = column_sums(grad_hidden)
     grad_first = grad_second + dot(grad_hidden, up_full.T)
     grad_sum, first_gain_grad, first_shift_grad = norm_backward(grad_first, normed_one, factor_one, gain_one)
-    grad_attended = grad_sum.astype(bf16)
-    merge_grad = dot(context.T, grad_attended)
+    grad_attended, down_others[0] = lax.optimization_barrier((grad_sum.astype(bf16), down_others[0]))
+    merge_grad = dot(context.T, grad_attended).astype(bf16)
     merge_bias_grad = column_sums(grad_attended)
     up_merge = jnp.concatenate([up_grad.reshape(shards, own, hidden_size), merge_grad.reshape(shards, own, width)], axis=2)
     up_kept, up_other = share_pair(here, up_merge)
     grad_context = dot(grad_attended, merge_full.T).astype(bf16)
-    up_share, up_others = share_plane(here, up_kept, after(up_other, grad_context))
+    up_share, up_lows = share_plane(here, up_kept, after(up_other, grad_context))
+    up_others = share_send(here, up_lows)
 
     def backward(part, grads):
         dq, kept, other = attention_backward(
@@ -747,26 +758,23 @@
     down_half, down_other = column_first(here, share_sum(down_share, down_others))
     up_others, up_share = after((up_others, up_share), one[0])
     up_half, up_other = column_first(here, share_sum(up_share, up_others))
-    output_slots = from_sequence_send(here, list(after(result_low, one[0]).reshape(here.columns, half, width)))
+    grad_context, output_far = lax.optimization_barrier((after(grad_context, one[0]), output_far))
+    output_slots = from_sequence_send(here, after(result_low[:3], one[0])) + output_far
     two = backward(1, after(grad_context, down_half, up_half))
+    one, up_half, up_other = after((one, up_half, up_other), two[0])
+    mixed_one = mixed_part(one)
     down_half, down_other = column_second(here, *after((down_half, down_other), two[0]))
-    up_half, up_other = column_second(here, *after((up_half, up_other), two[0]))
-    mixed_one = mixed_part(after(one, two[0]))
-    mix_grad_one = dot(flat.T, mixed_one)
-    mix_kept_one, mix_other_one = share_pair(here, mix_grad_one.reshape(shards, own, -1))
+    up_half, up_other = column_second(here, up_half, up_other)
     input_part = grad_sum + dot(mixed_one, mix_parts[0].T)
-    mix_share_one, mix_others_one = share_plane(here, mix_kept_one, after(mix_other_one, input_part))
-    three = backward(2, after(grad_context, down_half, up_half, mix_share_one, output_slots[:3]))
-    down_half, down_other, up_half, up_other = after((down_half, down_other, up_half, up_other), three[0])
-    mixed_two = mixed_part(after(two, three[0]))
+    three = backward(2, after(grad_context, down_half, up_half, input_part, output_slots[:3]))
+    two, down_half, down_other, up_half, up_other = after((two, down_half, down_other, up_half, up_other), three[0])
+    mixed_two = mixed_part(two)
     input_part = input_part + dot(mixed_two, mix_parts[1].T)
     mixed_three = mixed_part(after(three, input_part))
     input_low = (input_part + dot(mixed_three, mix_parts[2].T)).astype(bf16)
     input_slots = from_sequence_send(here, list(input_low.reshape(here.columns, half, width)))
-    mixed_rest = after(jnp.concatenate([mixed_two, mixed_three], axis=1), input_low)
-    mix_grad_rest = dot(flat.T, mixed_rest)
-    down_half, down_other = column_third(here, *after((down_half, down_other), mix_grad_rest))
-    up_half, up_other = column_third(here, *after((up_half, up_other), mix_grad_rest))
+    mixed_all = after(jnp.concatenate([mixed_one, mixed_two, mixed_three], axis=1), input_low)
+    mix_grad = dot(flat.T, mixed_all).astype(bf16)
 
     sums = [column_sums(m) for m in (mixed_one, mixed_two, mixed_three)]
     query_grad = jnp.concatenate([s[:part_width] for s in sums])
@@ -784,20 +792,20 @@
     up_lines = up_bias_grad.reshape(shards, ups, own).transpose(1, 0, 2).reshape(ups, width)
     lines_grad = jnp.concatenate([jnp.stack(vectors), up_lines], axis=0)
     columns_grad = jnp.pad(lines_grad, ((0, LANES - lines_grad.shape[0]), (0, 0))).T
-    rest = jnp.concatenate([mix_grad_rest, columns_grad], axis=1).reshape(shards, own, -1)
-    rest_kept, rest_other = share_pair(here, rest)
-    rest_share, rest_others = share_plane(here, rest_kept, rest_other)
-    mix_share = jnp.concatenate(
-        [
-            share_sum(mix_share_one, mix_others_one),
-            share_sum(rest_share, rest_others),
-        ],
-        axis=1,
-    )
-    mix_last = column_last(here, *column_third(here, *column_second(here, *column_first(here, mix_share))))
+    whole = jnp.concatenate([mix_grad, columns_grad.astype(bf16)], axis=1).reshape(shards, own, -1)
+    mix_share, mix_lows = share_plane(here, *share_pair(here, whole))
+    mix_others = share_send(here, mix_lows)
+    input_mark = mix_others[0]
+    mix_share = share_sum(mix_share, mix_others)
+    mix_half, mix_other = column_first(here, mix_share)
+    down_half, down_other = column_third(here, *after((down_half, down_other), mix_share))
+    up_half, up_other = column_third(here, *after((up_half, up_other), mix_share))
+    mix_half, mix_other = column_second(here, mix_half, mix_other)
+    down_half, down_other, up_half, up_other = after((down_half, down_other, up_half, up_other), mix_half)
+    mix_last = column_last(here, *column_third(here, mix_half, mix_other))
 
     output = from_sequence_end(here, after(output_slots, input_low), groups)
-    final_input = from_sequence_end(here, input_slots, groups).astype(f32)
+    final_input = from_sequence_end(here, after(input_slots, input_mark), groups).astype(f32)
     final_down = column_last(here, down_half, down_other).astype(f32)
     final_up_merge = column_last(here, up_half, up_other).astype(f32)
     final_mix = mix_last[:, : 3 * width].astype(f32).reshape(own, PARTS, 3, H // PARTS, HD)

time: 557 us -> 558 us (level)
  local copies, waits for them, and re-layouts: 58.4 us -> 41.9 us
  other arithmetic: 50.1 us -> 58.8 us
  starting transfers between devices: 88.9 us -> 97.2 us
    ppermute x24, waiting for transfers between devices: 79.2 us -> 56.8 us  [across(): return lax.ppermute(values, 'seq', xor_pairs(self.columns, bits))]
    ppermute x18 -> x15, waiting for transfers between devices: 30.1 us -> 45.4 us  [aside(): return lax.ppermute(values, 'fsdp', xor_pairs(self.shards, 2 * bits))]
    ppermute x23 -> x22, starting transfers between devices: 6.58 us -> 21 us  [mate(): return lax.ppermute(values, 'fsdp', xor_pairs(self.shards, 1))]
    ppermute x18 -> x15, starting transfers between devices: 31.7 us -> 18.4 us  [aside(): return lax.ppermute(values, 'fsdp', xor_pairs(self.shards, 2 * bits))]
    convert_element_type x3 -> x1, local copies, waits for them, and re-layouts: 7.7 us -> 0.04 us  [per_device(): columns_grad.astype(bf16)]
    ppermute x24, starting transfers between devices: 50.5 us -> 57.7 us  [across(): return lax.ppermute(values, 'seq', xor_pairs(self.columns, bits))]
    convert_element_type x4 -> x2, other arithmetic: 10.3 us -> 3.52 us  [share_plane(): total(k).astype(bf16)]
    unnamed x148 -> x171, local copies, waits for them, and re-layouts: 17.6 us -> 20.3 us
  transfers between devices with their start and end apart: 65 -> 61, of which waited for: 19 -> 19; matrix products, arithmetic and copies ran while one was open for 22% -> 14% of each run, Pallas kernels for 30% -> 30%
where the time goes in v6:
time: 558 us; the launch traced here: 550 us
  Pallas kernels  166 us (30%)
  waiting for transfers between devices  107 us (19%)
  starting transfers between devices  97.2 us (17%)
  matrix products  75.8 us (14%)
  other arithmetic  58.8 us (11%)
  local copies, waits for them, and re-layouts  41.9 us (8%)
    pallas_call x3, Pallas kernels, attention_backward(): pl.pallas_call(functools.partial(backward_kernel, size=size), grid_spec=p...  96.5 us
    dot_general x16, matrix products, dot(): return jnp.dot(a, b, preferred_element_type=f32)  75.8 us
    pallas_call x3, Pallas kernels, attention_forward(): pl.pallas_call(functools.partial(forward_kernel, size=size, plan=(len(pie...  62.6 us
    ppermute x24, starting transfers between devices, across(): return lax.ppermute(values, 'seq', xor_pairs(self.columns, bits))  57.7 us
    ppermute x24, waiting for transfers between devices, across(): return lax.ppermute(values, 'seq', xor_pairs(self.columns, bits))  56.8 us
    ppermute x15, waiting for transfers between devices, aside(): return lax.ppermute(values, 'fsdp', xor_pairs(self.shards, 2 * bits))  45.4 us
    ppermute x22, starting transfers between devices, mate(): return lax.ppermute(values, 'fsdp', xor_pairs(self.shards, 1))  21 us
    unnamed x171, local copies, waits for them, and re-layouts  20.3 us
  transfers between devices with their start and end apart: 61, of which 19 were waited for; matrix products, arithmetic and copies ran while one was open for 14% of the time, Pallas kernels for 30%

profile of v6, /device:TPU:0, one launch (start us, length us, event | category | flops | bytes accessed | tf_op | source)
XLA Modules:
  0.0 549.6 jit_solution(5582448982214151016)
XLA Ops:
  0.6 5.1 collective-permute-start.3
  8.8 2.0 pack_projection.1.refs_0_
  10.8 2.6 collective-permute-start.10
  20.6 2.3 collective-permute-start.5
  26.0 2.8 collective-permute-done.10.refs_3_
  29.7 10.5 %collective-permute-done.9.refs_2_ = bf16[96,3200]{1,0:T(8,128)(2,1)} collective-permute-done((bf16[96,3200]{1,0:T(8,128)(2,1)}, bf16[96,3200]{1,0:T(8,128)(2,1)}, u32[]{:S(2)}, u32[]{:S(2)}) %collective-permute-start.9) | collective-permute-done | bytes 614432 | tf_op jit(solution)/shard_map/ppermute | solution.py:426
  40.3 10.0 %collective-permute-done.5 = bf16[256,768]{1,0:T(8,128)(2,1)S(1)} collective-permute-done((bf16[256,768]{1,0:T(8,128)(2,1)S(1)}, bf16[256,768]{1,0:T(8,128)(2,1)S(1)}, u32[]{:S(2)}, u32[]{:S(2)}) %collective-permute-start.5) | collective-permute-done | bytes 393248 | tf_op jit(solution)/shard_map/ppermute | solution.py:423
  53.1 8.2 %collective-permute-start.4 = (bf16[256,768]{1,0:T(8,128)(2,1)}, bf16[256,768]{1,0:T(8,128)(2,1)}, u32[]{:S(2)}, u32[]{:S(2)}) collective-permute-start(bf16[256,768]{1,0:T(8,128)(2,1)} %get-tuple-element.167), channel_id=1, source_target_pairs={{0,8},{8,0},{16,24},{24,16},{1,9},{9,1},{17,25},{25,17},{2,10},{10... | collective-permute-start | bytes 1179656 | tf_op jit(solution)/shard_map/ppermute | solution.py:423
  63.4 5.2 place_parts.1
  77.5 2.7 collective-permute-start.22
  81.1 3.6 collective-permute-start.19
  84.7 20.7 %attention_forward.3 = (bf16[1024,256]{1,0:T(8,128)(2,1)}, bf16[1024,256]{1,0:T(8,128)(2,1)}) custom-call(s32[10]{0:T(128)} %pad_add_fusion.3.info, bf16[1024,768]{1,0:T(8,128)(2,1)} %copy-done.1, bf16[1024,768]{1,0:T(8,128)(2,1)} %copy-done.1, bf16[1024,768]{1,0:T(8,128)(2,1)} %copy-done.4, bf16[1024,768]{1,0:T(8,128)(2,1)} %copy-done.1, ...), custom_call_target="tpu_custom_call" | custom-call | flops 1073741824 | bytes 4194304 | tf_op jit(solution)/shard_map/attention_forward/pallas_call | solution.py:176
  105.4 20.5 %attention_forward.4 = (bf16[1024,256]{1,0:T(8,128)(2,1)}, bf16[1024,256]{1,0:T(8,128)(2,1)}) custom-call(s32[10]{0:T(128)} %pad_add_fusion.3.info, bf16[1024,768]{1,0:T(8,128)(2,1)} %copy-done, bf16[1024,768]{1,0:T(8,128)(2,1)} %copy-done, bf16[1024,768]{1,0:T(8,128)(2,1)} %copy-done.3, bf16[1024,768]{1,0:T(8,128)(2,1)} %copy-done, ...), custom_call_target="tpu_custom_call" | custom-call | flops 1073741824 | bytes 4194304 | tf_op jit(solution)/shard_map/attention_forward/pallas_call | solution.py:176
  126.0 6.0 %collective-permute-done.21.refs_2_ = bf16[768,768]{1,0:T(8,128)(2,1)} collective-permute-done((bf16[768,768]{1,0:T(8,128)(2,1)S(1)}, bf16[768,768]{1,0:T(8,128)(2,1)}, u32[]{:S(2)}, u32[]{:S(2)}) %collective-permute-start.21) | collective-permute-done | bytes 1179680 | tf_op jit(solution)/shard_map/ppermute | solution.py:426
  132.2 2.8 collective-permute-start.23
  138.5 2.9 collective-permute-start.28
  145.7 21.4 %attention_forward.5 = (bf16[1024,256]{1,0:T(8,128)(2,1)}, bf16[1024,256]{1,0:T(8,128)(2,1)}, bf16[8,96,3072]{2,1,0:T(8,128)(2,1)}, bf16[8,384,768]{2,1,0:T(8,128)(2,1)}) custom-call(s32[18]{0:T(128)} %concatenate.87.info, bf16[1024,768]{1,0:T(8,128)(2,1)} %copy-done.2, bf16[1024,768]{1,0:T(8,128)(2,1)} %copy-done.2, ...), custom_call_target="tpu_custom_call" | custom-call | flops 1073741824 | bytes 4194304 | tf_op jit(solution)/shard_map/attention_forward/pallas_call | solution.py:176
  167.1 2.2 constant_dynamic-update-slice_fusion.5
  169.4 3.9 fusion.61
  174.0 14.1 %fusion.4 = (bf16[1024,3072]{1,0:T(8,128)(2,1)}, bf16[1024,3072]{1,0:T(8,128)(2,1)S(1)}) fusion(f32[3072]{0:T(1024)S(1)} %copy-done.55, bf16[768,3072]{1,0:T(8,128)(2,1)S(1)} %bitcast.302, f32[1024,768]{1,0:T(8,128)S(1)} %get-tuple-element.505, f32[768]{0:T(1024)S(1)} %copy-done.58, f32[768]{0:T(1024)S(1)} %get-tuple-element.403, ...), kind=kOutput, calls=%fused_computation.5 | convolution fusion | flops 4873519104 | bytes 20473856 | tf_op jit(solution)/shard_map/dot_general | solution.py:387
  188.1 5.4 fusion.62
  194.8 4.9 fusion.11
  199.7 2.9 convert_reduce_fusion.2
  202.6 5.6 %convolution_convert_fusion.1 = bf16[3072,768]{1,0:T(8,128)(2,1)S(1)} fusion(bf16[1024,3072]{1,0:T(8,128)(2,1)S(1)} %get-tuple-element.229, f32[1024,768]{1,0:T(8,128)S(1)} %get-tuple-element.414), kind=kOutput, calls=%fused_computation.20 | convolution fusion | flops 4834983936 | bytes 14155776 | tf_op jit(solution)/shard_map/dot_general | solution.py:387
  208.3 2.1 copy-done.11
  212.0 5.0 collective-permute-start.29
  217.0 9.4 %multiply_convert_fusion = bf16[1024,3072]{1,0:T(8,128)(2,1)S(1)} fusion(bf16[1024,3072]{1,0:T(8,128)(2,1)} %get-tuple-element.243, bf16[3072,768]{1,0:T(8,128)(2,1)} %bitcast.303, f32[1024,768]{1,0:T(8,128)} %copy-done.20), kind=kOutput, calls=%fused_computation.6 | convolution fusion | flops 4842061824 | bytes 20447232 | tf_op jit(solution)/shard_map/dot_general | solution.py:387
  226.5 5.5 convert_add_fusion.4
  231.9 8.9 %multiply_reduce_fusion = (bf16[768]{0:T(1024)(128)(2,1)}, f32[1024]{0:T(1024)S(1)}, f32[1024]{0:T(1024)S(1)}, bf16[768]{0:T(1024)(128)(2,1)}, f32[1024,768]{1,0:T(8,128)S(1)}) fusion(f32[1024,768]{1,0:T(8,128)S(1)} %get-tuple-element.505, f32[1024]{0:T(1024)S(1)} %add_rsqrt_fusion.1, f32[1024]{0:T(1024)S(1)} %broadcast_multiply_fusion.5, ...), kind=kOutput, calls=%fused_computation.32 | convolution fusion | flops 4839698432 | bytes 20469760 | tf_op jit(solution)/shard_map/dot_general | solution.py:387
  240.9 6.3 %convolution_convert_fusion = bf16[768,3072]{1,0:T(8,128)(2,1)S(1)} fusion(bf16[1024,3072]{1,0:T(8,128)(2,1)S(1)} %multiply_convert_fusion, f32[1024,768]{1,0:T(8,128)S(1)} %get-tuple-element.505, f32[768]{0:T(1024)S(1)} %copy-done.59, f32[768]{0:T(1024)S(1)} %get-tuple-element.403, f32[1024]{0:T(1024)S(1)} %add_rsqrt_fusion.1, ...), kind=kOutput, calls=%fused_computation.19 | convolution fusion | flops 4838129664 | bytes 14170112 | tf_op jit(solution)/shard_map/dot_general | solution.py:387
  247.3 2.5 fusion.53
  249.8 12.7 %collective-permute-done.30 = bf16[384,768]{1,0:T(8,128)(2,1)S(1)} collective-permute-done((bf16[384,768]{1,0:T(8,128)(2,1)S(1)}, bf16[384,768]{1,0:T(8,128)(2,1)S(1)}, u32[]{:S(2)}, u32[]{:S(2)}) %collective-permute-start.30) | collective-permute-done | bytes 589856 | tf_op jit(solution)/shard_map/ppermute | solution.py:426
  266.1 2.7 convolution_convert_fusion.3.do_ref
  270.5 1.8 fusion.15
  280.4 1.8 collective-permute-start.34
  283.0 9.0 %collective-permute-done.36 = bf16[96,3840]{1,0:T(8,128)(2,1)} collective-permute-done((bf16[96,3840]{1,0:T(8,128)(2,1)}, bf16[96,3840]{1,0:T(8,128)(2,1)}, u32[]{:S(2)}, u32[]{:S(2)}) %collective-permute-start.36) | collective-permute-done | bytes 737312 | tf_op jit(solution)/shard_map/ppermute | solution.py:426
  293.5 3.8 reduce.6
  297.9 32.0 %attention_backward.3 = (bf16[1024,256]{1,0:T(8,128)(2,1)}, f32[2,1024,256]{2,1,0:T(8,128)}, bf16[2,1024,256]{2,1,0:T(8,128)(2,1)}) custom-call(s32[10]{0:T(128)} %pad_add_fusion.3.info, bf16[1024,768]{1,0:T(8,128)(2,1)} %copy-done.1, bf16[1024,256]{1,0:T(8,128)(2,1)} %get-tuple-element.231.ext_ref, bf16[1024,768]{1,0:T(8,128)(2,1)} %convolution_convert_fusion.3.do_ref, ...), custom_call_target="tpu_custom_call" | custom-call | flops 2684354560 | bytes 6291456 | tf_op jit(solution)/shard_map/attention_backward/pallas_call | solution.py:299
  329.9 1.8 add_convert_fusion.6
  332.5 2.0 collective-permute-start.32
  334.5 8.6 %collective-permute-start.33 = (bf16[256,768]{1,0:T(8,128)(2,1)}, bf16[256,768]{1,0:T(8,128)(2,1)}, u32[]{:S(2)}, u32[]{:S(2)}) collective-permute-start(bf16[256,768]{1,0:T(8,128)(2,1)} %get-tuple-element.253), channel_id=1, source_target_pairs={{0,16},{8,24},{16,0},{24,8},{1,17},{9,25},{17,1},{25,9},{2,18},{10... | collective-permute-start | bytes 1179656 | tf_op jit(solution)/shard_map/ppermute | solution.py:423
  343.4 1.9 add_convert_fusion.5
  345.4 1.8 collective-permute-start.39
  347.2 32.5 %attention_backward.4 = (bf16[1024,256]{1,0:T(8,128)(2,1)}, f32[2,1024,256]{2,1,0:T(8,128)}, bf16[2,1024,256]{2,1,0:T(8,128)(2,1)}) custom-call(s32[10]{0:T(128)} %pad_add_fusion.3.info, bf16[1024,768]{1,0:T(8,128)(2,1)} %copy-done, bf16[1024,256]{1,0:T(8,128)(2,1)} %get-tuple-element.263.ext_ref, bf16[1024,768]{1,0:T(8,128)(2,1)} %convolution_convert_fusion.3.do_ref, ...), custom_call_target="tpu_custom_call" | custom-call | flops 2684354560 | bytes 6291456 | tf_op jit(solution)/shard_map/attention_backward/pallas_call | solution.py:299
  379.7 1.7 add_convert_fusion.10
  381.5 9.2 %collective-permute-start.44 = (bf16[192,768]{1,0:T(8,128)(2,1)}, bf16[192,768]{1,0:T(8,128)(2,1)}, u32[]{:S(2)}, u32[]{:S(2)}) collective-permute-start(bf16[192,768]{1,0:T(8,128)(2,1)} %add_convert_fusion.10), channel_id=1, source_target_pairs={{0,16},{8,24},{16,0},{24,8},{1,17},{9,25},{17,1},{25,9},{2,18},{10... | collective-permute-start | bytes 884744 | tf_op jit(solution)/shard_map/ppermute | solution.py:423
  391.8 2.1 collective-permute-start.45
  395.5 3.1 convolution_add_fusion.1
  398.6 32.0 %attention_backward.5 = (bf16[1024,256]{1,0:T(8,128)(2,1)}, f32[2,1024,256]{2,1,0:T(8,128)}, bf16[2,1024,256]{2,1,0:T(8,128)(2,1)}) custom-call(s32[10]{0:T(128)} %pad_add_fusion.3.info, bf16[1024,768]{1,0:T(8,128)(2,1)} %copy-done.2, bf16[1024,256]{1,0:T(8,128)(2,1)} %get-tuple-element.284.ext_ref, bf16[1024,768]{1,0:T(8,128)(2,1)} %convolution_convert_fusion.3.do_ref, ...), custom_call_target="tpu_custom_call" | custom-call | flops 2684354560 | bytes 6291456 | tf_op jit(solution)/shard_map/attention_backward/pallas_call | solution.py:299
  430.7 8.9 %collective-permute-start.46 = (bf16[2,1024,256]{2,1,0:T(8,128)(2,1)}, bf16[2,1024,256]{2,1,0:T(8,128)(2,1)S(1)}, u32[]{:S(2)}, u32[]{:S(2)}) collective-permute-start(bf16[2,1024,256]{2,1,0:T(8,128)(2,1)} %get-tuple-element.291), channel_id=1, source_target_pairs={{0,1},{1,0},{2,3},{3,2},{4,5},{5,4},{6,7},{7,6},{8,9},{9,8},{10,11... | collective-permute-start | bytes 3145736 | tf_op jit(solution)/shard_map/ppermute | solution.py:420
  448.5 2.6 add_convert_fusion
  454.3 6.6 %convolution_convert_fusion.2 = bf16[768,2304]{1,0:T(8,128)(2,1)S(1)} fusion(bf16[1024,768]{1,0:T(8,128)(2,1)S(1)} %copy-done.51, bf16[1024,2304]{1,0:T(8,128)(2,1)} %constant_dynamic-update-slice_fusion.8), kind=kOutput, calls=%fused_computation.21 | convolution fusion | flops 3625648128 | bytes 9830400 | tf_op jit(solution)/shard_map/dot_general | solution.py:387
  461.2 1.8 copy-done.5
  471.0 3.1 collective-permute-start.50
  476.8 3.0 collective-permute-start.54
  479.8 4.0 collective-permute-done.52
  483.8 2.4 collective-permute-start.55
  487.5 20.5 %collective-permute-done.49 = bf16[256,768]{1,0:T(8,128)(2,1)S(1)} collective-permute-done((bf16[256,768]{1,0:T(8,128)(2,1)S(1)}, bf16[256,768]{1,0:T(8,128)(2,1)S(1)}, u32[]{:S(2)}, u32[]{:S(2)}) %collective-permute-start.49) | collective-permute-done | bytes 393248 | tf_op jit(solution)/shard_map/ppermute | solution.py:423
  511.1 2.1 collective-permute-start.59
  514.3 4.2 collective-permute-done.56
  519.6 1.9 maximum_convert_fusion
  521.5 8.3 %collective-permute-done.59 = bf16[192,768]{1,0:T(8,128)(2,1)S(1)} collective-permute-done((bf16[192,768]{1,0:T(8,128)(2,1)S(1)}, bf16[192,768]{1,0:T(8,128)(2,1)S(1)}, u32[]{:S(2)}, u32[]{:S(2)}) %collective-permute-start.59) | collective-permute-done | bytes 294944 | tf_op jit(solution)/shard_map/ppermute | solution.py:423
  529.8 7.4 %collective-permute-done.60 = bf16[48,3840]{1,0:T(8,128)(2,1)S(1)} collective-permute-done((bf16[48,3840]{1,0:T(8,128)(2,1)S(1)}, bf16[48,3840]{1,0:T(8,128)(2,1)S(1)}, u32[]{:S(2)}, u32[]{:S(2)}) %collective-permute-start.60) | collective-permute-done | bytes 368672 | tf_op jit(solution)/shard_map/ppermute | solution.py:423
  540.4 5.4 collective-permute-done.58
  (396 shorter events, 96.4 us)
Async XLA Ops:
  0.6 15.4 %collective-permute-start.3 = (s32[2,512]{1,0:T(2,128)}, s32[2,512]{1,0:T(2,128)S(1)}, u32[]{:S(2)}, u32[]{:S(2)}) collective-permute-start(s32[2,512]{1,0:T(2,128)} %param.17), channel_id=1, source_target_pairs={{0,24},{8,16},{16,8},{24,0},{1,25},{9,17},{17,9},{25,1},{2,26},{10... | collective-permute-start | bytes 12296 | tf_op jit(solution)/shard_map/ppermute | solution.py:423
  5.8 10.8 %collective-permute-start.2 = (s32[2,512]{1,0:T(2,128)}, s32[2,512]{1,0:T(2,128)S(1)}, u32[]{:S(2)}, u32[]{:S(2)}) collective-permute-start(s32[2,512]{1,0:T(2,128)} %param.17), channel_id=1, source_target_pairs={{0,16},{8,24},{16,0},{24,8},{1,17},{9,25},{17,1},{25,9},{2,18},{10... | collective-permute-start | bytes 12296 | tf_op jit(solution)/shard_map/ppermute | solution.py:423
  5.8 10.9 %collective-permute-start.1 = (s32[2,512]{1,0:T(2,128)}, s32[2,512]{1,0:T(2,128)S(1)}, u32[]{:S(2)}, u32[]{:S(2)}) collective-permute-start(s32[2,512]{1,0:T(2,128)} %param.17), channel_id=1, source_target_pairs={{0,8},{8,0},{16,24},{24,16},{1,9},{9,1},{17,25},{25,17},{2,10},{10... | collective-permute-start | bytes 12296 | tf_op jit(solution)/shard_map/ppermute | solution.py:423
  10.8 18.0 %collective-permute-start.10 = (bf16[96,3200]{1,0:T(8,128)(2,1)}, bf16[96,3200]{1,0:T(8,128)(2,1)}, u32[]{:S(2)}, u32[]{:S(2)}) collective-permute-start(bf16[96,3200]{1,0:T(8,128)(2,1)} %pack_projection.1.refs_0_), channel_id=1, source_target_pairs={{0,6},{1,7},{2,4},{3,5},{4,2},{5,3},{6,0},{7,1},{8,14},{9,15},{10,... | collective-permute-start | bytes 1843208 | tf_op jit(solution)/shard_map/ppermute | solution.py:426
  13.4 26.8 %collective-permute-start.9 = (bf16[96,3200]{1,0:T(8,128)(2,1)}, bf16[96,3200]{1,0:T(8,128)(2,1)}, u32[]{:S(2)}, u32[]{:S(2)}) collective-permute-start(bf16[96,3200]{1,0:T(8,128)(2,1)} %pack_projection.1.refs_0_), channel_id=1, source_target_pairs={{0,4},{1,5},{2,6},{3,7},{4,0},{5,1},{6,2},{7,3},{8,12},{9,13},{10,... | collective-permute-start | bytes 1843208 | tf_op jit(solution)/shard_map/ppermute | solution.py:426
  16.1 24.2 %collective-permute-start.8 = (bf16[96,3200]{1,0:T(8,128)(2,1)S(1)}, bf16[96,3200]{1,0:T(8,128)(2,1)}, u32[]{:S(2)}, u32[]{:S(2)}) collective-permute-start(bf16[96,3200]{1,0:T(8,128)(2,1)S(1)} %copy-done.22), channel_id=1, source_target_pairs={{0,2},{1,3},{2,0},{3,1},{4,6},{5,7},{6,4},{7,5},{8,10},{9,11},{10,... | collective-permute-start | bytes 1843208 | tf_op jit(solution)/shard_map/ppermute | solution.py:426
  16.6 3.1 collective-permute-start
  16.7 2.2 collective-permute-start.15
  20.6 29.7 %collective-permute-start.5 = (bf16[256,768]{1,0:T(8,128)(2,1)S(1)}, bf16[256,768]{1,0:T(8,128)(2,1)S(1)}, u32[]{:S(2)}, u32[]{:S(2)}) collective-permute-start(bf16[256,768]{1,0:T(8,128)(2,1)S(1)} %get-tuple-element.168), channel_id=1, source_target_pairs={{0,16},{8,24},{16,0},{24,8},{1,17},{9,25},{17,1},{25,9},{2,18},{10... | collective-permute-start | bytes 1179656 | tf_op jit(solution)/shard_map/ppermute | solution.py:423
  22.9 27.5 %collective-permute-start.6 = (bf16[256,768]{1,0:T(8,128)(2,1)S(1)}, bf16[256,768]{1,0:T(8,128)(2,1)S(1)}, u32[]{:S(2)}, u32[]{:S(2)}) collective-permute-start(bf16[256,768]{1,0:T(8,128)(2,1)S(1)} %get-tuple-element.169), channel_id=1, source_target_pairs={{0,24},{8,16},{16,8},{24,0},{1,25},{9,17},{17,9},{25,1},{2,26},{10... | collective-permute-start | bytes 1179656 | tf_op jit(solution)/shard_map/ppermute | solution.py:423
  28.8 24.3 %collective-permute-start.7 = (bf16[2,256,768]{2,1,0:T(8,128)(2,1)S(1)}, bf16[2,256,768]{2,1,0:T(8,128)(2,1)S(1)}, u32[]{:S(2)}, u32[]{:S(2)}) collective-permute-start(bf16[2,256,768]{2,1,0:T(8,128)(2,1)S(1)} %get-tuple-element.456), channel_id=1, source_target_pairs={{0,1},{1,0},{2,3},{3,2},{4,5},{5,4},{6,7},{7,6},{8,9},{9,8},{10,11... | collective-permute-start | bytes 2359304 | tf_op jit(solution)/shard_map/ppermute | solution.py:420
  50.3 12.0 %collective-permute-start.11 = (bf16[96,3200]{1,0:T(8,128)(2,1)S(1)}, bf16[96,3200]{1,0:T(8,128)(2,1)S(1)}, u32[]{:S(2)}, u32[]{:S(2)}) collective-permute-start(bf16[96,3200]{1,0:T(8,128)(2,1)S(1)} %copy-done.22), channel_id=1, source_target_pairs={{0,1},{1,0},{2,3},{3,2},{4,5},{5,4},{6,7},{7,6},{8,9},{9,8},{10,11... | collective-permute-start | bytes 1843208 | tf_op jit(solution)/shard_map/ppermute | solution.py:420
  50.3 12.0 %collective-permute-start.12 = (bf16[96,3200]{1,0:T(8,128)(2,1)}, bf16[96,3200]{1,0:T(8,128)(2,1)S(1)}, u32[]{:S(2)}, u32[]{:S(2)}) collective-permute-start(bf16[96,3200]{1,0:T(8,128)(2,1)} %collective-permute-done.8.refs_1_), channel_id=1, source_target_pairs={{0,1},{1,0},{2,3},{3,2},{4,5},{5,4},{6,7},{7,6},{8,9},{9,8},{10,11... | collective-permute-start | bytes 1843208 | tf_op jit(solution)/shard_map/ppermute | solution.py:420
  50.8 11.6 %collective-permute-start.13 = (bf16[96,3200]{1,0:T(8,128)(2,1)}, bf16[96,3200]{1,0:T(8,128)(2,1)}, u32[]{:S(2)}, u32[]{:S(2)}) collective-permute-start(bf16[96,3200]{1,0:T(8,128)(2,1)} %collective-permute-done.9.refs_2_), channel_id=1, source_target_pairs={{0,1},{1,0},{2,3},{3,2},{4,5},{5,4},{6,7},{7,6},{8,9},{9,8},{10,11... | collective-permute-start | bytes 1843208 | tf_op jit(solution)/shard_map/ppermute | solution.py:420
  50.9 11.5 %collective-permute-start.14 = (bf16[96,3200]{1,0:T(8,128)(2,1)}, bf16[96,3200]{1,0:T(8,128)(2,1)}, u32[]{:S(2)}, u32[]{:S(2)}) collective-permute-start(bf16[96,3200]{1,0:T(8,128)(2,1)} %collective-permute-done.10.refs_3_), channel_id=1, source_target_pairs={{0,1},{1,0},{2,3},{3,2},{4,5},{5,4},{6,7},{7,6},{8,9},{9,8},{10,11... | collective-permute-start | bytes 1843208 | tf_op jit(solution)/shard_map/ppermute | solution.py:420
  53.1 17.8 %collective-permute-start.4 = (bf16[256,768]{1,0:T(8,128)(2,1)}, bf16[256,768]{1,0:T(8,128)(2,1)}, u32[]{:S(2)}, u32[]{:S(2)}) collective-permute-start(bf16[256,768]{1,0:T(8,128)(2,1)} %get-tuple-element.167), channel_id=1, source_target_pairs={{0,8},{8,0},{16,24},{24,16},{1,9},{9,1},{17,25},{25,17},{2,10},{10... | collective-permute-start | bytes 1179656 | tf_op jit(solution)/shard_map/ppermute | solution.py:423
  73.5 7.2 %collective-permute-start.16 = (bf16[1024,768]{1,0:T(8,128)(2,1)S(1)}, bf16[1024,768]{1,0:T(8,128)(2,1)S(1)}, u32[]{:S(2)}, u32[]{:S(2)}) collective-permute-start(bf16[1024,768]{1,0:T(8,128)(2,1)S(1)} %multiply_convert_fusion.4.q_ref.k_own.v_own), channel_id=1, source_target_pairs={{0,1},{1,0},{2,3},{3,2},{4,5},{5,4},{6,7},{7,6},{8,9},{9,8},{10,11... | collective-permute-start | bytes 4718600 | tf_op jit(solution)/shard_map/ppermute | solution.py:420
  75.3 5.8 %collective-permute-start.17 = (bf16[1024,768]{1,0:T(8,128)(2,1)S(1)}, bf16[1024,768]{1,0:T(8,128)(2,1)S(1)}, u32[]{:S(2)}, u32[]{:S(2)}) collective-permute-start(bf16[1024,768]{1,0:T(8,128)(2,1)S(1)} %multiply_convert_fusion.3.q_ref.k_own.v_own), channel_id=1, source_target_pairs={{0,1},{1,0},{2,3},{3,2},{4,5},{5,4},{6,7},{7,6},{8,9},{9,8},{10,11... | collective-permute-start | bytes 4718600 | tf_op jit(solution)/shard_map/ppermute | solution.py:420
  77.0 7.6 %collective-permute-start.18 = (bf16[1024,768]{1,0:T(8,128)(2,1)S(1)}, bf16[1024,768]{1,0:T(8,128)(2,1)}, u32[]{:S(2)}, u32[]{:S(2)}) collective-permute-start(bf16[1024,768]{1,0:T(8,128)(2,1)S(1)} %multiply_convert_fusion.2.q_ref.k_own.v_own), channel_id=1, source_target_pairs={{0,1},{1,0},{2,3},{3,2},{4,5},{5,4},{6,7},{7,6},{8,9},{9,8},{10,11... | collective-permute-start | bytes 4718600 | tf_op jit(solution)/shard_map/ppermute | solution.py:420
  77.5 67.0 %copy-start.35 = (bf16[768,768]{1,0:T(8,128)(2,1)}, bf16[768,768]{1,0:T(8,128)(2,1)S(1)}, u32[]{:S(2)}) copy-start(bf16[768,768]{1,0:T(8,128)(2,1)S(1)} %constant_dynamic-update-slice_fusion.4.refs_0_) | copy-start | bytes 3538948
  77.5 48.4 %collective-permute-start.22 = (bf16[768,768]{1,0:T(8,128)(2,1)S(1)}, bf16[768,768]{1,0:T(8,128)(2,1)}, u32[]{:S(2)}, u32[]{:S(2)}) collective-permute-start(bf16[768,768]{1,0:T(8,128)(2,1)S(1)} %constant_dynamic-update-slice_fusion.4.refs_0_), channel_id=1, source_target_pairs={{0,6},{1,7},{2,4},{3,5},{4,2},{5,3},{6,0},{7,1},{8,14},{9,15},{10,... | collective-permute-start | bytes 3538952 | tf_op jit(solution)/shard_map/ppermute | solution.py:426
  80.2 51.8 %collective-permute-start.21 = (bf16[768,768]{1,0:T(8,128)(2,1)S(1)}, bf16[768,768]{1,0:T(8,128)(2,1)}, u32[]{:S(2)}, u32[]{:S(2)}) collective-permute-start(bf16[768,768]{1,0:T(8,128)(2,1)S(1)} %constant_dynamic-update-slice_fusion.4.refs_0_), channel_id=1, source_target_pairs={{0,4},{1,5},{2,6},{3,7},{4,0},{5,1},{6,2},{7,3},{8,12},{9,13},{10,... | collective-permute-start | bytes 3538952 | tf_op jit(solution)/shard_map/ppermute | solution.py:426
  80.7 51.5 %collective-permute-start.20 = (bf16[768,768]{1,0:T(8,128)(2,1)S(1)}, bf16[768,768]{1,0:T(8,128)(2,1)}, u32[]{:S(2)}, u32[]{:S(2)}) collective-permute-start(bf16[768,768]{1,0:T(8,128)(2,1)S(1)} %constant_dynamic-update-slice_fusion.4.refs_0_), channel_id=1, source_target_pairs={{0,2},{1,3},{2,0},{3,1},{4,6},{5,7},{6,4},{7,5},{8,10},{9,11},{10,... | collective-permute-start | bytes 3538952 | tf_op jit(solution)/shard_map/ppermute | solution.py:426
  81.1 24.3 %collective-permute-start.19 = (bf16[256,768]{1,0:T(8,128)(2,1)}, bf16[256,768]{1,0:T(8,128)(2,1)S(1)}, u32[]{:S(2)}, u32[]{:S(2)}) collective-permute-start(bf16[256,768]{1,0:T(8,128)(2,1)} %get-tuple-element.211), channel_id=1, source_target_pairs={{0,16},{8,24},{16,0},{24,8},{1,17},{9,25},{17,1},{25,9},{2,18},{10... | collective-permute-start | bytes 1179656 | tf_op jit(solution)/shard_map/ppermute | solution.py:423
  132.2 5.2 collective-permute-start.23
  135.0 9.6 %collective-permute-start.24 = (bf16[768,768]{1,0:T(8,128)(2,1)}, bf16[768,768]{1,0:T(8,128)(2,1)}, u32[]{:S(2)}, u32[]{:S(2)}) collective-permute-start(bf16[768,768]{1,0:T(8,128)(2,1)} %collective-permute-done.20.refs_1_), channel_id=1, source_target_pairs={{0,1},{1,0},{2,3},{3,2},{4,5},{5,4},{6,7},{7,6},{8,9},{9,8},{10,11... | collective-permute-start | bytes 3538952 | tf_op jit(solution)/shard_map/ppermute | solution.py:420
  135.0 10.6 %collective-permute-start.25 = (bf16[768,768]{1,0:T(8,128)(2,1)}, bf16[768,768]{1,0:T(8,128)(2,1)}, u32[]{:S(2)}, u32[]{:S(2)}) collective-permute-start(bf16[768,768]{1,0:T(8,128)(2,1)} %collective-permute-done.21.refs_2_), channel_id=1, source_target_pairs={{0,1},{1,0},{2,3},{3,2},{4,5},{5,4},{6,7},{7,6},{8,9},{9,8},{10,11... | collective-permute-start | bytes 3538952 | tf_op jit(solution)/shard_map/ppermute | solution.py:420
  135.5 10.2 %collective-permute-start.26 = (bf16[768,768]{1,0:T(8,128)(2,1)}, bf16[768,768]{1,0:T(8,128)(2,1)}, u32[]{:S(2)}, u32[]{:S(2)}) collective-permute-start(bf16[768,768]{1,0:T(8,128)(2,1)} %collective-permute-done.22.refs_3_), channel_id=1, source_target_pairs={{0,1},{1,0},{2,3},{3,2},{4,5},{5,4},{6,7},{7,6},{8,9},{9,8},{10,11... | collective-permute-start | bytes 3538952 | tf_op jit(solution)/shard_map/ppermute | solution.py:420
  135.5 31.5 %collective-permute-start.27 = (bf16[256,768]{1,0:T(8,128)(2,1)}, bf16[256,768]{1,0:T(8,128)(2,1)S(1)}, u32[]{:S(2)}, u32[]{:S(2)}) collective-permute-start(bf16[256,768]{1,0:T(8,128)(2,1)} %get-tuple-element.236), channel_id=1, source_target_pairs={{0,8},{8,0},{16,24},{24,16},{1,9},{9,1},{17,25},{25,17},{2,10},{10... | collective-permute-start | bytes 1179656 | tf_op jit(solution)/shard_map/ppermute | solution.py:423
  138.5 28.6 %collective-permute-start.28 = (bf16[256,768]{1,0:T(8,128)(2,1)}, bf16[256,768]{1,0:T(8,128)(2,1)S(1)}, u32[]{:S(2)}, u32[]{:S(2)}) collective-permute-start(bf16[256,768]{1,0:T(8,128)(2,1)} %get-tuple-element.238), channel_id=1, source_target_pairs={{0,24},{8,16},{16,8},{24,0},{1,25},{9,17},{17,9},{25,1},{2,26},{10... | collective-permute-start | bytes 1179656 | tf_op jit(solution)/shard_map/ppermute | solution.py:423
  212.0 14.4 %collective-permute-start.29 = (bf16[4,384,768]{2,1,0:T(8,128)(2,1)}, bf16[4,384,768]{2,1,0:T(8,128)(2,1)}, u32[]{:S(2)}, u32[]{:S(2)}) collective-permute-start(bf16[4,384,768]{2,1,0:T(8,128)(2,1)} %dynamic-slice_bitcast_fusion), channel_id=1, source_target_pairs={{0,1},{1,0},{2,3},{3,2},{4,5},{5,4},{6,7},{7,6},{8,9},{9,8},{10,11... | collective-permute-start | bytes 7077896 | tf_op jit(solution)/shard_map/ppermute | solution.py:420
  247.2 15.3 %collective-permute-start.30 = (bf16[384,768]{1,0:T(8,128)(2,1)S(1)}, bf16[384,768]{1,0:T(8,128)(2,1)S(1)}, u32[]{:S(2)}, u32[]{:S(2)}) collective-permute-start(bf16[384,768]{1,0:T(8,128)(2,1)S(1)} %get-tuple-element.246), channel_id=1, source_target_pairs={{0,2},{1,3},{2,0},{3,1},{4,6},{5,7},{6,4},{7,5},{8,10},{9,11},{10,... | collective-permute-start | bytes 1769480 | tf_op jit(solution)/shard_map/ppermute | solution.py:426
  265.1 5.4 collective-permute-start.31
  272.4 19.7 %collective-permute-start.36 = (bf16[96,3840]{1,0:T(8,128)(2,1)}, bf16[96,3840]{1,0:T(8,128)(2,1)}, u32[]{:S(2)}, u32[]{:S(2)}) collective-permute-start(bf16[96,3840]{1,0:T(8,128)(2,1)} %get-tuple-element.421), channel_id=1, source_target_pairs={{0,2},{1,3},{2,0},{3,1},{4,6},{5,7},{6,4},{7,5},{8,10},{9,11},{10,... | collective-permute-start | bytes 2211848 | tf_op jit(solution)/shard_map/ppermute | solution.py:426
  272.7 57.2 %collective-permute-start.40 = (bf16[384,768]{1,0:T(8,128)(2,1)}, bf16[384,768]{1,0:T(8,128)(2,1)}, u32[]{:S(2)}, u32[]{:S(2)}) collective-permute-start(bf16[384,768]{1,0:T(8,128)(2,1)} %get-tuple-element.266), channel_id=1, source_target_pairs={{0,4},{1,5},{2,6},{3,7},{4,0},{5,1},{6,2},{7,3},{8,12},{9,13},{10,... | collective-permute-start | bytes 1769480 | tf_op jit(solution)/shard_map/ppermute | solution.py:426
  274.3 55.5 %collective-permute-start.41 = (bf16[384,768]{1,0:T(8,128)(2,1)}, bf16[384,768]{1,0:T(8,128)(2,1)}, u32[]{:S(2)}, u32[]{:S(2)}) collective-permute-start(bf16[384,768]{1,0:T(8,128)(2,1)} %get-tuple-element.268), channel_id=1, source_target_pairs={{0,6},{1,7},{2,4},{3,5},{4,2},{5,3},{6,0},{7,1},{8,14},{9,15},{10,... | collective-permute-start | bytes 1769480 | tf_op jit(solution)/shard_map/ppermute | solution.py:426
  280.4 49.5 %collective-permute-start.34 = (bf16[256,768]{1,0:T(8,128)(2,1)}, bf16[256,768]{1,0:T(8,128)(2,1)S(1)}, u32[]{:S(2)}, u32[]{:S(2)}) collective-permute-start(bf16[256,768]{1,0:T(8,128)(2,1)} %get-tuple-element.447), channel_id=1, source_target_pairs={{0,24},{8,16},{16,8},{24,0},{1,25},{9,17},{17,9},{25,1},{2,26},{10... | collective-permute-start | bytes 1179656 | tf_op jit(solution)/shard_map/ppermute | solution.py:423
  282.2 60.9 %collective-permute-start.37 = (bf16[96,3840]{1,0:T(8,128)(2,1)}, bf16[96,3840]{1,0:T(8,128)(2,1)}, u32[]{:S(2)}, u32[]{:S(2)}) collective-permute-start(bf16[96,3840]{1,0:T(8,128)(2,1)} %get-tuple-element.420), channel_id=1, source_target_pairs={{0,4},{1,5},{2,6},{3,7},{4,0},{5,1},{6,2},{7,3},{8,12},{9,13},{10,... | collective-permute-start | bytes 2211848 | tf_op jit(solution)/shard_map/ppermute | solution.py:426
  292.1 51.4 %collective-permute-start.38 = (bf16[96,3840]{1,0:T(8,128)(2,1)}, bf16[96,3840]{1,0:T(8,128)(2,1)}, u32[]{:S(2)}, u32[]{:S(2)}) collective-permute-start(bf16[96,3840]{1,0:T(8,128)(2,1)} %get-tuple-element.258), channel_id=1, source_target_pairs={{0,6},{1,7},{2,4},{3,5},{4,2},{5,3},{6,0},{7,1},{8,14},{9,15},{10,... | collective-permute-start | bytes 2211848 | tf_op jit(solution)/shard_map/ppermute | solution.py:426
  332.5 47.2 %collective-permute-start.43 = (bf16[192,768]{1,0:T(8,128)(2,1)}, bf16[192,768]{1,0:T(8,128)(2,1)}, u32[]{:S(2)}, u32[]{:S(2)}) collective-permute-start(bf16[192,768]{1,0:T(8,128)(2,1)} %get-tuple-element.475), channel_id=1, source_target_pairs={{0,8},{8,0},{16,24},{24,16},{1,9},{9,1},{17,25},{25,17},{2,10},{10... | collective-permute-start | bytes 884744 | tf_op jit(solution)/shard_map/ppermute | solution.py:423
  332.5 66.1 %collective-permute-start.32 = (bf16[256,768]{1,0:T(8,128)(2,1)}, bf16[256,768]{1,0:T(8,128)(2,1)}, u32[]{:S(2)}, u32[]{:S(2)}) collective-permute-start(bf16[256,768]{1,0:T(8,128)(2,1)} %get-tuple-element.252), channel_id=1, source_target_pairs={{0,8},{8,0},{16,24},{24,16},{1,9},{9,1},{17,25},{25,17},{2,10},{10... | collective-permute-start | bytes 1179656 | tf_op jit(solution)/shard_map/ppermute | solution.py:423
  334.5 64.1 %collective-permute-start.33 = (bf16[256,768]{1,0:T(8,128)(2,1)}, bf16[256,768]{1,0:T(8,128)(2,1)}, u32[]{:S(2)}, u32[]{:S(2)}) collective-permute-start(bf16[256,768]{1,0:T(8,128)(2,1)} %get-tuple-element.253), channel_id=1, source_target_pairs={{0,16},{8,24},{16,0},{24,8},{1,17},{9,25},{17,1},{25,9},{2,18},{10... | collective-permute-start | bytes 1179656 | tf_op jit(solution)/shard_map/ppermute | solution.py:423
  343.2 47.5 %collective-permute-start.35 = (bf16[2,1024,256]{2,1,0:T(8,128)(2,1)}, bf16[2,1024,256]{2,1,0:T(8,128)(2,1)}, u32[]{:S(2)}, u32[]{:S(2)}) collective-permute-start(bf16[2,1024,256]{2,1,0:T(8,128)(2,1)} %get-tuple-element.257), channel_id=1, source_target_pairs={{0,1},{1,0},{2,3},{3,2},{4,5},{5,4},{6,7},{7,6},{8,9},{9,8},{10,11... | collective-permute-start | bytes 3145736 | tf_op jit(solution)/shard_map/ppermute | solution.py:420
  345.4 45.3 %collective-permute-start.39 = (bf16[48,3840]{1,0:T(8,128)(2,1)S(1)}, bf16[48,3840]{1,0:T(8,128)(2,1)}, u32[]{:S(2)}, u32[]{:S(2)}) collective-permute-start(bf16[48,3840]{1,0:T(8,128)(2,1)S(1)} %get-tuple-element.471), channel_id=1, source_target_pairs={{0,8},{8,0},{16,24},{24,16},{1,9},{9,1},{17,25},{25,17},{2,10},{10... | collective-permute-start | bytes 1105928 | tf_op jit(solution)/shard_map/ppermute | solution.py:423
  347.2 46.8 %copy-start.24 = (f32[2,1024,256]{2,1,0:T(8,128)S(1)}, f32[2,1024,256]{2,1,0:T(8,128)}, u32[]{:S(2)}) copy-start(f32[2,1024,256]{2,1,0:T(8,128)} %get-tuple-element.276) | copy-start | bytes 6291460
  381.5 58.6 %collective-permute-start.44 = (bf16[192,768]{1,0:T(8,128)(2,1)}, bf16[192,768]{1,0:T(8,128)(2,1)}, u32[]{:S(2)}, u32[]{:S(2)}) collective-permute-start(bf16[192,768]{1,0:T(8,128)(2,1)} %add_convert_fusion.10), channel_id=1, source_target_pairs={{0,16},{8,24},{16,0},{24,8},{1,17},{9,25},{17,1},{25,9},{2,18},{10... | collective-permute-start | bytes 884744 | tf_op jit(solution)/shard_map/ppermute | solution.py:423
  390.7 49.4 %collective-permute-start.42 = (bf16[2,1024,256]{2,1,0:T(8,128)(2,1)}, bf16[2,1024,256]{2,1,0:T(8,128)(2,1)}, u32[]{:S(2)}, u32[]{:S(2)}) collective-permute-start(bf16[2,1024,256]{2,1,0:T(8,128)(2,1)} %get-tuple-element.279), channel_id=1, source_target_pairs={{0,1},{1,0},{2,3},{3,2},{4,5},{5,4},{6,7},{7,6},{8,9},{9,8},{10,11... | collective-permute-start | bytes 3145736 | tf_op jit(solution)/shard_map/ppermute | solution.py:420
  391.8 48.2 %collective-permute-start.45 = (bf16[48,3840]{1,0:T(8,128)(2,1)S(1)}, bf16[48,3840]{1,0:T(8,128)(2,1)}, u32[]{:S(2)}, u32[]{:S(2)}) collective-permute-start(bf16[48,3840]{1,0:T(8,128)(2,1)S(1)} %add_convert_fusion.8), channel_id=1, source_target_pairs={{0,16},{8,24},{16,0},{24,8},{1,17},{9,25},{17,1},{25,9},{2,18},{10... | collective-permute-start | bytes 1105928 | tf_op jit(solution)/shard_map/ppermute | solution.py:423
  398.6 40.9 %copy-start.28 = (bf16[1024,256]{1,0:T(8,128)(2,1)S(1)}, bf16[1024,256]{1,0:T(8,128)(2,1)}, u32[]{:S(2)}) copy-start(bf16[1024,256]{1,0:T(8,128)(2,1)} %get-tuple-element.275) | copy-start | bytes 1572868
  430.7 15.6 %collective-permute-start.46 = (bf16[2,1024,256]{2,1,0:T(8,128)(2,1)}, bf16[2,1024,256]{2,1,0:T(8,128)(2,1)S(1)}, u32[]{:S(2)}, u32[]{:S(2)}) collective-permute-start(bf16[2,1024,256]{2,1,0:T(8,128)(2,1)} %get-tuple-element.291), channel_id=1, source_target_pairs={{0,1},{1,0},{2,3},{3,2},{4,5},{5,4},{6,7},{7,6},{8,9},{9,8},{10,11... | collective-permute-start | bytes 3145736 | tf_op jit(solution)/shard_map/ppermute | solution.py:420
  464.4 4.7 collective-permute-start.51
  468.7 6.8 %collective-permute-start.47 = (bf16[2,256,768]{2,1,0:T(8,128)(2,1)}, bf16[2,256,768]{2,1,0:T(8,128)(2,1)}, u32[]{:S(2)}, u32[]{:S(2)}) collective-permute-start(bf16[2,256,768]{2,1,0:T(8,128)(2,1)} %pad_maximum_fusion.9), channel_id=1, source_target_pairs={{0,1},{1,0},{2,3},{3,2},{4,5},{5,4},{6,7},{7,6},{8,9},{9,8},{10,11... | collective-permute-start | bytes 2359304 | tf_op jit(solution)/shard_map/ppermute | solution.py:420
  470.8 13.0 %collective-permute-start.52 = (bf16[96,2432]{1,0:T(8,128)(2,1)S(1)}, bf16[96,2432]{1,0:T(8,128)(2,1)S(1)}, u32[]{:S(2)}, u32[]{:S(2)}) collective-permute-start(bf16[96,2432]{1,0:T(8,128)(2,1)S(1)} %get-tuple-element.429), channel_id=1, source_target_pairs={{0,2},{1,3},{2,0},{3,1},{4,6},{5,7},{6,4},{7,5},{8,10},{9,11},{10,... | collective-permute-start | bytes 1400840 | tf_op jit(solution)/shard_map/ppermute | solution.py:426
  471.0 16.5 %collective-permute-start.50 = (bf16[256,768]{1,0:T(8,128)(2,1)S(1)}, bf16[256,768]{1,0:T(8,128)(2,1)S(1)}, u32[]{:S(2)}, u32[]{:S(2)}) collective-permute-start(bf16[256,768]{1,0:T(8,128)(2,1)S(1)} %get-tuple-element.437), channel_id=1, source_target_pairs={{0,24},{8,16},{16,8},{24,0},{1,25},{9,17},{17,9},{25,1},{2,26},{10... | collective-permute-start | bytes 1179656 | tf_op jit(solution)/shard_map/ppermute | solution.py:423
  474.0 33.9 %collective-permute-start.49 = (bf16[256,768]{1,0:T(8,128)(2,1)S(1)}, bf16[256,768]{1,0:T(8,128)(2,1)S(1)}, u32[]{:S(2)}, u32[]{:S(2)}) collective-permute-start(bf16[256,768]{1,0:T(8,128)(2,1)S(1)} %get-tuple-element.438), channel_id=1, source_target_pairs={{0,16},{8,24},{16,0},{24,8},{1,17},{9,25},{17,1},{25,9},{2,18},{10... | collective-permute-start | bytes 1179656 | tf_op jit(solution)/shard_map/ppermute | solution.py:423
  474.1 33.9 %collective-permute-start.48 = (bf16[256,768]{1,0:T(8,128)(2,1)S(1)}, bf16[256,768]{1,0:T(8,128)(2,1)S(1)}, u32[]{:S(2)}, u32[]{:S(2)}) collective-permute-start(bf16[256,768]{1,0:T(8,128)(2,1)S(1)} %get-tuple-element.439), channel_id=1, source_target_pairs={{0,8},{8,0},{16,24},{24,16},{1,9},{9,1},{17,25},{25,17},{2,10},{10... | collective-permute-start | bytes 1179656 | tf_op jit(solution)/shard_map/ppermute | solution.py:423
  476.8 31.7 %collective-permute-start.54 = (bf16[96,2432]{1,0:T(8,128)(2,1)S(1)}, bf16[96,2432]{1,0:T(8,128)(2,1)S(1)}, u32[]{:S(2)}, u32[]{:S(2)}) collective-permute-start(bf16[96,2432]{1,0:T(8,128)(2,1)S(1)} %get-tuple-element.427), channel_id=1, source_target_pairs={{0,4},{1,5},{2,6},{3,7},{4,0},{5,1},{6,2},{7,3},{8,12},{9,13},{10,... | collective-permute-start | bytes 1400840 | tf_op jit(solution)/shard_map/ppermute | solution.py:426
  483.8 24.6 %collective-permute-start.55 = (bf16[96,2432]{1,0:T(8,128)(2,1)S(1)}, bf16[96,2432]{1,0:T(8,128)(2,1)S(1)}, u32[]{:S(2)}, u32[]{:S(2)}) collective-permute-start(bf16[96,2432]{1,0:T(8,128)(2,1)S(1)} %get-tuple-element.304), channel_id=1, source_target_pairs={{0,6},{1,7},{2,4},{3,5},{4,2},{5,3},{6,0},{7,1},{8,14},{9,15},{10,... | collective-permute-start | bytes 1400840 | tf_op jit(solution)/shard_map/ppermute | solution.py:426
  508.4 11.1 %collective-permute-start.53 = (bf16[2,256,768]{2,1,0:T(8,128)(2,1)S(1)}, bf16[2,256,768]{2,1,0:T(8,128)(2,1)S(1)}, u32[]{:S(2)}, u32[]{:S(2)}) collective-permute-start(bf16[2,256,768]{2,1,0:T(8,128)(2,1)S(1)} %pad_maximum_fusion.11), channel_id=1, source_target_pairs={{0,1},{1,0},{2,3},{3,2},{4,5},{5,4},{6,7},{7,6},{8,9},{9,8},{10,11... | collective-permute-start | bytes 2359304 | tf_op jit(solution)/shard_map/ppermute | solution.py:420
  509.9 8.6 %collective-permute-start.56 = (bf16[48,2432]{1,0:T(8,128)(2,1)S(1)}, bf16[48,2432]{1,0:T(8,128)(2,1)S(1)}, u32[]{:S(2)}, u32[]{:S(2)}) collective-permute-start(bf16[48,2432]{1,0:T(8,128)(2,1)S(1)} %dynamic-slice_bitcast_fusion.10), channel_id=1, source_target_pairs={{0,8},{8,0},{16,24},{24,16},{1,9},{9,1},{17,25},{25,17},{2,10},{10... | collective-permute-start | bytes 700424 | tf_op jit(solution)/shard_map/ppermute | solution.py:423
  511.1 18.7 %collective-permute-start.59 = (bf16[192,768]{1,0:T(8,128)(2,1)S(1)}, bf16[192,768]{1,0:T(8,128)(2,1)S(1)}, u32[]{:S(2)}, u32[]{:S(2)}) collective-permute-start(bf16[192,768]{1,0:T(8,128)(2,1)S(1)} %add_convert_fusion.9), channel_id=1, source_target_pairs={{0,8},{8,0},{16,24},{24,16},{1,9},{9,1},{17,25},{25,17},{2,10},{10... | collective-permute-start | bytes 884744 | tf_op jit(solution)/shard_map/ppermute | solution.py:423
  514.2 23.0 %collective-permute-start.60 = (bf16[48,3840]{1,0:T(8,128)(2,1)S(1)}, bf16[48,3840]{1,0:T(8,128)(2,1)S(1)}, u32[]{:S(2)}, u32[]{:S(2)}) collective-permute-start(bf16[48,3840]{1,0:T(8,128)(2,1)S(1)} %add_convert_fusion.7), channel_id=1, source_target_pairs={{0,8},{8,0},{16,24},{24,16},{1,9},{9,1},{17,25},{25,17},{2,10},{10... | collective-permute-start | bytes 1105928 | tf_op jit(solution)/shard_map/ppermute | solution.py:423
  518.6 19.9 %collective-permute-start.57 = (bf16[48,2432]{1,0:T(8,128)(2,1)S(1)}, bf16[48,2432]{1,0:T(8,128)(2,1)S(1)}, u32[]{:S(2)}, u32[]{:S(2)}) collective-permute-start(bf16[48,2432]{1,0:T(8,128)(2,1)S(1)} %fusion.36), channel_id=1, source_target_pairs={{0,16},{8,24},{16,0},{24,8},{1,17},{9,25},{17,1},{25,9},{2,18},{10... | collective-permute-start | bytes 700424 | tf_op jit(solution)/shard_map/ppermute | solution.py:423
  538.5 7.3 %collective-permute-start.58 = (bf16[48,2432]{1,0:T(8,128)(2,1)S(1)}, bf16[48,2432]{1,0:T(8,128)(2,1)S(1)}, u32[]{:S(2)}, u32[]{:S(2)}) collective-permute-start(bf16[48,2432]{1,0:T(8,128)(2,1)S(1)} %add_convert_fusion.11), channel_id=1, source_target_pairs={{0,8},{8,0},{16,24},{24,16},{1,9},{9,1},{17,25},{25,17},{2,10},{10... | collective-permute-start | bytes 700424 | tf_op jit(solution)/shard_map/ppermute | solution.py:423
  (72 other events, 475.9 us)

commit v7 on v6

--- a/solution.py
+++ b/solution.py
@@ -561,10 +561,10 @@
     return total(0), [total(k).astype(bf16) for k in range(1, here.shards // 2)]
 
 
-def share_send(here, lows):
+def share_send(here, lows, apart=False):
     others = []
     for k, low in enumerate(lows, 1):
-        others.append(here.aside(after(low, others[k - 3]) if k > 2 else low, k))
+        others.append(here.aside(after(low, others[k - 3]) if apart and k > 2 else low, k))
     return others
 
 
@@ -717,7 +717,6 @@
     branch = dot(active_low, down_full) + down_bias_full
     result, normed_two, factor_two = norm_forward(first_out + branch, gain_two, shift_two)
     result_low = list(result.astype(bf16).reshape(here.columns, half, width))
-    output_far = from_sequence_send(here, result_low[3:], 3)
 
     grad_second, second_gain_grad, second_shift_grad = norm_backward(cotangent, normed_two, factor_two, gain_two)
     grad_branch = grad_second.astype(bf16)
@@ -727,13 +726,12 @@
     grad_active = dot(grad_branch, down_full.T)
     grad_hidden = (grad_active * slope_low.astype(f32)).astype(bf16)
     down_share, down_lows = share_plane(here, down_kept, after(down_other, grad_hidden))
-    grad_hidden, down_lows = lax.optimization_barrier((grad_hidden, down_lows))
     down_others = share_send(here, down_lows)
     up_grad = dot(first_low.T, grad_hidden).astype(bf16)
     up_bias_grad = column_sums(grad_hidden)
     grad_first = grad_second + dot(grad_hidden, up_full.T)
     grad_sum, first_gain_grad, first_shift_grad = norm_backward(grad_first, normed_one, factor_one, gain_one)
-    grad_attended, down_others[0] = lax.optimization_barrier((grad_sum.astype(bf16), down_others[0]))
+    grad_attended = grad_sum.astype(bf16)
     merge_grad = dot(context.T, grad_attended).astype(bf16)
     merge_bias_grad = column_sums(grad_attended)
     up_merge = jnp.concatenate([up_grad.reshape(shards, own, hidden_size), merge_grad.reshape(shards, own, width)], axis=2)
@@ -758,8 +756,7 @@
     down_half, down_other = column_first(here, share_sum(down_share, down_others))
     up_others, up_share = after((up_others, up_share), one[0])
     up_half, up_other = column_first(here, share_sum(up_share, up_others))
-    grad_context, output_far = lax.optimization_barrier((after(grad_context, one[0]), output_far))
-    output_slots = from_sequence_send(here, after(result_low[:3], one[0])) + output_far
+    output_slots = from_sequence_send(here, after(result_low, one[0]))
     two = backward(1, after(grad_context, down_half, up_half))
     one, up_half, up_other = after((one, up_half, up_other), two[0])
     mixed_one = mixed_part(one)
@@ -767,7 +764,9 @@
     up_half, up_other = column_second(here, up_half, up_other)
     input_part = grad_sum + dot(mixed_one, mix_parts[0].T)
     three = backward(2, after(grad_context, down_half, up_half, input_part, output_slots[:3]))
-    two, down_half, down_other, up_half, up_other = after((two, down_half, down_other, up_half, up_other), three[0])
+    two, down_half, down_other, up_half, up_other, output_slots[3:] = after(
+        (two, down_half, down_other, up_half, up_other, output_slots[3:]), three[0]
+    )
     mixed_two = mixed_part(two)
     input_part = input_part + dot(mixed_two, mix_parts[1].T)
     mixed_three = mixed_part(after(three, input_part))
@@ -792,9 +791,9 @@
     up_lines = up_bias_grad.reshape(shards, ups, own).transpose(1, 0, 2).reshape(ups, width)
     lines_grad = jnp.concatenate([jnp.stack(vectors), up_lines], axis=0)
     columns_grad = jnp.pad(lines_grad, ((0, LANES - lines_grad.shape[0]), (0, 0))).T
-    whole = jnp.concatenate([mix_grad, columns_grad.astype(bf16)], axis=1).reshape(shards, own, -1)
+    whole = jnp.concatenate([mix_grad, lax.optimization_barrier(columns_grad).astype(bf16)], axis=1).reshape(shards, own, -1)
     mix_share, mix_lows = share_plane(here, *share_pair(here, whole))
-    mix_others = share_send(here, mix_lows)
+    mix_others = share_send(here, mix_lows, True)
     input_mark = mix_others[0]
     mix_share = share_sum(mix_share, mix_others)
     mix_half, mix_other = column_first(here, mix_share)

time: 558 us -> 540 us (0.968)
  waiting for transfers between devices: 107 us -> 85.3 us
  starting transfers between devices: 97.2 us -> 107 us
  other arithmetic: 58.8 us -> 50.5 us
  matrix products: 75.8 us -> 82.6 us
    ppermute x15, starting transfers between devices: 18.4 us -> 50.7 us  [aside(): return lax.ppermute(values, 'fsdp', xor_pairs(self.shards, 2 * bits))]
    ppermute x15, waiting for transfers between devices: 45.4 us -> 18.9 us  [aside(): return lax.ppermute(values, 'fsdp', xor_pairs(self.shards, 2 * bits))]
    ppermute x22, starting transfers between devices: 21 us -> 4.32 us  [mate(): return lax.ppermute(values, 'fsdp', xor_pairs(self.shards, 1))]
    ppermute x24, waiting for transfers between devices: 56.8 us -> 64.9 us  [across(): return lax.ppermute(values, 'seq', xor_pairs(self.columns, bits))]
    dot_general x16, matrix products: 75.8 us -> 82.6 us  [dot(): return jnp.dot(a, b, preferred_element_type=f32)]
    convert_element_type x2 -> x3, other arithmetic: 3.52 us -> 10.1 us  [share_plane(): total(k).astype(bf16)]
    unnamed x171 -> x165, local copies, waits for them, and re-layouts: 20.3 us -> 17.4 us
  transfers between devices with their start and end apart: 61 -> 61, of which waited for: 19 -> 18; matrix products, arithmetic and copies ran while one was open for 14% -> 18% of each run, Pallas kernels for 30% -> 31%
where the time goes in v7:
time: 540 us; the launch traced here: 534 us
  Pallas kernels  166 us (31%)
  starting transfers between devices  107 us (20%)
  waiting for transfers between devices  85.3 us (16%)
  matrix products  82.6 us (15%)
  other arithmetic  50.5 us (9%)
  local copies, waits for them, and re-layouts  39.7 us (7%)
    pallas_call x3, Pallas kernels, attention_backward(): pl.pallas_call(functools.partial(backward_kernel, size=size), grid_spec=p...  96.4 us
    dot_general x16, matrix products, dot(): return jnp.dot(a, b, preferred_element_type=f32)  82.6 us
    ppermute x24, waiting for transfers between devices, across(): return lax.ppermute(values, 'seq', xor_pairs(self.columns, bits))  64.9 us
    pallas_call x3, Pallas kernels, attention_forward(): pl.pallas_call(functools.partial(forward_kernel, size=size, plan=(len(pie...  62.6 us
    ppermute x24, starting transfers between devices, across(): return lax.ppermute(values, 'seq', xor_pairs(self.columns, bits))  52.4 us
    ppermute x15, starting transfers between devices, aside(): return lax.ppermute(values, 'fsdp', xor_pairs(self.shards, 2 * bits))  50.7 us
    ppermute x15, waiting for transfers between devices, aside(): return lax.ppermute(values, 'fsdp', xor_pairs(self.shards, 2 * bits))  18.9 us
    unnamed x165, local copies, waits for them, and re-layouts  17.4 us
  transfers between devices with their start and end apart: 61, of which 18 were waited for; matrix products, arithmetic and copies ran while one was open for 18% of the time, Pallas kernels for 31%

profile of v7, /device:TPU:0, one launch (start us, length us, event | category | flops | bytes accessed | tf_op | source)
XLA Modules:
  0.0 534.1 jit_solution(4199124053706140353)
XLA Ops:
  3.0 2.0 pack_projection.1.refs_0_
  5.0 3.0 collective-permute-start.8
  9.5 2.1 collective-permute-start.1
  11.6 2.5 collective-permute-start.3
  18.0 3.7 collective-permute-done.2
  26.6 1.7 collective-permute-start.6
  31.0 5.8 %collective-permute-done.9.refs_2_ = bf16[96,3200]{1,0:T(8,128)(2,1)} collective-permute-done((bf16[96,3200]{1,0:T(8,128)(2,1)}, bf16[96,3200]{1,0:T(8,128)(2,1)}, u32[]{:S(2)}, u32[]{:S(2)}) %collective-permute-start.9) | collective-permute-done | bytes 614432 | tf_op jit(solution)/shard_map/ppermute | solution.py:426
  36.8 18.0 %collective-permute-done.5 = bf16[256,768]{1,0:T(8,128)(2,1)S(1)} collective-permute-done((bf16[256,768]{1,0:T(8,128)(2,1)}, bf16[256,768]{1,0:T(8,128)(2,1)S(1)}, u32[]{:S(2)}, u32[]{:S(2)}) %collective-permute-start.5) | collective-permute-done | bytes 393248 | tf_op jit(solution)/shard_map/ppermute | solution.py:423
  57.7 8.8 %collective-permute-start.4 = (bf16[256,768]{1,0:T(8,128)(2,1)}, bf16[256,768]{1,0:T(8,128)(2,1)}, u32[]{:S(2)}, u32[]{:S(2)}) collective-permute-start(bf16[256,768]{1,0:T(8,128)(2,1)} %get-tuple-element.158), channel_id=1, source_target_pairs={{0,8},{8,0},{16,24},{24,16},{1,9},{9,1},{17,25},{25,17},{2,10},{10... | collective-permute-start | bytes 1179656 | tf_op jit(solution)/shard_map/ppermute | solution.py:423
  69.3 5.2 place_parts.1
  86.5 2.2 collective-permute-start.19
  88.7 20.6 %attention_forward.3 = (bf16[1024,256]{1,0:T(8,128)(2,1)}, bf16[1024,256]{1,0:T(8,128)(2,1)}) custom-call(s32[10]{0:T(128)} %pad_add_fusion.3.info, bf16[1024,768]{1,0:T(8,128)(2,1)} %copy-done.1, bf16[1024,768]{1,0:T(8,128)(2,1)} %copy-done.1, bf16[1024,768]{1,0:T(8,128)(2,1)} %copy-done.4, bf16[1024,768]{1,0:T(8,128)(2,1)} %copy-done.1, ...), custom_call_target="tpu_custom_call" | custom-call | flops 1073741824 | bytes 4194304 | tf_op jit(solution)/shard_map/attention_forward/pallas_call | solution.py:176
  109.3 20.5 %attention_forward.4 = (bf16[1024,256]{1,0:T(8,128)(2,1)}, bf16[1024,256]{1,0:T(8,128)(2,1)}) custom-call(s32[10]{0:T(128)} %pad_add_fusion.3.info, bf16[1024,768]{1,0:T(8,128)(2,1)} %copy-done, bf16[1024,768]{1,0:T(8,128)(2,1)} %copy-done, bf16[1024,768]{1,0:T(8,128)(2,1)} %copy-done.3, bf16[1024,768]{1,0:T(8,128)(2,1)} %copy-done, ...), custom_call_target="tpu_custom_call" | custom-call | flops 1073741824 | bytes 4194304 | tf_op jit(solution)/shard_map/attention_forward/pallas_call | solution.py:176
  129.9 7.8 %collective-permute-done.21.refs_2_ = bf16[768,768]{1,0:T(8,128)(2,1)} collective-permute-done((bf16[768,768]{1,0:T(8,128)(2,1)S(1)}, bf16[768,768]{1,0:T(8,128)(2,1)}, u32[]{:S(2)}, u32[]{:S(2)}) %collective-permute-start.21) | collective-permute-done | bytes 1179680 | tf_op jit(solution)/shard_map/ppermute | solution.py:426
  139.5 1.8 collective-permute-start.27
  143.6 1.9 collective-permute-start.28
  145.7 21.5 %attention_forward.5 = (bf16[1024,256]{1,0:T(8,128)(2,1)}, bf16[1024,256]{1,0:T(8,128)(2,1)}, bf16[8,96,3072]{2,1,0:T(8,128)(2,1)}, bf16[8,384,768]{2,1,0:T(8,128)(2,1)}) custom-call(s32[18]{0:T(128)} %concatenate.84.info, bf16[1024,768]{1,0:T(8,128)(2,1)} %copy-done.2, bf16[1024,768]{1,0:T(8,128)(2,1)} %copy-done.2, ...), custom_call_target="tpu_custom_call" | custom-call | flops 1073741824 | bytes 4194304 | tf_op jit(solution)/shard_map/attention_forward/pallas_call | solution.py:176
  168.3 3.9 fusion.59
  172.8 13.4 %fusion.4 = (bf16[1024,3072]{1,0:T(8,128)(2,1)}, bf16[1024,3072]{1,0:T(8,128)(2,1)S(1)}) fusion(f32[3072]{0:T(1024)S(1)} %add.446, bf16[768,3072]{1,0:T(8,128)(2,1)S(1)} %bitcast.300, f32[1024,768]{1,0:T(8,128)S(1)} %get-tuple-element.488, f32[768]{0:T(1024)S(1)} %get-tuple-element.384, f32[768]{0:T(1024)S(1)} %get-tuple-element.385, ...), kind=kOutput, calls=%fused_computation.5 | convolution fusion | flops 4873519104 | bytes 20473856 | tf_op jit(solution)/shard_map/dot_general | solution.py:387
  186.3 5.5 %fusion.60 = (f32[1024]{0:T(1024)S(1)}, f32[1024,768]{1,0:T(8,128)S(1)}) fusion(f32[768]{0:T(1024)S(1)} %get-tuple-element.383, bf16[1024,3072]{1,0:T(8,128)(2,1)S(1)} %get-tuple-element.220, bf16[3072,768]{1,0:T(8,128)(2,1)S(1)} %bitcast.305, f32[768]{0:T(1024)S(1)} %get-tuple-element.384, f32[768]{0:T(1024)S(1)} %get-tuple-element.385, ...), kind=kOutput, calls=%fused_computation.266 | convolution fusion | flops 4837342208 | bytes 17323008 | tf_op jit(solution)/shard_map/dot_general | solution.py:387
  192.4 3.3 fusion.11
  195.7 3.0 convert_reduce_fusion.2
  198.8 5.7 %convolution_convert_fusion.1 = bf16[3072,768]{1,0:T(8,128)(2,1)S(1)} fusion(bf16[1024,3072]{1,0:T(8,128)(2,1)S(1)} %get-tuple-element.220, f32[1024,768]{1,0:T(8,128)S(1)} %get-tuple-element.396), kind=kOutput, calls=%fused_computation.21 | convolution fusion | flops 4834983936 | bytes 14155776 | tf_op jit(solution)/shard_map/dot_general | solution.py:387
  204.5 12.7 %convert_reduce_fusion = (bf16[3072]{0:T(1024)(128)(2,1)}, bf16[1024,3072]{1,0:T(8,128)(2,1)}) fusion(bf16[1024,3072]{1,0:T(8,128)(2,1)} %get-tuple-element.234, bf16[3072,768]{1,0:T(8,128)(2,1)} %bitcast.302, f32[1024,768]{1,0:T(8,128)S(1)} %get-tuple-element.396), kind=kOutput, calls=%fused_computation.6 | convolution fusion | flops 4848350208 | bytes 20453376 | tf_op jit(solution)/shard_map/dot_general | solution.py:387
  217.2 8.8 %multiply_reduce_fusion = (bf16[768]{0:T(1024)(128)(2,1)}, f32[1024]{0:T(1024)S(1)}, f32[1024]{0:T(1024)S(1)}, bf16[768]{0:T(1024)(128)(2,1)}, f32[1024,768]{1,0:T(8,128)S(1)}) fusion(f32[1024,768]{1,0:T(8,128)S(1)} %get-tuple-element.488, f32[1024]{0:T(1024)S(1)} %add_rsqrt_fusion.1, f32[1024]{0:T(1024)S(1)} %broadcast_multiply_fusion.5, ...), kind=kOutput, calls=%fused_computation.35 | convolution fusion | flops 4839698432 | bytes 20469760 | tf_op jit(solution)/shard_map/dot_general | solution.py:387
  225.9 8.5 %convolution_convert_fusion = bf16[768,3072]{1,0:T(8,128)(2,1)S(1)} fusion(bf16[1024,3072]{1,0:T(8,128)(2,1)} %get-tuple-element.493, f32[1024,768]{1,0:T(8,128)S(1)} %get-tuple-element.488, f32[768]{0:T(1024)S(1)} %get-tuple-element.384, f32[768]{0:T(1024)S(1)} %get-tuple-element.385, f32[1024]{0:T(1024)S(1)} %add_rsqrt_fusion.1, ...), kind=kOutput, calls=%fused_computation.20 | convolution fusion | flops 4838129664 | bytes 14170112 | tf_op jit(solution)/shard_map/dot_general | solution.py:387
  234.5 1.7 dynamic-slice_bitcast_fusion
  239.7 1.8 fusion.13
  241.5 4.3 fusion.18
  245.8 7.4 %collective-permute-start.33 = (bf16[384,768]{1,0:T(8,128)(2,1)S(1)}, bf16[384,768]{1,0:T(8,128)(2,1)S(1)}, u32[]{:S(2)}, u32[]{:S(2)}) collective-permute-start(bf16[384,768]{1,0:T(8,128)(2,1)S(1)} %get-tuple-element.407), channel_id=1, source_target_pairs={{0,2},{1,3},{2,0},{3,1},{4,6},{5,7},{6,4},{7,5},{8,10},{9,11},{10,... | collective-permute-start | bytes 1769480 | tf_op jit(solution)/shard_map/ppermute | solution.py:426
  253.2 4.6 convolution_convert_fusion.3.do_ref
  257.8 3.5 collective-permute-start.34
  262.8 4.1 fusion.15
  269.0 3.3 collective-permute-start.38
  276.1 32.0 %attention_backward.3 = (bf16[1024,256]{1,0:T(8,128)(2,1)}, f32[2,1024,256]{2,1,0:T(8,128)}, bf16[2,1024,256]{2,1,0:T(8,128)(2,1)}) custom-call(s32[10]{0:T(128)} %pad_add_fusion.3.info, bf16[1024,768]{1,0:T(8,128)(2,1)} %copy-done.1, bf16[1024,256]{1,0:T(8,128)(2,1)} %get-tuple-element.222.ext_ref, bf16[1024,768]{1,0:T(8,128)(2,1)} %convolution_convert_fusion.3.do_ref, ...), custom_call_target="tpu_custom_call" | custom-call | flops 2684354560 | bytes 6291456 | tf_op jit(solution)/shard_map/attention_backward/pallas_call | solution.py:299
  308.1 1.6 collective-permute-start.31
  309.7 4.0 collective-permute-start.32
  316.0 3.8 collective-permute-done.37
  319.8 1.7 add_convert_fusion.5
  323.3 32.3 %attention_backward.4 = (bf16[1024,256]{1,0:T(8,128)(2,1)}, f32[2,1024,256]{2,1,0:T(8,128)}, bf16[2,1024,256]{2,1,0:T(8,128)(2,1)}) custom-call(s32[10]{0:T(128)} %pad_add_fusion.3.info, bf16[1024,768]{1,0:T(8,128)(2,1)} %copy-done, bf16[1024,256]{1,0:T(8,128)(2,1)} %get-tuple-element.242.ext_ref, bf16[1024,768]{1,0:T(8,128)(2,1)} %convolution_convert_fusion.3.do_ref, ...), custom_call_target="tpu_custom_call" | custom-call | flops 2684354560 | bytes 6291456 | tf_op jit(solution)/shard_map/attention_backward/pallas_call | solution.py:299
  355.7 3.7 collective-permute-start.45
  359.4 1.7 add_convert_fusion.10
  362.1 1.6 add_convert_fusion.4
  365.2 3.1 convolution_add_fusion.1
  368.3 2.2 collective-permute-start.44
  370.5 32.0 %attention_backward.5 = (bf16[1024,256]{1,0:T(8,128)(2,1)}, f32[2,1024,256]{2,1,0:T(8,128)}, bf16[2,1024,256]{2,1,0:T(8,128)(2,1)}) custom-call(s32[10]{0:T(128)} %pad_add_fusion.3.info, bf16[1024,768]{1,0:T(8,128)(2,1)} %copy-done.2, bf16[1024,256]{1,0:T(8,128)(2,1)} %get-tuple-element.262.ext_ref, bf16[1024,768]{1,0:T(8,128)(2,1)} %convolution_convert_fusion.3.do_ref, ...), custom_call_target="tpu_custom_call" | custom-call | flops 2684354560 | bytes 6291456 | tf_op jit(solution)/shard_map/attention_backward/pallas_call | solution.py:299
  403.0 3.3 collective-permute-done.44
  406.3 1.6 add_convert_fusion.3
  414.8 2.6 add_convert_fusion
  420.7 6.7 %convolution_convert_fusion.2 = bf16[768,2304]{1,0:T(8,128)(2,1)S(1)} fusion(bf16[1024,768]{1,0:T(8,128)(2,1)S(1)} %copy-done.46, bf16[1024,2304]{1,0:T(8,128)(2,1)} %constant_dynamic-update-slice_fusion.8), kind=kOutput, calls=%fused_computation.22 | convolution fusion | flops 3625648128 | bytes 9830400 | tf_op jit(solution)/shard_map/dot_general | solution.py:387
  427.6 1.8 copy-done.6
  434.9 1.8 fusion.22
  436.7 16.6 %collective-permute-start.52 = (bf16[96,2432]{1,0:T(8,128)(2,1)S(1)}, bf16[96,2432]{1,0:T(8,128)(2,1)S(1)}, u32[]{:S(2)}, u32[]{:S(2)}) collective-permute-start(bf16[96,2432]{1,0:T(8,128)(2,1)S(1)} %get-tuple-element.411), channel_id=1, source_target_pairs={{0,2},{1,3},{2,0},{3,1},{4,6},{5,7},{6,4},{7,5},{8,10},{9,11},{10,... | collective-permute-start | bytes 1400840 | tf_op jit(solution)/shard_map/ppermute | solution.py:426
  453.4 2.7 collective-permute-start.48
  459.9 3.2 collective-permute-start.54
  464.6 4.9 collective-permute-start.55
  472.1 13.7 %collective-permute-done.49 = bf16[256,768]{1,0:T(8,128)(2,1)S(1)} collective-permute-done((bf16[256,768]{1,0:T(8,128)(2,1)S(1)}, bf16[256,768]{1,0:T(8,128)(2,1)S(1)}, u32[]{:S(2)}, u32[]{:S(2)}) %collective-permute-start.49) | collective-permute-done | bytes 393248 | tf_op jit(solution)/shard_map/ppermute | solution.py:423
  487.8 8.0 %collective-permute-start.56 = (bf16[48,2432]{1,0:T(8,128)(2,1)S(1)}, bf16[48,2432]{1,0:T(8,128)(2,1)S(1)}, u32[]{:S(2)}, u32[]{:S(2)}) collective-permute-start(bf16[48,2432]{1,0:T(8,128)(2,1)S(1)} %dynamic-slice_bitcast_fusion.10), channel_id=1, source_target_pairs={{0,8},{8,0},{16,24},{24,16},{1,9},{9,1},{17,25},{25,17},{2,10},{10... | collective-permute-start | bytes 700424 | tf_op jit(solution)/shard_map/ppermute | solution.py:423
  498.1 2.1 collective-permute-start.60
  500.1 2.2 collective-permute-done.56
  503.9 1.9 maximum_convert_fusion
  505.8 7.8 %collective-permute-done.59 = bf16[192,768]{1,0:T(8,128)(2,1)S(1)} collective-permute-done((bf16[192,768]{1,0:T(8,128)(2,1)S(1)}, bf16[192,768]{1,0:T(8,128)(2,1)S(1)}, u32[]{:S(2)}, u32[]{:S(2)}) %collective-permute-start.59) | collective-permute-done | bytes 294944 | tf_op jit(solution)/shard_map/ppermute | solution.py:423
  513.6 7.7 %collective-permute-done.60 = bf16[48,3840]{1,0:T(8,128)(2,1)S(1)} collective-permute-done((bf16[48,3840]{1,0:T(8,128)(2,1)S(1)}, bf16[48,3840]{1,0:T(8,128)(2,1)S(1)}, u32[]{:S(2)}, u32[]{:S(2)}) %collective-permute-start.60) | collective-permute-done | bytes 368672 | tf_op jit(solution)/shard_map/ppermute | solution.py:423
  524.5 5.7 %collective-permute-done.58 = bf16[48,2432]{1,0:T(8,128)(2,1)S(1)} collective-permute-done((bf16[48,2432]{1,0:T(8,128)(2,1)S(1)}, bf16[48,2432]{1,0:T(8,128)(2,1)S(1)}, u32[]{:S(2)}, u32[]{:S(2)}) %collective-permute-start.58) | collective-permute-done | bytes 233504 | tf_op jit(solution)/shard_map/ppermute | solution.py:423
  (384 shorter events, 93.0 us)
Async XLA Ops:
  5.0 24.9 %collective-permute-start.8 = (bf16[96,3200]{1,0:T(8,128)(2,1)}, bf16[96,3200]{1,0:T(8,128)(2,1)S(1)}, u32[]{:S(2)}, u32[]{:S(2)}) collective-permute-start(bf16[96,3200]{1,0:T(8,128)(2,1)} %pack_projection.1.refs_0_), channel_id=1, source_target_pairs={{0,2},{1,3},{2,0},{3,1},{4,6},{5,7},{6,4},{7,5},{8,10},{9,11},{10,... | collective-permute-start | bytes 1843208 | tf_op jit(solution)/shard_map/ppermute | solution.py:426
  8.0 28.8 %collective-permute-start.9 = (bf16[96,3200]{1,0:T(8,128)(2,1)}, bf16[96,3200]{1,0:T(8,128)(2,1)}, u32[]{:S(2)}, u32[]{:S(2)}) collective-permute-start(bf16[96,3200]{1,0:T(8,128)(2,1)} %pack_projection.1.refs_0_), channel_id=1, source_target_pairs={{0,4},{1,5},{2,6},{3,7},{4,0},{5,1},{6,2},{7,3},{8,12},{9,13},{10,... | collective-permute-start | bytes 1843208 | tf_op jit(solution)/shard_map/ppermute | solution.py:426
  9.5 27.3 %collective-permute-start.10 = (bf16[96,3200]{1,0:T(8,128)(2,1)}, bf16[96,3200]{1,0:T(8,128)(2,1)}, u32[]{:S(2)}, u32[]{:S(2)}) collective-permute-start(bf16[96,3200]{1,0:T(8,128)(2,1)} %pack_projection.1.refs_0_), channel_id=1, source_target_pairs={{0,6},{1,7},{2,4},{3,5},{4,2},{5,3},{6,0},{7,1},{8,14},{9,15},{10,... | collective-permute-start | bytes 1843208 | tf_op jit(solution)/shard_map/ppermute | solution.py:426
  9.5 12.2 %collective-permute-start.1 = (s32[2,512]{1,0:T(2,128)}, s32[2,512]{1,0:T(2,128)S(1)}, u32[]{:S(2)}, u32[]{:S(2)}) collective-permute-start(s32[2,512]{1,0:T(2,128)} %param.17), channel_id=1, source_target_pairs={{0,8},{8,0},{16,24},{24,16},{1,9},{9,1},{17,25},{25,17},{2,10},{10... | collective-permute-start | bytes 12296 | tf_op jit(solution)/shard_map/ppermute | solution.py:423
  11.6 5.6 %collective-permute-start.3 = (s32[2,512]{1,0:T(2,128)}, s32[2,512]{1,0:T(2,128)S(1)}, u32[]{:S(2)}, u32[]{:S(2)}) collective-permute-start(s32[2,512]{1,0:T(2,128)} %param.17), channel_id=1, source_target_pairs={{0,24},{8,16},{16,8},{24,0},{1,25},{9,17},{17,9},{25,1},{2,26},{10... | collective-permute-start | bytes 12296 | tf_op jit(solution)/shard_map/ppermute | solution.py:423
  17.2 4.5 collective-permute-start.2
  21.7 3.0 collective-permute-start
  21.8 2.2 collective-permute-start.15
  25.8 29.0 %collective-permute-start.5 = (bf16[256,768]{1,0:T(8,128)(2,1)}, bf16[256,768]{1,0:T(8,128)(2,1)S(1)}, u32[]{:S(2)}, u32[]{:S(2)}) collective-permute-start(bf16[256,768]{1,0:T(8,128)(2,1)} %get-tuple-element.159), channel_id=1, source_target_pairs={{0,16},{8,24},{16,0},{24,8},{1,17},{9,25},{17,1},{25,9},{2,18},{10... | collective-permute-start | bytes 1179656 | tf_op jit(solution)/shard_map/ppermute | solution.py:423
  26.6 28.2 %collective-permute-start.6 = (bf16[256,768]{1,0:T(8,128)(2,1)}, bf16[256,768]{1,0:T(8,128)(2,1)S(1)}, u32[]{:S(2)}, u32[]{:S(2)}) collective-permute-start(bf16[256,768]{1,0:T(8,128)(2,1)} %get-tuple-element.160), channel_id=1, source_target_pairs={{0,24},{8,16},{16,8},{24,0},{1,25},{9,17},{17,9},{25,1},{2,26},{10... | collective-permute-start | bytes 1179656 | tf_op jit(solution)/shard_map/ppermute | solution.py:423
  30.0 39.3 %copy-start.28 = (bf16[96,3200]{1,0:T(8,128)(2,1)}, bf16[96,3200]{1,0:T(8,128)(2,1)S(1)}, u32[]{:S(2)}) copy-start(bf16[96,3200]{1,0:T(8,128)(2,1)S(1)} %collective-permute-done.8.refs_1_) | copy-start | bytes 1843204
  30.0 27.7 %collective-permute-start.7 = (bf16[2,256,768]{2,1,0:T(8,128)(2,1)S(1)}, bf16[2,256,768]{2,1,0:T(8,128)(2,1)S(1)}, u32[]{:S(2)}, u32[]{:S(2)}) collective-permute-start(bf16[2,256,768]{2,1,0:T(8,128)(2,1)S(1)} %get-tuple-element.439), channel_id=1, source_target_pairs={{0,1},{1,0},{2,3},{3,2},{4,5},{5,4},{6,7},{7,6},{8,9},{9,8},{10,11... | collective-permute-start | bytes 2359304 | tf_op jit(solution)/shard_map/ppermute | solution.py:420
  54.9 12.8 %collective-permute-start.11 = (bf16[96,3200]{1,0:T(8,128)(2,1)S(1)}, bf16[96,3200]{1,0:T(8,128)(2,1)S(1)}, u32[]{:S(2)}, u32[]{:S(2)}) collective-permute-start(bf16[96,3200]{1,0:T(8,128)(2,1)S(1)} %copy-done.12), channel_id=1, source_target_pairs={{0,1},{1,0},{2,3},{3,2},{4,5},{5,4},{6,7},{7,6},{8,9},{9,8},{10,11... | collective-permute-start | bytes 1843208 | tf_op jit(solution)/shard_map/ppermute | solution.py:420
  54.9 12.7 %collective-permute-start.12 = (bf16[96,3200]{1,0:T(8,128)(2,1)S(1)}, bf16[96,3200]{1,0:T(8,128)(2,1)S(1)}, u32[]{:S(2)}, u32[]{:S(2)}) collective-permute-start(bf16[96,3200]{1,0:T(8,128)(2,1)S(1)} %collective-permute-done.8.refs_1_), channel_id=1, source_target_pairs={{0,1},{1,0},{2,3},{3,2},{4,5},{5,4},{6,7},{7,6},{8,9},{9,8},{10,11... | collective-permute-start | bytes 1843208 | tf_op jit(solution)/shard_map/ppermute | solution.py:420
  55.4 13.1 %collective-permute-start.13 = (bf16[96,3200]{1,0:T(8,128)(2,1)}, bf16[96,3200]{1,0:T(8,128)(2,1)S(1)}, u32[]{:S(2)}, u32[]{:S(2)}) collective-permute-start(bf16[96,3200]{1,0:T(8,128)(2,1)} %collective-permute-done.9.refs_2_), channel_id=1, source_target_pairs={{0,1},{1,0},{2,3},{3,2},{4,5},{5,4},{6,7},{7,6},{8,9},{9,8},{10,11... | collective-permute-start | bytes 1843208 | tf_op jit(solution)/shard_map/ppermute | solution.py:420
  55.5 13.8 %collective-permute-start.14 = (bf16[96,3200]{1,0:T(8,128)(2,1)}, bf16[96,3200]{1,0:T(8,128)(2,1)}, u32[]{:S(2)}, u32[]{:S(2)}) collective-permute-start(bf16[96,3200]{1,0:T(8,128)(2,1)} %collective-permute-done.10.refs_3_), channel_id=1, source_target_pairs={{0,1},{1,0},{2,3},{3,2},{4,5},{5,4},{6,7},{7,6},{8,9},{9,8},{10,11... | collective-permute-start | bytes 1843208 | tf_op jit(solution)/shard_map/ppermute | solution.py:420
  57.7 18.5 %collective-permute-start.4 = (bf16[256,768]{1,0:T(8,128)(2,1)}, bf16[256,768]{1,0:T(8,128)(2,1)}, u32[]{:S(2)}, u32[]{:S(2)}) collective-permute-start(bf16[256,768]{1,0:T(8,128)(2,1)} %get-tuple-element.158), channel_id=1, source_target_pairs={{0,8},{8,0},{16,24},{24,16},{1,9},{9,1},{17,25},{25,17},{2,10},{10... | collective-permute-start | bytes 1179656 | tf_op jit(solution)/shard_map/ppermute | solution.py:423
  78.8 7.1 %collective-permute-start.16 = (bf16[1024,768]{1,0:T(8,128)(2,1)S(1)}, bf16[1024,768]{1,0:T(8,128)(2,1)S(1)}, u32[]{:S(2)}, u32[]{:S(2)}) collective-permute-start(bf16[1024,768]{1,0:T(8,128)(2,1)S(1)} %multiply_convert_fusion.4.q_ref.k_own.v_own), channel_id=1, source_target_pairs={{0,1},{1,0},{2,3},{3,2},{4,5},{5,4},{6,7},{7,6},{8,9},{9,8},{10,11... | collective-permute-start | bytes 4718600 | tf_op jit(solution)/shard_map/ppermute | solution.py:420
  80.6 5.8 %collective-permute-start.17 = (bf16[1024,768]{1,0:T(8,128)(2,1)S(1)}, bf16[1024,768]{1,0:T(8,128)(2,1)S(1)}, u32[]{:S(2)}, u32[]{:S(2)}) collective-permute-start(bf16[1024,768]{1,0:T(8,128)(2,1)S(1)} %multiply_convert_fusion.3.q_ref.k_own.v_own), channel_id=1, source_target_pairs={{0,1},{1,0},{2,3},{3,2},{4,5},{5,4},{6,7},{7,6},{8,9},{9,8},{10,11... | collective-permute-start | bytes 4718600 | tf_op jit(solution)/shard_map/ppermute | solution.py:420
  82.4 6.3 %collective-permute-start.18 = (bf16[1024,768]{1,0:T(8,128)(2,1)S(1)}, bf16[1024,768]{1,0:T(8,128)(2,1)}, u32[]{:S(2)}, u32[]{:S(2)}) collective-permute-start(bf16[1024,768]{1,0:T(8,128)(2,1)S(1)} %multiply_convert_fusion.2.q_ref.k_own.v_own), channel_id=1, source_target_pairs={{0,1},{1,0},{2,3},{3,2},{4,5},{5,4},{6,7},{7,6},{8,9},{9,8},{10,11... | collective-permute-start | bytes 4718600 | tf_op jit(solution)/shard_map/ppermute | solution.py:420
  82.9 59.6 %copy-start.24 = (bf16[768,768]{1,0:T(8,128)(2,1)}, bf16[768,768]{1,0:T(8,128)(2,1)S(1)}, u32[]{:S(2)}) copy-start(bf16[768,768]{1,0:T(8,128)(2,1)S(1)} %constant_dynamic-update-slice_fusion.4.refs_0_) | copy-start | bytes 3538948
  82.9 47.0 %collective-permute-start.20 = (bf16[768,768]{1,0:T(8,128)(2,1)S(1)}, bf16[768,768]{1,0:T(8,128)(2,1)}, u32[]{:S(2)}, u32[]{:S(2)}) collective-permute-start(bf16[768,768]{1,0:T(8,128)(2,1)S(1)} %constant_dynamic-update-slice_fusion.4.refs_0_), channel_id=1, source_target_pairs={{0,2},{1,3},{2,0},{3,1},{4,6},{5,7},{6,4},{7,5},{8,10},{9,11},{10,... | collective-permute-start | bytes 3538952 | tf_op jit(solution)/shard_map/ppermute | solution.py:426
  84.5 53.2 %collective-permute-start.21 = (bf16[768,768]{1,0:T(8,128)(2,1)S(1)}, bf16[768,768]{1,0:T(8,128)(2,1)}, u32[]{:S(2)}, u32[]{:S(2)}) collective-permute-start(bf16[768,768]{1,0:T(8,128)(2,1)S(1)} %constant_dynamic-update-slice_fusion.4.refs_0_), channel_id=1, source_target_pairs={{0,4},{1,5},{2,6},{3,7},{4,0},{5,1},{6,2},{7,3},{8,12},{9,13},{10,... | collective-permute-start | bytes 3538952 | tf_op jit(solution)/shard_map/ppermute | solution.py:426
  86.0 51.7 %collective-permute-start.22 = (bf16[768,768]{1,0:T(8,128)(2,1)S(1)}, bf16[768,768]{1,0:T(8,128)(2,1)}, u32[]{:S(2)}, u32[]{:S(2)}) collective-permute-start(bf16[768,768]{1,0:T(8,128)(2,1)S(1)} %constant_dynamic-update-slice_fusion.4.refs_0_), channel_id=1, source_target_pairs={{0,6},{1,7},{2,4},{3,5},{4,2},{5,3},{6,0},{7,1},{8,14},{9,15},{10,... | collective-permute-start | bytes 3538952 | tf_op jit(solution)/shard_map/ppermute | solution.py:426
  86.5 22.8 %collective-permute-start.19 = (bf16[256,768]{1,0:T(8,128)(2,1)S(1)}, bf16[256,768]{1,0:T(8,128)(2,1)S(1)}, u32[]{:S(2)}, u32[]{:S(2)}) collective-permute-start(bf16[256,768]{1,0:T(8,128)(2,1)S(1)} %copy-done.38), channel_id=1, source_target_pairs={{0,16},{8,24},{16,0},{24,8},{1,17},{9,25},{17,1},{25,9},{2,18},{10... | collective-permute-start | bytes 1179656 | tf_op jit(solution)/shard_map/ppermute | solution.py:423
  137.7 4.8 collective-permute-start.23
  137.7 7.8 %collective-permute-start.24 = (bf16[768,768]{1,0:T(8,128)(2,1)}, bf16[768,768]{1,0:T(8,128)(2,1)}, u32[]{:S(2)}, u32[]{:S(2)}) collective-permute-start(bf16[768,768]{1,0:T(8,128)(2,1)} %collective-permute-done.20.refs_1_), channel_id=1, source_target_pairs={{0,1},{1,0},{2,3},{3,2},{4,5},{5,4},{6,7},{7,6},{8,9},{9,8},{10,11... | collective-permute-start | bytes 3538952 | tf_op jit(solution)/shard_map/ppermute | solution.py:420
  138.2 7.3 %collective-permute-start.25 = (bf16[768,768]{1,0:T(8,128)(2,1)}, bf16[768,768]{1,0:T(8,128)(2,1)}, u32[]{:S(2)}, u32[]{:S(2)}) collective-permute-start(bf16[768,768]{1,0:T(8,128)(2,1)} %collective-permute-done.21.refs_2_), channel_id=1, source_target_pairs={{0,1},{1,0},{2,3},{3,2},{4,5},{5,4},{6,7},{7,6},{8,9},{9,8},{10,11... | collective-permute-start | bytes 3538952 | tf_op jit(solution)/shard_map/ppermute | solution.py:420
  138.2 7.5 %collective-permute-start.26 = (bf16[768,768]{1,0:T(8,128)(2,1)}, bf16[768,768]{1,0:T(8,128)(2,1)}, u32[]{:S(2)}, u32[]{:S(2)}) collective-permute-start(bf16[768,768]{1,0:T(8,128)(2,1)} %collective-permute-done.22.refs_3_), channel_id=1, source_target_pairs={{0,1},{1,0},{2,3},{3,2},{4,5},{5,4},{6,7},{7,6},{8,9},{9,8},{10,11... | collective-permute-start | bytes 3538952 | tf_op jit(solution)/shard_map/ppermute | solution.py:420
  139.5 52.8 %collective-permute-start.27 = (bf16[256,768]{1,0:T(8,128)(2,1)}, bf16[256,768]{1,0:T(8,128)(2,1)S(1)}, u32[]{:S(2)}, u32[]{:S(2)}) collective-permute-start(bf16[256,768]{1,0:T(8,128)(2,1)} %get-tuple-element.227), channel_id=1, source_target_pairs={{0,8},{8,0},{16,24},{24,16},{1,9},{9,1},{17,25},{25,17},{2,10},{10... | collective-permute-start | bytes 1179656 | tf_op jit(solution)/shard_map/ppermute | solution.py:423
  143.6 48.8 %collective-permute-start.28 = (bf16[256,768]{1,0:T(8,128)(2,1)}, bf16[256,768]{1,0:T(8,128)(2,1)S(1)}, u32[]{:S(2)}, u32[]{:S(2)}) collective-permute-start(bf16[256,768]{1,0:T(8,128)(2,1)} %get-tuple-element.229), channel_id=1, source_target_pairs={{0,24},{8,16},{16,8},{24,0},{1,25},{9,17},{17,9},{25,1},{2,26},{10... | collective-permute-start | bytes 1179656 | tf_op jit(solution)/shard_map/ppermute | solution.py:423
  236.2 5.3 collective-permute-start.29
  241.5 21.2 %collective-permute-start.30 = (bf16[4,96,3840]{2,1,0:T(8,128)(2,1)}, bf16[4,96,3840]{2,1,0:T(8,128)(2,1)}, u32[]{:S(2)}, u32[]{:S(2)}) collective-permute-start(bf16[4,96,3840]{2,1,0:T(8,128)(2,1)} %fusion.13), channel_id=1, source_target_pairs={{0,1},{1,0},{2,3},{3,2},{4,5},{5,4},{6,7},{7,6},{8,9},{9,8},{10,11... | collective-permute-start | bytes 8847368 | tf_op jit(solution)/shard_map/ppermute | solution.py:420
  245.8 23.2 %collective-permute-start.33 = (bf16[384,768]{1,0:T(8,128)(2,1)S(1)}, bf16[384,768]{1,0:T(8,128)(2,1)S(1)}, u32[]{:S(2)}, u32[]{:S(2)}) collective-permute-start(bf16[384,768]{1,0:T(8,128)(2,1)S(1)} %get-tuple-element.407), channel_id=1, source_target_pairs={{0,2},{1,3},{2,0},{3,1},{4,6},{5,7},{6,4},{7,5},{8,10},{9,11},{10,... | collective-permute-start | bytes 1769480 | tf_op jit(solution)/shard_map/ppermute | solution.py:426
  257.8 50.3 %collective-permute-start.34 = (bf16[384,768]{1,0:T(8,128)(2,1)}, bf16[384,768]{1,0:T(8,128)(2,1)}, u32[]{:S(2)}, u32[]{:S(2)}) collective-permute-start(bf16[384,768]{1,0:T(8,128)(2,1)} %get-tuple-element.406), channel_id=1, source_target_pairs={{0,4},{1,5},{2,6},{3,7},{4,0},{5,1},{6,2},{7,3},{8,12},{9,13},{10,... | collective-permute-start | bytes 1769480 | tf_op jit(solution)/shard_map/ppermute | solution.py:426
  261.3 48.4 %collective-permute-start.35 = (bf16[384,768]{1,0:T(8,128)(2,1)}, bf16[384,768]{1,0:T(8,128)(2,1)}, u32[]{:S(2)}, u32[]{:S(2)}) collective-permute-start(bf16[384,768]{1,0:T(8,128)(2,1)} %get-tuple-element.405), channel_id=1, source_target_pairs={{0,6},{1,7},{2,4},{3,5},{4,2},{5,3},{6,0},{7,1},{8,14},{9,15},{10,... | collective-permute-start | bytes 1769480 | tf_op jit(solution)/shard_map/ppermute | solution.py:426
  266.9 49.1 %collective-permute-start.36 = (bf16[96,3840]{1,0:T(8,128)(2,1)}, bf16[96,3840]{1,0:T(8,128)(2,1)S(1)}, u32[]{:S(2)}, u32[]{:S(2)}) collective-permute-start(bf16[96,3840]{1,0:T(8,128)(2,1)} %get-tuple-element.403), channel_id=1, source_target_pairs={{0,2},{1,3},{2,0},{3,1},{4,6},{5,7},{6,4},{7,5},{8,10},{9,11},{10,... | collective-permute-start | bytes 2211848 | tf_op jit(solution)/shard_map/ppermute | solution.py:426
  267.5 52.3 %collective-permute-start.37 = (bf16[96,3840]{1,0:T(8,128)(2,1)}, bf16[96,3840]{1,0:T(8,128)(2,1)}, u32[]{:S(2)}, u32[]{:S(2)}) collective-permute-start(bf16[96,3840]{1,0:T(8,128)(2,1)} %get-tuple-element.402), channel_id=1, source_target_pairs={{0,4},{1,5},{2,6},{3,7},{4,0},{5,1},{6,2},{7,3},{8,12},{9,13},{10,... | collective-permute-start | bytes 2211848 | tf_op jit(solution)/shard_map/ppermute | solution.py:426
  269.0 50.8 %collective-permute-start.38 = (bf16[96,3840]{1,0:T(8,128)(2,1)}, bf16[96,3840]{1,0:T(8,128)(2,1)}, u32[]{:S(2)}, u32[]{:S(2)}) collective-permute-start(bf16[96,3840]{1,0:T(8,128)(2,1)} %get-tuple-element.401), channel_id=1, source_target_pairs={{0,6},{1,7},{2,4},{3,5},{4,2},{5,3},{6,0},{7,1},{8,14},{9,15},{10,... | collective-permute-start | bytes 2211848 | tf_op jit(solution)/shard_map/ppermute | solution.py:426
  308.1 60.2 %collective-permute-start.31 = (bf16[256,768]{1,0:T(8,128)(2,1)}, bf16[256,768]{1,0:T(8,128)(2,1)}, u32[]{:S(2)}, u32[]{:S(2)}) collective-permute-start(bf16[256,768]{1,0:T(8,128)(2,1)} %get-tuple-element.240), channel_id=1, source_target_pairs={{0,8},{8,0},{16,24},{24,16},{1,9},{9,1},{17,25},{25,17},{2,10},{10... | collective-permute-start | bytes 1179656 | tf_op jit(solution)/shard_map/ppermute | solution.py:423
  309.7 60.8 %collective-permute-start.32 = (bf16[256,768]{1,0:T(8,128)(2,1)}, bf16[256,768]{1,0:T(8,128)(2,1)}, u32[]{:S(2)}, u32[]{:S(2)}) collective-permute-start(bf16[256,768]{1,0:T(8,128)(2,1)} %get-tuple-element.241), channel_id=1, source_target_pairs={{0,16},{8,24},{16,0},{24,8},{1,17},{9,25},{17,1},{25,9},{2,18},{10... | collective-permute-start | bytes 1179656 | tf_op jit(solution)/shard_map/ppermute | solution.py:423
  315.9 39.7 %collective-permute-start.40 = (bf16[192,768]{1,0:T(8,128)(2,1)}, bf16[192,768]{1,0:T(8,128)(2,1)}, u32[]{:S(2)}, u32[]{:S(2)}) collective-permute-start(bf16[192,768]{1,0:T(8,128)(2,1)} %get-tuple-element.458), channel_id=1, source_target_pairs={{0,8},{8,0},{16,24},{24,16},{1,9},{9,1},{17,25},{25,17},{2,10},{10... | collective-permute-start | bytes 884744 | tf_op jit(solution)/shard_map/ppermute | solution.py:423
  319.8 41.3 %collective-permute-start.42 = (bf16[2,1024,256]{2,1,0:T(8,128)(2,1)}, bf16[2,1024,256]{2,1,0:T(8,128)(2,1)}, u32[]{:S(2)}, u32[]{:S(2)}) collective-permute-start(bf16[2,1024,256]{2,1,0:T(8,128)(2,1)} %get-tuple-element.258), channel_id=1, source_target_pairs={{0,1},{1,0},{2,3},{3,2},{4,5},{5,4},{6,7},{7,6},{8,9},{9,8},{10,11... | collective-permute-start | bytes 3145736 | tf_op jit(solution)/shard_map/ppermute | solution.py:420
  322.3 39.0 %collective-permute-start.43 = (bf16[48,3840]{1,0:T(8,128)(2,1)S(1)}, bf16[48,3840]{1,0:T(8,128)(2,1)S(1)}, u32[]{:S(2)}, u32[]{:S(2)}) collective-permute-start(bf16[48,3840]{1,0:T(8,128)(2,1)S(1)} %get-tuple-element.454), channel_id=1, source_target_pairs={{0,8},{8,0},{16,24},{24,16},{1,9},{9,1},{17,25},{25,17},{2,10},{10... | collective-permute-start | bytes 1105928 | tf_op jit(solution)/shard_map/ppermute | solution.py:423
  323.3 38.8 %copy-start.14 = (f32[2,1024,256]{2,1,0:T(8,128)S(1)}, f32[2,1024,256]{2,1,0:T(8,128)}, u32[]{:S(2)}) copy-start(f32[2,1024,256]{2,1,0:T(8,128)} %get-tuple-element.264) | copy-start | bytes 6291460
  355.7 47.3 %collective-permute-start.45 = (bf16[256,768]{1,0:T(8,128)(2,1)}, bf16[256,768]{1,0:T(8,128)(2,1)}, u32[]{:S(2)}, u32[]{:S(2)}) collective-permute-start(bf16[256,768]{1,0:T(8,128)(2,1)} %get-tuple-element.261), channel_id=1, source_target_pairs={{0,24},{8,16},{16,8},{24,0},{1,25},{9,17},{17,9},{25,1},{2,26},{10... | collective-permute-start | bytes 1179656 | tf_op jit(solution)/shard_map/ppermute | solution.py:423
  361.1 45.2 %collective-permute-start.39 = (bf16[2,1024,256]{2,1,0:T(8,128)(2,1)}, bf16[2,1024,256]{2,1,0:T(8,128)(2,1)}, u32[]{:S(2)}, u32[]{:S(2)}) collective-permute-start(bf16[2,1024,256]{2,1,0:T(8,128)(2,1)} %get-tuple-element.254), channel_id=1, source_target_pairs={{0,1},{1,0},{2,3},{3,2},{4,5},{5,4},{6,7},{7,6},{8,9},{9,8},{10,11... | collective-permute-start | bytes 3145736 | tf_op jit(solution)/shard_map/ppermute | solution.py:420
  361.3 41.7 %collective-permute-start.41 = (bf16[192,768]{1,0:T(8,128)(2,1)}, bf16[192,768]{1,0:T(8,128)(2,1)}, u32[]{:S(2)}, u32[]{:S(2)}) collective-permute-start(bf16[192,768]{1,0:T(8,128)(2,1)} %add_convert_fusion.10), channel_id=1, source_target_pairs={{0,16},{8,24},{16,0},{24,8},{1,17},{9,25},{17,1},{25,9},{2,18},{10... | collective-permute-start | bytes 884744 | tf_op jit(solution)/shard_map/ppermute | solution.py:423
  368.3 38.0 %collective-permute-start.44 = (bf16[48,3840]{1,0:T(8,128)(2,1)S(1)}, bf16[48,3840]{1,0:T(8,128)(2,1)}, u32[]{:S(2)}, u32[]{:S(2)}) collective-permute-start(bf16[48,3840]{1,0:T(8,128)(2,1)S(1)} %add_convert_fusion.8), channel_id=1, source_target_pairs={{0,16},{8,24},{16,0},{24,8},{1,17},{9,25},{17,1},{25,9},{2,18},{10... | collective-permute-start | bytes 1105928 | tf_op jit(solution)/shard_map/ppermute | solution.py:423
  402.5 10.1 %collective-permute-start.46 = (bf16[2,1024,256]{2,1,0:T(8,128)(2,1)}, bf16[2,1024,256]{2,1,0:T(8,128)(2,1)S(1)}, u32[]{:S(2)}, u32[]{:S(2)}) collective-permute-start(bf16[2,1024,256]{2,1,0:T(8,128)(2,1)} %get-tuple-element.273), channel_id=1, source_target_pairs={{0,1},{1,0},{2,3},{3,2},{4,5},{5,4},{6,7},{7,6},{8,9},{9,8},{10,11... | collective-permute-start | bytes 3145736 | tf_op jit(solution)/shard_map/ppermute | solution.py:420
  430.9 4.0 collective-permute-start.51
  434.3 24.3 %collective-permute-start.47 = (bf16[2,256,768]{2,1,0:T(8,128)(2,1)}, bf16[2,256,768]{2,1,0:T(8,128)(2,1)}, u32[]{:S(2)}, u32[]{:S(2)}) collective-permute-start(bf16[2,256,768]{2,1,0:T(8,128)(2,1)} %pad_maximum_fusion.9), channel_id=1, source_target_pairs={{0,1},{1,0},{2,3},{3,2},{4,5},{5,4},{6,7},{7,6},{8,9},{9,8},{10,11... | collective-permute-start | bytes 2359304 | tf_op jit(solution)/shard_map/ppermute | solution.py:420
  436.7 27.9 %collective-permute-start.52 = (bf16[96,2432]{1,0:T(8,128)(2,1)S(1)}, bf16[96,2432]{1,0:T(8,128)(2,1)S(1)}, u32[]{:S(2)}, u32[]{:S(2)}) collective-permute-start(bf16[96,2432]{1,0:T(8,128)(2,1)S(1)} %get-tuple-element.411), channel_id=1, source_target_pairs={{0,2},{1,3},{2,0},{3,1},{4,6},{5,7},{6,4},{7,5},{8,10},{9,11},{10,... | collective-permute-start | bytes 1400840 | tf_op jit(solution)/shard_map/ppermute | solution.py:426
  453.4 18.8 %collective-permute-start.48 = (bf16[256,768]{1,0:T(8,128)(2,1)S(1)}, bf16[256,768]{1,0:T(8,128)(2,1)S(1)}, u32[]{:S(2)}, u32[]{:S(2)}) collective-permute-start(bf16[256,768]{1,0:T(8,128)(2,1)S(1)} %get-tuple-element.422), channel_id=1, source_target_pairs={{0,8},{8,0},{16,24},{24,16},{1,9},{9,1},{17,25},{25,17},{2,10},{10... | collective-permute-start | bytes 1179656 | tf_op jit(solution)/shard_map/ppermute | solution.py:423
  456.1 29.7 %collective-permute-start.49 = (bf16[256,768]{1,0:T(8,128)(2,1)S(1)}, bf16[256,768]{1,0:T(8,128)(2,1)S(1)}, u32[]{:S(2)}, u32[]{:S(2)}) collective-permute-start(bf16[256,768]{1,0:T(8,128)(2,1)S(1)} %get-tuple-element.421), channel_id=1, source_target_pairs={{0,16},{8,24},{16,0},{24,8},{1,17},{9,25},{17,1},{25,9},{2,18},{10... | collective-permute-start | bytes 1179656 | tf_op jit(solution)/shard_map/ppermute | solution.py:423
  457.5 28.3 %collective-permute-start.50 = (bf16[256,768]{1,0:T(8,128)(2,1)S(1)}, bf16[256,768]{1,0:T(8,128)(2,1)S(1)}, u32[]{:S(2)}, u32[]{:S(2)}) collective-permute-start(bf16[256,768]{1,0:T(8,128)(2,1)S(1)} %get-tuple-element.420), channel_id=1, source_target_pairs={{0,24},{8,16},{16,8},{24,0},{1,25},{9,17},{17,9},{25,1},{2,26},{10... | collective-permute-start | bytes 1179656 | tf_op jit(solution)/shard_map/ppermute | solution.py:423
  459.9 26.5 %collective-permute-start.54 = (bf16[96,2432]{1,0:T(8,128)(2,1)S(1)}, bf16[96,2432]{1,0:T(8,128)(2,1)S(1)}, u32[]{:S(2)}, u32[]{:S(2)}) collective-permute-start(bf16[96,2432]{1,0:T(8,128)(2,1)S(1)} %get-tuple-element.409), channel_id=1, source_target_pairs={{0,4},{1,5},{2,6},{3,7},{4,0},{5,1},{6,2},{7,3},{8,12},{9,13},{10,... | collective-permute-start | bytes 1400840 | tf_op jit(solution)/shard_map/ppermute | solution.py:426
  464.6 21.8 %collective-permute-start.55 = (bf16[96,2432]{1,0:T(8,128)(2,1)S(1)}, bf16[96,2432]{1,0:T(8,128)(2,1)S(1)}, u32[]{:S(2)}, u32[]{:S(2)}) collective-permute-start(bf16[96,2432]{1,0:T(8,128)(2,1)S(1)} %get-tuple-element.286), channel_id=1, source_target_pairs={{0,6},{1,7},{2,4},{3,5},{4,2},{5,3},{6,0},{7,1},{8,14},{9,15},{10,... | collective-permute-start | bytes 1400840 | tf_op jit(solution)/shard_map/ppermute | solution.py:426
  486.3 17.6 %collective-permute-start.53 = (bf16[2,256,768]{2,1,0:T(8,128)(2,1)S(1)}, bf16[2,256,768]{2,1,0:T(8,128)(2,1)S(1)}, u32[]{:S(2)}, u32[]{:S(2)}) collective-permute-start(bf16[2,256,768]{2,1,0:T(8,128)(2,1)S(1)} %pad_maximum_fusion.11), channel_id=1, source_target_pairs={{0,1},{1,0},{2,3},{3,2},{4,5},{5,4},{6,7},{7,6},{8,9},{9,8},{10,11... | collective-permute-start | bytes 2359304 | tf_op jit(solution)/shard_map/ppermute | solution.py:420
  487.8 14.6 %collective-permute-start.56 = (bf16[48,2432]{1,0:T(8,128)(2,1)S(1)}, bf16[48,2432]{1,0:T(8,128)(2,1)S(1)}, u32[]{:S(2)}, u32[]{:S(2)}) collective-permute-start(bf16[48,2432]{1,0:T(8,128)(2,1)S(1)} %dynamic-slice_bitcast_fusion.10), channel_id=1, source_target_pairs={{0,8},{8,0},{16,24},{24,16},{1,9},{9,1},{17,25},{25,17},{2,10},{10... | collective-permute-start | bytes 700424 | tf_op jit(solution)/shard_map/ppermute | solution.py:423
  496.9 16.7 %collective-permute-start.59 = (bf16[192,768]{1,0:T(8,128)(2,1)S(1)}, bf16[192,768]{1,0:T(8,128)(2,1)S(1)}, u32[]{:S(2)}, u32[]{:S(2)}) collective-permute-start(bf16[192,768]{1,0:T(8,128)(2,1)S(1)} %add_convert_fusion.9), channel_id=1, source_target_pairs={{0,8},{8,0},{16,24},{24,16},{1,9},{9,1},{17,25},{25,17},{2,10},{10... | collective-permute-start | bytes 884744 | tf_op jit(solution)/shard_map/ppermute | solution.py:423
  498.1 23.3 %collective-permute-start.60 = (bf16[48,3840]{1,0:T(8,128)(2,1)S(1)}, bf16[48,3840]{1,0:T(8,128)(2,1)S(1)}, u32[]{:S(2)}, u32[]{:S(2)}) collective-permute-start(bf16[48,3840]{1,0:T(8,128)(2,1)S(1)} %add_convert_fusion.7), channel_id=1, source_target_pairs={{0,8},{8,0},{16,24},{24,16},{1,9},{9,1},{17,25},{25,17},{2,10},{10... | collective-permute-start | bytes 1105928 | tf_op jit(solution)/shard_map/ppermute | solution.py:423
  502.4 20.2 %collective-permute-start.57 = (bf16[48,2432]{1,0:T(8,128)(2,1)S(1)}, bf16[48,2432]{1,0:T(8,128)(2,1)S(1)}, u32[]{:S(2)}, u32[]{:S(2)}) collective-permute-start(bf16[48,2432]{1,0:T(8,128)(2,1)S(1)} %fusion.33), channel_id=1, source_target_pairs={{0,16},{8,24},{16,0},{24,8},{1,17},{9,25},{17,1},{25,9},{2,18},{10... | collective-permute-start | bytes 700424 | tf_op jit(solution)/shard_map/ppermute | solution.py:423
  522.6 7.6 %collective-permute-start.58 = (bf16[48,2432]{1,0:T(8,128)(2,1)S(1)}, bf16[48,2432]{1,0:T(8,128)(2,1)S(1)}, u32[]{:S(2)}, u32[]{:S(2)}) collective-permute-start(bf16[48,2432]{1,0:T(8,128)(2,1)S(1)} %add_convert_fusion.11), channel_id=1, source_target_pairs={{0,8},{8,0},{16,24},{24,16},{1,9},{9,1},{17,25},{25,17},{2,10},{10... | collective-permute-start | bytes 700424 | tf_op jit(solution)/shard_map/ppermute | solution.py:423
  (69 other events, 617.7 us)

commit v8 on v7

--- a/solution.py
+++ b/solution.py
@@ -772,7 +772,11 @@
     mixed_three = mixed_part(after(three, input_part))
     input_low = (input_part + dot(mixed_three, mix_parts[2].T)).astype(bf16)
     input_slots = from_sequence_send(here, list(input_low.reshape(here.columns, half, width)))
-    mixed_all = after(jnp.concatenate([mixed_one, mixed_two, mixed_three], axis=1), input_low)
+    down_half, down_other = column_third(here, down_half, down_other)
+    mixed_all, down_half, down_other = after(
+        (jnp.concatenate([mixed_one, mixed_two, mixed_three], axis=1), down_half, down_other), input_low
+    )
+    up_half, up_other = column_third(here, *after((up_half, up_other), down_other))
     mix_grad = dot(flat.T, mixed_all).astype(bf16)
 
     sums = [column_sums(m) for m in (mixed_one, mixed_two, mixed_three)]
@@ -793,17 +797,16 @@
     columns_grad = jnp.pad(lines_grad, ((0, LANES - lines_grad.shape[0]), (0, 0))).T
     whole = jnp.concatenate([mix_grad, lax.optimization_barrier(columns_grad).astype(bf16)], axis=1).reshape(shards, own, -1)
     mix_share, mix_lows = share_plane(here, *share_pair(here, whole))
+    mix_lows, up_half, up_other = lax.optimization_barrier((mix_lows, up_half, up_other))
     mix_others = share_send(here, mix_lows, True)
     input_mark = mix_others[0]
     mix_share = share_sum(mix_share, mix_others)
     mix_half, mix_other = column_first(here, mix_share)
-    down_half, down_other = column_third(here, *after((down_half, down_other), mix_share))
-    up_half, up_other = column_third(here, *after((up_half, up_other), mix_share))
     mix_half, mix_other = column_second(here, mix_half, mix_other)
     down_half, down_other, up_half, up_other = after((down_half, down_other, up_half, up_other), mix_half)
     mix_last = column_last(here, *column_third(here, mix_half, mix_other))
 
-    output = from_sequence_end(here, after(output_slots, input_low), groups)
+    output = from_sequence_end(here, after(output_slots, mix_half), groups)
     final_input = from_sequence_end(here, after(input_slots, input_mark), groups).astype(f32)
     final_down = column_last(here, down_half, down_other).astype(f32)
     final_up_merge = column_last(here, up_half, up_other).astype(f32)

time: 540 us -> 534 us (0.989)
  starting transfers between devices: 107 us -> 83 us
  Pallas kernels: 166 us -> 173 us
  waiting for transfers between devices: 85.3 us -> 91.5 us
    ppermute x15, starting transfers between devices: 50.7 us -> 33.1 us  [aside(): return lax.ppermute(values, 'fsdp', xor_pairs(self.shards, 2 * bits))]
    ppermute x24, starting transfers between devices: 52.4 us -> 40.8 us  [across(): return lax.ppermute(values, 'seq', xor_pairs(self.columns, bits))]
    ppermute x15, waiting for transfers between devices: 18.9 us -> 26.5 us  [aside(): return lax.ppermute(values, 'fsdp', xor_pairs(self.shards, 2 * bits))]
    unnamed x165 -> x173, local copies, waits for them, and re-layouts: 17.4 us -> 17.3 us
  transfers between devices with their start and end apart: 61 -> 61, of which waited for: 18 -> 18; matrix products, arithmetic and copies ran while one was open for 18% -> 20% of each run, Pallas kernels for 31% -> 33%
where the time goes in v8:
time: 534 us; the launch traced here: 524 us
  Pallas kernels  173 us (32%)
  waiting for transfers between devices  91.5 us (17%)
  starting transfers between devices  83 us (16%)
  matrix products  82.6 us (15%)
  other arithmetic  52.2 us (10%)
  local copies, waits for them, and re-layouts  39.2 us (7%)
    pallas_call x3, Pallas kernels, attention_backward(): pl.pallas_call(functools.partial(backward_kernel, size=size), grid_spec=p...  101 us
    dot_general x16, matrix products, dot(): return jnp.dot(a, b, preferred_element_type=f32)  82.6 us
    pallas_call x3, Pallas kernels, attention_forward(): pl.pallas_call(functools.partial(forward_kernel, size=size, plan=(len(pie...  65.1 us
    ppermute x24, waiting for transfers between devices, across(): return lax.ppermute(values, 'seq', xor_pairs(self.columns, bits))  63.1 us
    ppermute x24, starting transfers between devices, across(): return lax.ppermute(values, 'seq', xor_pairs(self.columns, bits))  40.8 us
    ppermute x15, starting transfers between devices, aside(): return lax.ppermute(values, 'fsdp', xor_pairs(self.shards, 2 * bits))  33.1 us
    ppermute x15, waiting for transfers between devices, aside(): return lax.ppermute(values, 'fsdp', xor_pairs(self.shards, 2 * bits))  26.5 us
    unnamed x173, local copies, waits for them, and re-layouts  17.3 us
  transfers between devices with their start and end apart: 61, of which 18 were waited for; matrix products, arithmetic and copies ran while one was open for 20% of the time, Pallas kernels for 33%

profile of v8, /device:TPU:0, one launch (start us, length us, event | category | flops | bytes accessed | tf_op | source)
XLA Modules:
  0.0 524.0 jit_solution(11051672434843863991)
XLA Ops:
  3.0 2.0 pack_projection.1.refs_0_
  5.0 3.0 collective-permute-start.8
  8.0 1.5 collective-permute-start.9
  9.5 2.1 collective-permute-start.1
  11.6 2.5 collective-permute-start.3
  18.0 3.7 collective-permute-done.2
  26.6 1.7 collective-permute-start.6
  31.0 5.8 %collective-permute-done.9.refs_2_ = bf16[96,3200]{1,0:T(8,128)(2,1)} collective-permute-done((bf16[96,3200]{1,0:T(8,128)(2,1)}, bf16[96,3200]{1,0:T(8,128)(2,1)}, u32[]{:S(2)}, u32[]{:S(2)}) %collective-permute-start.9) | collective-permute-done | bytes 614432 | tf_op jit(solution)/shard_map/ppermute | solution.py:426
  36.8 18.0 %collective-permute-done.5 = bf16[256,768]{1,0:T(8,128)(2,1)S(1)} collective-permute-done((bf16[256,768]{1,0:T(8,128)(2,1)}, bf16[256,768]{1,0:T(8,128)(2,1)S(1)}, u32[]{:S(2)}, u32[]{:S(2)}) %collective-permute-start.5) | collective-permute-done | bytes 393248 | tf_op jit(solution)/shard_map/ppermute | solution.py:423
  57.8 8.8 %collective-permute-start.4 = (bf16[256,768]{1,0:T(8,128)(2,1)}, bf16[256,768]{1,0:T(8,128)(2,1)}, u32[]{:S(2)}, u32[]{:S(2)}) collective-permute-start(bf16[256,768]{1,0:T(8,128)(2,1)} %get-tuple-element.163), channel_id=1, source_target_pairs={{0,8},{8,0},{16,24},{24,16},{1,9},{9,1},{17,25},{25,17},{2,10},{10... | collective-permute-start | bytes 1179656 | tf_op jit(solution)/shard_map/ppermute | solution.py:423
  69.3 5.2 place_parts.1
  82.9 1.6 collective-permute-start.20
  86.5 2.2 collective-permute-start.19
  88.7 21.4 %attention_forward.3 = (bf16[1024,256]{1,0:T(8,128)(2,1)}, bf16[1024,256]{1,0:T(8,128)(2,1)}) custom-call(s32[10]{0:T(128)} %pad_add_fusion.3.info, bf16[1024,768]{1,0:T(8,128)(2,1)} %copy-done.1, bf16[1024,768]{1,0:T(8,128)(2,1)} %copy-done.1, bf16[1024,768]{1,0:T(8,128)(2,1)} %copy-done.4, bf16[1024,768]{1,0:T(8,128)(2,1)} %copy-done.1, ...), custom_call_target="tpu_custom_call" | custom-call | flops 1073741824 | bytes 4194304 | tf_op jit(solution)/shard_map/attention_forward/pallas_call | solution.py:176
  110.2 21.3 %attention_forward.4 = (bf16[1024,256]{1,0:T(8,128)(2,1)}, bf16[1024,256]{1,0:T(8,128)(2,1)}) custom-call(s32[10]{0:T(128)} %pad_add_fusion.3.info, bf16[1024,768]{1,0:T(8,128)(2,1)} %copy-done, bf16[1024,768]{1,0:T(8,128)(2,1)} %copy-done, bf16[1024,768]{1,0:T(8,128)(2,1)} %copy-done.3, bf16[1024,768]{1,0:T(8,128)(2,1)} %copy-done, ...), custom_call_target="tpu_custom_call" | custom-call | flops 1073741824 | bytes 4194304 | tf_op jit(solution)/shard_map/attention_forward/pallas_call | solution.py:176
  131.5 6.2 %collective-permute-done.21.refs_2_ = bf16[768,768]{1,0:T(8,128)(2,1)} collective-permute-done((bf16[768,768]{1,0:T(8,128)(2,1)S(1)}, bf16[768,768]{1,0:T(8,128)(2,1)}, u32[]{:S(2)}, u32[]{:S(2)}) %collective-permute-start.21) | collective-permute-done | bytes 1179680 | tf_op jit(solution)/shard_map/ppermute | solution.py:426
  139.6 1.8 collective-permute-start.27
  143.6 1.9 collective-permute-start.28
  145.7 22.3 %attention_forward.5 = (bf16[1024,256]{1,0:T(8,128)(2,1)}, bf16[1024,256]{1,0:T(8,128)(2,1)}, bf16[8,96,3072]{2,1,0:T(8,128)(2,1)}, bf16[8,384,768]{2,1,0:T(8,128)(2,1)}) custom-call(s32[18]{0:T(128)} %concatenate.84.info, bf16[1024,768]{1,0:T(8,128)(2,1)} %copy-done.2, bf16[1024,768]{1,0:T(8,128)(2,1)} %copy-done.2, ...), custom_call_target="tpu_custom_call" | custom-call | flops 1073741824 | bytes 4194304 | tf_op jit(solution)/shard_map/attention_forward/pallas_call | solution.py:176
  169.2 3.9 fusion.59
  173.7 13.4 %fusion.4 = (bf16[1024,3072]{1,0:T(8,128)(2,1)}, bf16[1024,3072]{1,0:T(8,128)(2,1)S(1)}) fusion(f32[3072]{0:T(1024)S(1)} %add.446, bf16[768,3072]{1,0:T(8,128)(2,1)S(1)} %bitcast.297, f32[1024,768]{1,0:T(8,128)S(1)} %get-tuple-element.498, f32[768]{0:T(1024)S(1)} %get-tuple-element.394, f32[768]{0:T(1024)S(1)} %get-tuple-element.395, ...), kind=kOutput, calls=%fused_computation.5 | convolution fusion | flops 4873519104 | bytes 20473856 | tf_op jit(solution)/shard_map/dot_general | solution.py:387
  187.2 5.5 %fusion.60 = (f32[1024]{0:T(1024)S(1)}, f32[1024,768]{1,0:T(8,128)S(1)}) fusion(f32[768]{0:T(1024)S(1)} %get-tuple-element.393, bf16[1024,3072]{1,0:T(8,128)(2,1)S(1)} %get-tuple-element.225, bf16[3072,768]{1,0:T(8,128)(2,1)S(1)} %bitcast.302, f32[768]{0:T(1024)S(1)} %get-tuple-element.394, f32[768]{0:T(1024)S(1)} %get-tuple-element.395, ...), kind=kOutput, calls=%fused_computation.266 | convolution fusion | flops 4837342208 | bytes 17323008 | tf_op jit(solution)/shard_map/dot_general | solution.py:387
  193.3 3.3 fusion.11
  196.6 3.0 convert_reduce_fusion.2
  199.6 5.7 %convolution_convert_fusion.1 = bf16[3072,768]{1,0:T(8,128)(2,1)S(1)} fusion(bf16[1024,3072]{1,0:T(8,128)(2,1)S(1)} %get-tuple-element.225, f32[1024,768]{1,0:T(8,128)S(1)} %get-tuple-element.406), kind=kOutput, calls=%fused_computation.21 | convolution fusion | flops 4834983936 | bytes 14155776 | tf_op jit(solution)/shard_map/dot_general | solution.py:387
  205.3 12.7 %convert_reduce_fusion = (bf16[3072]{0:T(1024)(128)(2,1)}, bf16[1024,3072]{1,0:T(8,128)(2,1)}) fusion(bf16[1024,3072]{1,0:T(8,128)(2,1)} %get-tuple-element.239, bf16[3072,768]{1,0:T(8,128)(2,1)} %bitcast.299, f32[1024,768]{1,0:T(8,128)S(1)} %get-tuple-element.406), kind=kOutput, calls=%fused_computation.6 | convolution fusion | flops 4848350208 | bytes 20453376 | tf_op jit(solution)/shard_map/dot_general | solution.py:387
  218.0 8.8 %multiply_reduce_fusion = (bf16[768]{0:T(1024)(128)(2,1)}, f32[1024]{0:T(1024)S(1)}, f32[1024]{0:T(1024)S(1)}, bf16[768]{0:T(1024)(128)(2,1)}, f32[1024,768]{1,0:T(8,128)S(1)}) fusion(f32[1024,768]{1,0:T(8,128)S(1)} %get-tuple-element.498, f32[1024]{0:T(1024)S(1)} %add_rsqrt_fusion.1, f32[1024]{0:T(1024)S(1)} %broadcast_multiply_fusion.5, ...), kind=kOutput, calls=%fused_computation.35 | convolution fusion | flops 4839698432 | bytes 20469760 | tf_op jit(solution)/shard_map/dot_general | solution.py:387
  226.8 8.5 %convolution_convert_fusion = bf16[768,3072]{1,0:T(8,128)(2,1)S(1)} fusion(bf16[1024,3072]{1,0:T(8,128)(2,1)} %get-tuple-element.503, f32[1024,768]{1,0:T(8,128)S(1)} %get-tuple-element.498, f32[768]{0:T(1024)S(1)} %get-tuple-element.394, f32[768]{0:T(1024)S(1)} %get-tuple-element.395, f32[1024]{0:T(1024)S(1)} %add_rsqrt_fusion.1, ...), kind=kOutput, calls=%fused_computation.20 | convolution fusion | flops 4838129664 | bytes 14170112 | tf_op jit(solution)/shard_map/dot_general | solution.py:387
  235.3 1.7 dynamic-slice_bitcast_fusion
  240.5 1.8 fusion.13
  242.4 4.3 fusion.18
  246.6 9.1 %collective-permute-start.33 = (bf16[384,768]{1,0:T(8,128)(2,1)S(1)}, bf16[384,768]{1,0:T(8,128)(2,1)S(1)}, u32[]{:S(2)}, u32[]{:S(2)}) collective-permute-start(bf16[384,768]{1,0:T(8,128)(2,1)S(1)} %get-tuple-element.417), channel_id=1, source_target_pairs={{0,2},{1,3},{2,0},{3,1},{4,6},{5,7},{6,4},{7,5},{8,10},{9,11},{10,... | collective-permute-start | bytes 1769480 | tf_op jit(solution)/shard_map/ppermute | solution.py:426
  255.7 4.6 convolution_convert_fusion.3.do_ref
  261.8 4.1 fusion.15
  265.9 2.1 collective-permute-start.36
  267.9 1.9 collective-permute-done.33
  273.7 33.5 %attention_backward.3 = (bf16[1024,256]{1,0:T(8,128)(2,1)}, f32[2,1024,256]{2,1,0:T(8,128)}, bf16[2,1024,256]{2,1,0:T(8,128)(2,1)}) custom-call(s32[10]{0:T(128)} %pad_add_fusion.3.info, bf16[1024,768]{1,0:T(8,128)(2,1)} %copy-done.1, bf16[1024,256]{1,0:T(8,128)(2,1)} %get-tuple-element.227.ext_ref, bf16[1024,768]{1,0:T(8,128)(2,1)} %convolution_convert_fusion.3.do_ref, ...), custom_call_target="tpu_custom_call" | custom-call | flops 2684354560 | bytes 6291456 | tf_op jit(solution)/shard_map/attention_backward/pallas_call | solution.py:299
  307.4 2.3 collective-permute-start.32
  312.0 7.8 %collective-permute-done.37 = bf16[96,3840]{1,0:T(8,128)(2,1)} collective-permute-done((bf16[96,3840]{1,0:T(8,128)(2,1)}, bf16[96,3840]{1,0:T(8,128)(2,1)}, u32[]{:S(2)}, u32[]{:S(2)}) %collective-permute-start.37) | collective-permute-done | bytes 737312 | tf_op jit(solution)/shard_map/ppermute | solution.py:426
  319.8 1.7 add_convert_fusion.5
  322.3 33.8 %attention_backward.4 = (bf16[1024,256]{1,0:T(8,128)(2,1)}, f32[2,1024,256]{2,1,0:T(8,128)}, bf16[2,1024,256]{2,1,0:T(8,128)(2,1)}) custom-call(s32[10]{0:T(128)} %pad_add_fusion.3.info, bf16[1024,768]{1,0:T(8,128)(2,1)} %copy-done, bf16[1024,256]{1,0:T(8,128)(2,1)} %get-tuple-element.247.ext_ref, bf16[1024,768]{1,0:T(8,128)(2,1)} %convolution_convert_fusion.3.do_ref, ...), custom_call_target="tpu_custom_call" | custom-call | flops 2684354560 | bytes 6291456 | tf_op jit(solution)/shard_map/attention_backward/pallas_call | solution.py:299
  356.2 1.7 add_convert_fusion.10
  358.0 5.4 %collective-permute-start.39 = (bf16[2,1024,256]{2,1,0:T(8,128)(2,1)}, bf16[2,1024,256]{2,1,0:T(8,128)(2,1)}, u32[]{:S(2)}, u32[]{:S(2)}) collective-permute-start(bf16[2,1024,256]{2,1,0:T(8,128)(2,1)} %get-tuple-element.259), channel_id=1, source_target_pairs={{0,1},{1,0},{2,3},{3,2},{4,5},{5,4},{6,7},{7,6},{8,9},{9,8},{10,11... | collective-permute-start | bytes 3145736 | tf_op jit(solution)/shard_map/ppermute | solution.py:420
  364.1 1.6 add_convert_fusion.4
  367.0 3.1 convolution_add_fusion.1
  370.2 2.2 collective-permute-start.44
  372.3 33.5 %attention_backward.5 = (bf16[1024,256]{1,0:T(8,128)(2,1)}, f32[2,1024,256]{2,1,0:T(8,128)}, bf16[2,1024,256]{2,1,0:T(8,128)(2,1)}) custom-call(s32[10]{0:T(128)} %pad_add_fusion.3.info, bf16[1024,768]{1,0:T(8,128)(2,1)} %copy-done.2, bf16[1024,256]{1,0:T(8,128)(2,1)} %get-tuple-element.267.ext_ref, bf16[1024,768]{1,0:T(8,128)(2,1)} %convolution_convert_fusion.3.do_ref, ...), custom_call_target="tpu_custom_call" | custom-call | flops 2684354560 | bytes 6291456 | tf_op jit(solution)/shard_map/attention_backward/pallas_call | solution.py:299
  407.4 1.6 add_convert_fusion.3
  416.1 2.6 add_convert_fusion
  421.8 6.8 %convolution_convert_fusion.2 = bf16[768,2304]{1,0:T(8,128)(2,1)S(1)} fusion(bf16[1024,768]{1,0:T(8,128)(2,1)S(1)} %copy-done.50, bf16[1024,2304]{1,0:T(8,128)(2,1)} %constant_dynamic-update-slice_fusion.8), kind=kOutput, calls=%fused_computation.22 | convolution fusion | flops 3625648128 | bytes 9830400 | tf_op jit(solution)/shard_map/dot_general | solution.py:387
  429.1 1.8 add_convert_fusion.7
  430.9 1.5 collective-permute-start.49
  434.1 7.8 %collective-permute-done.49 = bf16[48,3840]{1,0:T(8,128)(2,1)S(1)} collective-permute-done((bf16[48,3840]{1,0:T(8,128)(2,1)S(1)}, bf16[48,3840]{1,0:T(8,128)(2,1)S(1)}, u32[]{:S(2)}, u32[]{:S(2)}) %collective-permute-start.49) | collective-permute-done | bytes 368672 | tf_op jit(solution)/shard_map/ppermute | solution.py:423
  442.6 12.4 %collective-permute-start.50 = (bf16[96,2432]{1,0:T(8,128)(2,1)S(1)}, bf16[96,2432]{1,0:T(8,128)(2,1)S(1)}, u32[]{:S(2)}, u32[]{:S(2)}) collective-permute-start(bf16[96,2432]{1,0:T(8,128)(2,1)S(1)} %get-tuple-element.290), channel_id=1, source_target_pairs={{0,2},{1,3},{2,0},{3,1},{4,6},{5,7},{6,4},{7,5},{8,10},{9,11},{10,... | collective-permute-start | bytes 1400840 | tf_op jit(solution)/shard_map/ppermute | solution.py:426
  457.2 3.2 collective-permute-start.57
  460.4 4.7 collective-permute-done.50
  465.9 6.0 %collective-permute-done.55 = bf16[256,768]{1,0:T(8,128)(2,1)} collective-permute-done((bf16[256,768]{1,0:T(8,128)(2,1)}, bf16[256,768]{1,0:T(8,128)(2,1)}, u32[]{:S(2)}, u32[]{:S(2)}) %collective-permute-start.55) | collective-permute-done | bytes 393248 | tf_op jit(solution)/shard_map/ppermute | solution.py:423
  471.9 15.3 %collective-permute-done.56 = bf16[256,768]{1,0:T(8,128)(2,1)} collective-permute-done((bf16[256,768]{1,0:T(8,128)(2,1)}, bf16[256,768]{1,0:T(8,128)(2,1)}, u32[]{:S(2)}, u32[]{:S(2)}) %collective-permute-start.56) | collective-permute-done | bytes 393248 | tf_op jit(solution)/shard_map/ppermute | solution.py:423
  488.7 1.6 fusion.27
  490.4 6.6 %collective-permute-start.53 = (bf16[48,2432]{1,0:T(8,128)(2,1)S(1)}, bf16[48,2432]{1,0:T(8,128)(2,1)S(1)}, u32[]{:S(2)}, u32[]{:S(2)}) collective-permute-start(bf16[48,2432]{1,0:T(8,128)(2,1)S(1)} %dynamic-slice_bitcast_fusion.10), channel_id=1, source_target_pairs={{0,8},{8,0},{16,24},{24,16},{1,9},{9,1},{17,25},{25,17},{2,10},{10... | collective-permute-start | bytes 700424 | tf_op jit(solution)/shard_map/ppermute | solution.py:423
  497.2 4.2 collective-permute-done.53
  508.8 2.5 collective-permute-done.59
  511.6 1.9 maximum_convert_fusion
  513.5 4.0 collective-permute-done.60
  (392 shorter events, 83.1 us)
Async XLA Ops:
  5.0 24.9 %collective-permute-start.8 = (bf16[96,3200]{1,0:T(8,128)(2,1)}, bf16[96,3200]{1,0:T(8,128)(2,1)S(1)}, u32[]{:S(2)}, u32[]{:S(2)}) collective-permute-start(bf16[96,3200]{1,0:T(8,128)(2,1)} %pack_projection.1.refs_0_), channel_id=1, source_target_pairs={{0,2},{1,3},{2,0},{3,1},{4,6},{5,7},{6,4},{7,5},{8,10},{9,11},{10,... | collective-permute-start | bytes 1843208 | tf_op jit(solution)/shard_map/ppermute | solution.py:426
  8.0 28.8 %collective-permute-start.9 = (bf16[96,3200]{1,0:T(8,128)(2,1)}, bf16[96,3200]{1,0:T(8,128)(2,1)}, u32[]{:S(2)}, u32[]{:S(2)}) collective-permute-start(bf16[96,3200]{1,0:T(8,128)(2,1)} %pack_projection.1.refs_0_), channel_id=1, source_target_pairs={{0,4},{1,5},{2,6},{3,7},{4,0},{5,1},{6,2},{7,3},{8,12},{9,13},{10,... | collective-permute-start | bytes 1843208 | tf_op jit(solution)/shard_map/ppermute | solution.py:426
  9.5 27.3 %collective-permute-start.10 = (bf16[96,3200]{1,0:T(8,128)(2,1)}, bf16[96,3200]{1,0:T(8,128)(2,1)}, u32[]{:S(2)}, u32[]{:S(2)}) collective-permute-start(bf16[96,3200]{1,0:T(8,128)(2,1)} %pack_projection.1.refs_0_), channel_id=1, source_target_pairs={{0,6},{1,7},{2,4},{3,5},{4,2},{5,3},{6,0},{7,1},{8,14},{9,15},{10,... | collective-permute-start | bytes 1843208 | tf_op jit(solution)/shard_map/ppermute | solution.py:426
  9.5 12.2 %collective-permute-start.1 = (s32[2,512]{1,0:T(2,128)}, s32[2,512]{1,0:T(2,128)S(1)}, u32[]{:S(2)}, u32[]{:S(2)}) collective-permute-start(s32[2,512]{1,0:T(2,128)} %param.17), channel_id=1, source_target_pairs={{0,8},{8,0},{16,24},{24,16},{1,9},{9,1},{17,25},{25,17},{2,10},{10... | collective-permute-start | bytes 12296 | tf_op jit(solution)/shard_map/ppermute | solution.py:423
  11.6 5.6 %collective-permute-start.3 = (s32[2,512]{1,0:T(2,128)}, s32[2,512]{1,0:T(2,128)S(1)}, u32[]{:S(2)}, u32[]{:S(2)}) collective-permute-start(s32[2,512]{1,0:T(2,128)} %param.17), channel_id=1, source_target_pairs={{0,24},{8,16},{16,8},{24,0},{1,25},{9,17},{17,9},{25,1},{2,26},{10... | collective-permute-start | bytes 12296 | tf_op jit(solution)/shard_map/ppermute | solution.py:423
  17.2 4.5 collective-permute-start.2
  21.7 3.0 collective-permute-start
  21.8 2.2 collective-permute-start.15
  25.8 29.0 %collective-permute-start.5 = (bf16[256,768]{1,0:T(8,128)(2,1)}, bf16[256,768]{1,0:T(8,128)(2,1)S(1)}, u32[]{:S(2)}, u32[]{:S(2)}) collective-permute-start(bf16[256,768]{1,0:T(8,128)(2,1)} %get-tuple-element.164), channel_id=1, source_target_pairs={{0,16},{8,24},{16,0},{24,8},{1,17},{9,25},{17,1},{25,9},{2,18},{10... | collective-permute-start | bytes 1179656 | tf_op jit(solution)/shard_map/ppermute | solution.py:423
  26.6 28.2 %collective-permute-start.6 = (bf16[256,768]{1,0:T(8,128)(2,1)}, bf16[256,768]{1,0:T(8,128)(2,1)S(1)}, u32[]{:S(2)}, u32[]{:S(2)}) collective-permute-start(bf16[256,768]{1,0:T(8,128)(2,1)} %get-tuple-element.165), channel_id=1, source_target_pairs={{0,24},{8,16},{16,8},{24,0},{1,25},{9,17},{17,9},{25,1},{2,26},{10... | collective-permute-start | bytes 1179656 | tf_op jit(solution)/shard_map/ppermute | solution.py:423
  29.9 39.4 %copy-start.26 = (bf16[96,3200]{1,0:T(8,128)(2,1)}, bf16[96,3200]{1,0:T(8,128)(2,1)S(1)}, u32[]{:S(2)}) copy-start(bf16[96,3200]{1,0:T(8,128)(2,1)S(1)} %collective-permute-done.8.refs_1_) | copy-start | bytes 1843204
  30.0 27.8 %collective-permute-start.7 = (bf16[2,256,768]{2,1,0:T(8,128)(2,1)S(1)}, bf16[2,256,768]{2,1,0:T(8,128)(2,1)S(1)}, u32[]{:S(2)}, u32[]{:S(2)}) collective-permute-start(bf16[2,256,768]{2,1,0:T(8,128)(2,1)S(1)} %get-tuple-element.449), channel_id=1, source_target_pairs={{0,1},{1,0},{2,3},{3,2},{4,5},{5,4},{6,7},{7,6},{8,9},{9,8},{10,11... | collective-permute-start | bytes 2359304 | tf_op jit(solution)/shard_map/ppermute | solution.py:420
  54.8 12.8 %collective-permute-start.11 = (bf16[96,3200]{1,0:T(8,128)(2,1)S(1)}, bf16[96,3200]{1,0:T(8,128)(2,1)S(1)}, u32[]{:S(2)}, u32[]{:S(2)}) collective-permute-start(bf16[96,3200]{1,0:T(8,128)(2,1)S(1)} %copy-done.12), channel_id=1, source_target_pairs={{0,1},{1,0},{2,3},{3,2},{4,5},{5,4},{6,7},{7,6},{8,9},{9,8},{10,11... | collective-permute-start | bytes 1843208 | tf_op jit(solution)/shard_map/ppermute | solution.py:420
  54.9 12.8 %collective-permute-start.12 = (bf16[96,3200]{1,0:T(8,128)(2,1)S(1)}, bf16[96,3200]{1,0:T(8,128)(2,1)S(1)}, u32[]{:S(2)}, u32[]{:S(2)}) collective-permute-start(bf16[96,3200]{1,0:T(8,128)(2,1)S(1)} %collective-permute-done.8.refs_1_), channel_id=1, source_target_pairs={{0,1},{1,0},{2,3},{3,2},{4,5},{5,4},{6,7},{7,6},{8,9},{9,8},{10,11... | collective-permute-start | bytes 1843208 | tf_op jit(solution)/shard_map/ppermute | solution.py:420
  55.4 13.1 %collective-permute-start.13 = (bf16[96,3200]{1,0:T(8,128)(2,1)}, bf16[96,3200]{1,0:T(8,128)(2,1)S(1)}, u32[]{:S(2)}, u32[]{:S(2)}) collective-permute-start(bf16[96,3200]{1,0:T(8,128)(2,1)} %collective-permute-done.9.refs_2_), channel_id=1, source_target_pairs={{0,1},{1,0},{2,3},{3,2},{4,5},{5,4},{6,7},{7,6},{8,9},{9,8},{10,11... | collective-permute-start | bytes 1843208 | tf_op jit(solution)/shard_map/ppermute | solution.py:420
  55.5 13.8 %collective-permute-start.14 = (bf16[96,3200]{1,0:T(8,128)(2,1)}, bf16[96,3200]{1,0:T(8,128)(2,1)}, u32[]{:S(2)}, u32[]{:S(2)}) collective-permute-start(bf16[96,3200]{1,0:T(8,128)(2,1)} %collective-permute-done.10.refs_3_), channel_id=1, source_target_pairs={{0,1},{1,0},{2,3},{3,2},{4,5},{5,4},{6,7},{7,6},{8,9},{9,8},{10,11... | collective-permute-start | bytes 1843208 | tf_op jit(solution)/shard_map/ppermute | solution.py:420
  57.8 18.5 %collective-permute-start.4 = (bf16[256,768]{1,0:T(8,128)(2,1)}, bf16[256,768]{1,0:T(8,128)(2,1)}, u32[]{:S(2)}, u32[]{:S(2)}) collective-permute-start(bf16[256,768]{1,0:T(8,128)(2,1)} %get-tuple-element.163), channel_id=1, source_target_pairs={{0,8},{8,0},{16,24},{24,16},{1,9},{9,1},{17,25},{25,17},{2,10},{10... | collective-permute-start | bytes 1179656 | tf_op jit(solution)/shard_map/ppermute | solution.py:423
  78.9 7.1 %collective-permute-start.16 = (bf16[1024,768]{1,0:T(8,128)(2,1)S(1)}, bf16[1024,768]{1,0:T(8,128)(2,1)S(1)}, u32[]{:S(2)}, u32[]{:S(2)}) collective-permute-start(bf16[1024,768]{1,0:T(8,128)(2,1)S(1)} %multiply_convert_fusion.4.q_ref.k_own.v_own), channel_id=1, source_target_pairs={{0,1},{1,0},{2,3},{3,2},{4,5},{5,4},{6,7},{7,6},{8,9},{9,8},{10,11... | collective-permute-start | bytes 4718600 | tf_op jit(solution)/shard_map/ppermute | solution.py:420
  80.7 5.8 %collective-permute-start.17 = (bf16[1024,768]{1,0:T(8,128)(2,1)S(1)}, bf16[1024,768]{1,0:T(8,128)(2,1)S(1)}, u32[]{:S(2)}, u32[]{:S(2)}) collective-permute-start(bf16[1024,768]{1,0:T(8,128)(2,1)S(1)} %multiply_convert_fusion.3.q_ref.k_own.v_own), channel_id=1, source_target_pairs={{0,1},{1,0},{2,3},{3,2},{4,5},{5,4},{6,7},{7,6},{8,9},{9,8},{10,11... | collective-permute-start | bytes 4718600 | tf_op jit(solution)/shard_map/ppermute | solution.py:420
  82.4 6.3 %collective-permute-start.18 = (bf16[1024,768]{1,0:T(8,128)(2,1)S(1)}, bf16[1024,768]{1,0:T(8,128)(2,1)}, u32[]{:S(2)}, u32[]{:S(2)}) collective-permute-start(bf16[1024,768]{1,0:T(8,128)(2,1)S(1)} %multiply_convert_fusion.2.q_ref.k_own.v_own), channel_id=1, source_target_pairs={{0,1},{1,0},{2,3},{3,2},{4,5},{5,4},{6,7},{7,6},{8,9},{9,8},{10,11... | collective-permute-start | bytes 4718600 | tf_op jit(solution)/shard_map/ppermute | solution.py:420
  82.9 59.6 %copy-start.22 = (bf16[768,768]{1,0:T(8,128)(2,1)}, bf16[768,768]{1,0:T(8,128)(2,1)S(1)}, u32[]{:S(2)}) copy-start(bf16[768,768]{1,0:T(8,128)(2,1)S(1)} %constant_dynamic-update-slice_fusion.4.refs_0_) | copy-start | bytes 3538948
  82.9 48.6 %collective-permute-start.20 = (bf16[768,768]{1,0:T(8,128)(2,1)S(1)}, bf16[768,768]{1,0:T(8,128)(2,1)}, u32[]{:S(2)}, u32[]{:S(2)}) collective-permute-start(bf16[768,768]{1,0:T(8,128)(2,1)S(1)} %constant_dynamic-update-slice_fusion.4.refs_0_), channel_id=1, source_target_pairs={{0,2},{1,3},{2,0},{3,1},{4,6},{5,7},{6,4},{7,5},{8,10},{9,11},{10,... | collective-permute-start | bytes 3538952 | tf_op jit(solution)/shard_map/ppermute | solution.py:426
  84.5 53.2 %collective-permute-start.21 = (bf16[768,768]{1,0:T(8,128)(2,1)S(1)}, bf16[768,768]{1,0:T(8,128)(2,1)}, u32[]{:S(2)}, u32[]{:S(2)}) collective-permute-start(bf16[768,768]{1,0:T(8,128)(2,1)S(1)} %constant_dynamic-update-slice_fusion.4.refs_0_), channel_id=1, source_target_pairs={{0,4},{1,5},{2,6},{3,7},{4,0},{5,1},{6,2},{7,3},{8,12},{9,13},{10,... | collective-permute-start | bytes 3538952 | tf_op jit(solution)/shard_map/ppermute | solution.py:426
  86.0 51.7 %collective-permute-start.22 = (bf16[768,768]{1,0:T(8,128)(2,1)S(1)}, bf16[768,768]{1,0:T(8,128)(2,1)}, u32[]{:S(2)}, u32[]{:S(2)}) collective-permute-start(bf16[768,768]{1,0:T(8,128)(2,1)S(1)} %constant_dynamic-update-slice_fusion.4.refs_0_), channel_id=1, source_target_pairs={{0,6},{1,7},{2,4},{3,5},{4,2},{5,3},{6,0},{7,1},{8,14},{9,15},{10,... | collective-permute-start | bytes 3538952 | tf_op jit(solution)/shard_map/ppermute | solution.py:426
  86.5 23.6 %collective-permute-start.19 = (bf16[256,768]{1,0:T(8,128)(2,1)S(1)}, bf16[256,768]{1,0:T(8,128)(2,1)S(1)}, u32[]{:S(2)}, u32[]{:S(2)}) collective-permute-start(bf16[256,768]{1,0:T(8,128)(2,1)S(1)} %copy-done.38), channel_id=1, source_target_pairs={{0,16},{8,24},{16,0},{24,8},{1,17},{9,25},{17,1},{25,9},{2,18},{10... | collective-permute-start | bytes 1179656 | tf_op jit(solution)/shard_map/ppermute | solution.py:423
  137.7 4.8 collective-permute-start.23
  137.7 7.8 %collective-permute-start.24 = (bf16[768,768]{1,0:T(8,128)(2,1)}, bf16[768,768]{1,0:T(8,128)(2,1)}, u32[]{:S(2)}, u32[]{:S(2)}) collective-permute-start(bf16[768,768]{1,0:T(8,128)(2,1)} %collective-permute-done.20.refs_1_), channel_id=1, source_target_pairs={{0,1},{1,0},{2,3},{3,2},{4,5},{5,4},{6,7},{7,6},{8,9},{9,8},{10,11... | collective-permute-start | bytes 3538952 | tf_op jit(solution)/shard_map/ppermute | solution.py:420
  138.2 7.3 %collective-permute-start.25 = (bf16[768,768]{1,0:T(8,128)(2,1)}, bf16[768,768]{1,0:T(8,128)(2,1)}, u32[]{:S(2)}, u32[]{:S(2)}) collective-permute-start(bf16[768,768]{1,0:T(8,128)(2,1)} %collective-permute-done.21.refs_2_), channel_id=1, source_target_pairs={{0,1},{1,0},{2,3},{3,2},{4,5},{5,4},{6,7},{7,6},{8,9},{9,8},{10,11... | collective-permute-start | bytes 3538952 | tf_op jit(solution)/shard_map/ppermute | solution.py:420
  138.2 7.5 %collective-permute-start.26 = (bf16[768,768]{1,0:T(8,128)(2,1)}, bf16[768,768]{1,0:T(8,128)(2,1)}, u32[]{:S(2)}, u32[]{:S(2)}) collective-permute-start(bf16[768,768]{1,0:T(8,128)(2,1)} %collective-permute-done.22.refs_3_), channel_id=1, source_target_pairs={{0,1},{1,0},{2,3},{3,2},{4,5},{5,4},{6,7},{7,6},{8,9},{9,8},{10,11... | collective-permute-start | bytes 3538952 | tf_op jit(solution)/shard_map/ppermute | solution.py:420
  139.6 53.7 %collective-permute-start.27 = (bf16[256,768]{1,0:T(8,128)(2,1)}, bf16[256,768]{1,0:T(8,128)(2,1)S(1)}, u32[]{:S(2)}, u32[]{:S(2)}) collective-permute-start(bf16[256,768]{1,0:T(8,128)(2,1)} %get-tuple-element.232), channel_id=1, source_target_pairs={{0,8},{8,0},{16,24},{24,16},{1,9},{9,1},{17,25},{25,17},{2,10},{10... | collective-permute-start | bytes 1179656 | tf_op jit(solution)/shard_map/ppermute | solution.py:423
  143.6 49.6 %collective-permute-start.28 = (bf16[256,768]{1,0:T(8,128)(2,1)}, bf16[256,768]{1,0:T(8,128)(2,1)S(1)}, u32[]{:S(2)}, u32[]{:S(2)}) collective-permute-start(bf16[256,768]{1,0:T(8,128)(2,1)} %get-tuple-element.234), channel_id=1, source_target_pairs={{0,24},{8,16},{16,8},{24,0},{1,25},{9,17},{17,9},{25,1},{2,26},{10... | collective-permute-start | bytes 1179656 | tf_op jit(solution)/shard_map/ppermute | solution.py:423
  237.0 5.3 %collective-permute-start.29 = (bf16[4,384,768]{2,1,0:T(8,128)(2,1)}, bf16[4,384,768]{2,1,0:T(8,128)(2,1)}, u32[]{:S(2)}, u32[]{:S(2)}) collective-permute-start(bf16[4,384,768]{2,1,0:T(8,128)(2,1)} %dynamic-slice_bitcast_fusion), channel_id=1, source_target_pairs={{0,1},{1,0},{2,3},{3,2},{4,5},{5,4},{6,7},{7,6},{8,9},{9,8},{10,11... | collective-permute-start | bytes 7077896 | tf_op jit(solution)/shard_map/ppermute | solution.py:420
  242.3 19.4 %collective-permute-start.30 = (bf16[4,96,3840]{2,1,0:T(8,128)(2,1)}, bf16[4,96,3840]{2,1,0:T(8,128)(2,1)}, u32[]{:S(2)}, u32[]{:S(2)}) collective-permute-start(bf16[4,96,3840]{2,1,0:T(8,128)(2,1)} %fusion.13), channel_id=1, source_target_pairs={{0,1},{1,0},{2,3},{3,2},{4,5},{5,4},{6,7},{7,6},{8,9},{9,8},{10,11... | collective-permute-start | bytes 8847368 | tf_op jit(solution)/shard_map/ppermute | solution.py:420
  246.6 23.3 %collective-permute-start.33 = (bf16[384,768]{1,0:T(8,128)(2,1)S(1)}, bf16[384,768]{1,0:T(8,128)(2,1)S(1)}, u32[]{:S(2)}, u32[]{:S(2)}) collective-permute-start(bf16[384,768]{1,0:T(8,128)(2,1)S(1)} %get-tuple-element.417), channel_id=1, source_target_pairs={{0,2},{1,3},{2,0},{3,1},{4,6},{5,7},{6,4},{7,5},{8,10},{9,11},{10,... | collective-permute-start | bytes 1769480 | tf_op jit(solution)/shard_map/ppermute | solution.py:426
  260.3 47.0 %collective-permute-start.34 = (bf16[384,768]{1,0:T(8,128)(2,1)}, bf16[384,768]{1,0:T(8,128)(2,1)}, u32[]{:S(2)}, u32[]{:S(2)}) collective-permute-start(bf16[384,768]{1,0:T(8,128)(2,1)} %get-tuple-element.416), channel_id=1, source_target_pairs={{0,4},{1,5},{2,6},{3,7},{4,0},{5,1},{6,2},{7,3},{8,12},{9,13},{10,... | collective-permute-start | bytes 1769480 | tf_op jit(solution)/shard_map/ppermute | solution.py:426
  260.3 47.1 %collective-permute-start.35 = (bf16[384,768]{1,0:T(8,128)(2,1)}, bf16[384,768]{1,0:T(8,128)(2,1)}, u32[]{:S(2)}, u32[]{:S(2)}) collective-permute-start(bf16[384,768]{1,0:T(8,128)(2,1)} %get-tuple-element.415), channel_id=1, source_target_pairs={{0,6},{1,7},{2,4},{3,5},{4,2},{5,3},{6,0},{7,1},{8,14},{9,15},{10,... | collective-permute-start | bytes 1769480 | tf_op jit(solution)/shard_map/ppermute | solution.py:426
  265.9 46.1 %collective-permute-start.36 = (bf16[96,3840]{1,0:T(8,128)(2,1)}, bf16[96,3840]{1,0:T(8,128)(2,1)S(1)}, u32[]{:S(2)}, u32[]{:S(2)}) collective-permute-start(bf16[96,3840]{1,0:T(8,128)(2,1)} %get-tuple-element.413), channel_id=1, source_target_pairs={{0,2},{1,3},{2,0},{3,1},{4,6},{5,7},{6,4},{7,5},{8,10},{9,11},{10,... | collective-permute-start | bytes 2211848 | tf_op jit(solution)/shard_map/ppermute | solution.py:426
  267.9 51.9 %collective-permute-start.37 = (bf16[96,3840]{1,0:T(8,128)(2,1)}, bf16[96,3840]{1,0:T(8,128)(2,1)}, u32[]{:S(2)}, u32[]{:S(2)}) collective-permute-start(bf16[96,3840]{1,0:T(8,128)(2,1)} %get-tuple-element.412), channel_id=1, source_target_pairs={{0,4},{1,5},{2,6},{3,7},{4,0},{5,1},{6,2},{7,3},{8,12},{9,13},{10,... | collective-permute-start | bytes 2211848 | tf_op jit(solution)/shard_map/ppermute | solution.py:426
  269.9 49.9 %collective-permute-start.38 = (bf16[96,3840]{1,0:T(8,128)(2,1)}, bf16[96,3840]{1,0:T(8,128)(2,1)}, u32[]{:S(2)}, u32[]{:S(2)}) collective-permute-start(bf16[96,3840]{1,0:T(8,128)(2,1)} %get-tuple-element.411), channel_id=1, source_target_pairs={{0,6},{1,7},{2,4},{3,5},{4,2},{5,3},{6,0},{7,1},{8,14},{9,15},{10,... | collective-permute-start | bytes 2211848 | tf_op jit(solution)/shard_map/ppermute | solution.py:426
  307.3 62.9 %collective-permute-start.31 = (bf16[256,768]{1,0:T(8,128)(2,1)}, bf16[256,768]{1,0:T(8,128)(2,1)}, u32[]{:S(2)}, u32[]{:S(2)}) collective-permute-start(bf16[256,768]{1,0:T(8,128)(2,1)} %get-tuple-element.245), channel_id=1, source_target_pairs={{0,8},{8,0},{16,24},{24,16},{1,9},{9,1},{17,25},{25,17},{2,10},{10... | collective-permute-start | bytes 1179656 | tf_op jit(solution)/shard_map/ppermute | solution.py:423
  307.4 65.0 %collective-permute-start.32 = (bf16[256,768]{1,0:T(8,128)(2,1)}, bf16[256,768]{1,0:T(8,128)(2,1)}, u32[]{:S(2)}, u32[]{:S(2)}) collective-permute-start(bf16[256,768]{1,0:T(8,128)(2,1)} %get-tuple-element.246), channel_id=1, source_target_pairs={{0,16},{8,24},{16,0},{24,8},{1,17},{9,25},{17,1},{25,9},{2,18},{10... | collective-permute-start | bytes 1179656 | tf_op jit(solution)/shard_map/ppermute | solution.py:423
  311.9 44.2 %collective-permute-start.40 = (bf16[192,768]{1,0:T(8,128)(2,1)}, bf16[192,768]{1,0:T(8,128)(2,1)}, u32[]{:S(2)}, u32[]{:S(2)}) collective-permute-start(bf16[192,768]{1,0:T(8,128)(2,1)} %get-tuple-element.468), channel_id=1, source_target_pairs={{0,8},{8,0},{16,24},{24,16},{1,9},{9,1},{17,25},{25,17},{2,10},{10... | collective-permute-start | bytes 884744 | tf_op jit(solution)/shard_map/ppermute | solution.py:423
  319.8 38.2 %collective-permute-start.42 = (bf16[2,1024,256]{2,1,0:T(8,128)(2,1)}, bf16[2,1024,256]{2,1,0:T(8,128)(2,1)}, u32[]{:S(2)}, u32[]{:S(2)}) collective-permute-start(bf16[2,1024,256]{2,1,0:T(8,128)(2,1)} %get-tuple-element.263), channel_id=1, source_target_pairs={{0,1},{1,0},{2,3},{3,2},{4,5},{5,4},{6,7},{7,6},{8,9},{9,8},{10,11... | collective-permute-start | bytes 3145736 | tf_op jit(solution)/shard_map/ppermute | solution.py:420
  322.3 41.0 %collective-permute-start.43 = (bf16[48,3840]{1,0:T(8,128)(2,1)S(1)}, bf16[48,3840]{1,0:T(8,128)(2,1)S(1)}, u32[]{:S(2)}, u32[]{:S(2)}) collective-permute-start(bf16[48,3840]{1,0:T(8,128)(2,1)S(1)} %get-tuple-element.464), channel_id=1, source_target_pairs={{0,8},{8,0},{16,24},{24,16},{1,9},{9,1},{17,25},{25,17},{2,10},{10... | collective-permute-start | bytes 1105928 | tf_op jit(solution)/shard_map/ppermute | solution.py:423
  322.3 41.8 %copy-start.14 = (f32[2,1024,256]{2,1,0:T(8,128)S(1)}, f32[2,1024,256]{2,1,0:T(8,128)}, u32[]{:S(2)}) copy-start(f32[2,1024,256]{2,1,0:T(8,128)} %get-tuple-element.269) | copy-start | bytes 6291460
  356.1 50.2 %collective-permute-start.45 = (bf16[256,768]{1,0:T(8,128)(2,1)}, bf16[256,768]{1,0:T(8,128)(2,1)}, u32[]{:S(2)}, u32[]{:S(2)}) collective-permute-start(bf16[256,768]{1,0:T(8,128)(2,1)} %get-tuple-element.266), channel_id=1, source_target_pairs={{0,24},{8,16},{16,8},{24,0},{1,25},{9,17},{17,9},{25,1},{2,26},{10... | collective-permute-start | bytes 1179656 | tf_op jit(solution)/shard_map/ppermute | solution.py:423
  358.0 48.4 %collective-permute-start.39 = (bf16[2,1024,256]{2,1,0:T(8,128)(2,1)}, bf16[2,1024,256]{2,1,0:T(8,128)(2,1)}, u32[]{:S(2)}, u32[]{:S(2)}) collective-permute-start(bf16[2,1024,256]{2,1,0:T(8,128)(2,1)} %get-tuple-element.259), channel_id=1, source_target_pairs={{0,1},{1,0},{2,3},{3,2},{4,5},{5,4},{6,7},{7,6},{8,9},{9,8},{10,11... | collective-permute-start | bytes 3145736 | tf_op jit(solution)/shard_map/ppermute | solution.py:420
  363.3 43.0 %collective-permute-start.41 = (bf16[192,768]{1,0:T(8,128)(2,1)}, bf16[192,768]{1,0:T(8,128)(2,1)}, u32[]{:S(2)}, u32[]{:S(2)}) collective-permute-start(bf16[192,768]{1,0:T(8,128)(2,1)} %add_convert_fusion.10), channel_id=1, source_target_pairs={{0,16},{8,24},{16,0},{24,8},{1,17},{9,25},{17,1},{25,9},{2,18},{10... | collective-permute-start | bytes 884744 | tf_op jit(solution)/shard_map/ppermute | solution.py:423
  370.2 36.2 %collective-permute-start.44 = (bf16[48,3840]{1,0:T(8,128)(2,1)S(1)}, bf16[48,3840]{1,0:T(8,128)(2,1)}, u32[]{:S(2)}, u32[]{:S(2)}) collective-permute-start(bf16[48,3840]{1,0:T(8,128)(2,1)S(1)} %add_convert_fusion.8), channel_id=1, source_target_pairs={{0,16},{8,24},{16,0},{24,8},{1,17},{9,25},{17,1},{25,9},{2,18},{10... | collective-permute-start | bytes 1105928 | tf_op jit(solution)/shard_map/ppermute | solution.py:423
  405.8 8.0 %collective-permute-start.46 = (bf16[2,1024,256]{2,1,0:T(8,128)(2,1)}, bf16[2,1024,256]{2,1,0:T(8,128)(2,1)S(1)}, u32[]{:S(2)}, u32[]{:S(2)}) collective-permute-start(bf16[2,1024,256]{2,1,0:T(8,128)(2,1)} %get-tuple-element.278), channel_id=1, source_target_pairs={{0,1},{1,0},{2,3},{3,2},{4,5},{5,4},{6,7},{7,6},{8,9},{9,8},{10,11... | collective-permute-start | bytes 3145736 | tf_op jit(solution)/shard_map/ppermute | solution.py:420
  410.7 11.0 %collective-permute-start.47 = (bf16[192,768]{1,0:T(8,128)(2,1)S(1)}, bf16[192,768]{1,0:T(8,128)(2,1)S(1)}, u32[]{:S(2)}, u32[]{:S(2)}) collective-permute-start(bf16[192,768]{1,0:T(8,128)(2,1)S(1)} %add_convert_fusion.9), channel_id=1, source_target_pairs={{0,8},{8,0},{16,24},{24,16},{1,9},{9,1},{17,25},{25,17},{2,10},{10... | collective-permute-start | bytes 884744 | tf_op jit(solution)/shard_map/ppermute | solution.py:423
  429.0 3.9 collective-permute-start.48
  430.9 11.0 %collective-permute-start.49 = (bf16[48,3840]{1,0:T(8,128)(2,1)S(1)}, bf16[48,3840]{1,0:T(8,128)(2,1)S(1)}, u32[]{:S(2)}, u32[]{:S(2)}) collective-permute-start(bf16[48,3840]{1,0:T(8,128)(2,1)S(1)} %add_convert_fusion.7), channel_id=1, source_target_pairs={{0,8},{8,0},{16,24},{24,16},{1,9},{9,1},{17,25},{25,17},{2,10},{10... | collective-permute-start | bytes 1105928 | tf_op jit(solution)/shard_map/ppermute | solution.py:423
  442.6 22.5 %collective-permute-start.50 = (bf16[96,2432]{1,0:T(8,128)(2,1)S(1)}, bf16[96,2432]{1,0:T(8,128)(2,1)S(1)}, u32[]{:S(2)}, u32[]{:S(2)}) collective-permute-start(bf16[96,2432]{1,0:T(8,128)(2,1)S(1)} %get-tuple-element.290), channel_id=1, source_target_pairs={{0,2},{1,3},{2,0},{3,1},{4,6},{5,7},{6,4},{7,5},{8,10},{9,11},{10,... | collective-permute-start | bytes 1400840 | tf_op jit(solution)/shard_map/ppermute | solution.py:426
  456.0 15.9 %collective-permute-start.55 = (bf16[256,768]{1,0:T(8,128)(2,1)}, bf16[256,768]{1,0:T(8,128)(2,1)}, u32[]{:S(2)}, u32[]{:S(2)}) collective-permute-start(bf16[256,768]{1,0:T(8,128)(2,1)} %get-tuple-element.431), channel_id=1, source_target_pairs={{0,8},{8,0},{16,24},{24,16},{1,9},{9,1},{17,25},{25,17},{2,10},{10... | collective-permute-start | bytes 1179656 | tf_op jit(solution)/shard_map/ppermute | solution.py:423
  457.2 30.1 %collective-permute-start.56 = (bf16[256,768]{1,0:T(8,128)(2,1)}, bf16[256,768]{1,0:T(8,128)(2,1)}, u32[]{:S(2)}, u32[]{:S(2)}) collective-permute-start(bf16[256,768]{1,0:T(8,128)(2,1)} %get-tuple-element.430), channel_id=1, source_target_pairs={{0,16},{8,24},{16,0},{24,8},{1,17},{9,25},{17,1},{25,9},{2,18},{10... | collective-permute-start | bytes 1179656 | tf_op jit(solution)/shard_map/ppermute | solution.py:423
  457.2 30.1 %collective-permute-start.57 = (bf16[256,768]{1,0:T(8,128)(2,1)}, bf16[256,768]{1,0:T(8,128)(2,1)}, u32[]{:S(2)}, u32[]{:S(2)}) collective-permute-start(bf16[256,768]{1,0:T(8,128)(2,1)} %get-tuple-element.429), channel_id=1, source_target_pairs={{0,24},{8,16},{16,8},{24,0},{1,25},{9,17},{17,9},{25,1},{2,26},{10... | collective-permute-start | bytes 1179656 | tf_op jit(solution)/shard_map/ppermute | solution.py:423
  460.4 28.3 %collective-permute-start.51 = (bf16[96,2432]{1,0:T(8,128)(2,1)}, bf16[96,2432]{1,0:T(8,128)(2,1)}, u32[]{:S(2)}, u32[]{:S(2)}) collective-permute-start(bf16[96,2432]{1,0:T(8,128)(2,1)} %get-tuple-element.291), channel_id=1, source_target_pairs={{0,4},{1,5},{2,6},{3,7},{4,0},{5,1},{6,2},{7,3},{8,12},{9,13},{10,... | collective-permute-start | bytes 1400840 | tf_op jit(solution)/shard_map/ppermute | solution.py:426
  465.8 22.8 %collective-permute-start.52 = (bf16[96,2432]{1,0:T(8,128)(2,1)S(1)}, bf16[96,2432]{1,0:T(8,128)(2,1)}, u32[]{:S(2)}, u32[]{:S(2)}) collective-permute-start(bf16[96,2432]{1,0:T(8,128)(2,1)S(1)} %get-tuple-element.293), channel_id=1, source_target_pairs={{0,6},{1,7},{2,4},{3,5},{4,2},{5,3},{6,0},{7,1},{8,14},{9,15},{10,... | collective-permute-start | bytes 1400840 | tf_op jit(solution)/shard_map/ppermute | solution.py:426
  490.4 11.0 %collective-permute-start.53 = (bf16[48,2432]{1,0:T(8,128)(2,1)S(1)}, bf16[48,2432]{1,0:T(8,128)(2,1)S(1)}, u32[]{:S(2)}, u32[]{:S(2)}) collective-permute-start(bf16[48,2432]{1,0:T(8,128)(2,1)S(1)} %dynamic-slice_bitcast_fusion.10), channel_id=1, source_target_pairs={{0,8},{8,0},{16,24},{24,16},{1,9},{9,1},{17,25},{25,17},{2,10},{10... | collective-permute-start | bytes 700424 | tf_op jit(solution)/shard_map/ppermute | solution.py:423
  497.1 14.4 %collective-permute-start.58 = (bf16[2,256,768]{2,1,0:T(8,128)(2,1)S(1)}, bf16[2,256,768]{2,1,0:T(8,128)(2,1)S(1)}, u32[]{:S(2)}, u32[]{:S(2)}) collective-permute-start(bf16[2,256,768]{2,1,0:T(8,128)(2,1)S(1)} %pad_maximum_fusion.11), channel_id=1, source_target_pairs={{0,1},{1,0},{2,3},{3,2},{4,5},{5,4},{6,7},{7,6},{8,9},{9,8},{10,11... | collective-permute-start | bytes 2359304 | tf_op jit(solution)/shard_map/ppermute | solution.py:420
  501.4 9.9 %collective-permute-start.59 = (bf16[48,2432]{1,0:T(8,128)(2,1)S(1)}, bf16[48,2432]{1,0:T(8,128)(2,1)S(1)}, u32[]{:S(2)}, u32[]{:S(2)}) collective-permute-start(bf16[48,2432]{1,0:T(8,128)(2,1)S(1)} %fusion.33), channel_id=1, source_target_pairs={{0,16},{8,24},{16,0},{24,8},{1,17},{9,25},{17,1},{25,9},{2,18},{10... | collective-permute-start | bytes 700424 | tf_op jit(solution)/shard_map/ppermute | solution.py:423
  505.7 15.4 %collective-permute-start.54 = (bf16[2,256,768]{2,1,0:T(8,128)(2,1)}, bf16[2,256,768]{2,1,0:T(8,128)(2,1)}, u32[]{:S(2)}, u32[]{:S(2)}) collective-permute-start(bf16[2,256,768]{2,1,0:T(8,128)(2,1)} %pad_maximum_fusion.9), channel_id=1, source_target_pairs={{0,1},{1,0},{2,3},{3,2},{4,5},{5,4},{6,7},{7,6},{8,9},{9,8},{10,11... | collective-permute-start | bytes 2359304 | tf_op jit(solution)/shard_map/ppermute | solution.py:420
  511.4 6.1 %collective-permute-start.60 = (bf16[48,2432]{1,0:T(8,128)(2,1)S(1)}, bf16[48,2432]{1,0:T(8,128)(2,1)S(1)}, u32[]{:S(2)}, u32[]{:S(2)}) collective-permute-start(bf16[48,2432]{1,0:T(8,128)(2,1)S(1)} %add_convert_fusion.11), channel_id=1, source_target_pairs={{0,8},{8,0},{16,24},{24,16},{1,9},{9,1},{17,25},{25,17},{2,10},{10... | collective-permute-start | bytes 700424 | tf_op jit(solution)/shard_map/ppermute | solution.py:423
  (73 other events, 588.8 us)
